TPU v7x, 32 devices: a whole 2x2x4 slice. The times are simulated.
32 devices in a mesh: ctx: 8 (over z, x), fsdp: 4 (over y, core).
Axes of the slice: x: 2, y: 2, z: 4, core: 2. Of those that a mesh axis runs over, the one named last changes fastest.
Arguments:
- hidden: bfloat16 [8, 1024, 1024], P('fsdp', 'ctx'), may hold values from -6 to 6
- segment_ids: int32 [8, 1024], P('fsdp', 'ctx'), may hold values from 0 to 3, never falling along the last dimension, each value on 1 to 512 neighbouring positions
- cotangent: bfloat16 [8, 1024, 1024], P('fsdp', 'ctx'), may hold values from -6 to 6
- w_qkv: bfloat16 [1024, 3072], P('fsdp'), may hold values from -0.1875 to 0.1875
- w_attn_out: bfloat16 [1024, 1024], P('fsdp'), may hold values from -3 to 3
- w_in: bfloat16 [1024, 5248], P('fsdp'), may hold values from -0.1875 to 0.1875
- w_mlp_out: bfloat16 [2624, 1024], P('fsdp'), may hold values from -0.15625 to 0.15625
- gain_attn: bfloat16 [1024], P('fsdp'), may hold values from 0.099609375 to 1.8984375
- gain_mlp: bfloat16 [1024], P('fsdp'), may hold values from 0.099609375 to 1.8984375
Outputs:
- output: bfloat16 [8, 1024, 1024], P('fsdp', 'ctx')
- input_grad: float32 [8, 1024, 1024], P('fsdp', 'ctx')
- grad_w_qkv: float32 [1024, 3072], P('fsdp')
- grad_w_attn_out: float32 [1024, 1024], P('fsdp')
- grad_w_in: float32 [1024, 5248], P('fsdp')
- grad_w_mlp_out: float32 [2624, 1024], P('fsdp')
- grad_gain_attn: float32 [1024], P('fsdp')
- grad_gain_mlp: float32 [1024], P('fsdp')
Inputs may be any that keep to these rules, and one draw needn't show every extreme that they name: `segment_ids`: along each sequence the document numbers never fall; every document spans at most half of 1024 positions, and one in each sequence spans exactly that many.
All inputs are finite; a program needn't handle non-finite values.
Results may differ from a plain program's by a relative error of at most 0.024.
Values may be sent and summed in bfloat16 or wider, within the bound.
No kernel may reach another device: no remote copies, remote signals or barrier semaphores. Data moves between devices by JAX's collectives and lax.ppermute only.
A program may use at most 192 MiB of HBM per device.

v0:
```python
import jax
import jax.numpy as jnp
from jax import lax
from jax.sharding import PartitionSpec as P

HEADS = 16
MICRO = 2


rope_base = 160000.0
norm_eps = 1e-05
masked_score = -1e30


def shortened(value):
    return jax.tree.map(lambda a: a.astype(jnp.bfloat16) if a.dtype == jnp.float32 else a, value)


def norm_scale(values, gain):
    center = values - jnp.mean(values, axis=-1, keepdims=True)
    spread = jnp.mean(center * center, axis=-1, keepdims=True)
    return center * lax.rsqrt(spread + norm_eps) * gain


def rope_tables(positions, head_size):
    half = head_size // 2
    inverse = rope_base ** (-(jnp.arange(half, dtype=jnp.float32) * 2.0 / head_size))
    angles = positions.astype(jnp.float32)[:, None] * inverse[None, :]
    return (jnp.cos(angles), jnp.sin(angles))


def rotate_heads(values, cosine, sine, heads):
    shape = values.shape
    split = values.reshape(shape[:-1] + (heads, shape[-1] // heads))
    half = split.shape[-1] // 2
    first = split[..., :half]
    second = split[..., half:]
    cos_heads = cosine[:, None, :]
    sin_heads = sine[:, None, :]
    turned = jnp.concatenate(
        [first * cos_heads - second * sin_heads, second * cos_heads + first * sin_heads], axis=-1
    )
    return turned.reshape(shape)


def gated_units(values):
    units = values.shape[-1] // 2
    return jax.nn.gelu(values[..., :units], approximate=False) * values[..., units:]


def block_scores(query_heads, key_block, query_segments, segment_block, heads):
    batch, block, width = key_block.shape
    key_heads = key_block.reshape(batch, block, heads, width // heads)
    raw = jnp.einsum("bqhd,bkhd->bhqk", query_heads, key_heads, preferred_element_type=jnp.float32)
    allowed = query_segments[:, None, :, None] == segment_block[:, None, None, :]
    return jnp.where(allowed, raw, masked_score)


def attention_forward(queries, key_all, value_all, query_segments, key_segments, heads):
    batch, rows, width = queries.shape
    size = width // heads
    length = key_all.shape[1]
    block = min(512, length)
    count = length // block
    query_heads = queries.reshape(batch, rows, heads, size)

    def take(index):
        start = index * block
        return (
            lax.dynamic_slice_in_dim(key_all, start, block, 1),
            lax.dynamic_slice_in_dim(value_all, start, block, 1),
            lax.dynamic_slice_in_dim(key_segments, start, block, 1),
        )

    def stats_step(carry, index):
        running, total = carry
        key_block, value_block, segment_block = take(index)
        scores = block_scores(query_heads, key_block, query_segments, segment_block, heads)
        newest = jnp.maximum(running, jnp.max(scores, axis=-1))
        total = total * jnp.exp(running - newest) + jnp.sum(
            jnp.exp(scores - newest[..., None]), axis=-1
        )
        return ((newest, total), None)

    start_max = jnp.full((batch, heads, rows), masked_score, jnp.float32)
    start_total = jnp.zeros((batch, heads, rows), jnp.float32)
    (maximum, total), unused = lax.scan(stats_step, (start_max, start_total), jnp.arange(count))

    def value_step(carry, index):
        key_block, value_block, segment_block = take(index)
        scores = block_scores(query_heads, key_block, query_segments, segment_block, heads)
        weights = (jnp.exp(scores - maximum[..., None]) / total[..., None]).astype(jnp.bfloat16)
        value_heads = value_block.reshape(batch, block, heads, size)
        return (
            carry
            + jnp.einsum(
                "bhqk,bkhd->bqhd", weights, value_heads, preferred_element_type=jnp.float32
            ),
            None,
        )

    attended, unused = lax.scan(
        value_step, jnp.zeros((batch, rows, heads, size), jnp.float32), jnp.arange(count)
    )
    return (attended.reshape(batch, rows, width), maximum, total)


def attention_backward(
    queries, key_all, value_all, query_segments, key_segments, grad_attended, maximum, total, heads
):
    batch, rows, width = queries.shape
    size = width // heads
    length = key_all.shape[1]
    block = min(512, length)
    count = length // block
    query_heads = queries.reshape(batch, rows, heads, size)
    grad_heads = grad_attended.reshape(batch, rows, heads, size)

    def probs_block(index):
        start = index * block
        key_block = lax.dynamic_slice_in_dim(key_all, start, block, 1)
        value_block = lax.dynamic_slice_in_dim(value_all, start, block, 1)
        segment_block = lax.dynamic_slice_in_dim(key_segments, start, block, 1)
        scores = block_scores(query_heads, key_block, query_segments, segment_block, heads)
        probs = jnp.exp(scores - maximum[..., None]) / total[..., None]
        value_heads = value_block.reshape(batch, block, heads, size)
        grad_probs = jnp.einsum(
            "bqhd,bkhd->bhqk", grad_heads, value_heads, preferred_element_type=jnp.float32
        )
        return (key_block, probs, grad_probs)

    def delta_step(carry, index):
        key_block, probs, grad_probs = probs_block(index)
        return (carry + jnp.sum(probs * grad_probs, axis=-1), None)

    delta, unused = lax.scan(
        delta_step, jnp.zeros((batch, heads, rows), jnp.float32), jnp.arange(count)
    )

    def grad_step(carry, index):
        grad_query, grad_keys, grad_values = carry
        key_block, probs, grad_probs = probs_block(index)
        grad_scores = (probs * (grad_probs - delta[..., None])).astype(jnp.bfloat16)
        key_heads = key_block.reshape(batch, block, heads, size)
        grad_query = grad_query + jnp.einsum(
            "bhqk,bkhd->bqhd", grad_scores, key_heads, preferred_element_type=jnp.float32
        )
        weights = probs.astype(jnp.bfloat16)
        key_part = jnp.einsum(
            "bhqk,bqhd->bkhd", grad_scores, query_heads, preferred_element_type=jnp.float32
        )
        value_part = jnp.einsum(
            "bhqk,bqhd->bkhd", weights, grad_heads, preferred_element_type=jnp.float32
        )
        grad_keys = lax.dynamic_update_slice_in_dim(
            grad_keys, key_part.reshape(batch, block, width), index * block, 1
        )
        grad_values = lax.dynamic_update_slice_in_dim(
            grad_values, value_part.reshape(batch, block, width), index * block, 1
        )
        return ((grad_query, grad_keys, grad_values), None)

    start = (
        jnp.zeros((batch, rows, heads, size), jnp.float32),
        jnp.zeros((batch, length, width), jnp.float32),
        jnp.zeros((batch, length, width), jnp.float32),
    )
    (grad_query, grad_keys, grad_values), unused = lax.scan(grad_step, start, jnp.arange(count))
    return (grad_query.reshape(batch, rows, width), grad_keys, grad_values, delta)


def layer_pass(rows, query_segments, key_segments, cotangent, weights, cosine, sine):
    w_qkv, w_attn_out, w_in, w_mlp_out, gain_attn, gain_mlp = weights
    heads = HEADS
    width = rows.shape[-1]
    scale = (width // heads) ** (-0.5)
    rows_wide = rows.astype(jnp.float32)
    normed, norm_back = jax.vjp(norm_scale, rows_wide, gain_attn.astype(jnp.float32))
    normed_low = normed.astype(jnp.bfloat16)
    mixed = jnp.einsum("bcd,de->bce", normed_low, w_qkv, preferred_element_type=jnp.float32)

    def turn_query(values):
        return rotate_heads(values, cosine, sine, heads) * scale

    def turn_key(values):
        return rotate_heads(values, cosine, sine, heads)

    query_wide, query_back = jax.vjp(turn_query, mixed[..., :width])
    key_wide, key_back = jax.vjp(turn_key, mixed[..., width : 2 * width])
    queries = query_wide.astype(jnp.bfloat16)
    key_local = key_wide.astype(jnp.bfloat16)
    value_local = mixed[..., 2 * width :].astype(jnp.bfloat16)
    key_all, value_all = (
        lax.all_gather(key_local, "ctx", axis=1, tiled=True),
        lax.all_gather(value_local, "ctx", axis=1, tiled=True),
    )
    attended_wide, maximum, total = attention_forward(
        queries, key_all, value_all, query_segments, key_segments, heads
    )
    attended = attended_wide.astype(jnp.bfloat16)
    residual = rows_wide + jnp.einsum(
        "bcd,de->bce", attended, w_attn_out, preferred_element_type=jnp.float32
    )
    normed_mlp, norm_mlp_back = jax.vjp(norm_scale, residual, gain_mlp.astype(jnp.float32))
    normed_mlp_low = normed_mlp.astype(jnp.bfloat16)
    inner = jnp.einsum("bcd,de->bce", normed_mlp_low, w_in, preferred_element_type=jnp.float32)
    activated_wide, gated_back = jax.vjp(gated_units, inner)
    activated = activated_wide.astype(jnp.bfloat16)
    branch = jnp.einsum("bcf,fd->bcd", activated, w_mlp_out, preferred_element_type=jnp.float32)
    output = (residual + branch).astype(jnp.bfloat16)
    grad_w_mlp_out = jnp.einsum(
        "bcf,bcd->fd", activated, cotangent, preferred_element_type=jnp.float32
    )
    grad_activated = jnp.einsum(
        "bcd,fd->bcf", cotangent, w_mlp_out, preferred_element_type=jnp.float32
    )
    (grad_inner_wide,) = gated_back(grad_activated)
    grad_inner = grad_inner_wide.astype(jnp.bfloat16)
    grad_w_in = jnp.einsum(
        "bcd,bce->de", normed_mlp_low, grad_inner, preferred_element_type=jnp.float32
    )
    grad_normed_mlp = jnp.einsum(
        "bce,de->bcd", grad_inner, w_in, preferred_element_type=jnp.float32
    )
    grad_residual_part, grad_gain_mlp = norm_mlp_back(grad_normed_mlp)
    grad_residual = cotangent.astype(jnp.float32) + grad_residual_part
    grad_residual_low = grad_residual.astype(jnp.bfloat16)
    grad_w_attn_out = jnp.einsum(
        "bcd,bce->de", attended, grad_residual_low, preferred_element_type=jnp.float32
    )
    grad_attended = jnp.einsum(
        "bce,de->bcd", grad_residual_low, w_attn_out, preferred_element_type=jnp.float32
    ).astype(jnp.bfloat16)
    grad_query, grad_keys, grad_values, delta = attention_backward(
        queries,
        key_all,
        value_all,
        query_segments,
        key_segments,
        grad_attended,
        maximum,
        total,
        heads,
    )
    grad_key_local, grad_value_local = (
        lax.psum_scatter(
            grad_keys.astype(jnp.bfloat16), "ctx", scatter_dimension=1, tiled=True
        ).astype(jnp.float32),
        lax.psum_scatter(
            grad_values.astype(jnp.bfloat16), "ctx", scatter_dimension=1, tiled=True
        ).astype(jnp.float32),
    )
    (grad_query_raw,) = query_back(grad_query)
    (grad_key_raw,) = key_back(grad_key_local)
    grad_mixed = jnp.concatenate([grad_query_raw, grad_key_raw, grad_value_local], axis=-1).astype(
        jnp.bfloat16
    )
    grad_w_qkv = jnp.einsum(
        "bcd,bce->de", normed_low, grad_mixed, preferred_element_type=jnp.float32
    )
    grad_normed = jnp.einsum("bce,de->bcd", grad_mixed, w_qkv, preferred_element_type=jnp.float32)
    grad_rows_part, grad_gain_attn = norm_back(grad_normed)
    input_grad = grad_residual + grad_rows_part
    gradients = (
        grad_w_qkv,
        grad_w_attn_out,
        grad_w_in,
        grad_w_mlp_out,
        grad_gain_attn,
        grad_gain_mlp,
    )
    return (output, input_grad, gradients)


def on_device(
    hidden, segment_ids, cotangent, w_qkv, w_attn_out, w_in, w_mlp_out, gain_attn, gain_mlp
):
    shard_rows = hidden.shape[1]
    positions = lax.axis_index("ctx") * shard_rows + jnp.arange(shard_rows, dtype=jnp.int32)
    cosine, sine = rope_tables(positions, hidden.shape[2] // HEADS)
    key_segments = lax.all_gather(segment_ids, "ctx", axis=1, tiled=True)
    local_weights = (w_qkv, w_attn_out, w_in, w_mlp_out, gain_attn, gain_mlp)
    fsdp_size = lax.axis_size("fsdp")
    totals = tuple(
        (
            jnp.zeros((piece.shape[0] * fsdp_size,) + piece.shape[1:], jnp.float32)
            for piece in local_weights
        )
    )
    group = hidden.shape[0] // MICRO
    outputs = []
    input_grads = []
    for micro in range(MICRO):
        full_weights = (
            lax.all_gather(local_weights[0], "fsdp", axis=0, tiled=True),
            lax.all_gather(local_weights[1], "fsdp", axis=0, tiled=True),
            lax.all_gather(local_weights[2], "fsdp", axis=0, tiled=True),
            lax.all_gather(local_weights[3], "fsdp", axis=0, tiled=True),
            lax.all_gather(local_weights[4], "fsdp", axis=0, tiled=True),
            lax.all_gather(local_weights[5], "fsdp", axis=0, tiled=True),
        )
        lower = micro * group
        upper = lower + group
        output, input_grad, gradients = layer_pass(
            hidden[lower:upper],
            segment_ids[lower:upper],
            key_segments[lower:upper],
            cotangent[lower:upper],
            full_weights,
            cosine,
            sine,
        )
        totals = tuple((before + extra for before, extra in zip(totals, gradients)))
        outputs.append(output)
        input_grads.append(input_grad)
    shards = jax.tree.map(
        lambda part: part.astype(jnp.float32),
        lax.psum_scatter(shortened(totals), "fsdp", scatter_dimension=0, tiled=True),
    )
    summed = jax.tree.map(lambda part: part.astype(jnp.float32), lax.psum(shortened(shards), "ctx"))
    return (
        jnp.concatenate(outputs, axis=0),
        jnp.concatenate(input_grads, axis=0),
        summed[0],
        summed[1],
        summed[2],
        summed[3],
        summed[4],
        summed[5],
    )


def solution(mesh):
    in_specs = (
        P("fsdp", "ctx", None),
        P("fsdp", "ctx"),
        P("fsdp", "ctx", None),
        P("fsdp", None),
        P("fsdp", None),
        P("fsdp", None),
        P("fsdp", None),
        P("fsdp"),
        P("fsdp"),
    )
    out_specs = (
        P("fsdp", "ctx", None),
        P("fsdp", "ctx", None),
        P("fsdp", None),
        P("fsdp", None),
        P("fsdp", None),
        P("fsdp", None),
        P("fsdp"),
        P("fsdp"),
    )
    return jax.shard_map(
        on_device, mesh=mesh, in_specs=in_specs, out_specs=out_specs, check_vma=False
    )
```

profile of v0, /device:TPU:0, one launch (start us, length us, event | category | flops | bytes accessed | tf_op | source)
XLA Modules:
  0.0 1262.1 jit_solution(18199181610584061792)
XLA Ops:
  8.0 6.0 all-gather
  15.8 42.9 %all-gather.11.cloned.1.call-done = bf16[1024,3072]{1,0:T(8,128)(2,1)} async-done(((bf16[256,3072]{1,0:T(8,128)(2,1)}), bf16[1024,3072]{1,0:T(8,128)(2,1)}) %all-gather.11.cloned.1.call-update) | async-done | bytes 6291472 | tf_op jit(solution)/shard_map/all_gather | solution.py:295
  83.8 20.6 %all_gather.42 = s32[2,1024]{1,0:T(2,128)S(1)} all-gather(s32[2,128]{1,0:T(2,128)S(1)} %copy-done.115), channel_id=1, replica_groups=mesh['ctx'=8,'fsdp'=4] {'ctx'}, dimensions={1}, use_global_device_ids=true | all-gather | bytes 9216 | tf_op jit(solution)/shard_map/all_gather | solution.py:281
  104.5 5.3 all-gather.1
  109.9 19.5 %all-gather.25.cloned.1.call-done = bf16[1,1024,1024]{1,2,0:T(8,128)(2,1)} async-done(((bf16[1,128,1024]{1,2,0:T(8,128)(2,1)}), bf16[1,1024,1024]{1,2,0:T(8,128)(2,1)}) %all-gather.25.cloned.1.call-update) | async-done | bytes 2097168 | tf_op jit(solution)/shard_map/all_gather | solution.py:194
  129.4 17.1 %while.102 = (s32[]{:T(128)}, f32[1,16,128]{2,1,0:T(8,128)S(1)}, f32[1,16,128]{2,1,0:T(8,128)S(1)}, s32[1,128]{1,0:T(1,128)S(1)}, s32[2]{0:T(128)S(1)}, /*index=...) while((s32[]{:T(128)}, f32[1,16,128]{2,1,0:T(8,128)S(1)}, ...), condition=%wide.region_15.16_spmd.clone, body=%wide.region_12.0_spmd.clone.sunk | while | flops 139536384 | bytes 12106442 | solution.py:87
  146.5 33.1 %all-gather.23.cloned.1.call-done = bf16[1,1024,1024]{2,1,0:T(8,128)(2,1)} async-done(((bf16[1,128,1024]{2,1,0:T(8,128)(2,1)}), bf16[1,1024,1024]{2,1,0:T(8,128)(2,1)}) %all-gather.23.cloned.1.call-update) | async-done | bytes 2097168 | tf_op jit(solution)/shard_map/all_gather | solution.py:195
  183.5 16.4 %while.103 = (s32[]{:T(128)}, f32[1,128,16,64]{1,3,2,0:T(8,128)}, s32[2]{0:T(128)S(1)}, bf16[1,1024,1024]{1,2,0:T(8,128)(2,1)}, s32[1,128]{1,0:T(1,128)S(1)}, /*...) while((s32[]{:T(128)}, f32[1,128,16,64]{1,3,2,0:T(8,128)}, ...), condition=%wide.region_17.18_spmd.clone, body=%wide.region_16.17_spmd.clone.sunk | while | flops 272957440 | bytes 7756505 | solution.py:102
  187.7 4.0 fusion.289
  195.9 4.1 fusion.289
  201.8 27.6 %all-gather.13.cloned.1.call-done = bf16[1,1024,1024]{2,1,0:T(8,128)(2,1)} async-done(((bf16[1,128,1024]{2,1,0:T(8,128)(2,1)}), bf16[1,1024,1024]{2,1,0:T(8,128)(2,1)}) %all-gather.13.cloned.1.call-update) | async-done | bytes 2097168 | tf_op jit(solution)/shard_map/all_gather | solution.py:195
  233.3 47.6 %all-gather.15.cloned.1.call-done = bf16[1,1024,1024]{1,2,0:T(8,128)(2,1)} async-done(((bf16[1,128,1024]{1,2,0:T(8,128)(2,1)}), bf16[1,1024,1024]{1,2,0:T(8,128)(2,1)}) %all-gather.15.cloned.1.call-update) | async-done | bytes 2097168 | tf_op jit(solution)/shard_map/all_gather | solution.py:194
  280.9 17.5 %while.100 = (s32[]{:T(128)}, f32[1,16,128]{2,1,0:T(8,128)S(1)}, f32[1,16,128]{2,1,0:T(8,128)S(1)}, s32[1,128]{1,0:T(1,128)S(1)}, s32[2]{0:T(128)S(1)}, /*index=...) while((s32[]{:T(128)}, f32[1,16,128]{2,1,0:T(8,128)S(1)}, ...), condition=%wide.region_5.6_spmd.clone, body=%wide.region_2.5_spmd.clone.sunk | while | flops 139536384 | bytes 12106442 | solution.py:87
  298.4 17.7 %while.101 = (s32[]{:T(128)}, f32[1,128,16,64]{1,3,2,0:T(8,128)}, s32[2]{0:T(128)S(1)}, bf16[1,1024,1024]{1,2,0:T(8,128)(2,1)}, s32[1,128]{1,0:T(1,128)S(1)}, /*...) while((s32[]{:T(128)}, f32[1,128,16,64]{1,3,2,0:T(8,128)}, ...), condition=%wide.region_7.8_spmd.clone, body=%wide.region_6.7_spmd.clone.sunk | while | flops 272957440 | bytes 7756505 | solution.py:102
  302.8 4.0 fusion.283
  311.1 4.5 fusion.283
  322.0 54.4 %all-gather.19.cloned.1.call-done = bf16[1024,5248]{1,0:T(8,128)(2,1)} async-done(((bf16[256,5248]{1,0:T(8,128)(2,1)}), bf16[1024,5248]{1,0:T(8,128)(2,1)}) %all-gather.19.cloned.1.call-update) | async-done | bytes 10747920 | tf_op jit(solution)/shard_map/all_gather | solution.py:297
  376.4 7.5 convolution_bitcast_fusion.2
  383.8 35.3 %all-gather.21.cloned.1.call-done = bf16[2624,1024]{1,0:T(8,128)(2,1)} async-done(((bf16[656,1024]{1,0:T(8,128)(2,1)}), bf16[2624,1024]{1,0:T(8,128)(2,1)}) %all-gather.21.cloned.1.call-update) | async-done | bytes 5373968 | tf_op jit(solution)/shard_map/all_gather | solution.py:298
  419.1 8.1 fusion.114
  430.9 5.3 fusion.115
  437.9 5.5 fusion.137
  443.3 6.4 fusion.111
  454.5 10.5 while.106
  468.3 28.0 %while.107 = (s32[]{:T(128)}, f32[1,128,16,64]{1,3,2,0:T(8,128)}, bf16[1,1024,1024]{1,2,0:T(8,128)(2,1)}, bf16[1,1024,1024]{1,2,0:T(8,128)(2,1)}, s32[2]{0:T(128...) while((s32[]{:T(128)}, f32[1,128,16,64]{1,3,2,0:T(8,128)}, ...), condition=%wide.region_37.38_spmd.clone, body=%wide.region_36.37_spmd.clone.sunk | while | flops 678756352 | bytes 129137728 | solution.py:168
  496.3 10.7 copy.107
  507.0 4.4 copy.117
  514.1 11.4 while.104
  528.6 32.8 %while.105 = (s32[]{:T(128)}, f32[1,128,16,64]{1,3,2,0:T(8,128)}, bf16[1,1024,1024]{1,2,0:T(8,128)(2,1)}, bf16[1,1024,1024]{1,2,0:T(8,128)(2,1)}, s32[2]{0:T(128...) while((s32[]{:T(128)}, f32[1,128,16,64]{1,3,2,0:T(8,128)}, ...), condition=%wide.region_26.27_spmd.clone, body=%wide.region_25.26_spmd.clone.sunk | while | flops 678756352 | bytes 103971808 | solution.py:168
  561.4 10.8 copy.101
  572.2 4.4 copy.120
  578.2 7.5 copy.105
  585.7 4.3 copy.118
  591.6 7.5 copy.103
  599.1 4.4 copy.119
  610.1 4.0 add_convert_fusion.2
  617.1 32.3 %reduce-scatter.25.cloned.1.call-done = bf16[128,1024]{1,0:T(8,128)(2,1)} async-done(((bf16[1024,1024]{1,0:T(8,128)(2,1)}), bf16[128,1024]{1,0:T(8,128)(2,1)}) %reduce-scatter.25.cloned.1.call-update) | async-done | bytes 262160
  651.2 69.1 %reduce-scatter.29.cloned.1.call-done = bf16[128,1024]{1,0:T(8,128)(2,1)} async-done(((bf16[1024,1024]{1,0:T(8,128)(2,1)}), bf16[128,1024]{1,0:T(8,128)(2,1)}) %reduce-scatter.29.cloned.1.call-update) | async-done | bytes 262160
  723.6 67.0 %reduce-scatter.27.cloned.1.call-done = bf16[128,1024]{1,0:T(8,128)(2,1)} async-done(((bf16[1024,1024]{1,0:T(8,128)(2,1)}), bf16[128,1024]{1,0:T(8,128)(2,1)}) %reduce-scatter.27.cloned.1.call-update) | async-done | bytes 262160
  796.7 4.8 add_convert_fusion.1
  802.5 11.0 fusion.139
  813.5 12.7 %add_convert_fusion = bf16[1024,5248]{1,0:T(8,128)(2,1)} fusion(f32[1024,5248]{1,0:T(8,128)} %fusion.139, f32[1,128,2624]{2,1,0:T(8,128)S(1)} %copy-done.29, f32[1,128,2624]{2,1,0:T(8,128)} %get-tuple-element.1168, f32[1,128,1024]{2,1,0:T(8,128)S(1)} %copy-done.22, f32[128]{0:T(128)S(1)} %copy-done.114, f32[128]{0:T(128)S(1)} %copy-done.110, ...), kind=kOutput, calls=%fused_computation.120 | convolution fusion | flops 1388347392 | bytes 35460096 | tf_op jit(solution)/shard_map/bcd,bce->de/dot_general | solution.py:219
  826.4 52.7 %reduce-scatter.23.cloned.1.call-done = bf16[656,1024]{1,0:T(8,128)(2,1)} async-done(((bf16[2624,1024]{1,0:T(8,128)(2,1)}), bf16[656,1024]{1,0:T(8,128)(2,1)}) %reduce-scatter.23.cloned.1.call-update) | async-done | bytes 1343504 | tf_op jit(solution)/shard_map/reduce_scatter | solution.py:318
  879.1 60.8 %reduce-scatter.17.cloned.1.call-done = bf16[256,3072]{1,0:T(8,128)(2,1)} async-done(((bf16[1024,3072]{1,0:T(8,128)(2,1)}), bf16[256,3072]{1,0:T(8,128)(2,1)}) %reduce-scatter.17.cloned.1.call-update) | async-done | bytes 1572880 | tf_op jit(solution)/shard_map/reduce_scatter | solution.py:318
  939.9 89.7 %reduce-scatter.21.cloned.1.call-done = bf16[256,5248]{1,0:T(8,128)(2,1)} async-done(((bf16[1024,5248]{1,0:T(8,128)(2,1)}), bf16[256,5248]{1,0:T(8,128)(2,1)}) %reduce-scatter.21.cloned.1.call-update) | async-done | bytes 2686992 | tf_op jit(solution)/shard_map/reduce_scatter | solution.py:318
  1045.1 6.1 all-reduce.16
  1051.3 22.7 %all-reduce.14 = (bf16[256]{0:T(256)(128)(2,1)S(1)}, bf16[256]{0:T(256)(128)(2,1)S(1)}) all-reduce(bf16[256]{0:T(256)(128)(2,1)S(1)} %dynamic-slice.1, bf16[256]{0:T(256)(128)(2,1)S(1)} %dynamic-slice.3), channel_id=1, replica_groups=mesh['ctx'=8,'fsdp'=4] {'ctx'}, use_global_device_ids=true, to_apply=%region_53.54 | all-reduce | flops 512 | bytes 2048 | tf_op jit(solution)/shard_map/psum | solution.py:320
  1076.7 169.4 %all-reduce.19.cloned.1.call-done = (bf16[256,3072]{1,0:T(8,128)(2,1)}, bf16[256,1024]{1,0:T(8,128)(2,1)}, bf16[256,5248]{1,0:T(8,128)(2,1)}, bf16[656,1024]{1,0:T(8,128)(2,1)}) async-done(((bf16[256,3072]{1,0:T(8,128)(2,1)}, bf16[256,1024]{1,0:T(8,128)(2,1)}, bf16[256,5248]{1,0:T(8,128)(2,1)}, bf16[656,1024]{1,0:T(8,128)(2,1)}), (bf16[256,3072]{1,0:T(8,128)(2,1)}, bf16[256,1024]{1,0:T(8,128)(2,1)}, ...) | async-done | bytes 6127632 | tf_op jit(solution)/shard_map/psum | solution.py:320
  (583 shorter events, 235.5 us)
Async XLA Ops:
  7.2 51.5 %all-gather.11.cloned.1.call-start = ((), (), s32[]{:S(2)}) async-start(), calls=%async_computation.8 | async-start | bytes 7864320 | tf_op jit(solution)/shard_map/all_gather | solution.py:295
  7.9 121.4 %all-gather.25.cloned.1.call-start = ((), (), s32[]{:S(2)}) async-start(), calls=%async_computation.15 | async-start | bytes 2359296 | tf_op jit(solution)/shard_map/all_gather | solution.py:194
  14.0 49.7 %copy-start.78 = (f32[4,1,256]{2,1,0:T(1,128)}, f32[4,1,256]{2,1,0:T(1,128)S(1)}, u32[]{:S(2)}) copy-start(f32[4,1,256]{2,1,0:T(1,128)S(1)} %convert_element_type.286) | copy-start | bytes 12292
  14.2 48.4 %copy-start.97 = (f32[128]{0:T(128)}, f32[128]{0:T(128)S(1)}, u32[]{:S(2)}) copy-start(f32[128]{0:T(128)S(1)} %get-tuple-element.1245) | copy-start | bytes 1540
  14.2 49.5 %copy-start.101 = (f32[128]{0:T(128)}, f32[128]{0:T(128)S(1)}, u32[]{:S(2)}) copy-start(f32[128]{0:T(128)S(1)} %get-tuple-element.1244) | copy-start | bytes 1540
  14.5 48.0 %copy-start.122 = (f32[128]{0:T(128)}, f32[128]{0:T(128)S(1)}, u32[]{:S(2)}) copy-start(f32[128]{0:T(128)S(1)} %get-tuple-element.978) | copy-start | bytes 1540
  15.1 48.6 %copy-start.107 = (f32[128]{0:T(128)}, f32[128]{0:T(128)S(1)}, u32[]{:S(2)}) copy-start(f32[128]{0:T(128)S(1)} %fusion.145) | copy-start | bytes 1540
  15.1 47.5 %copy-start.103 = (f32[128]{0:T(128)}, f32[128]{0:T(128)S(1)}, u32[]{:S(2)}) copy-start(f32[128]{0:T(128)S(1)} %fusion.143) | copy-start | bytes 1540
  15.8 59.2 %copy-start.94 = (f32[128,32]{0,1:T(8,128)}, f32[128,32]{0,1:T(8,128)S(1)}, u32[]{:S(2)}) copy-start(f32[128,32]{0,1:T(8,128)S(1)} %get-tuple-element.1234) | copy-start | bytes 49156
  78.1 101.4 %all-gather.23.cloned.1.call-start = ((), (), s32[]{:S(2)}) async-start(), calls=%async_computation.14 | async-start | bytes 2359296 | tf_op jit(solution)/shard_map/all_gather | solution.py:195
  80.0 149.4 %all-gather.13.cloned.1.call-start = ((), (), s32[]{:S(2)}) async-start(), calls=%async_computation.9 | async-start | bytes 2359296 | tf_op jit(solution)/shard_map/all_gather | solution.py:195
  80.8 200.1 %all-gather.15.cloned.1.call-start = ((), (), s32[]{:S(2)}) async-start(), calls=%async_computation.10 | async-start | bytes 2359296 | tf_op jit(solution)/shard_map/all_gather | solution.py:194
  81.6 235.9 %all-gather.17.cloned.1.call-start = ((), (), s32[]{:S(2)}) async-start(), calls=%async_computation.11 | async-start | bytes 2621440 | tf_op jit(solution)/shard_map/all_gather | solution.py:296
  82.2 22.2 %copy-start.125 = (bf16[256]{0:T(256)(128)(2,1)S(1)}, bf16[256]{0:T(256)(128)(2,1)}, u32[]{:S(2)}) copy-start(bf16[256]{0:T(256)(128)(2,1)} %param.33) | copy-start | bytes 1540
  82.2 27.5 %copy-start.71 = (f32[1,128,16,32]{1,3,2,0:T(8,128)S(1)}, f32[1,128,16,32]{1,3,2,0:T(8,128)}, u32[]{:S(2)}) copy-start(f32[1,128,16,32]{1,3,2,0:T(8,128)} %get-tuple-element.1223) | copy-start | bytes 786436
  82.2 294.1 %all-gather.19.cloned.1.call-start = ((), (), s32[]{:S(2)}) async-start(), calls=%async_computation.12 | async-start | bytes 13434880 | tf_op jit(solution)/shard_map/all_gather | solution.py:297
  83.0 26.8 %copy-start.69 = (f32[1,128,16,32]{1,3,2,0:T(8,128)S(1)}, f32[1,128,16,32]{1,3,2,0:T(8,128)}, u32[]{:S(2)}) copy-start(f32[1,128,16,32]{1,3,2,0:T(8,128)} %get-tuple-element.1204) | copy-start | bytes 786436
  83.0 26.8 %copy-start.70 = (f32[1,128,16,32]{1,3,2,0:T(8,128)S(1)}, f32[1,128,16,32]{1,3,2,0:T(8,128)}, u32[]{:S(2)}) copy-start(f32[1,128,16,32]{1,3,2,0:T(8,128)} %get-tuple-element.1205) | copy-start | bytes 786436
  83.0 336.1 %all-gather.21.cloned.1.call-start = ((), (), s32[]{:S(2)}) async-start(), calls=%async_computation.13 | async-start | bytes 6717440 | tf_op jit(solution)/shard_map/all_gather | solution.py:298
  83.8 531.6 %reduce-scatter.31.cloned.1.call-start = ((), (), s32[]{:S(2)}) async-start(), calls=%async_computation.23 | async-start | bytes 2359296
  109.8 340.0 %copy-start.80 = (f32[4,1,256]{2,1,0:T(1,128)}, f32[4,1,256]{2,1,0:T(1,128)S(1)}, u32[]{:S(2)}) copy-start(f32[4,1,256]{2,1,0:T(1,128)S(1)} %convert_element_type.287) | copy-start | bytes 12292
  146.5 37.0 %copy-start.5 = (bf16[1,1024,1024]{1,2,0:T(8,128)(2,1)S(1)}, bf16[1,1024,1024]{1,2,0:T(8,128)(2,1)}, u32[]{:S(2)}) copy-start(bf16[1,1024,1024]{1,2,0:T(8,128)(2,1)} %get-tuple-element.2186) | copy-start | bytes 6291460
  320.1 129.6 %copy-start.109 = (f32[128]{0:T(128)}, f32[128]{0:T(128)S(1)}, u32[]{:S(2)}) copy-start(f32[128]{0:T(128)S(1)} %broadcast_multiply_fusion.2) | copy-start | bytes 1540
  321.0 128.8 %copy-start.99 = (f32[128]{0:T(128)}, f32[128]{0:T(128)S(1)}, u32[]{:S(2)}) copy-start(f32[128]{0:T(128)S(1)} %broadcast_multiply_fusion.4) | copy-start | bytes 1540
  321.9 127.8 %copy-start.113 = (f32[128]{0:T(128)}, f32[128]{0:T(128)S(1)}, u32[]{:S(2)}) copy-start(f32[128]{0:T(128)S(1)} %fusion.146) | copy-start | bytes 1540
  322.0 127.8 %copy-start.105 = (f32[128]{0:T(128)}, f32[128]{0:T(128)S(1)}, u32[]{:S(2)}) copy-start(f32[128]{0:T(128)S(1)} %fusion.144) | copy-start | bytes 1540
  376.4 42.8 %copy-start.47 = (bf16[2,128,1024]{2,1,0:T(8,128)(2,1)S(1)}, bf16[2,128,1024]{2,1,0:T(8,128)(2,1)}, u32[]{:S(2)}) copy-start(bf16[2,128,1024]{2,1,0:T(8,128)(2,1)} %param.27) | copy-start | bytes 1572868
  419.1 9.8 copy-start.4
  428.9 8.9 copy-start.28
  511.4 138.0 %reduce-scatter.25.cloned.1.call-start = ((), (), s32[]{:S(2)}) async-start(), calls=%async_computation.20 | async-start | bytes 2359296
  576.6 143.7 %reduce-scatter.29.cloned.1.call-start = ((), (), s32[]{:S(2)}) async-start(), calls=%async_computation.22 | async-start | bytes 2359296
  590.0 200.6 %reduce-scatter.27.cloned.1.call-start = ((), (), s32[]{:S(2)}) async-start(), calls=%async_computation.21 | async-start | bytes 2359296
  603.5 222.8 %reduce-scatter.19.cloned.1.call-start = ((), (), s32[]{:S(2)}) async-start(), calls=%async_computation.17 | async-start | bytes 2621440 | tf_op jit(solution)/shard_map/reduce_scatter | solution.py:318
  607.3 271.8 %reduce-scatter.23.cloned.1.call-start = ((), (), s32[]{:S(2)}) async-start(), calls=%async_computation.19 | async-start | bytes 6717440 | tf_op jit(solution)/shard_map/reduce_scatter | solution.py:318
  614.2 325.7 %reduce-scatter.17.cloned.1.call-start = ((), (), s32[]{:S(2)}) async-start(), calls=%async_computation.16 | async-start | bytes 7864320 | tf_op jit(solution)/shard_map/reduce_scatter | solution.py:318
  617.1 179.5 %copy-start.63 = (bf16[1,128,1024]{1,2,0:T(8,128)(2,1)}, bf16[1,128,1024]{1,2,0:T(8,128)(2,1)S(1)}, u32[]{:S(2)}) copy-start(bf16[1,128,1024]{1,2,0:T(8,128)(2,1)S(1)} %copy.108) | copy-start | bytes 786436
  721.5 71.3 %copy-start.95 = (f32[128,32]{0,1:T(8,128)S(1)}, f32[128,32]{0,1:T(8,128)}, u32[]{:S(2)}) copy-start(f32[128,32]{0,1:T(8,128)} %copy-done.94) | copy-start | bytes 49156
  721.5 71.3 %copy-start.96 = (f32[128,32]{0,1:T(8,128)S(1)}, f32[128,32]{0,1:T(8,128)}, u32[]{:S(2)}) copy-start(f32[128,32]{0,1:T(8,128)} %get-tuple-element.1235) | copy-start | bytes 49156
  801.4 12.1 copy-start.22
  801.5 12.1 copy-start.29
  801.5 12.0 copy-start.110
  801.5 12.0 copy-start.114
  801.5 228.1 %reduce-scatter.21.cloned.1.call-start = ((), (), s32[]{:S(2)}) async-start(), calls=%async_computation.18 | async-start | bytes 13434880 | tf_op jit(solution)/shard_map/reduce_scatter | solution.py:318
  826.3 419.8 %all-reduce.19.cloned.1.call-start = ((), (), s32[]{:S(2)}) async-start(), calls=%async_computation.24 | async-start | bytes 12255232 | tf_op jit(solution)/shard_map/psum | solution.py:320
  1044.4 30.7 %copy-start.51 = (f32[1,128,1024]{2,1,0:T(8,128)S(1)}, f32[1,128,1024]{2,1,0:T(8,128)}, u32[]{:S(2)}) copy-start(f32[1,128,1024]{2,1,0:T(8,128)} %copy-done.50) | copy-start | bytes 1572868
  1044.4 30.7 %copy-start.53 = (f32[1,128,1024]{2,1,0:T(8,128)S(1)}, f32[1,128,1024]{2,1,0:T(8,128)}, u32[]{:S(2)}) copy-start(f32[1,128,1024]{2,1,0:T(8,128)} %copy-done.52) | copy-start | bytes 1572868
  1044.4 30.7 %copy-start.117 = (f32[128]{0:T(128)S(1)}, f32[128]{0:T(128)}, u32[]{:S(2)}) copy-start(f32[128]{0:T(128)} %copy-done.116) | copy-start | bytes 1540
  1044.4 30.7 %copy-start.119 = (f32[128]{0:T(128)S(1)}, f32[128]{0:T(128)}, u32[]{:S(2)}) copy-start(f32[128]{0:T(128)} %copy-done.118) | copy-start | bytes 1540
  (119 other events, 289.1 us)
Sparse Core Ops, SparseCore 0:
  9.6 49.0 all-gather.10
  78.3 51.0 all-gather.24
  132.1 47.4 all-gather.22
  181.6 47.7 all-gather.12
  231.3 49.5 all-gather.14
  282.3 20.7 all-gather.16
  304.6 71.6 all-gather.18
  377.9 41.1 all-gather.20
  511.5 67.7 reduce-scatter.30
  582.7 66.7 reduce-scatter.24
  653.5 66.7 reduce-scatter.28
  723.7 66.8 reduce-scatter.26
  793.1 30.4 reduce-scatter.18
  826.8 52.2 reduce-scatter.22
  881.4 58.3 reduce-scatter.16
  942.5 86.9 reduce-scatter.20
  1034.8 211.1 all-reduce.18
where the time goes:
time: 1270 us; the launch traced here: 1260 us
  waiting for transfers between devices  804 us (63%)
  matrix products  167 us (13%)
  local copies, waits for them, and re-layouts  157 us (12%)
  blocking collectives  60.6 us (5%)
  other arithmetic  43.5 us (3%)
  between operations  16.5 us (1%)
    reduce_scatter x4, waiting for transfers between devices, on_device(): lax.psum_scatter(shortened(totals), 'fsdp', scatter_dimension=0, tiled=True)  203 us
    unnamed x21, waiting for transfers between devices  171 us
    psum x1, waiting for transfers between devices, on_device(): lax.psum(shortened(shards), 'ctx')  169 us
    unnamed x247, local copies, waits for them, and re-layouts  85 us
    all_gather x2, waiting for transfers between devices, layer_pass(): lax.all_gather(key_local, 'ctx', axis=1, tiled=True)  67 us
    all_gather x2, waiting for transfers between devices, layer_pass(): lax.all_gather(value_local, 'ctx', axis=1, tiled=True)  60.7 us
    all_gather x1, waiting for transfers between devices, on_device(): lax.all_gather(local_weights[2], 'fsdp', axis=0, tiled=True)  54.4 us
    all_gather x1, waiting for transfers between devices, on_device(): lax.all_gather(local_weights[0], 'fsdp', axis=0, tiled=True)  42.9 us
  transfers between devices with their start and end apart: 17, of which 14 were waited for; matrix products, arithmetic and copies ran while one was open for 18% of the time, Pallas kernels for 0%

commit v1 on v0

v1 whole, which is shorter than its diff:
```python
import functools

import jax
import jax.numpy as jnp
from jax import lax
from jax.experimental import pallas as pl
from jax.experimental.pallas import tpu as pltpu
from jax.sharding import PartitionSpec as P

HEADS = 16
rope_base = 160000.0
norm_eps = 1e-05
masked_score = -1e30
bf16 = jnp.bfloat16
f32 = jnp.float32
NT = (((1,), (1,)), ((), ()))
NN = (((1,), (0,)), ((), ()))
TN = (((0,), (0,)), ((), ()))


def mm(a, b, dims=NN):
    return lax.dot_general(a, b, dims, preferred_element_type=f32)


def head_mask(shape, head, size):
    return lax.broadcasted_iota(jnp.int32, shape, 1) // size == head


def attend_kernel(q_ref, k_ref, v_ref, sq_ref, sk_ref, o_ref, *, heads):
    q, k, v = q_ref[0], k_ref[0], v_ref[0]
    size = q.shape[1] // heads
    allowed = sq_ref[0] == sk_ref[0]
    total = jnp.zeros(q.shape, f32)
    for head in range(heads):
        here = head_mask(q.shape, head, size)
        scores = mm(jnp.where(here, q, jnp.zeros_like(q)), k, NT)
        scores = jnp.where(allowed, scores, masked_score)
        weights = jnp.exp(scores - jnp.max(scores, axis=1, keepdims=True))
        row = mm(weights.astype(bf16), v) / jnp.sum(weights, axis=1, keepdims=True)
        total = jnp.where(here, row, total)
    o_ref[0] = total.astype(bf16)


def attend(q, k, v, segments, heads):
    n, length, width = q.shape
    block = min(256, length)
    rows = pl.BlockSpec((1, block, width), lambda i, j: (i, j, 0))
    whole = pl.BlockSpec((1, length, width), lambda i, j: (i, 0, 0))
    return pl.pallas_call(
        functools.partial(attend_kernel, heads=heads),
        grid=(n, length // block),
        in_specs=[
            rows,
            whole,
            whole,
            pl.BlockSpec((1, block, 1), lambda i, j: (i, j, 0)),
            pl.BlockSpec((1, 1, length), lambda i, j: (i, 0, 0)),
        ],
        out_specs=rows,
        out_shape=jax.ShapeDtypeStruct(q.shape, bf16),
        compiler_params=pltpu.CompilerParams(vmem_limit_bytes=40 << 20),
        name="attend",
    )(q, k, v, segments[:, :, None], segments[:, None, :])


def attend_back_kernel(
    q_ref, g_ref, k_ref, v_ref, sq_ref, sk_ref, dq_ref, dk_ref, dv_ref, kt, dqt, *, heads
):
    step = pl.program_id(1)
    q, g, k, v = q_ref[0], g_ref[0], k_ref[0], v_ref[0]
    size = q.shape[1] // heads

    @pl.when(step == 0)
    def _():
        kt[...] = k.T
        dk_ref[...] = jnp.zeros_like(dk_ref)
        dv_ref[...] = jnp.zeros_like(dv_ref)

    allowed = sk_ref[0] == sq_ref[0]
    zero = jnp.zeros_like(q)
    for head in range(heads):
        here = head_mask(q.shape, head, size)
        own_q, own_g = jnp.where(here, q, zero), jnp.where(here, g, zero)
        scores = jnp.where(allowed, mm(k, own_q, NT), masked_score)
        weights = jnp.exp(scores - jnp.max(scores, axis=0, keepdims=True))
        probs = weights * (1.0 / jnp.sum(weights, axis=0, keepdims=True))
        grad = mm(v, own_g, NT)
        delta = jnp.sum(probs * grad, axis=0, keepdims=True)
        grad = (probs * (grad - delta)).astype(bf16)
        dv_ref[0] += mm(probs.astype(bf16), own_g)
        dk_ref[0] += mm(grad, own_q)
        dqt[pl.ds(head * size, size), :] = mm(kt[pl.ds(head * size, size), :], grad)
    dq_ref[0] = dqt[...].T


def attend_back(q, k, v, g, segments, heads):
    n, length, width = q.shape
    block = min(256, length)
    rows = pl.BlockSpec((1, block, width), lambda i, j: (i, j, 0))
    whole = pl.BlockSpec((1, length, width), lambda i, j: (i, 0, 0))
    return pl.pallas_call(
        functools.partial(attend_back_kernel, heads=heads),
        grid=(n, length // block),
        in_specs=[
            rows,
            rows,
            whole,
            whole,
            pl.BlockSpec((1, 1, block), lambda i, j: (i, 0, j)),
            pl.BlockSpec((1, length, 1), lambda i, j: (i, 0, 0)),
        ],
        out_specs=[rows, whole, whole],
        out_shape=[jax.ShapeDtypeStruct(q.shape, f32)] * 3,
        scratch_shapes=[pltpu.VMEM((width, length), bf16), pltpu.VMEM((width, block), f32)],
        compiler_params=pltpu.CompilerParams(vmem_limit_bytes=48 << 20),
        name="attend_back",
    )(q, g, k, v, segments[:, None, :], segments[:, :, None])


def swap_halves(values, heads):
    shape = values.shape
    split = values.reshape(shape[:-1] + (heads, 2, shape[-1] // heads // 2))
    return jnp.concatenate([-split[..., 1:, :], split[..., :1, :]], axis=-2).reshape(shape)


def on_device(
    hidden, segment_ids, cotangent, w_qkv, w_attn_out, w_in, w_mlp_out, gain_attn, gain_mlp
):
    fsdp, ctx = lax.axis_size("fsdp"), lax.axis_size("ctx")
    f, c = lax.axis_index("fsdp"), lax.axis_index("ctx")
    batch, span, width = hidden.shape
    pieces = ctx // fsdp
    n = batch // pieces
    own = n * pieces * span
    length = span * ctx
    heads = HEADS // fsdp
    size = width // HEADS
    cols = heads * size
    units = w_mlp_out.shape[0]
    rows = w_in.shape[0]
    both = ("ctx", "fsdp")

    def route(j):
        pairs = []
        for cc in range(ctx):
            for ff in range(fsdp):
                to_c, to_f = pieces * ff + (cc + j) % pieces, cc // pieces
                pairs.append((cc * fsdp + ff, to_c * fsdp + to_f))
        return pairs

    def deal(values):
        parts = []
        for j in range(pieces):
            part = lax.dynamic_slice_in_dim(values, (c + j) % pieces * n, n, 0)
            parts.append(lax.ppermute(part, both, route(j)))
        return jnp.stack(parts, axis=1)

    def undeal(values):
        out = jnp.zeros((batch,) + values.shape[2:], values.dtype)
        for j in range(pieces):
            part = lax.ppermute(values[:, j], both, [(b, a) for a, b in route(j)])
            out = lax.dynamic_update_slice_in_dim(out, part, (c + j) % pieces * n, 0)
        return out

    def partner(values, bit):
        return lax.ppermute(values, "fsdp", [(i, i ^ bit) for i in range(fsdp)])

    bits = []
    bit = fsdp // 2
    while bit:
        bits.append(bit)
        bit //= 2
    order = [0]
    for bit in bits:
        order = order + [o ^ bit for o in order]

    def collect(values):
        stack = values[None]
        for bit in bits:
            stack = jnp.concatenate([stack, partner(stack, bit)], axis=0)
        return stack

    def reduce(stack):
        for bit in reversed(bits):
            half = stack.shape[0] // 2
            got = partner(stack[half:], bit)
            stack = (stack[:half].astype(f32) + got.astype(f32)).astype(
                bf16 if half > 1 else f32
            )
        return stack[0]

    def to_sequences(stack):
        feat = stack.shape[-1]
        parts = stack.reshape(fsdp, n, pieces * span, feat)
        return jnp.swapaxes(parts, 0, 1).reshape(n, length, feat)

    def from_sequences(values):
        feat = values.shape[-1]
        parts = values.reshape(n, fsdp, pieces * span, feat)
        return jnp.swapaxes(parts, 0, 1).reshape(fsdp, own, feat)

    blocks = [
        (f ^ o) * pieces + (c % pieces - j) % pieces for o in order for j in range(pieces)
    ]
    positions = (jnp.stack(blocks)[:, None] * span + jnp.arange(span)[None, :]).reshape(length)
    everyone = lax.all_gather(segment_ids, both).reshape(ctx, fsdp, batch, span)
    everyone = everyone.transpose(1, 2, 0, 3).reshape(fsdp * batch, ctx, span)
    everyone = lax.dynamic_slice_in_dim(everyone, c * n, n, 0)
    segments = jnp.concatenate(
        [lax.dynamic_slice_in_dim(everyone, b, 1, 1) for b in blocks], axis=1
    ).reshape(n, length)
    half = size // 2
    inverse = rope_base ** (-(jnp.arange(half, dtype=f32) * 2.0 / size))
    angles = positions.astype(f32)[:, None] * jnp.tile(inverse, 2 * heads)[None, :]
    cosine, sine = jnp.cos(angles), jnp.sin(angles)
    scale = size**-0.5

    hidden_own = deal(hidden).reshape(own, width)
    cot_own = deal(cotangent).reshape(own, width)

    gain_a, gain_m = gain_attn.astype(f32)[:, None], gain_mlp.astype(f32)[:, None]
    qkv_rows = (w_qkv.astype(f32) * gain_a).astype(bf16).reshape(rows, 3, fsdp, cols)
    in_rows = (w_in.astype(f32) * gain_m).astype(bf16).reshape(rows, 2, fsdp, units)

    def to_columns(parts):
        feat = parts.shape[1] * parts.shape[3]
        out = jnp.zeros((fsdp * rows, feat), bf16)
        for o in range(fsdp):
            part = lax.dynamic_slice_in_dim(parts, f ^ o, 1, 2).reshape(rows, feat)
            if o:
                part = lax.ppermute(part, "fsdp", [(i, i ^ o) for i in range(fsdp)])
            out = lax.dynamic_update_slice_in_dim(out, part, (f ^ o) * rows, 0)
        return out

    def to_rows(total, groups):
        feat = total.shape[-1]
        small = total.shape[0] // (fsdp * ctx)
        parts = total.astype(bf16).reshape(fsdp, ctx, small, feat).transpose(1, 0, 2, 3)
        parts = lax.psum_scatter(parts, "ctx", scatter_dimension=0, tiled=False)
        parts = lax.all_to_all(parts, "fsdp", 0, 0, tiled=True)
        parts = parts.reshape(fsdp, small, groups, feat // groups).transpose(1, 2, 0, 3)
        parts = parts.reshape(small, fsdp * feat)
        return lax.all_gather(parts, "ctx", axis=0, tiled=True).astype(f32)

    w_qkv_cols = to_columns(qkv_rows)
    w_in_cols = to_columns(in_rows)

    def normalise(values):
        center = values - jnp.mean(values, axis=-1, keepdims=True)
        rate = lax.rsqrt(jnp.mean(center * center, axis=-1, keepdims=True) + norm_eps)
        return center * rate, rate

    def norm_back(grad, unit, rate):
        return rate * (
            grad
            - jnp.mean(grad, axis=-1, keepdims=True)
            - unit * jnp.mean(grad * unit, axis=-1, keepdims=True)
        )

    hidden_wide = hidden_own.astype(f32)
    unit1, rate1 = normalise(hidden_wide)
    unit1_all = to_sequences(collect(unit1.astype(bf16))).reshape(n * length, width)
    cot_all = collect(cot_own).reshape(fsdp * own, width)

    mixed = mm(unit1_all, w_qkv_cols).reshape(n, length, 3 * cols)
    q_wide, k_wide = mixed[..., :cols], mixed[..., cols : 2 * cols]
    q = ((q_wide * cosine + swap_halves(q_wide, heads) * sine) * scale).astype(bf16)
    k = (k_wide * cosine + swap_halves(k_wide, heads) * sine).astype(bf16)
    v = mixed[..., 2 * cols :].astype(bf16)
    attended = attend(q, k, v, segments, heads).reshape(n * length, cols)

    partial = from_sequences(mm(attended, w_attn_out).astype(bf16).reshape(n, length, width))
    residual = hidden_wide + reduce(partial)
    unit2, rate2 = normalise(residual)
    unit2_all = collect(unit2.astype(bf16)).reshape(fsdp * own, width)

    inner = mm(unit2_all, w_in_cols)
    act, gate = inner[:, :units], inner[:, units:]
    phi = 0.5 * (1.0 + lax.erf(act * (2.0**-0.5)))
    activated = (act * phi * gate).astype(bf16)
    output = residual + reduce(mm(activated, w_mlp_out).astype(bf16).reshape(fsdp, own, width))

    grad_activated = mm(cot_all, w_mlp_out, NT)
    density = jnp.exp(-0.5 * act * act) * (2.0 * jnp.pi) ** -0.5
    grad_inner = jnp.concatenate(
        [grad_activated * gate * (phi + act * density), grad_activated * act * phi], axis=1
    ).astype(bf16)
    sum_mlp_out = mm(activated, cot_all, TN)
    sum_in = mm(unit2_all, grad_inner, TN)
    u2 = reduce(mm(grad_inner, w_in_cols, NT).astype(bf16).reshape(fsdp, own, width))
    grad_residual = cot_own.astype(f32) + norm_back(u2, unit2, rate2)
    grad_low = to_sequences(collect(grad_residual.astype(bf16))).reshape(n * length, width)

    sum_attn_out = mm(attended, grad_low, TN)
    grad_attended = mm(grad_low, w_attn_out, NT).astype(bf16).reshape(n, length, cols)
    dq, dk, dv = attend_back(q, k, v, grad_attended, segments, heads)
    dq = (dq * cosine - swap_halves(dq * sine, heads)) * scale
    dk = dk * cosine - swap_halves(dk * sine, heads)
    grad_mixed = jnp.concatenate([dq, dk, dv], axis=-1).astype(bf16).reshape(n * length, 3 * cols)
    sum_qkv = mm(unit1_all, grad_mixed, TN)
    u1 = from_sequences(
        mm(grad_mixed, w_qkv_cols, NT).astype(bf16).reshape(n, length, width)
    )
    input_grad = grad_residual + norm_back(reduce(u1), unit1, rate1)

    out = undeal(output.astype(bf16).reshape(n, pieces, span, width))
    back = undeal(input_grad.astype(bf16).reshape(n, pieces, span, width)).astype(f32)

    def over_ctx(total):
        return lax.psum(total.astype(bf16), "ctx").astype(f32)

    grad_mlp_out = over_ctx(sum_mlp_out)
    grad_attn_out = over_ctx(sum_attn_out)
    sum_in_rows = to_rows(sum_in, 2)
    sum_qkv_rows = to_rows(sum_qkv, 3)
    return (
        out,
        back,
        sum_qkv_rows * gain_a,
        grad_attn_out,
        sum_in_rows * gain_m,
        grad_mlp_out,
        jnp.sum(sum_qkv_rows * w_qkv.astype(f32), axis=1),
        jnp.sum(sum_in_rows * w_in.astype(f32), axis=1),
    )


def solution(mesh):
    in_specs = (
        P("fsdp", "ctx", None),
        P("fsdp", "ctx"),
        P("fsdp", "ctx", None),
        P("fsdp", None),
        P("fsdp", None),
        P("fsdp", None),
        P("fsdp", None),
        P("fsdp"),
        P("fsdp"),
    )
    out_specs = (
        P("fsdp", "ctx", None),
        P("fsdp", "ctx", None),
        P("fsdp", None),
        P("fsdp", None),
        P("fsdp", None),
        P("fsdp", None),
        P("fsdp"),
        P("fsdp"),
    )
    return jax.shard_map(
        on_device, mesh=mesh, in_specs=in_specs, out_specs=out_specs, check_vma=False
    )
```

time: 1270 us -> 721 us (0.57)
  the two profiles are of different devices: /device:TPU:0 before, /device:TPU:17 now
where the time goes in v1:
time: 721 us; the launch traced here: 711 us
  waiting for transfers between devices  420 us (58%)
  local copies, waits for them, and re-layouts  65.7 us (9%)
  other arithmetic  58.1 us (8%)
  blocking collectives  48.7 us (7%)
  starting transfers between devices  38.9 us (5%)
  matrix products  34.5 us (5%)
  Pallas kernels  29.6 us (4%)
  between operations  15.5 us (2%)
    psum x1, waiting for transfers between devices, over_ctx(): return lax.psum(total.astype(bf16), 'ctx').astype(f32)  162 us
    ppermute x16, waiting for transfers between devices, partner(): return lax.ppermute(values, 'fsdp', [(i, i ^ bit) for i in range(fsdp)])  78.1 us
    ppermute x4, waiting for transfers between devices, undeal(): part = lax.ppermute(values[:, j], both, [(b, a) for a, b in route(j)])  69.2 us
    reduce_scatter x1, waiting for transfers between devices, to_rows(): parts = lax.psum_scatter(parts, 'ctx', scatter_dimension=0, tiled=False)  43.9 us
    ppermute x4, waiting for transfers between devices, deal(): parts.append(lax.ppermute(part, both, route(j)))  39.4 us
    all_gather x1, blocking collectives, on_device(): everyone = lax.all_gather(segment_ids, both).reshape(ctx, fsdp, batch, span)  38.9 us
    dot_general x12, matrix products, mm(): return lax.dot_general(a, b, dims, preferred_element_type=f32)  34.5 us
    ppermute x6, waiting for transfers between devices, to_columns(): part = lax.ppermute(part, 'fsdp', [(i, i ^ o) for i in range(fsdp)])  26.8 us
  transfers between devices with their start and end apart: 35, of which 24 were waited for; matrix products, arithmetic and copies ran while one was open for 11% of the time, Pallas kernels for 0%

profile of v1, /device:TPU:17, one launch (start us, length us, event | category | flops | bytes accessed | tf_op | source)
XLA Modules:
  0.0 711.0 jit_solution(2826554866971136040)
XLA Ops:
  9.2 3.6 collective-permute-start
  16.5 15.2 %collective-permute-done = bf16[1,128,1024]{2,1,0:T(8,128)(2,1)S(1)} collective-permute-done((bf16[1,128,1024]{2,1,0:T(8,128)(2,1)}, bf16[1,128,1024]{2,1,0:T(8,128)(2,1)S(1)}, u32[]{:S(2)}, u32[]{:S(2)}) %collective-permute-start) | collective-permute-done | bytes 262176 | tf_op jit(solution)/shard_map/ppermute | solution.py:155
  31.7 6.5 collective-permute-done.1
  45.9 8.2 %collective-permute-done.2 = bf16[1,256,1024]{2,1,0:T(8,128)(2,1)} collective-permute-done((bf16[1,256,1024]{2,1,0:T(8,128)(2,1)}, bf16[1,256,1024]{2,1,0:T(8,128)(2,1)}, u32[]{:S(2)}, u32[]{:S(2)}) %collective-permute-start.2) | collective-permute-done | bytes 524320 | tf_op jit(solution)/shard_map/ppermute | solution.py:166
  55.5 38.9 %all-gather.1 = s32[32,2,128]{2,1,0:T(2,128)S(1)} all-gather(s32[1,2,128]{2,1,0:T(2,128)S(1)} %bitcast.247), channel_id=2, replica_groups=mesh['ctx'=8,'fsdp'=4] {'ctx','fsdp'}, dimensions={0}, use_global_device_ids=true | all-gather | bytes 33792 | tf_op jit(solution)/shard_map/all_gather | solution.py:206
  110.9 5.7 fusion.27
  116.7 9.0 %attend.1 = bf16[1,1024,256]{2,1,0:T(8,128)(2,1)S(1)} custom-call(bf16[1,1024,256]{2,1,0:T(8,128)(2,1)S(1)} %get-tuple-element.45.q_ref, bf16[1,1024,256]{2,1,0:T(8,128)(2,1)S(1)} %get-tuple-element.44.k_ref, bf16[1,1024,256]{2,1,0:T(8,128)(2,1)S(1)} %slice.233.v_ref, s32[1,1024,1]{2,1,0:T(8,128)S(1)} %copy.66.sq_ref.sk_ref, s32[1,1,1024]{2,1,0:T(1,128)S(1)} %bitcast.180), custom_call_target="tpu_custom_call" | custom-call | tf_op jit(solution)/shard_map/attend/pallas_call | solution.py:49
  132.4 3.2 collective-permute-start.18
  136.6 4.6 copy.67
  141.2 14.1 %collective-permute-done.18 = bf16[1,128,1024]{2,1,0:T(8,128)(2,1)} collective-permute-done((bf16[1,128,1024]{2,1,0:T(8,128)(2,1)}, bf16[1,128,1024]{2,1,0:T(8,128)(2,1)}, u32[]{:S(2)}, u32[]{:S(2)}) %collective-permute-start.18) | collective-permute-done | bytes 262176 | tf_op jit(solution)/shard_map/ppermute | solution.py:155
  155.3 3.6 collective-permute-done.19
  169.3 4.1 collective-permute-done.20
  175.0 9.6 %collective-permute-done.9 = bf16[1,256,1024]{2,1,0:T(8,128)(2,1)S(1)} collective-permute-done((bf16[1,256,1024]{2,1,0:T(8,128)(2,1)S(1)}, bf16[1,256,1024]{2,1,0:T(8,128)(2,1)S(1)}, u32[]{:S(2)}, u32[]{:S(2)}) %collective-permute-start.9) | collective-permute-done | bytes 524320 | tf_op jit(solution)/shard_map/ppermute | solution.py:166
  186.8 12.2 %collective-permute-done.12 = bf16[256,1312]{0,1:T(8,128)(2,1)S(1)} collective-permute-done((bf16[256,1312]{0,1:T(8,128)(2,1)S(1)}, bf16[256,1312]{0,1:T(8,128)(2,1)S(1)}, u32[]{:S(2)}, u32[]{:S(2)}) %collective-permute-start.12) | collective-permute-done | bytes 671776 | tf_op jit(solution)/shard_map/ppermute | solution.py:231
  199.1 14.6 %collective-permute-done.13 = bf16[256,1312]{0,1:T(8,128)(2,1)S(1)} collective-permute-done((bf16[256,1312]{0,1:T(8,128)(2,1)S(1)}, bf16[256,1312]{0,1:T(8,128)(2,1)S(1)}, u32[]{:S(2)}, u32[]{:S(2)}) %collective-permute-start.13) | collective-permute-done | bytes 671776 | tf_op jit(solution)/shard_map/ppermute | solution.py:231
  214.2 3.0 fusion.71
  217.3 3.9 fusion.9
  221.2 3.8 convolution_convert_fusion.1
  225.4 2.5 collective-permute-done.22
  228.5 13.4 %collective-permute-done.23 = bf16[1,256,1024]{2,1,0:T(8,128)(2,1)S(1)} collective-permute-done((bf16[1,256,1024]{2,1,0:T(8,128)(2,1)S(1)}, bf16[1,256,1024]{2,1,0:T(8,128)(2,1)S(1)}, u32[]{:S(2)}, u32[]{:S(2)}) %collective-permute-start.23) | collective-permute-done | bytes 524320 | tf_op jit(solution)/shard_map/ppermute | solution.py:166
  244.5 2.5 add_convert_fusion
  247.0 12.5 %collective-permute-done.24 = bf16[1,256,1024]{2,1,0:T(8,128)(2,1)S(1)} collective-permute-done((bf16[1,256,1024]{2,1,0:T(8,128)(2,1)S(1)}, bf16[1,256,1024]{2,1,0:T(8,128)(2,1)S(1)}, u32[]{:S(2)}, u32[]{:S(2)}) %collective-permute-start.24) | collective-permute-done | bytes 524320 | tf_op jit(solution)/shard_map/ppermute | solution.py:166
  265.4 20.6 %attend_back.1 = (f32[1,1024,256]{2,1,0:T(8,128)S(1)}, f32[1,1024,256]{2,1,0:T(8,128)S(1)}, f32[1,1024,256]{2,1,0:T(8,128)S(1)}) custom-call(bf16[1,1024,256]{2,1,0:T(8,128)(2,1)S(1)} %get-tuple-element.45.q_ref, bf16[1,1024,256]{2,1,0:T(8,128)(2,1)S(1)} %fusion.22.g_ref, bf16[1,1024,256]{2,1,0:T(8,128)(2,1)S(1)} %get-tuple-element.44.k_ref, ...), custom_call_target="tpu_custom_call" | custom-call | tf_op jit(solution)/shard_map/attend_back/pallas_call | solution.py:101
  286.0 4.5 fusion.19
  295.1 2.7 copy.70
  299.3 5.4 fusion.50
  308.9 5.9 convolution_convert_fusion
  314.8 4.7 copy.76
  319.5 4.1 convolution_convert_fusion.6
  325.2 43.9 %reduce-scatter.3.cloned.1.call-done = bf16[1,4,32,768]{3,2,1,0:T(8,128)(2,1)} async-done(((bf16[8,4,32,768]{3,2,1,0:T(8,128)(2,1)}), bf16[1,4,32,768]{3,2,1,0:T(8,128)(2,1)}) %reduce-scatter.3.cloned.1.call-update) | async-done | bytes 196624 | tf_op jit(solution)/shard_map/reduce_scatter | solution.py:239
  369.1 9.8 %all_to_all.10 = bf16[4,32,768]{2,1,0:T(8,128)(2,1)S(1)} all-to-all(bf16[4,32,768]{2,1,0:T(8,128)(2,1)} %bitcast.244), channel_id=1, replica_groups=mesh['ctx'=8,'fsdp'=4] {'fsdp'}, dimensions={0} | all-to-all | bytes 393216 | tf_op jit(solution)/shard_map/all_to_all | solution.py:240
  384.5 161.7 %all-reduce.4.cloned.1.call-done = (bf16[256,1024]{1,0:T(8,128)(2,1)}, bf16[8,4,32,1312]{3,2,0,1:T(8,128)(2,1)}, bf16[656,1024]{1,0:T(8,128)(2,1)}) async-done(((bf16[256,1024]{1,0:T(8,128)(2,1)}, bf16[8,4,32,1312]{3,2,0,1:T(8,128)(2,1)}, bf16[656,1024]{1,0:T(8,128)(2,1)}), (bf16[256,1024]{1,0:T(8,128)(2,1)}, bf16[8,4,32,1312]{3,2,0,1:T(8,128)(2,1)}, ...) | async-done | bytes 4554768 | tf_op jit(solution)/shard_map/psum | solution.py:310
  548.6 4.1 all-to-all-start.1
  552.9 5.0 convolution_convert_fusion.3
  567.2 11.6 %collective-permute-done.15 = bf16[1,256,1024]{2,1,0:T(8,128)(2,1)S(1)} collective-permute-done((bf16[1,256,1024]{2,1,0:T(8,128)(2,1)S(1)}, bf16[1,256,1024]{2,1,0:T(8,128)(2,1)S(1)}, u32[]{:S(2)}, u32[]{:S(2)}) %collective-permute-start.15) | collective-permute-done | bytes 524320 | tf_op jit(solution)/shard_map/ppermute | solution.py:166
  579.0 11.0 %collective-permute-done.27 = bf16[1,256,1024]{2,1,0:T(8,128)(2,1)S(1)} collective-permute-done((bf16[1,256,1024]{2,1,0:T(8,128)(2,1)S(1)}, bf16[1,256,1024]{2,1,0:T(8,128)(2,1)S(1)}, u32[]{:S(2)}, u32[]{:S(2)}) %collective-permute-start.27) | collective-permute-done | bytes 524320 | tf_op jit(solution)/shard_map/ppermute | solution.py:166
  594.5 3.7 collective-permute-start.29
  600.2 2.6 collective-permute-start.17
  602.8 34.0 %collective-permute-done.28 = bf16[1,128,1024]{2,1,0:T(8,128)(2,1)S(1)} collective-permute-done((bf16[1,128,1024]{2,1,0:T(8,128)(2,1)S(1)}, bf16[1,128,1024]{2,1,0:T(8,128)(2,1)S(1)}, u32[]{:S(2)}, u32[]{:S(2)}) %collective-permute-start.28) | collective-permute-done | bytes 262176 | tf_op jit(solution)/shard_map/ppermute | solution.py:161
  636.9 6.9 collective-permute-done.29
  644.9 11.6 %collective-permute-done.16 = bf16[1,128,1024]{2,1,0:T(8,128)(2,1)S(1)} collective-permute-done((bf16[1,128,1024]{2,1,0:T(8,128)(2,1)S(1)}, bf16[1,128,1024]{2,1,0:T(8,128)(2,1)S(1)}, u32[]{:S(2)}, u32[]{:S(2)}) %collective-permute-start.16) | collective-permute-done | bytes 262176 | tf_op jit(solution)/shard_map/ppermute | solution.py:161
  656.6 16.7 %collective-permute-done.17 = bf16[1,128,1024]{2,1,0:T(8,128)(2,1)S(1)} collective-permute-done((bf16[1,128,1024]{2,1,0:T(8,128)(2,1)S(1)}, bf16[1,128,1024]{2,1,0:T(8,128)(2,1)S(1)}, u32[]{:S(2)}, u32[]{:S(2)}) %collective-permute-start.17) | collective-permute-done | bytes 262176 | tf_op jit(solution)/shard_map/ppermute | solution.py:161
  676.3 2.6 copy.75
  678.9 4.4 fusion.3
  683.3 3.5 copy.79
  686.8 4.5 copy.78
  691.3 6.8 fusion.1
  698.0 6.0 copy.80
  (258 shorter events, 102.6 us)
Async XLA Ops:
  7.2 210.1 %copy-start = (bf16[656,1024]{1,0:T(8,128)(2,1)S(1)}, bf16[656,1024]{1,0:T(8,128)(2,1)}, u32[]{:S(2)}) copy-start(bf16[656,1024]{1,0:T(8,128)(2,1)} %param.15) | copy-start | bytes 4030468
  7.2 361.9 %reduce-scatter.3.cloned.1.call-start = ((), (), s32[]{:S(2)}) async-start(), calls=%async_computation.3 | async-start | bytes 1769472 | tf_op jit(solution)/shard_map/reduce_scatter | solution.py:239
  9.2 22.5 %collective-permute-start = (bf16[1,128,1024]{2,1,0:T(8,128)(2,1)}, bf16[1,128,1024]{2,1,0:T(8,128)(2,1)S(1)}, u32[]{:S(2)}, u32[]{:S(2)}) collective-permute-start(bf16[1,128,1024]{2,1,0:T(8,128)(2,1)} %get-tuple-element.90), channel_id=1, source_target_pairs={{0,0},{1,8},{2,16},{3,24},{4,4},{5,12},{6,20},{7,28},{8,1},{9,9},{... | collective-permute-start | bytes 786440 | tf_op jit(solution)/shard_map/ppermute | solution.py:155
  12.8 25.4 %collective-permute-start.1 = (bf16[1,128,1024]{2,1,0:T(8,128)(2,1)}, bf16[1,128,1024]{2,1,0:T(8,128)(2,1)S(1)}, u32[]{:S(2)}, u32[]{:S(2)}) collective-permute-start(bf16[1,128,1024]{2,1,0:T(8,128)(2,1)} %get-tuple-element.91), channel_id=1, source_target_pairs={{0,4},{1,12},{2,20},{3,28},{4,0},{5,8},{6,16},{7,24},{8,5},{9,13},... | collective-permute-start | bytes 786440 | tf_op jit(solution)/shard_map/ppermute | solution.py:155
  16.5 24.8 %copy-start.17 = (bf16[256,3072]{0,1:T(8,128)(2,1)}, bf16[256,3072]{0,1:T(8,128)(2,1)S(1)}, u32[]{:S(2)}) copy-start(bf16[256,3072]{0,1:T(8,128)(2,1)S(1)} %copy.59) | copy-start | bytes 4718596
  39.7 14.3 %collective-permute-start.2 = (bf16[1,256,1024]{2,1,0:T(8,128)(2,1)}, bf16[1,256,1024]{2,1,0:T(8,128)(2,1)}, u32[]{:S(2)}, u32[]{:S(2)}) collective-permute-start(bf16[1,256,1024]{2,1,0:T(8,128)(2,1)} %fusion.45), channel_id=1, source_target_pairs={{0,2},{1,3},{2,0},{3,1},{4,6},{5,7},{6,4},{7,5},{8,10},{9,11},{10,... | collective-permute-start | bytes 1572872 | tf_op jit(solution)/shard_map/ppermute | solution.py:166
  41.2 14.3 %copy-start.41 = (s32[2,128]{1,0:T(2,128)S(1)}, s32[2,128]{1,0:T(2,128)}, u32[]{:S(2)}) copy-start(s32[2,128]{1,0:T(2,128)} %param.10) | copy-start | bytes 3076
  43.6 51.5 %collective-permute-start.4 = (bf16[256,768]{0,1:T(8,128)(2,1)}, bf16[256,768]{0,1:T(8,128)(2,1)}, u32[]{:S(2)}, u32[]{:S(2)}) collective-permute-start(bf16[256,768]{0,1:T(8,128)(2,1)} %bitcast.8), channel_id=1, source_target_pairs={{0,1},{1,0},{2,3},{3,2},{4,5},{5,4},{6,7},{7,6},{8,9},{9,8},{10,11... | collective-permute-start | bytes 1179656 | tf_op jit(solution)/shard_map/ppermute | solution.py:231
  43.7 52.5 %collective-permute-start.5 = (bf16[256,768]{0,1:T(8,128)(2,1)}, bf16[256,768]{0,1:T(8,128)(2,1)}, u32[]{:S(2)}, u32[]{:S(2)}) collective-permute-start(bf16[256,768]{0,1:T(8,128)(2,1)} %bitcast.9), channel_id=1, source_target_pairs={{0,2},{1,3},{2,0},{3,1},{4,6},{5,7},{6,4},{7,5},{8,10},{9,11},{10,... | collective-permute-start | bytes 1179656 | tf_op jit(solution)/shard_map/ppermute | solution.py:231
  45.1 52.1 %collective-permute-start.6 = (bf16[256,768]{0,1:T(8,128)(2,1)}, bf16[256,768]{0,1:T(8,128)(2,1)}, u32[]{:S(2)}, u32[]{:S(2)}) collective-permute-start(bf16[256,768]{0,1:T(8,128)(2,1)} %bitcast.10), channel_id=1, source_target_pairs={{0,3},{1,2},{2,1},{3,0},{4,7},{5,6},{6,5},{7,4},{8,11},{9,10},{10,... | collective-permute-start | bytes 1179656 | tf_op jit(solution)/shard_map/ppermute | solution.py:231
  55.3 43.0 %collective-permute-start.3 = (bf16[2,256,1024]{2,1,0:T(8,128)(2,1)S(1)}, bf16[2,256,1024]{2,1,0:T(8,128)(2,1)}, u32[]{:S(2)}, u32[]{:S(2)}) collective-permute-start(bf16[2,256,1024]{2,1,0:T(8,128)(2,1)S(1)} %pad_maximum_fusion.8), channel_id=1, source_target_pairs={{0,1},{1,0},{2,3},{3,2},{4,5},{5,4},{6,7},{7,6},{8,9},{9,8},{10,11... | collective-permute-start | bytes 3145736 | tf_op jit(solution)/shard_map/ppermute | solution.py:166
  126.6 2.7 collective-permute-start.7
  131.6 28.5 %collective-permute-start.8 = (bf16[1,256,1024]{2,1,0:T(8,128)(2,1)}, bf16[1,256,1024]{2,1,0:T(8,128)(2,1)}, u32[]{:S(2)}, u32[]{:S(2)}) collective-permute-start(bf16[1,256,1024]{2,1,0:T(8,128)(2,1)} %slice.163), channel_id=1, source_target_pairs={{0,2},{1,3},{2,0},{3,1},{4,6},{5,7},{6,4},{7,5},{8,10},{9,11},{10,... | collective-permute-start | bytes 1572872 | tf_op jit(solution)/shard_map/ppermute | solution.py:166
  132.4 22.9 %collective-permute-start.18 = (bf16[1,128,1024]{2,1,0:T(8,128)(2,1)}, bf16[1,128,1024]{2,1,0:T(8,128)(2,1)}, u32[]{:S(2)}, u32[]{:S(2)}) collective-permute-start(bf16[1,128,1024]{2,1,0:T(8,128)(2,1)} %get-tuple-element.86), channel_id=1, source_target_pairs={{0,0},{1,8},{2,16},{3,24},{4,4},{5,12},{6,20},{7,28},{8,1},{9,9},{... | collective-permute-start | bytes 786440 | tf_op jit(solution)/shard_map/ppermute | solution.py:155
  135.6 23.2 %collective-permute-start.19 = (bf16[1,128,1024]{2,1,0:T(8,128)(2,1)}, bf16[1,128,1024]{2,1,0:T(8,128)(2,1)}, u32[]{:S(2)}, u32[]{:S(2)}) collective-permute-start(bf16[1,128,1024]{2,1,0:T(8,128)(2,1)} %get-tuple-element.87), channel_id=1, source_target_pairs={{0,4},{1,12},{2,20},{3,28},{4,0},{5,8},{6,16},{7,24},{8,5},{9,13},... | collective-permute-start | bytes 786440 | tf_op jit(solution)/shard_map/ppermute | solution.py:155
  141.2 20.5 %copy-start.9 = (bf16[1,128,1024]{2,1,0:T(8,128)(2,1)S(1)}, bf16[1,128,1024]{2,1,0:T(8,128)(2,1)}, u32[]{:S(2)}) copy-start(bf16[1,128,1024]{2,1,0:T(8,128)(2,1)} %copy-done.8) | copy-start | bytes 786436
  141.2 20.5 %copy-start.12 = (bf16[1,128,1024]{2,1,0:T(8,128)(2,1)S(1)}, bf16[1,128,1024]{2,1,0:T(8,128)(2,1)}, u32[]{:S(2)}) copy-start(bf16[1,128,1024]{2,1,0:T(8,128)(2,1)} %copy-done.11) | copy-start | bytes 786436
  141.2 20.5 %copy-start.16 = (bf16[2,256,1024]{2,1,0:T(8,128)(2,1)S(1)}, bf16[2,256,1024]{2,1,0:T(8,128)(2,1)}, u32[]{:S(2)}) copy-start(bf16[2,256,1024]{2,1,0:T(8,128)(2,1)} %copy-done.15) | copy-start | bytes 3145732
  159.9 13.4 %collective-permute-start.20 = (bf16[1,256,1024]{2,1,0:T(8,128)(2,1)S(1)}, bf16[1,256,1024]{2,1,0:T(8,128)(2,1)S(1)}, u32[]{:S(2)}, u32[]{:S(2)}) collective-permute-start(bf16[1,256,1024]{2,1,0:T(8,128)(2,1)S(1)} %bitcast.206), channel_id=1, source_target_pairs={{0,2},{1,3},{2,0},{3,1},{4,6},{5,7},{6,4},{7,5},{8,10},{9,11},{10,... | collective-permute-start | bytes 1572872 | tf_op jit(solution)/shard_map/ppermute | solution.py:166
  164.6 20.0 %collective-permute-start.9 = (bf16[1,256,1024]{2,1,0:T(8,128)(2,1)S(1)}, bf16[1,256,1024]{2,1,0:T(8,128)(2,1)S(1)}, u32[]{:S(2)}, u32[]{:S(2)}) collective-permute-start(bf16[1,256,1024]{2,1,0:T(8,128)(2,1)S(1)} %fusion.48), channel_id=1, source_target_pairs={{0,2},{1,3},{2,0},{3,1},{4,6},{5,7},{6,4},{7,5},{8,10},{9,11},{10,... | collective-permute-start | bytes 1572872 | tf_op jit(solution)/shard_map/ppermute | solution.py:166
  166.8 19.9 %collective-permute-start.11 = (bf16[256,1312]{0,1:T(8,128)(2,1)S(1)}, bf16[256,1312]{0,1:T(8,128)(2,1)S(1)}, u32[]{:S(2)}, u32[]{:S(2)}) collective-permute-start(bf16[256,1312]{0,1:T(8,128)(2,1)S(1)} %bitcast.243), channel_id=1, source_target_pairs={{0,1},{1,0},{2,3},{3,2},{4,5},{5,4},{6,7},{7,6},{8,9},{9,8},{10,11... | collective-permute-start | bytes 2015240 | tf_op jit(solution)/shard_map/ppermute | solution.py:231
  167.6 31.4 %collective-permute-start.12 = (bf16[256,1312]{0,1:T(8,128)(2,1)S(1)}, bf16[256,1312]{0,1:T(8,128)(2,1)S(1)}, u32[]{:S(2)}, u32[]{:S(2)}) collective-permute-start(bf16[256,1312]{0,1:T(8,128)(2,1)S(1)} %bitcast.242), channel_id=1, source_target_pairs={{0,2},{1,3},{2,0},{3,1},{4,6},{5,7},{6,4},{7,5},{8,10},{9,11},{10,... | collective-permute-start | bytes 2015240 | tf_op jit(solution)/shard_map/ppermute | solution.py:231
  167.6 46.1 %collective-permute-start.13 = (bf16[256,1312]{0,1:T(8,128)(2,1)S(1)}, bf16[256,1312]{0,1:T(8,128)(2,1)S(1)}, u32[]{:S(2)}, u32[]{:S(2)}) collective-permute-start(bf16[256,1312]{0,1:T(8,128)(2,1)S(1)} %bitcast.241), channel_id=1, source_target_pairs={{0,3},{1,2},{2,1},{3,0},{4,7},{5,6},{6,5},{7,4},{8,11},{9,10},{10,... | collective-permute-start | bytes 2015240 | tf_op jit(solution)/shard_map/ppermute | solution.py:231
  173.5 40.3 %collective-permute-start.21 = (bf16[2,256,1024]{2,1,0:T(8,128)(2,1)S(1)}, bf16[2,256,1024]{2,1,0:T(8,128)(2,1)S(1)}, u32[]{:S(2)}, u32[]{:S(2)}) collective-permute-start(bf16[2,256,1024]{2,1,0:T(8,128)(2,1)S(1)} %pad_maximum_fusion.12), channel_id=1, source_target_pairs={{0,1},{1,0},{2,3},{3,2},{4,5},{5,4},{6,7},{7,6},{8,9},{9,8},{10,11... | collective-permute-start | bytes 3145736 | tf_op jit(solution)/shard_map/ppermute | solution.py:166
  184.7 29.3 %collective-permute-start.10 = (bf16[2,256,1024]{2,1,0:T(8,128)(2,1)S(1)}, bf16[2,256,1024]{2,1,0:T(8,128)(2,1)S(1)}, u32[]{:S(2)}, u32[]{:S(2)}) collective-permute-start(bf16[2,256,1024]{2,1,0:T(8,128)(2,1)S(1)} %pad_maximum_fusion.11), channel_id=1, source_target_pairs={{0,1},{1,0},{2,3},{3,2},{4,5},{5,4},{6,7},{7,6},{8,9},{9,8},{10,11... | collective-permute-start | bytes 3145736 | tf_op jit(solution)/shard_map/ppermute | solution.py:166
  225.2 2.7 collective-permute-start.22
  228.4 13.4 %collective-permute-start.23 = (bf16[1,256,1024]{2,1,0:T(8,128)(2,1)S(1)}, bf16[1,256,1024]{2,1,0:T(8,128)(2,1)S(1)}, u32[]{:S(2)}, u32[]{:S(2)}) collective-permute-start(bf16[1,256,1024]{2,1,0:T(8,128)(2,1)S(1)} %slice.175), channel_id=1, source_target_pairs={{0,2},{1,3},{2,0},{3,1},{4,6},{5,7},{6,4},{7,5},{8,10},{9,11},{10,... | collective-permute-start | bytes 1572872 | tf_op jit(solution)/shard_map/ppermute | solution.py:166
  247.0 12.5 %collective-permute-start.24 = (bf16[1,256,1024]{2,1,0:T(8,128)(2,1)S(1)}, bf16[1,256,1024]{2,1,0:T(8,128)(2,1)S(1)}, u32[]{:S(2)}, u32[]{:S(2)}) collective-permute-start(bf16[1,256,1024]{2,1,0:T(8,128)(2,1)S(1)} %get-tuple-element.70), channel_id=1, source_target_pairs={{0,2},{1,3},{2,0},{3,1},{4,6},{5,7},{6,4},{7,5},{8,10},{9,11},{10,... | collective-permute-start | bytes 1572872 | tf_op jit(solution)/shard_map/ppermute | solution.py:166
  259.6 4.2 collective-permute-start.25
  308.0 238.1 %all-reduce.4.cloned.1.call-start = ((), (), s32[]{:S(2)}) async-start(), calls=%async_computation.6 | async-start | bytes 9502720 | tf_op jit(solution)/shard_map/psum | solution.py:310
  325.2 54.9 %copy-start.44 = (u32[32]{0:T(128)S(1)}, u32[32]{0:T(128)}, u32[]{:S(2)}) copy-start(u32[32]{0:T(128)} %constant.253) | copy-start | bytes 388
  325.2 55.5 %copy-start.45 = (bf16[1024,656]{0,1:T(8,128)(2,1)S(1)}, bf16[1024,656]{0,1:T(8,128)(2,1)}, u32[]{:S(2)}) copy-start(bf16[1024,656]{0,1:T(8,128)(2,1)} %get-tuple-element.43) | copy-start | bytes 4030468
  325.2 351.1 %all-gather.5.cloned.1.call-start = ((), (), s32[]{:S(2)}) async-start(), calls=%async_computation.4 | async-start | bytes 1769472 | tf_op jit(solution)/shard_map/all_gather | solution.py:243
  383.7 179.8 %collective-permute-start.14 = (bf16[2,256,1024]{2,1,0:T(8,128)(2,1)}, bf16[2,256,1024]{2,1,0:T(8,128)(2,1)}, u32[]{:S(2)}, u32[]{:S(2)}) collective-permute-start(bf16[2,256,1024]{2,1,0:T(8,128)(2,1)} %bitcast.45), channel_id=1, source_target_pairs={{0,1},{1,0},{2,3},{3,2},{4,5},{5,4},{6,7},{7,6},{8,9},{9,8},{10,11... | collective-permute-start | bytes 3145736 | tf_op jit(solution)/shard_map/ppermute | solution.py:166
  548.6 10.4 %all-to-all-start.1 = ((bf16[4,32,1312]{2,1,0:T(8,128)(2,1)}), bf16[4,32,1312]{2,1,0:T(8,128)(2,1)S(1)}, u32[]{:S(2)}, u32[]{:S(2)}) async-start(bf16[4,32,1312]{2,1,0:T(8,128)(2,1)} %dynamic-slice_bitcast_fusion), calls=%async_computation.2 | async-start | bytes 720896 | tf_op jit(solution)/shard_map/all_to_all | solution.py:240
  552.7 134.1 %all-gather.7.cloned.1.call-start = ((), (), s32[]{:S(2)}) async-start(), calls=%async_computation.5 | async-start | bytes 3022848 | tf_op jit(solution)/shard_map/all_gather | solution.py:243
  562.6 3.1 collective-permute-start.26
  565.1 13.7 %collective-permute-start.15 = (bf16[1,256,1024]{2,1,0:T(8,128)(2,1)S(1)}, bf16[1,256,1024]{2,1,0:T(8,128)(2,1)S(1)}, u32[]{:S(2)}, u32[]{:S(2)}) collective-permute-start(bf16[1,256,1024]{2,1,0:T(8,128)(2,1)S(1)} %slice.169), channel_id=1, source_target_pairs={{0,2},{1,3},{2,0},{3,1},{4,6},{5,7},{6,4},{7,5},{8,10},{9,11},{10,... | collective-permute-start | bytes 1572872 | tf_op jit(solution)/shard_map/ppermute | solution.py:166
  566.2 23.9 %copy-start.10 = (bf16[1,128,1024]{2,1,0:T(8,128)(2,1)S(1)}, bf16[1,128,1024]{2,1,0:T(8,128)(2,1)}, u32[]{:S(2)}) copy-start(bf16[1,128,1024]{2,1,0:T(8,128)(2,1)} %copy-done.8) | copy-start | bytes 786436
  566.2 23.9 %copy-start.13 = (bf16[1,128,1024]{2,1,0:T(8,128)(2,1)S(1)}, bf16[1,128,1024]{2,1,0:T(8,128)(2,1)}, u32[]{:S(2)}) copy-start(bf16[1,128,1024]{2,1,0:T(8,128)(2,1)} %copy-done.11) | copy-start | bytes 786436
  566.2 23.8 %collective-permute-start.27 = (bf16[1,256,1024]{2,1,0:T(8,128)(2,1)S(1)}, bf16[1,256,1024]{2,1,0:T(8,128)(2,1)S(1)}, u32[]{:S(2)}, u32[]{:S(2)}) collective-permute-start(bf16[1,256,1024]{2,1,0:T(8,128)(2,1)S(1)} %slice.183), channel_id=1, source_target_pairs={{0,2},{1,3},{2,0},{3,1},{4,6},{5,7},{6,4},{7,5},{8,10},{9,11},{10,... | collective-permute-start | bytes 1572872 | tf_op jit(solution)/shard_map/ppermute | solution.py:166
  579.0 11.7 %copy-start.23 = (f32[1,256,1024]{2,1,0:T(8,128)S(1)}, f32[1,256,1024]{2,1,0:T(8,128)}, u32[]{:S(2)}) copy-start(f32[1,256,1024]{2,1,0:T(8,128)} %get-tuple-element.68) | copy-start | bytes 3145732
  579.0 11.7 %copy-start.24 = (f32[1,256,1024]{2,1,0:T(8,128)S(1)}, f32[1,256,1024]{2,1,0:T(8,128)}, u32[]{:S(2)}) copy-start(f32[1,256,1024]{2,1,0:T(8,128)} %get-tuple-element.71) | copy-start | bytes 3145732
  592.6 44.2 %collective-permute-start.28 = (bf16[1,128,1024]{2,1,0:T(8,128)(2,1)S(1)}, bf16[1,128,1024]{2,1,0:T(8,128)(2,1)S(1)}, u32[]{:S(2)}, u32[]{:S(2)}) collective-permute-start(bf16[1,128,1024]{2,1,0:T(8,128)(2,1)S(1)} %get-tuple-element.85), channel_id=1, source_target_pairs={{0,0},{8,1},{16,2},{24,3},{4,4},{12,5},{20,6},{28,7},{1,8},{9,9},{... | collective-permute-start | bytes 786440 | tf_op jit(solution)/shard_map/ppermute | solution.py:161
  594.5 49.3 %collective-permute-start.29 = (bf16[1,128,1024]{2,1,0:T(8,128)(2,1)S(1)}, bf16[1,128,1024]{2,1,0:T(8,128)(2,1)S(1)}, u32[]{:S(2)}, u32[]{:S(2)}) collective-permute-start(bf16[1,128,1024]{2,1,0:T(8,128)(2,1)S(1)} %get-tuple-element.84), channel_id=1, source_target_pairs={{4,0},{12,1},{20,2},{28,3},{0,4},{8,5},{16,6},{24,7},{5,8},{13,9},... | collective-permute-start | bytes 786440 | tf_op jit(solution)/shard_map/ppermute | solution.py:161
  598.2 58.3 %collective-permute-start.16 = (bf16[1,128,1024]{2,1,0:T(8,128)(2,1)S(1)}, bf16[1,128,1024]{2,1,0:T(8,128)(2,1)S(1)}, u32[]{:S(2)}, u32[]{:S(2)}) collective-permute-start(bf16[1,128,1024]{2,1,0:T(8,128)(2,1)S(1)} %get-tuple-element.89), channel_id=1, source_target_pairs={{0,0},{8,1},{16,2},{24,3},{4,4},{12,5},{20,6},{28,7},{1,8},{9,9},{... | collective-permute-start | bytes 786440 | tf_op jit(solution)/shard_map/ppermute | solution.py:161
  600.2 73.2 %collective-permute-start.17 = (bf16[1,128,1024]{2,1,0:T(8,128)(2,1)S(1)}, bf16[1,128,1024]{2,1,0:T(8,128)(2,1)S(1)}, u32[]{:S(2)}, u32[]{:S(2)}) collective-permute-start(bf16[1,128,1024]{2,1,0:T(8,128)(2,1)S(1)} %get-tuple-element.88), channel_id=1, source_target_pairs={{4,0},{12,1},{20,2},{28,3},{0,4},{8,5},{16,6},{24,7},{5,8},{13,9},... | collective-permute-start | bytes 786440 | tf_op jit(solution)/shard_map/ppermute | solution.py:161
  636.9 36.5 %copy-start.32 = (bf16[656,1024]{1,0:T(8,128)(2,1)S(1)}, bf16[656,1024]{1,0:T(8,128)(2,1)}, u32[]{:S(2)}) copy-start(bf16[656,1024]{1,0:T(8,128)(2,1)} %get-tuple-element.40) | copy-start | bytes 4030468
  (35 other events, 133.0 us)
Sparse Core Ops, SparseCore 0:
  308.1 60.9 reduce-scatter.2
  374.2 171.9 all-reduce.3
  548.6 43.5 all-gather.4
  594.4 78.4 all-gather.6

commit v2 on v1

v2 whole, which is shorter than its diff:
```python
import functools

import jax
import jax.numpy as jnp
from jax import lax
from jax.experimental import pallas as pl
from jax.experimental.pallas import tpu as pltpu
from jax.sharding import PartitionSpec as P

HEADS = 16
rope_base = 160000.0
norm_eps = 1e-05
masked_score = -1e30
bf16 = jnp.bfloat16
f32 = jnp.float32
NT = (((1,), (1,)), ((), ()))
NN = (((1,), (0,)), ((), ()))
TN = (((0,), (0,)), ((), ()))
TAG = 16


def mm(a, b, dims=NN):
    return lax.dot_general(a, b, dims, preferred_element_type=f32)


def call(kernel, name, out_shape, grid, scratch, args, flops, limit=56):
    def spec(a):
        if isinstance(a, tuple):
            return a[1]
        if a.dtype == jnp.int32:
            return pl.BlockSpec(memory_space=pltpu.SMEM)
        return pl.BlockSpec(
            a.shape, lambda s, nd=len(a.shape): (0,) * nd, pipeline_mode=pl.Buffered(1)
        )

    specs = [spec(a) for a in args]
    args = [a[0] if isinstance(a, tuple) else a for a in args]
    moved = sum(a.size * a.dtype.itemsize for a in args)
    moved += sum(a.size * a.dtype.itemsize for a in out_shape)
    return pl.pallas_call(
        kernel,
        grid=(grid,),
        in_specs=specs,
        out_specs=[spec(a) for a in out_shape],
        out_shape=out_shape,
        scratch_shapes=scratch,
        compiler_params=pltpu.CompilerParams(vmem_limit_bytes=limit << 20),
        cost_estimate=pl.CostEstimate(
            flops=int(flops), bytes_accessed=int(moved), transcendentals=0
        ),
        name=name,
    )(*args)


def shape_of(shape, dtype=bf16):
    return jax.ShapeDtypeStruct(shape, dtype)


def head_mask(shape, head, size):
    return lax.broadcasted_iota(jnp.int32, shape, 1) // size == head


def swap(values, size):
    width, half = values.shape[1], size // 2
    if width == size:
        return jnp.concatenate([values[:, half:], values[:, :half]], axis=1)
    lane = lax.broadcasted_iota(jnp.int32, values.shape, 1) % size
    return jnp.where(
        lane < half, pltpu.roll(values, width - half, 1), pltpu.roll(values, half, 1)
    )


def norm_stats(values):
    center = values - jnp.mean(values, axis=-1, keepdims=True)
    rate = lax.rsqrt(jnp.mean(center * center, axis=-1, keepdims=True) + norm_eps)
    return center * rate, rate


def norm_back(grad, unit, rate):
    return rate * (
        grad
        - jnp.mean(grad, axis=-1, keepdims=True)
        - unit * jnp.mean(grad * unit, axis=-1, keepdims=True)
    )


class Plan:
    def __init__(self, fsdp, ctx, batch, span, width, units, rows):
        self.fsdp, self.ctx, self.span, self.width = fsdp, ctx, span, width
        self.pieces = ctx // fsdp
        self.n = batch // self.pieces
        self.part = self.pieces * span
        self.own = self.n * self.part
        self.length = span * ctx
        self.heads = HEADS // fsdp
        self.size = width // HEADS
        self.cols = self.heads * self.size
        self.units, self.rows = units, rows
        self.padded = -(-units // 256) * 256
        self.small = rows // ctx
        self.groups = 2 if self.heads % 2 == 0 else 1
        self.lanes = self.cols // self.groups
        self.slab = self.lanes // ctx
        self.table = min(128, self.cols)
        bits = [1 << b for b in range(ctx.bit_length() - 1)]
        self.order = bits

    def locations(self):
        return [
            (i, j, (i * self.pieces + j) * self.span)
            for i in range(self.n)
            for j in range(self.pieces)
        ]


def storage(x, order):
    at = 0
    for bit in order:
        at = at * 2 + x // bit % 2
    return at


def cut_kernel(qkv, w_in, gain_a, gain_m, out, *, p):
    fs, cols, units, rows, small = p.fsdp, p.cols, p.units, p.rows, p.small
    if 3 * cols != units:
        out[:, rows:, units:] = jnp.zeros((fs, 2 * small, 3 * cols - units), bf16)
    for t in range(fs):
        for m in range(3):
            at = m * p.width + t * cols
            value = qkv[:, at : at + cols].astype(f32) * gain_a[...]
            out[t, :rows, m * cols : (m + 1) * cols] = value.astype(bf16)
        for m in range(2):
            at = (m * fs + t) * units
            value = w_in[:, at : at + units].astype(f32) * gain_m[...]
            out[t, rows + m * small : rows + (m + 1) * small, :units] = value.astype(bf16)


def unit_kernel(*refs, p):
    pieces, unit = refs[:-1], refs[-1]
    unit[p.own :, :] = jnp.zeros((TAG, p.width), bf16)
    for i, j, at in p.locations():
        ref = pieces[j]
        value, _ = norm_stats(ref[i, : p.span].astype(f32))
        unit[at : at + p.span] = value.astype(bf16)
        unit[p.own :, at : at + p.span] = ref[i, p.span :, : p.span]


def project_kernel(*refs, p):
    fs, gs = p.fsdp, p.part
    xs, rest = refs[:fs], refs[fs:]
    cut, cos, sin, q_ref, k_ref, v_ref, seg_ref, w, x = rest
    step = pl.program_id(0)
    scale = p.size**-0.5

    @pl.when(step == 0)
    def _():
        for ff in range(fs):
            w[ff * p.rows : (ff + 1) * p.rows] = cut[ff, : p.rows]

    for o in range(fs):

        @pl.when(step == o)
        def _(o=o):
            x[...] = xs[o][: p.own]
            for i in range(p.n):
                tag = xs[o][p.own : p.own + TAG, i * gs : (i + 1) * gs].astype(f32)
                seg_ref[i, :, o * gs : (o + 1) * gs] = tag[:8]

    mixed = mm(x[...], w[...])
    rows = pl.ds(pl.multiple_of(step * gs, gs), gs)
    reps = p.cols // p.table
    cosine = jnp.concatenate([cos[rows, :]] * reps, axis=1)
    sine = jnp.concatenate([sin[rows, :]] * reps, axis=1)
    for i in range(p.n):
        own = mixed[i * gs : (i + 1) * gs]
        query, key = own[:, : p.cols], own[:, p.cols : 2 * p.cols]
        query = (query * cosine + swap(query, p.size) * sine) * scale
        q_ref[i, rows, :] = query.astype(bf16)
        k_ref[i, rows, :] = (key * cosine + swap(key, p.size) * sine).astype(bf16)
        v_ref[i, rows, :] = own[:, 2 * p.cols :].astype(bf16)


def attend_kernel(q_ref, k_ref, v_ref, seg_ref, wo, *rest, p):
    fs, gs = p.fsdp, p.part
    parts, (att_ref, made) = rest[:fs], rest[fs:]
    step = pl.program_id(0)
    i, o = step // fs, step % fs
    rows = pl.ds(pl.multiple_of(o * gs, gs), gs)
    q, k, v = q_ref[i, rows, :], k_ref[i], v_ref[i]
    allowed = seg_ref[i, :, rows].T[:, :1] == seg_ref[i, :1, :]
    total = jnp.zeros(q.shape, f32)
    for head in range(p.heads):
        here = head_mask(q.shape, head, p.size)
        scores = mm(jnp.where(here, q, jnp.zeros_like(q)), k, NT)
        scores = jnp.where(allowed, scores, masked_score)
        weights = jnp.exp(scores - jnp.max(scores, axis=1, keepdims=True))
        row = mm(weights.astype(bf16), v) / jnp.sum(weights, axis=1, keepdims=True)
        total = jnp.where(here, row, total)
    attended = total.astype(bf16)
    att_ref[i, rows, :] = attended
    made[...] = mm(attended, wo[...]).astype(bf16)
    for oo in range(fs):

        @pl.when(o == oo)
        def _(oo=oo):
            parts[oo][pl.ds(pl.multiple_of(i * gs, gs), gs), :] = made[...]


def backward_kernel(*refs, p):
    fs, gs, cols = p.fsdp, p.part, p.lanes
    gls, xs, rest = refs[:fs], refs[fs : 2 * fs], refs[2 * fs :]
    wo, q_ref, k_ref, v_ref, att_ref, seg_ref, cos, sin, c_ref = rest[:9]
    gm, sums = rest[9:11]
    kt, dqt, dk, dv, gl, x, seg_col, sum_qkv, sum_out = rest[11:]
    step = pl.program_id(0)
    scale = p.size**-0.5
    reps = cols // p.table

    def turned(grad, rows):
        cosine = jnp.concatenate([cos[rows, :]] * reps, axis=1)
        sine = jnp.concatenate([sin[rows, :]] * reps, axis=1)
        return grad * cosine - swap(grad, p.size) * sine

    @pl.when(step == 0)
    def _():
        sum_out[...] = jnp.zeros_like(sum_out)
        sum_qkv[...] = jnp.zeros_like(sum_qkv)

    @pl.when(step < p.n * fs)
    def _():
        i, o = step // fs, step % fs
        rows = pl.ds(pl.multiple_of(o * gs, gs), gs)
        for oo in range(fs):

            @pl.when(o == oo)
            def _(oo=oo):
                gl[...] = gls[oo][pl.ds(pl.multiple_of(i * gs, gs), gs), :]

        q, k, v = q_ref[i, rows, :], k_ref[i], v_ref[i]

        @pl.when(o == 0)
        def _():
            kt[...] = k.T
            dk[...] = jnp.zeros_like(dk)
            dv[...] = jnp.zeros_like(dv)
            seg_col[...] = seg_ref[i].T[:, :1]

        low = gl[...]
        g = mm(low, wo[...], NT).astype(bf16)
        sum_out[...] += mm(att_ref[i, rows, :], low, TN)
        allowed = seg_col[...] == seg_ref[i, :1, rows]
        zero = jnp.zeros_like(q)
        for head in range(p.heads // p.groups):
            here = head_mask(q.shape, head, p.size)
            own_q, own_g = jnp.where(here, q, zero), jnp.where(here, g, zero)
            scores = jnp.where(allowed, mm(k, own_q, NT), masked_score)
            weights = jnp.exp(scores - jnp.max(scores, axis=0, keepdims=True))
            probs = weights * (1.0 / jnp.sum(weights, axis=0, keepdims=True))
            grad = mm(v, own_g, NT)
            delta = jnp.sum(probs * grad, axis=0, keepdims=True)
            grad = (probs * (grad - delta)).astype(bf16)
            dv[...] += mm(probs.astype(bf16), own_g)
            dk[...] += mm(grad, own_q)
            at = pl.ds(head * p.size, p.size)
            dqt[at, :] = mm(kt[at, :], grad)
        gm[i, rows, :cols] = (turned(dqt[...].T, rows) * scale).astype(bf16)

        @pl.when(o == fs - 1)
        def _():
            gm[i, :, cols : 2 * cols] = turned(dk[...], slice(None)).astype(bf16)
            gm[i, :, 2 * cols :] = dv[...].astype(bf16)

    @pl.when(step >= p.n * fs)
    def _():
        o = step - p.n * fs
        rows = pl.ds(pl.multiple_of(o * gs, gs), gs)
        for oo in range(fs):

            @pl.when(o == oo)
            def _(oo=oo):
                x[...] = xs[oo][: p.own]

        grad = jnp.concatenate([gm[i, rows, :] for i in range(p.n)], axis=0)
        sum_qkv[...] += mm(x[...], grad, TN)

    @pl.when(step == p.n * fs + fs - 1)
    def _():
        small, slab = p.small, p.slab
        for cc in range(p.ctx):
            away = storage(c_ref[0] ^ cc, p.order)
            for ff in range(fs):
                for m in range(3):
                    part = sum_qkv[
                        ff * p.rows + cc * small : ff * p.rows + (cc + 1) * small,
                        m * cols : (m + 1) * cols,
                    ]
                    at = (ff * 3 + m) * small
                    sums[away, at : at + small, :] = part.astype(bf16)
            for d in range(p.width // cols):
                part = sum_out[cc * slab : (cc + 1) * slab, d * cols : (d + 1) * cols]
                at = 3 * fs * small + d * slab
                sums[away, at : at + slab, :] = part.astype(bf16)


def spread_kernel(*refs, p):
    gms, w, parts, made = refs[: p.groups], refs[p.groups], refs[p.groups + 1 : -1], refs[-1]
    o, lanes = pl.program_id(0), p.lanes
    rows = pl.ds(pl.multiple_of(o * p.part, p.part), p.part)
    for i in range(p.n):
        grad = jnp.concatenate(
            [gm[i, rows, m * lanes : (m + 1) * lanes] for m in range(3) for gm in gms], axis=1
        )
        made[i * p.part : (i + 1) * p.part] = mm(grad, w[...], NT).astype(bf16)
    for oo in range(p.fsdp):

        @pl.when(o == oo)
        def _(oo=oo):
            parts[oo][...] = made[...]


def mlp_kernel(*refs, p):
    fs, units, pad = p.fsdp, p.units, p.padded
    xs, cs, rest = refs[:fs], refs[fs : 2 * fs], refs[2 * fs :]
    w_in, w_out = rest[:2]
    outs, us, rest = rest[2 : 2 + fs], rest[2 + fs : 2 + 2 * fs], rest[2 + 2 * fs :]
    act_ref, da_ref, dg_ref, wa, wg, wm, x, ct, made, made_u = rest
    step = pl.program_id(0)

    @pl.when(step == 0)
    def _():
        if pad != units:
            wa[:, units:] = jnp.zeros((p.width, pad - units), bf16)
            wg[:, units:] = jnp.zeros((p.width, pad - units), bf16)
            wm[units:, :] = jnp.zeros((pad - units, p.width), bf16)
        wm[:units, :] = w_out[...]
        for cc in range(p.ctx):
            for ff in range(fs):
                at = ff * p.rows + cc * p.small
                wa[at : at + p.small, :units] = w_in[cc, ff, : p.small]
                wg[at : at + p.small, :units] = w_in[cc, ff, p.small :]

    for o in range(fs):

        @pl.when(step == o)
        def _(o=o):
            x[...] = xs[o][...]
            ct[...] = cs[o][...]

    act, gate = mm(x[...], wa[...]), mm(x[...], wg[...])
    phi = 0.5 * (1.0 + lax.erf(act * (2.0**-0.5)))
    gelu = act * phi
    active = (gelu * gate).astype(bf16)
    made[...] = mm(active, wm[...]).astype(bf16)
    grad = mm(ct[...], wm[...], NT)
    slope = phi + act * (jnp.exp(-0.5 * act * act) * 0.3989422804014327)
    da, dg = (grad * gate * slope).astype(bf16), (grad * gelu).astype(bf16)
    made_u[...] = (mm(da, wa[...], NT) + mm(dg, wg[...], NT)).astype(bf16)
    rows = pl.ds(pl.multiple_of(step * p.own, p.own), p.own)
    act_ref[rows, :], da_ref[rows, :], dg_ref[rows, :] = active, da, dg
    for o in range(fs):

        @pl.when(step == o)
        def _(o=o):
            outs[o][...] = made[...]
            us[o][...] = made_u[...]


def mlp_sums_kernel(*refs, p):
    fs, units = p.fsdp, p.units
    xs, cs, rest = refs[:fs], refs[fs : 2 * fs], refs[2 * fs :]
    act_ref, da_ref, dg_ref, c_ref, in_out, mlp_out, sa, sg, sm, x, ct = rest
    step = pl.program_id(0)

    @pl.when(step == 0)
    def _():
        sa[...] = jnp.zeros_like(sa)
        sg[...] = jnp.zeros_like(sg)
        sm[...] = jnp.zeros_like(sm)

    for o in range(fs):

        @pl.when(step == o)
        def _(o=o):
            x[...] = xs[o][...]
            ct[...] = cs[o][...]

    rows = pl.ds(pl.multiple_of(step * p.own, p.own), p.own)
    sa[...] += mm(x[...], da_ref[rows, :], TN)
    sg[...] += mm(x[...], dg_ref[rows, :], TN)
    sm[...] += mm(act_ref[rows, :], ct[...], TN)

    @pl.when(step == fs - 1)
    def _():
        slab = p.width // p.ctx
        for cc in range(p.ctx):
            for ff in range(fs):
                at = ff * p.rows + cc * p.small
                in_out[cc, ff, 0] = sa[at : at + p.small, :units].astype(bf16)
                in_out[cc, ff, 1] = sg[at : at + p.small, :units].astype(bf16)
            away = storage(c_ref[0] ^ cc, p.order)
            mlp_out[away] = sm[:units, cc * slab : (cc + 1) * slab].astype(bf16)


def middle_kernel(*refs, p):
    g = p.pieces
    hidden, (a, b, c), (residual, unit) = refs[:g], refs[g : g + 3], refs[g + 3 :]
    for i, j, at in p.locations():
        rows = slice(at, at + p.span)
        total = a[rows].astype(f32) + b[rows].astype(f32) + c[rows].astype(f32)
        total = total + hidden[j][i, : p.span].astype(f32)
        residual[rows] = total
        unit[rows] = norm_stats(total)[0].astype(bf16)


def turn_kernel(a, b, c, residual, cot, grad, low, *, p):
    for _, _, at in p.locations():
        rows = slice(at, at + p.span)
        u = a[rows].astype(f32) + b[rows].astype(f32) + c[rows].astype(f32)
        unit, rate = norm_stats(residual[rows])
        total = cot[rows].astype(f32) + norm_back(u, unit, rate)
        grad[rows] = total
        low[rows] = total.astype(bf16)


def result_kernel(*refs, p):
    (a, b, c, residual), outs = refs[:4], refs[4:]
    for i, j, at in p.locations():
        rows = slice(at, at + p.span)
        total = a[rows].astype(f32) + b[rows].astype(f32) + c[rows].astype(f32)
        outs[j][i] = (total + residual[rows]).astype(bf16)


def last_kernel(*refs, p):
    g = p.pieces
    hidden, (a, b, c, grad), outs = refs[:g], refs[g : g + 4], refs[g + 4 :]
    for i, j, at in p.locations():
        rows = slice(at, at + p.span)
        u = a[rows].astype(f32) + b[rows].astype(f32) + c[rows].astype(f32)
        unit, rate = norm_stats(hidden[j][i, : p.span].astype(f32))
        outs[j][i] = (grad[rows] + norm_back(u, unit, rate)).astype(bf16)


def qkv_grad_kernel(*refs, p):
    stacks, rest = refs[: p.groups], refs[p.groups :]
    w, gain, c_ref, qkv, out, gain_grad = rest
    fs, small, slab, lanes = p.fsdp, p.small, p.slab, p.lanes
    for cc in range(p.ctx):
        away = storage(c_ref[0] ^ cc, p.order)
        rows = slice(cc * small, (cc + 1) * small)
        scale = gain[rows, :]
        total = jnp.zeros((small, lanes), f32)
        for g in range(p.groups):
            for ff in range(fs):
                for m in range(3):
                    at = (ff * 3 + m) * small
                    value = stacks[g][away, at : at + small, :].astype(f32)
                    there = m * p.width + ff * p.cols + g * lanes
                    qkv[rows, there : there + lanes] = value * scale
                    total = total + value * w[rows, there : there + lanes].astype(f32)
            for d in range(p.width // lanes):
                at = 3 * fs * small + d * slab
                value = stacks[g][away, at : at + slab, :].astype(f32)
                row = g * lanes + cc * slab
                out[row : row + slab, d * lanes : (d + 1) * lanes] = value
        gain_grad[rows, :] = jnp.sum(total, axis=1, keepdims=True)


def in_grad_kernel(sums, w, gain, grad, gain_grad):
    value = sums[...].astype(f32)
    grad[...] = value * gain[...]
    gain_grad[...] = jnp.sum(value * w[...].astype(f32), axis=1, keepdims=True)


def out_grad_kernel(stack, c_ref, grad, *, p):
    slab = p.width // p.ctx
    for cc in range(p.ctx):
        away = storage(c_ref[0] ^ cc, p.order)
        grad[:, cc * slab : (cc + 1) * slab] = stack[away].astype(f32)


def on_device(
    hidden, segment_ids, cotangent, w_qkv, w_attn_out, w_in, w_mlp_out, gain_attn, gain_mlp
):
    fsdp, ctx = lax.axis_size("fsdp"), lax.axis_size("ctx")
    f, c = lax.axis_index("fsdp"), lax.axis_index("ctx")
    batch, span, width = hidden.shape
    p = Plan(fsdp, ctx, batch, span, width, w_mlp_out.shape[0], w_in.shape[0])
    n, own, cols, units, rows, small = p.n, p.own, p.cols, p.units, p.rows, p.small
    length, pieces = p.length, p.pieces
    both = ("ctx", "fsdp")
    slots = range(fsdp)
    tile = shape_of((own, width))
    bits = [fsdp >> 1 + b for b in range(fsdp.bit_length() - 1)]

    def mixed_bits(index):
        out = 0
        for bit in bits:
            out = out + index // (fsdp // 2 // bit) % 2 * bit
        return out

    def route(j):
        pairs = []
        for cc in range(ctx):
            for ff in range(fsdp):
                to_c, to_f = (cc + j) % pieces * fsdp + mixed_bits(ff), cc // pieces
                pairs.append((cc * fsdp + ff, to_c * fsdp + to_f))
        return pairs

    def dealt(values):
        return [
            lax.dynamic_slice_in_dim(values, (c + j) % pieces * n, n, 0) for j in range(pieces)
        ]

    def deal(parts):
        return [lax.ppermute(part, both, route(j)) for j, part in enumerate(parts)]

    def undeal(parts):
        back = [
            lax.ppermute(part, both, [(b, a) for a, b in route(j)])
            for j, part in enumerate(parts)
        ]
        if pieces == 1:
            return back[0]
        blocks = []
        for b in range(pieces):
            block = back[0]
            for j in range(1, pieces):
                block = jnp.where((c + j) % pieces == b, back[j], block)
            blocks.append(block)
        return jnp.concatenate(blocks, axis=0)

    def partner(values, bit):
        return lax.ppermute(values, "fsdp", [(i, i ^ bit) for i in range(fsdp)])

    def collect(value):
        held = {0: value}
        for bit in bits:
            for o in list(held):
                held[o ^ bit] = partner(held[o], bit)
        return [held[o] for o in slots]

    def reduce(parts):
        held, side, last = dict(enumerate(parts)), None, None
        for bit in reversed(bits):
            for o in sorted(held, reverse=True):
                if not o & bit:
                    continue
                got, mine = partner(held.pop(o), bit), held[o ^ bit]
                if o == bits[0]:
                    last = got
                elif o == bits[1]:
                    side = got
                else:
                    held[o ^ bit] = (mine.astype(f32) + got.astype(f32)).astype(bf16)
        return held[0], side, last

    def away(values, bit):
        return lax.ppermute(values, "ctx", [(i, i ^ bit) for i in range(ctx)])

    def fold(stack, bit):
        half = stack.shape[0] // 2
        got = away(stack[half:], bit)
        return (stack[:half].astype(f32) + got.astype(f32)).astype(bf16)

    def double(value):
        stack = value[None]
        for bit in reversed(p.order):
            stack = jnp.concatenate([stack, away(stack, bit)], axis=0)
        return stack

    blocks = [
        (f ^ o) * pieces + (c // fsdp - j) % pieces for o in slots for j in range(pieces)
    ]
    positions = (jnp.stack(blocks)[:, None] * span + jnp.arange(span)[None, :]).reshape(length)
    half = p.size // 2
    inverse = rope_base ** (-(jnp.arange(half, dtype=f32) * 2.0 / p.size))
    angles = positions.astype(f32)[:, None] * inverse[None, :]
    cosine, sine = jnp.cos(angles), jnp.sin(angles)
    reps = p.table // p.size
    cosine = jnp.concatenate([cosine, cosine] * reps, axis=1)
    sine = jnp.concatenate([-sine, sine] * reps, axis=1)

    tags = jnp.pad(
        segment_ids.astype(bf16)[:, None, :], ((0, 0), (0, TAG - 1), (0, width - span))
    )
    hidden_cut, w_qkv, w_in = lax.optimization_barrier(
        (dealt(jnp.concatenate([hidden, tags], axis=1)), w_qkv, w_in)
    )
    hidden_parts = deal(hidden_cut)

    gain_a, gain_m = gain_attn.astype(f32)[:, None], gain_mlp.astype(f32)[:, None]
    here = jnp.reshape(c, (1,))
    (cut,) = call(
        functools.partial(cut_kernel, p=p),
        "cut",
        [shape_of((fsdp, rows + 2 * small, 3 * cols))],
        1,
        [],
        [
            w_qkv,
            lax.dynamic_slice_in_dim(w_in, c * small, small, 0),
            gain_a,
            lax.dynamic_slice_in_dim(gain_m, c * small, small, 0),
        ],
        1e6,
    )
    hidden_parts, cut, cotangent = lax.optimization_barrier((hidden_parts, cut, cotangent))
    cut = lax.all_to_all(cut, "fsdp", 0, 0, tiled=True)
    cot_parts = deal(dealt(cotangent))

    unit1 = call(
        functools.partial(unit_kernel, p=p),
        "unit1",
        [shape_of((own + TAG, width))],
        1,
        [],
        hidden_parts,
        1e6,
    )[0]
    unit1_slots = collect(unit1)
    unit1_slots, cut, cot_parts = lax.optimization_barrier((unit1_slots, cut, cot_parts))
    w_in_cols = lax.all_gather(cut[:, rows:, :units], "ctx", axis=0)
    cot_own = jnp.stack(cot_parts, axis=1).reshape(own, width)
    cot_slots = collect(cot_own)

    whole = shape_of((n, length, cols))
    q, k, v, segments, w_qkv_cols = call(
        functools.partial(project_kernel, p=p),
        "project",
        [whole] * 3 + [shape_of((n, 8, length), f32), shape_of((width, 3 * cols))],
        fsdp,
        [pltpu.VMEM((own, width), bf16)],
        unit1_slots + [cut, cosine, sine],
        4e9,
    )
    q, cot_slots = lax.optimization_barrier((q, cot_slots))
    made = call(
        functools.partial(attend_kernel, p=p),
        "attend",
        [tile] * fsdp + [whole],
        n * fsdp,
        [pltpu.VMEM((p.part, width), bf16)],
        [q, k, v, segments, w_attn_out],
        1.2e10,
    )
    attended_parts, attended = made[:fsdp], made[fsdp]

    residual, unit2 = call(
        functools.partial(middle_kernel, p=p),
        "middle",
        [shape_of((own, width), f32), tile],
        1,
        [],
        hidden_parts + list(reduce(attended_parts)),
        1e6,
    )
    unit2_slots = collect(unit2)

    wide = shape_of((fsdp * own, p.padded))
    made = call(
        functools.partial(mlp_kernel, p=p),
        "mlp",
        [tile] * (2 * fsdp) + [wide] * 3,
        fsdp,
        [pltpu.VMEM((width, p.padded), bf16)] * 2
        + [pltpu.VMEM((p.padded, width), bf16)]
        + [pltpu.VMEM((own, width), bf16)] * 4,
        unit2_slots + cot_slots + [w_in_cols, w_mlp_out],
        1.2e10,
    )
    out_parts, u2_parts, (active, da, dg) = made[:fsdp], made[fsdp : 2 * fsdp], made[2 * fsdp :]

    u2 = reduce(u2_parts)
    in_sums, mlp_sums = call(
        functools.partial(mlp_sums_kernel, p=p),
        "mlp_sums",
        [
            shape_of((ctx, fsdp, 2, small, units)),
            shape_of((ctx, units, width // ctx)),
        ],
        fsdp,
        [pltpu.VMEM((width, p.padded), f32)] * 2
        + [pltpu.VMEM((p.padded, width), f32)]
        + [pltpu.VMEM((own, width), bf16)] * 2,
        unit2_slots + cot_slots + [active, da, dg, here],
        6e9,
    )
    u2, in_sums, mlp_sums = lax.optimization_barrier((u2, in_sums, mlp_sums))
    grad_residual, grad_low = call(
        functools.partial(turn_kernel, p=p),
        "turn",
        [shape_of((own, width), f32), tile],
        1,
        [],
        list(u2) + [residual, cot_own],
        1e6,
    )
    low_slots = collect(grad_low)

    mlp_left = fold(mlp_sums, p.order[0])
    low_slots, mlp_left = lax.optimization_barrier((low_slots, mlp_left))
    mixed, attention_sums = [], []
    for group in range(p.groups):
        some = pl.BlockSpec(
            (n, length, p.lanes),
            lambda s, group=group: (0, 0, group),
            pipeline_mode=pl.Buffered(1),
        )
        wo_rows = pl.BlockSpec(
            (p.lanes, width), lambda s, group=group: (group, 0), pipeline_mode=pl.Buffered(1)
        )
        grad_mixed, sums = call(
            functools.partial(backward_kernel, p=p),
            "attention_back",
            [
                shape_of((n, length, 3 * p.lanes)),
                shape_of((ctx, 4 * fsdp * small, p.lanes)),
            ],
            n * fsdp + fsdp,
            [
                pltpu.VMEM((p.lanes, length), bf16),
                pltpu.VMEM((p.lanes, p.part), f32),
                pltpu.VMEM((length, p.lanes), f32),
                pltpu.VMEM((length, p.lanes), f32),
                pltpu.VMEM((p.part, width), bf16),
                pltpu.VMEM((own, width), bf16),
                pltpu.VMEM((length, 1), f32),
                pltpu.VMEM((width, 3 * p.lanes), f32),
                pltpu.VMEM((p.lanes, width), f32),
            ],
            low_slots
            + unit1_slots
            + [(w_attn_out, wo_rows), (q, some), (k, some), (v, some), (attended, some)]
            + [segments, cosine, sine, here],
            1.5e10,
        )
        if group < p.groups - 1:
            mlp_left = fold(mlp_left, p.order[1])
            low_slots, mlp_left = lax.optimization_barrier((low_slots, mlp_left))
        mixed.append(grad_mixed)
        attention_sums.append(sums)
    in_small = lax.psum_scatter(in_sums, "ctx", scatter_dimension=0, tiled=False)
    mixed, out_parts, in_small = lax.optimization_barrier((mixed, list(out_parts), in_small))
    u1_parts = call(
        functools.partial(spread_kernel, p=p),
        "spread",
        [tile] * fsdp,
        fsdp,
        [pltpu.VMEM((own, width), bf16)],
        mixed + [w_qkv_cols],
        2e9,
    )
    piece = [shape_of((n, span, width))] * pieces
    back_parts = call(
        functools.partial(last_kernel, p=p),
        "last",
        piece,
        1,
        [],
        hidden_parts + list(reduce(u1_parts)) + [grad_residual],
        1e6,
    )
    result_parts = call(
        functools.partial(result_kernel, p=p),
        "result",
        piece,
        1,
        [],
        list(reduce(out_parts)) + [residual],
        1e6,
    )
    out = undeal(result_parts)
    back = undeal(back_parts).astype(f32)

    in_small = lax.all_to_all(in_small, "fsdp", 0, 0, tiled=True)
    in_small = in_small.transpose(2, 1, 0, 3).reshape(small, 2 * fsdp * units)
    in_rows = lax.all_gather(in_small, "ctx", axis=0, tiled=True)

    while mlp_left.shape[0] > 1:
        mlp_left = fold(mlp_left, p.order[ctx.bit_length() - mlp_left.shape[0].bit_length()])
    mlp_stack = double(mlp_left[0])

    stacks = []
    for sums in attention_sums:
        for bit in p.order:
            sums = fold(sums, bit)
        mine = sums[0, : 3 * fsdp * small].reshape(fsdp, 3 * small, p.lanes)
        mine = lax.all_to_all(mine, "fsdp", 0, 0, tiled=True)
        mine = mine.reshape(3 * fsdp * small, p.lanes)
        stacks.append(double(jnp.concatenate([mine, sums[0, 3 * fsdp * small :]], axis=0)))

    grad_qkv, grad_out, grad_gain_a = call(
        functools.partial(qkv_grad_kernel, p=p),
        "qkv_grad",
        [
            shape_of((rows, 3 * width), f32),
            shape_of((cols, width), f32),
            shape_of((rows, 1), f32),
        ],
        1,
        [],
        stacks + [w_qkv, gain_a, here],
        1e6,
    )
    block = min(64, rows)
    some = pl.BlockSpec((block, 2 * fsdp * units), lambda s: (s, 0))
    thin = pl.BlockSpec((block, 1), lambda s: (s, 0))
    grad_in, grad_gain_m = pl.pallas_call(
        in_grad_kernel,
        grid=(rows // block,),
        in_specs=[some, some, thin],
        out_specs=[some, thin],
        out_shape=[shape_of(w_in.shape, f32), shape_of((rows, 1), f32)],
        compiler_params=pltpu.CompilerParams(vmem_limit_bytes=40 << 20),
        cost_estimate=pl.CostEstimate(
            flops=1000000, bytes_accessed=8 * w_in.size, transcendentals=0
        ),
        name="in_grad",
    )(in_rows, w_in, gain_m)
    (grad_mlp_out,) = call(
        functools.partial(out_grad_kernel, p=p),
        "out_grad",
        [shape_of((units, width), f32)],
        1,
        [],
        [mlp_stack, here],
        1e6,
    )
    return (
        out,
        back,
        grad_qkv,
        grad_out,
        grad_in,
        grad_mlp_out,
        grad_gain_a.reshape(rows),
        grad_gain_m.reshape(rows),
    )


def solution(mesh):
    in_specs = (
        P("fsdp", "ctx", None),
        P("fsdp", "ctx"),
        P("fsdp", "ctx", None),
        P("fsdp", None),
        P("fsdp", None),
        P("fsdp", None),
        P("fsdp", None),
        P("fsdp"),
        P("fsdp"),
    )
    out_specs = (
        P("fsdp", "ctx", None),
        P("fsdp", "ctx", None),
        P("fsdp", None),
        P("fsdp", None),
        P("fsdp", None),
        P("fsdp", None),
        P("fsdp"),
        P("fsdp"),
    )
    return jax.shard_map(
        on_device, mesh=mesh, in_specs=in_specs, out_specs=out_specs, check_vma=False
    )
```

time: 721 us -> 472 us (0.65)
  the two profiles are of different devices: /device:TPU:17 before, /device:TPU:0 now
where the time goes in v2:
time: 472 us; the launch traced here: 463 us
  waiting for transfers between devices  195 us (41%)
  Pallas kernels  132 us (28%)
  starting transfers between devices  76.8 us (16%)
  other arithmetic  26.3 us (6%)
  local copies, waits for them, and re-layouts  18.2 us (4%)
  between operations  14.8 us (3%)
    pallas_call x15, Pallas kernels, call(): pl.pallas_call(kernel, grid=(grid,), in_specs=specs, out_specs=[spec(a) f...  128 us
    ppermute x24, waiting for transfers between devices, partner(): return lax.ppermute(values, 'fsdp', [(i, i ^ bit) for i in range(fsdp)])  88.5 us
    ppermute x18, waiting for transfers between devices, away(): return lax.ppermute(values, 'ctx', [(i, i ^ bit) for i in range(ctx)])  51.6 us
    ppermute x24, starting transfers between devices, partner(): return lax.ppermute(values, 'fsdp', [(i, i ^ bit) for i in range(fsdp)])  20.7 us
    ppermute x4, waiting for transfers between devices, undeal(): lax.ppermute(part, both, [(b, a) for a, b in route(j)])  17.7 us
    ppermute x18, starting transfers between devices, away(): return lax.ppermute(values, 'ctx', [(i, i ^ bit) for i in range(ctx)])  15.7 us
    reduce_scatter x1, waiting for transfers between devices, on_device(): lax.psum_scatter(in_sums, 'ctx', scatter_dimension=0, tiled=False)  14.4 us
    ppermute x4, starting transfers between devices, deal(): return [lax.ppermute(part, both, route(j)) for j, part in enumerate(parts)]  12 us
  transfers between devices with their start and end apart: 57, of which 24 were waited for; matrix products, arithmetic and copies ran while one was open for 8% of the time, Pallas kernels for 23%

profile of v2, /device:TPU:0, one launch (start us, length us, event | category | flops | bytes accessed | tf_op | source)
XLA Modules:
  0.0 462.6 jit_solution(10399141439503033293)
XLA Ops:
  9.8 6.6 %collective-permute-start.1 = (bf16[1,144,1024]{2,1,0:T(8,128)(2,1)S(1)}, bf16[1,144,1024]{2,1,0:T(8,128)(2,1)S(1)}, u32[]{:S(2)}, u32[]{:S(2)}) collective-permute-start(bf16[1,144,1024]{2,1,0:T(8,128)(2,1)S(1)} %get-tuple-element.95), channel_id=1, source_target_pairs={{0,16},{1,24},{2,20},{3,28},{4,0},{5,8},{6,4},{7,12},{8,17},{9,25}... | collective-permute-start | bytes 884744 | tf_op jit(solution)/shard_map/ppermute | solution.py:515
  19.7 3.8 cut.1
  23.5 2.3 collective-permute-done.1.refs_1_
  26.5 10.0 %all-to-all-start = ((bf16[4,320,768]{2,1,0:T(8,128)(2,1)}), bf16[4,320,768]{2,1,0:T(8,128)(2,1)S(1)}, u32[]{:S(2)}, u32[]{:S(2)}) async-start(bf16[4,320,768]{2,1,0:T(8,128)(2,1)} %cut.1), calls=%async_computation | async-start | bytes 3932160 | tf_op jit(solution)/shard_map/all_to_all | solution.py:608
  36.5 2.3 unit1.1.refs_0_.refs_4_
  38.8 2.4 collective-permute-start.3
  41.1 31.7 %collective-permute-done.3.refs_2_.refs_6_ = bf16[272,1024]{1,0:T(8,128)(2,1)} collective-permute-done((bf16[272,1024]{1,0:T(8,128)(2,1)}, bf16[272,1024]{1,0:T(8,128)(2,1)}, u32[]{:S(2)}, u32[]{:S(2)}) %collective-permute-start.3) | collective-permute-done | bytes 557088 | tf_op jit(solution)/shard_map/ppermute | solution.py:533
  73.5 4.0 collective-permute-start.6
  77.6 7.0 %collective-permute-done.6 = bf16[1,128,1024]{2,1,0:T(8,128)(2,1)S(1)} collective-permute-done((bf16[1,128,1024]{2,1,0:T(8,128)(2,1)S(1)}, bf16[1,128,1024]{2,1,0:T(8,128)(2,1)S(1)}, u32[]{:S(2)}, u32[]{:S(2)}) %collective-permute-start.6) | collective-permute-done | bytes 262176 | tf_op jit(solution)/shard_map/ppermute | solution.py:515
  84.7 8.5 %collective-permute-start.8 = (bf16[256,1024]{1,0:T(8,128)(2,1)S(1)}, bf16[256,1024]{1,0:T(8,128)(2,1)S(1)}, u32[]{:S(2)}, u32[]{:S(2)}) collective-permute-start(bf16[256,1024]{1,0:T(8,128)(2,1)S(1)} %bitcast.35), channel_id=1, source_target_pairs={{0,2},{1,3},{2,0},{3,1},{4,6},{5,7},{6,4},{7,5},{8,10},{9,11},{10,... | collective-permute-start | bytes 1572872 | tf_op jit(solution)/shard_map/ppermute | solution.py:533
  94.2 7.6 %collective-permute-done.8.refs_6_ = bf16[256,1024]{1,0:T(8,128)(2,1)S(1)} collective-permute-done((bf16[256,1024]{1,0:T(8,128)(2,1)S(1)}, bf16[256,1024]{1,0:T(8,128)(2,1)S(1)}, u32[]{:S(2)}, u32[]{:S(2)}) %collective-permute-start.8) | collective-permute-done | bytes 524320 | tf_op jit(solution)/shard_map/ppermute | solution.py:533
  105.6 7.3 %project.1 = (bf16[1,1024,256]{2,1,0:T(8,128)(2,1)}, bf16[1,1024,256]{2,1,0:T(8,128)(2,1)}, bf16[1,1024,256]{2,1,0:T(8,128)(2,1)}, f32[1,8,1024]{2,1,0:T(8,128)}, bf16[1024,768]{1,0:T(8,128)(2,1)}) custom-call(bf16[272,1024]{1,0:T(8,128)(2,1)} %unit1.1.refs_0_.refs_4_, bf16[272,1024]{1,0:T(8,128)(2,1)} %collective-permute-done.2.refs_1_.refs_5_, ...), custom_call_target="tpu_custom_call" | custom-call | flops 4000000000 | bytes 8421376 | tf_op jit(solution)/shard_map/project/pallas_call | solution.py:40
  113.0 13.0 %attend.1 = (bf16[256,1024]{1,0:T(8,128)(2,1)}, bf16[256,1024]{1,0:T(8,128)(2,1)}, bf16[256,1024]{1,0:T(8,128)(2,1)}, bf16[256,1024]{1,0:T(8,128)(2,1)}, bf16[1,1024,256]{2,1,0:T(8,128)(2,1)}) custom-call(bf16[1,1024,256]{2,1,0:T(8,128)(2,1)} %get-tuple-element.110.q_ref.refs_9_, bf16[1,1024,256]{2,1,0:T(8,128)(2,1)} %get-tuple-element.111.k_ref.refs_10_, ...), custom_call_target="tpu_custom_call" | custom-call | flops 12000000000 | bytes 4751360 | tf_op jit(solution)/shard_map/attend/pallas_call | solution.py:40
  129.6 2.5 collective-permute-start.12
  132.0 12.4 %collective-permute-done.12.refs_4_ = bf16[256,1024]{1,0:T(8,128)(2,1)S(1)} collective-permute-done((bf16[256,1024]{1,0:T(8,128)(2,1)S(1)}, bf16[256,1024]{1,0:T(8,128)(2,1)S(1)}, u32[]{:S(2)}, u32[]{:S(2)}) %collective-permute-start.12) | collective-permute-done | bytes 524320 | tf_op jit(solution)/shard_map/ppermute | solution.py:533
  145.3 2.9 middle.1
  149.9 12.2 %collective-permute-done.14.refs_2_ = bf16[256,1024]{1,0:T(8,128)(2,1)S(1)} collective-permute-done((bf16[256,1024]{1,0:T(8,128)(2,1)}, bf16[256,1024]{1,0:T(8,128)(2,1)S(1)}, u32[]{:S(2)}, u32[]{:S(2)}) %collective-permute-start.14) | collective-permute-done | bytes 524320 | tf_op jit(solution)/shard_map/ppermute | solution.py:533
  164.9 21.7 %mlp.1 = (bf16[256,1024]{1,0:T(8,128)(2,1)}, bf16[256,1024]{1,0:T(8,128)(2,1)}, bf16[256,1024]{1,0:T(8,128)(2,1)}, bf16[256,1024]{1,0:T(8,128)(2,1)}, bf16[256,1...) custom-call(bf16[256,1024]{1,0:T(8,128)(2,1)} %get-tuple-element.118, ...), custom_call_target="tpu_custom_call" | custom-call | flops 12000000000 | bytes 17137664 | tf_op jit(solution)/shard_map/mlp/pallas_call | solution.py:40
  191.5 13.2 %mlp_sums.1 = (bf16[8,4,2,32,656]{4,3,2,1,0:T(8,128)(2,1)}, bf16[8,656,128]{2,1,0:T(8,128)(2,1)}) custom-call(bf16[256,1024]{1,0:T(8,128)(2,1)} %get-tuple-element.118.refs_0_, bf16[256,1024]{1,0:T(8,128)(2,1)} %copy-done.25, bf16[256,1024]{1,0:T(8,128)(2,1)} %copy-done.24, bf16[256,1024]{1,0:T(8,128)(2,1)} %copy-done.27, bf16[256,1024]{1,0:T(8,128)(2,1)} %bitcast.38, ...), custom_call_target="tpu_custom_call" | custom-call | flops 6000000000 | bytes 12943364 | tf_op jit(solution)/shard_map/mlp_sums/pallas_call | solution.py:40
  205.8 3.8 turn.1
  210.7 12.8 %collective-permute-done.20.refs_2_ = bf16[256,1024]{1,0:T(8,128)(2,1)S(1)} collective-permute-done((bf16[256,1024]{1,0:T(8,128)(2,1)}, bf16[256,1024]{1,0:T(8,128)(2,1)S(1)}, u32[]{:S(2)}, u32[]{:S(2)}) %collective-permute-start.20) | collective-permute-done | bytes 524320 | tf_op jit(solution)/shard_map/ppermute | solution.py:533
  223.5 10.5 %collective-permute-done.22 = bf16[4,656,128]{2,1,0:T(8,128)(2,1)S(1)} collective-permute-done((bf16[4,656,128]{2,1,0:T(8,128)(2,1)S(1)}, bf16[4,656,128]{2,1,0:T(8,128)(2,1)S(1)}, u32[]{:S(2)}, u32[]{:S(2)}) %collective-permute-start.22) | collective-permute-done | bytes 671776 | tf_op jit(solution)/shard_map/ppermute | solution.py:558
  235.2 20.3 %attention_back.2 = (bf16[1,1024,384]{2,1,0:T(8,128)(2,1)}, bf16[8,512,128]{2,1,0:T(8,128)(2,1)}) custom-call(bf16[256,1024]{1,0:T(8,128)(2,1)} %get-tuple-element.145.refs_0_, bf16[256,1024]{1,0:T(8,128)(2,1)} %copy-done.23, bf16[256,1024]{1,0:T(8,128)(2,1)} %copy-done.22, bf16[256,1024]{1,0:T(8,128)(2,1)} %copy-done.26, ...), custom_call_target="tpu_custom_call" | custom-call | flops 15000000512 | bytes 9863172 | tf_op jit(solution)/shard_map/attention_back/pallas_call | solution.py:40
  256.9 2.4 collective-permute-start.46
  259.2 20.2 %attention_back.3 = (bf16[1,1024,384]{2,1,0:T(8,128)(2,1)}, bf16[8,512,128]{2,1,0:T(8,128)(2,1)}) custom-call(bf16[256,1024]{1,0:T(8,128)(2,1)} %get-tuple-element.145.refs_0_, bf16[256,1024]{1,0:T(8,128)(2,1)} %copy-done.23, bf16[256,1024]{1,0:T(8,128)(2,1)} %copy-done.22, bf16[256,1024]{1,0:T(8,128)(2,1)} %copy-done.26, ...), custom_call_target="tpu_custom_call" | custom-call | flops 15000000512 | bytes 9863172 | tf_op jit(solution)/shard_map/attention_back/pallas_call | solution.py:40
  284.1 14.4 %reduce-scatter.2.cloned.1.call-done = bf16[1,4,2,32,656]{4,3,2,1,0:T(8,128)(2,1)} async-done(((bf16[8,4,2,32,656]{4,3,2,1,0:T(8,128)(2,1)}), bf16[1,4,2,32,656]{4,3,2,1,0:T(8,128)(2,1)}) %reduce-scatter.2.cloned.1.call-update) | async-done | bytes 335888 | tf_op jit(solution)/shard_map/reduce_scatter | solution.py:742
  298.5 3.5 all-to-all-start.3
  304.2 5.2 %all-to-all-done.3 = bf16[4,2,32,656]{3,2,1,0:T(8,128)(2,1)S(1)} async-done(((bf16[4,2,32,656]{3,2,1,0:T(8,128)(2,1)}), bf16[4,2,32,656]{3,2,1,0:T(8,128)(2,1)S(1)}, u32[]{:S(2)}, u32[]{:S(2)}) %all-to-all-start.3) | async-done | bytes 335904 | tf_op jit(solution)/shard_map/all_to_all | solution.py:775
  315.6 12.4 %collective-permute-done.36 = bf16[1,512,128]{2,1,0:T(8,128)(2,1)S(1)} collective-permute-done((bf16[1,512,128]{2,1,0:T(8,128)(2,1)S(1)}, bf16[1,512,128]{2,1,0:T(8,128)(2,1)S(1)}, u32[]{:S(2)}, u32[]{:S(2)}) %collective-permute-start.36) | collective-permute-done | bytes 131104 | tf_op jit(solution)/shard_map/ppermute | solution.py:558
  328.7 3.3 all-to-all-start.1
  332.0 4.2 all-to-all-done.1
  336.3 3.4 collective-permute-start.37
  340.8 3.7 collective-permute-start.49
  344.5 6.7 %collective-permute-done.37 = bf16[1,512,128]{2,1,0:T(8,128)(2,1)S(1)} collective-permute-done((bf16[1,512,128]{2,1,0:T(8,128)(2,1)S(1)}, bf16[1,512,128]{2,1,0:T(8,128)(2,1)S(1)}, u32[]{:S(2)}, u32[]{:S(2)}) %collective-permute-start.37) | collective-permute-done | bytes 131104 | tf_op jit(solution)/shard_map/ppermute | solution.py:558
  351.3 7.2 %collective-permute-done.42 = bf16[1,512,128]{2,1,0:T(8,128)(2,1)S(1)} collective-permute-done((bf16[1,512,128]{2,1,0:T(8,128)(2,1)S(1)}, bf16[1,512,128]{2,1,0:T(8,128)(2,1)S(1)}, u32[]{:S(2)}, u32[]{:S(2)}) %collective-permute-start.42) | collective-permute-done | bytes 131104 | tf_op jit(solution)/shard_map/ppermute | solution.py:558
  359.2 3.3 all-to-all-start.2
  363.0 3.8 all-to-all-done.2
  366.9 5.9 %spread.1 = (bf16[256,1024]{1,0:T(8,128)(2,1)}, bf16[256,1024]{1,0:T(8,128)(2,1)}, bf16[256,1024]{1,0:T(8,128)(2,1)}, bf16[256,1024]{1,0:T(8,128)(2,1)}) custom-call(bf16[1,1024,384]{2,1,0:T(8,128)(2,1)} %get-tuple-element.161.refs_0_, bf16[1,1024,384]{2,1,0:T(8,128)(2,1)} %get-tuple-element.162.refs_1_, bf16[1024,768]{1,0:T(8,128)(2,1)} %get-tuple-element.163.refs_2_), custom_call_target="tpu_custom_call" | custom-call | flops 2000000000 | bytes 5242880 | tf_op jit(solution)/shard_map/spread/pallas_call | solution.py:40
  374.9 6.3 %collective-permute-done.43 = bf16[1,512,128]{2,1,0:T(8,128)(2,1)S(1)} collective-permute-done((bf16[1,512,128]{2,1,0:T(8,128)(2,1)S(1)}, bf16[1,512,128]{2,1,0:T(8,128)(2,1)S(1)}, u32[]{:S(2)}, u32[]{:S(2)}) %collective-permute-start.43) | collective-permute-done | bytes 131104 | tf_op jit(solution)/shard_map/ppermute | solution.py:558
  383.7 6.1 %collective-permute-done.44 = bf16[2,512,128]{2,1,0:T(8,128)(2,1)S(1)} collective-permute-done((bf16[2,512,128]{2,1,0:T(8,128)(2,1)S(1)}, bf16[2,512,128]{2,1,0:T(8,128)(2,1)S(1)}, u32[]{:S(2)}, u32[]{:S(2)}) %collective-permute-start.44) | collective-permute-done | bytes 262176 | tf_op jit(solution)/shard_map/ppermute | solution.py:558
  395.2 3.2 out_grad.1
  398.4 6.5 %collective-permute-done.26.refs_2_ = bf16[256,1024]{1,0:T(8,128)(2,1)} collective-permute-done((bf16[256,1024]{1,0:T(8,128)(2,1)}, bf16[256,1024]{1,0:T(8,128)(2,1)}, u32[]{:S(2)}, u32[]{:S(2)}) %collective-permute-start.26) | collective-permute-done | bytes 524320 | tf_op jit(solution)/shard_map/ppermute | solution.py:533
  404.9 2.6 result.1
  413.5 4.8 %qkv_grad.1 = (f32[256,3072]{1,0:T(8,128)}, f32[256,1024]{1,0:T(8,128)}, f32[256,1]{1,0:T(8,128)}) custom-call(bf16[8,512,128]{2,1,0:T(8,128)(2,1)} %pad_maximum_fusion.1.refs_0_, bf16[8,512,128]{2,1,0:T(8,128)(2,1)} %pad_maximum_fusion.2.refs_1_, bf16[256,3072]{1,0:T(8,128)(2,1)} %refs_2_, f32[256,1]{1,0:T(8,128)} %copy.32.gain_a.refs_3_, ...), custom_call_target="tpu_custom_call" | custom-call | flops 1000000 | bytes 7866372 | tf_op jit(solution)/shard_map/qkv_grad/pallas_call | solution.py:40
  420.6 3.4 last.1
  424.0 4.7 %collective-permute-start.32 = (bf16[1,128,1024]{2,1,0:T(8,128)(2,1)}, bf16[1,128,1024]{2,1,0:T(8,128)(2,1)S(1)}, u32[]{:S(2)}, u32[]{:S(2)}) collective-permute-start(bf16[1,128,1024]{2,1,0:T(8,128)(2,1)} %get-tuple-element.169), channel_id=1, source_target_pairs={{16,0},{24,1},{20,2},{28,3},{0,4},{8,5},{4,6},{12,7},{17,8},{25,9}... | collective-permute-start | bytes 786440 | tf_op jit(solution)/shard_map/ppermute | solution.py:519
  431.2 17.7 %collective-permute-done.32 = bf16[1,128,1024]{2,1,0:T(8,128)(2,1)S(1)} collective-permute-done((bf16[1,128,1024]{2,1,0:T(8,128)(2,1)}, bf16[1,128,1024]{2,1,0:T(8,128)(2,1)S(1)}, u32[]{:S(2)}, u32[]{:S(2)}) %collective-permute-start.32) | collective-permute-done | bytes 262176 | tf_op jit(solution)/shard_map/ppermute | solution.py:519
  451.7 3.3 in_grad.1
  (210 shorter events, 70.8 us)
Async XLA Ops:
  9.1 14.4 %collective-permute-start = (bf16[1,144,1024]{2,1,0:T(8,128)(2,1)S(1)}, bf16[1,144,1024]{2,1,0:T(8,128)(2,1)S(1)}, u32[]{:S(2)}, u32[]{:S(2)}) collective-permute-start(bf16[1,144,1024]{2,1,0:T(8,128)(2,1)S(1)} %get-tuple-element.94), channel_id=1, source_target_pairs={{0,0},{1,8},{2,4},{3,12},{4,16},{5,24},{6,20},{7,28},{8,1},{9,9},{... | collective-permute-start | bytes 884744 | tf_op jit(solution)/shard_map/ppermute | solution.py:515
  9.8 16.0 %collective-permute-start.1 = (bf16[1,144,1024]{2,1,0:T(8,128)(2,1)S(1)}, bf16[1,144,1024]{2,1,0:T(8,128)(2,1)S(1)}, u32[]{:S(2)}, u32[]{:S(2)}) collective-permute-start(bf16[1,144,1024]{2,1,0:T(8,128)(2,1)S(1)} %get-tuple-element.95), channel_id=1, source_target_pairs={{0,16},{1,24},{2,20},{3,28},{4,0},{5,8},{6,4},{7,12},{8,17},{9,25}... | collective-permute-start | bytes 884744 | tf_op jit(solution)/shard_map/ppermute | solution.py:515
  26.5 58.2 %all-to-all-start = ((bf16[4,320,768]{2,1,0:T(8,128)(2,1)}), bf16[4,320,768]{2,1,0:T(8,128)(2,1)S(1)}, u32[]{:S(2)}, u32[]{:S(2)}) async-start(bf16[4,320,768]{2,1,0:T(8,128)(2,1)} %cut.1), calls=%async_computation | async-start | bytes 3932160 | tf_op jit(solution)/shard_map/all_to_all | solution.py:608
  36.5 127.6 %all-gather.6.cloned.1.call-start = ((), (), s32[]{:S(2)}) async-start(), calls=%async_computation.7 | async-start | bytes 3538944 | tf_op jit(solution)/shard_map/all_gather | solution.py:622
  38.8 34.0 %collective-permute-start.3 = (bf16[272,1024]{1,0:T(8,128)(2,1)}, bf16[272,1024]{1,0:T(8,128)(2,1)}, u32[]{:S(2)}, u32[]{:S(2)}) collective-permute-start(bf16[272,1024]{1,0:T(8,128)(2,1)} %unit1.1.refs_0_.refs_4_), channel_id=1, source_target_pairs={{0,2},{1,3},{2,0},{3,1},{4,6},{5,7},{6,4},{7,5},{8,10},{9,11},{10,... | collective-permute-start | bytes 1671176 | tf_op jit(solution)/shard_map/ppermute | solution.py:533
  41.1 43.5 %collective-permute-start.2 = (bf16[272,1024]{1,0:T(8,128)(2,1)}, bf16[272,1024]{1,0:T(8,128)(2,1)}, u32[]{:S(2)}, u32[]{:S(2)}) collective-permute-start(bf16[272,1024]{1,0:T(8,128)(2,1)} %unit1.1.refs_0_.refs_4_), channel_id=1, source_target_pairs={{0,1},{1,0},{2,3},{3,2},{4,5},{5,4},{6,7},{7,6},{8,9},{9,8},{10,11... | collective-permute-start | bytes 1671176 | tf_op jit(solution)/shard_map/ppermute | solution.py:533
  72.8 11.8 %collective-permute-start.4 = (bf16[272,1024]{1,0:T(8,128)(2,1)}, bf16[272,1024]{1,0:T(8,128)(2,1)}, u32[]{:S(2)}, u32[]{:S(2)}) collective-permute-start(bf16[272,1024]{1,0:T(8,128)(2,1)} %collective-permute-done.3.refs_2_.refs_6_), channel_id=1, source_target_pairs={{0,1},{1,0},{2,3},{3,2},{4,5},{5,4},{6,7},{7,6},{8,9},{9,8},{10,11... | collective-permute-start | bytes 1671176 | tf_op jit(solution)/shard_map/ppermute | solution.py:533
  73.5 11.1 %collective-permute-start.6 = (bf16[1,128,1024]{2,1,0:T(8,128)(2,1)S(1)}, bf16[1,128,1024]{2,1,0:T(8,128)(2,1)S(1)}, u32[]{:S(2)}, u32[]{:S(2)}) collective-permute-start(bf16[1,128,1024]{2,1,0:T(8,128)(2,1)S(1)} %get-tuple-element.186), channel_id=1, source_target_pairs={{0,16},{1,24},{2,20},{3,28},{4,0},{5,8},{6,4},{7,12},{8,17},{9,25}... | collective-permute-start | bytes 786440 | tf_op jit(solution)/shard_map/ppermute | solution.py:515
  84.7 17.1 %collective-permute-start.8 = (bf16[256,1024]{1,0:T(8,128)(2,1)S(1)}, bf16[256,1024]{1,0:T(8,128)(2,1)S(1)}, u32[]{:S(2)}, u32[]{:S(2)}) collective-permute-start(bf16[256,1024]{1,0:T(8,128)(2,1)S(1)} %bitcast.35), channel_id=1, source_target_pairs={{0,2},{1,3},{2,0},{3,1},{4,6},{5,7},{6,4},{7,5},{8,10},{9,11},{10,... | collective-permute-start | bytes 1572872 | tf_op jit(solution)/shard_map/ppermute | solution.py:533
  94.1 204.4 %reduce-scatter.2.cloned.1.call-start = ((), (), s32[]{:S(2)}) async-start(), calls=%async_computation.5 | async-start | bytes 3538944 | tf_op jit(solution)/shard_map/reduce_scatter | solution.py:742
  94.2 18.8 %collective-permute-start.7 = (bf16[256,1024]{1,0:T(8,128)(2,1)S(1)}, bf16[256,1024]{1,0:T(8,128)(2,1)S(1)}, u32[]{:S(2)}, u32[]{:S(2)}) collective-permute-start(bf16[256,1024]{1,0:T(8,128)(2,1)S(1)} %bitcast.36), channel_id=1, source_target_pairs={{0,1},{1,0},{2,3},{3,2},{4,5},{5,4},{6,7},{7,6},{8,9},{9,8},{10,11... | collective-permute-start | bytes 1572872 | tf_op jit(solution)/shard_map/ppermute | solution.py:533
  101.9 11.2 %collective-permute-start.9 = (bf16[256,1024]{1,0:T(8,128)(2,1)S(1)}, bf16[256,1024]{1,0:T(8,128)(2,1)S(1)}, u32[]{:S(2)}, u32[]{:S(2)}) collective-permute-start(bf16[256,1024]{1,0:T(8,128)(2,1)S(1)} %collective-permute-done.8.refs_6_), channel_id=1, source_target_pairs={{0,1},{1,0},{2,3},{3,2},{4,5},{5,4},{6,7},{7,6},{8,9},{9,8},{10,11... | collective-permute-start | bytes 1572872 | tf_op jit(solution)/shard_map/ppermute | solution.py:533
  129.6 14.9 %collective-permute-start.12 = (bf16[256,1024]{1,0:T(8,128)(2,1)S(1)}, bf16[256,1024]{1,0:T(8,128)(2,1)S(1)}, u32[]{:S(2)}, u32[]{:S(2)}) collective-permute-start(bf16[256,1024]{1,0:T(8,128)(2,1)S(1)} %add_convert_fusion.6), channel_id=1, source_target_pairs={{0,2},{1,3},{2,0},{3,1},{4,6},{5,7},{6,4},{7,5},{8,10},{9,11},{10,... | collective-permute-start | bytes 1572872 | tf_op jit(solution)/shard_map/ppermute | solution.py:533
  148.2 13.9 %collective-permute-start.14 = (bf16[256,1024]{1,0:T(8,128)(2,1)}, bf16[256,1024]{1,0:T(8,128)(2,1)S(1)}, u32[]{:S(2)}, u32[]{:S(2)}) collective-permute-start(bf16[256,1024]{1,0:T(8,128)(2,1)} %get-tuple-element.118.refs_0_), channel_id=1, source_target_pairs={{0,2},{1,3},{2,0},{3,1},{4,6},{5,7},{6,4},{7,5},{8,10},{9,11},{10,... | collective-permute-start | bytes 1572872 | tf_op jit(solution)/shard_map/ppermute | solution.py:533
  149.9 12.2 %collective-permute-start.13 = (bf16[256,1024]{1,0:T(8,128)(2,1)}, bf16[256,1024]{1,0:T(8,128)(2,1)S(1)}, u32[]{:S(2)}, u32[]{:S(2)}) collective-permute-start(bf16[256,1024]{1,0:T(8,128)(2,1)} %get-tuple-element.118.refs_0_), channel_id=1, source_target_pairs={{0,1},{1,0},{2,3},{3,2},{4,5},{5,4},{6,7},{7,6},{8,9},{9,8},{10,11... | collective-permute-start | bytes 1572872 | tf_op jit(solution)/shard_map/ppermute | solution.py:533
  186.7 18.0 %collective-permute-start.16 = (bf16[256,1024]{1,0:T(8,128)(2,1)}, bf16[256,1024]{1,0:T(8,128)(2,1)S(1)}, u32[]{:S(2)}, u32[]{:S(2)}) collective-permute-start(bf16[256,1024]{1,0:T(8,128)(2,1)} %get-tuple-element.124), channel_id=1, source_target_pairs={{0,1},{1,0},{2,3},{3,2},{4,5},{5,4},{6,7},{7,6},{8,9},{9,8},{10,11... | collective-permute-start | bytes 1572872 | tf_op jit(solution)/shard_map/ppermute | solution.py:533
  189.9 14.8 %collective-permute-start.18 = (bf16[256,1024]{1,0:T(8,128)(2,1)S(1)}, bf16[256,1024]{1,0:T(8,128)(2,1)S(1)}, u32[]{:S(2)}, u32[]{:S(2)}) collective-permute-start(bf16[256,1024]{1,0:T(8,128)(2,1)S(1)} %add_convert_fusion.5), channel_id=1, source_target_pairs={{0,2},{1,3},{2,0},{3,1},{4,6},{5,7},{6,4},{7,5},{8,10},{9,11},{10,... | collective-permute-start | bytes 1572872 | tf_op jit(solution)/shard_map/ppermute | solution.py:533
  209.6 13.9 %collective-permute-start.20 = (bf16[256,1024]{1,0:T(8,128)(2,1)}, bf16[256,1024]{1,0:T(8,128)(2,1)S(1)}, u32[]{:S(2)}, u32[]{:S(2)}) collective-permute-start(bf16[256,1024]{1,0:T(8,128)(2,1)} %get-tuple-element.145.refs_0_), channel_id=1, source_target_pairs={{0,2},{1,3},{2,0},{3,1},{4,6},{5,7},{6,4},{7,5},{8,10},{9,11},{10,... | collective-permute-start | bytes 1572872 | tf_op jit(solution)/shard_map/ppermute | solution.py:533
  210.2 23.9 %collective-permute-start.22 = (bf16[4,656,128]{2,1,0:T(8,128)(2,1)S(1)}, bf16[4,656,128]{2,1,0:T(8,128)(2,1)S(1)}, u32[]{:S(2)}, u32[]{:S(2)}) collective-permute-start(bf16[4,656,128]{2,1,0:T(8,128)(2,1)S(1)} %slice.71), channel_id=1, source_target_pairs={{0,4},{4,0},{8,12},{12,8},{16,20},{20,16},{24,28},{28,24},{1,5},{5... | collective-permute-start | bytes 2015240 | tf_op jit(solution)/shard_map/ppermute | solution.py:558
  210.7 23.5 %collective-permute-start.19 = (bf16[256,1024]{1,0:T(8,128)(2,1)S(1)}, bf16[256,1024]{1,0:T(8,128)(2,1)S(1)}, u32[]{:S(2)}, u32[]{:S(2)}) collective-permute-start(bf16[256,1024]{1,0:T(8,128)(2,1)S(1)} %copy-done.21), channel_id=1, source_target_pairs={{0,1},{1,0},{2,3},{3,2},{4,5},{5,4},{6,7},{7,6},{8,9},{9,8},{10,11... | collective-permute-start | bytes 1572872 | tf_op jit(solution)/shard_map/ppermute | solution.py:533
  223.5 10.7 %collective-permute-start.21 = (bf16[256,1024]{1,0:T(8,128)(2,1)S(1)}, bf16[256,1024]{1,0:T(8,128)(2,1)S(1)}, u32[]{:S(2)}, u32[]{:S(2)}) collective-permute-start(bf16[256,1024]{1,0:T(8,128)(2,1)S(1)} %collective-permute-done.20.refs_2_), channel_id=1, source_target_pairs={{0,1},{1,0},{2,3},{3,2},{4,5},{5,4},{6,7},{7,6},{8,9},{9,8},{10,11... | collective-permute-start | bytes 1572872 | tf_op jit(solution)/shard_map/ppermute | solution.py:533
  234.3 22.4 %collective-permute-start.23 = (bf16[2,656,128]{2,1,0:T(8,128)(2,1)S(1)}, bf16[2,656,128]{2,1,0:T(8,128)(2,1)S(1)}, u32[]{:S(2)}, u32[]{:S(2)}) collective-permute-start(bf16[2,656,128]{2,1,0:T(8,128)(2,1)S(1)} %slice.73), channel_id=1, source_target_pairs={{0,8},{4,12},{8,0},{12,4},{16,24},{20,28},{24,16},{28,20},{1,9},{5... | collective-permute-start | bytes 1007624 | tf_op jit(solution)/shard_map/ppermute | solution.py:558
  256.6 45.7 %collective-permute-start.34 = (bf16[4,512,128]{2,1,0:T(8,128)(2,1)S(1)}, bf16[4,512,128]{2,1,0:T(8,128)(2,1)}, u32[]{:S(2)}, u32[]{:S(2)}) collective-permute-start(bf16[4,512,128]{2,1,0:T(8,128)(2,1)S(1)} %slice.75), channel_id=1, source_target_pairs={{0,4},{4,0},{8,12},{12,8},{16,20},{20,16},{24,28},{28,24},{1,5},{5... | collective-permute-start | bytes 1572872 | tf_op jit(solution)/shard_map/ppermute | solution.py:558
  256.9 25.5 %collective-permute-start.46 = (bf16[1,656,128]{2,1,0:T(8,128)(2,1)S(1)}, bf16[1,656,128]{2,1,0:T(8,128)(2,1)S(1)}, u32[]{:S(2)}, u32[]{:S(2)}) collective-permute-start(bf16[1,656,128]{2,1,0:T(8,128)(2,1)S(1)} %slice.91), channel_id=1, source_target_pairs={{0,16},{4,20},{8,24},{12,28},{16,0},{20,4},{24,8},{28,12},{1,17},{... | collective-permute-start | bytes 503816 | tf_op jit(solution)/shard_map/ppermute | solution.py:558
  281.4 32.9 %collective-permute-start.40 = (bf16[4,512,128]{2,1,0:T(8,128)(2,1)}, bf16[4,512,128]{2,1,0:T(8,128)(2,1)S(1)}, u32[]{:S(2)}, u32[]{:S(2)}) collective-permute-start(bf16[4,512,128]{2,1,0:T(8,128)(2,1)} %slice.83), channel_id=1, source_target_pairs={{0,4},{4,0},{8,12},{12,8},{16,20},{20,16},{24,28},{28,24},{1,5},{5... | collective-permute-start | bytes 1572872 | tf_op jit(solution)/shard_map/ppermute | solution.py:558
  282.4 28.4 %collective-permute-start.47 = (bf16[1,656,128]{2,1,0:T(8,128)(2,1)S(1)}, bf16[1,656,128]{2,1,0:T(8,128)(2,1)S(1)}, u32[]{:S(2)}, u32[]{:S(2)}) collective-permute-start(bf16[1,656,128]{2,1,0:T(8,128)(2,1)S(1)} %add_convert_fusion.10), channel_id=1, source_target_pairs={{0,16},{4,20},{8,24},{12,28},{16,0},{20,4},{24,8},{28,12},{1,17},{... | collective-permute-start | bytes 503816 | tf_op jit(solution)/shard_map/ppermute | solution.py:558
  298.5 10.9 %all-to-all-start.3 = ((bf16[4,2,32,656]{3,2,1,0:T(8,128)(2,1)}), bf16[4,2,32,656]{3,2,1,0:T(8,128)(2,1)S(1)}, u32[]{:S(2)}, u32[]{:S(2)}) async-start(bf16[4,2,32,656]{3,2,1,0:T(8,128)(2,1)} %bitcast.41), calls=%async_computation.4 | async-start | bytes 786432 | tf_op jit(solution)/shard_map/all_to_all | solution.py:775
  301.9 148.0 %all-gather.4.cloned.1.call-start = ((), (), s32[]{:S(2)}) async-start(), calls=%async_computation.6 | async-start | bytes 3022848 | tf_op jit(solution)/shard_map/all_gather | solution.py:777
  311.6 29.1 %collective-permute-start.48 = (bf16[2,656,128]{2,1,0:T(8,128)(2,1)}, bf16[2,656,128]{2,1,0:T(8,128)(2,1)S(1)}, u32[]{:S(2)}, u32[]{:S(2)}) collective-permute-start(bf16[2,656,128]{2,1,0:T(8,128)(2,1)} %pad_maximum_fusion.10), channel_id=1, source_target_pairs={{0,8},{4,12},{8,0},{12,4},{16,24},{20,28},{24,16},{28,20},{1,9},{5... | collective-permute-start | bytes 1007624 | tf_op jit(solution)/shard_map/ppermute | solution.py:558
  314.2 13.8 %collective-permute-start.36 = (bf16[1,512,128]{2,1,0:T(8,128)(2,1)S(1)}, bf16[1,512,128]{2,1,0:T(8,128)(2,1)S(1)}, u32[]{:S(2)}, u32[]{:S(2)}) collective-permute-start(bf16[1,512,128]{2,1,0:T(8,128)(2,1)S(1)} %slice.95), channel_id=1, source_target_pairs={{0,16},{4,20},{8,24},{12,28},{16,0},{20,4},{24,8},{28,12},{1,17},{... | collective-permute-start | bytes 393224 | tf_op jit(solution)/shard_map/ppermute | solution.py:558
  314.5 26.0 %collective-permute-start.41 = (bf16[2,512,128]{2,1,0:T(8,128)(2,1)S(1)}, bf16[2,512,128]{2,1,0:T(8,128)(2,1)S(1)}, u32[]{:S(2)}, u32[]{:S(2)}) collective-permute-start(bf16[2,512,128]{2,1,0:T(8,128)(2,1)S(1)} %slice.99), channel_id=1, source_target_pairs={{0,8},{4,12},{8,0},{12,4},{16,24},{20,28},{24,16},{28,20},{1,9},{5... | collective-permute-start | bytes 786440 | tf_op jit(solution)/shard_map/ppermute | solution.py:558
  336.3 14.9 %collective-permute-start.37 = (bf16[1,512,128]{2,1,0:T(8,128)(2,1)S(1)}, bf16[1,512,128]{2,1,0:T(8,128)(2,1)S(1)}, u32[]{:S(2)}, u32[]{:S(2)}) collective-permute-start(bf16[1,512,128]{2,1,0:T(8,128)(2,1)S(1)} %maximum_bitcast_fusion), channel_id=1, source_target_pairs={{0,16},{4,20},{8,24},{12,28},{16,0},{20,4},{24,8},{28,12},{1,17},{... | collective-permute-start | bytes 393224 | tf_op jit(solution)/shard_map/ppermute | solution.py:558
  340.7 17.8 %collective-permute-start.42 = (bf16[1,512,128]{2,1,0:T(8,128)(2,1)S(1)}, bf16[1,512,128]{2,1,0:T(8,128)(2,1)S(1)}, u32[]{:S(2)}, u32[]{:S(2)}) collective-permute-start(bf16[1,512,128]{2,1,0:T(8,128)(2,1)S(1)} %slice.101), channel_id=1, source_target_pairs={{0,16},{4,20},{8,24},{12,28},{16,0},{20,4},{24,8},{28,12},{1,17},{... | collective-permute-start | bytes 393224 | tf_op jit(solution)/shard_map/ppermute | solution.py:558
  340.8 51.3 %collective-permute-start.49 = (bf16[4,656,128]{2,1,0:T(8,128)(2,1)S(1)}, bf16[4,656,128]{2,1,0:T(8,128)(2,1)S(1)}, u32[]{:S(2)}, u32[]{:S(2)}) collective-permute-start(bf16[4,656,128]{2,1,0:T(8,128)(2,1)S(1)} %pad_maximum_fusion.3), channel_id=1, source_target_pairs={{0,4},{4,0},{8,12},{12,8},{16,20},{20,16},{24,28},{28,24},{1,5},{5... | collective-permute-start | bytes 2015240 | tf_op jit(solution)/shard_map/ppermute | solution.py:558
  351.2 21.6 %collective-permute-start.38 = (bf16[2,512,128]{2,1,0:T(8,128)(2,1)S(1)}, bf16[2,512,128]{2,1,0:T(8,128)(2,1)S(1)}, u32[]{:S(2)}, u32[]{:S(2)}) collective-permute-start(bf16[2,512,128]{2,1,0:T(8,128)(2,1)S(1)} %pad_maximum_fusion.11), channel_id=1, source_target_pairs={{0,8},{4,12},{8,0},{12,4},{16,24},{20,28},{24,16},{28,20},{1,9},{5... | collective-permute-start | bytes 786440 | tf_op jit(solution)/shard_map/ppermute | solution.py:558
  362.5 18.8 %collective-permute-start.25 = (bf16[256,1024]{1,0:T(8,128)(2,1)}, bf16[256,1024]{1,0:T(8,128)(2,1)}, u32[]{:S(2)}, u32[]{:S(2)}) collective-permute-start(bf16[256,1024]{1,0:T(8,128)(2,1)} %get-tuple-element.158), channel_id=1, source_target_pairs={{0,1},{1,0},{2,3},{3,2},{4,5},{5,4},{6,7},{7,6},{8,9},{9,8},{10,11... | collective-permute-start | bytes 1572872 | tf_op jit(solution)/shard_map/ppermute | solution.py:533
  366.8 14.4 %collective-permute-start.43 = (bf16[1,512,128]{2,1,0:T(8,128)(2,1)S(1)}, bf16[1,512,128]{2,1,0:T(8,128)(2,1)S(1)}, u32[]{:S(2)}, u32[]{:S(2)}) collective-permute-start(bf16[1,512,128]{2,1,0:T(8,128)(2,1)S(1)} %maximum_bitcast_fusion.1), channel_id=1, source_target_pairs={{0,16},{4,20},{8,24},{12,28},{16,0},{20,4},{24,8},{28,12},{1,17},{... | collective-permute-start | bytes 393224 | tf_op jit(solution)/shard_map/ppermute | solution.py:558
  372.7 17.9 %collective-permute-start.30 = (bf16[256,1024]{1,0:T(8,128)(2,1)}, bf16[256,1024]{1,0:T(8,128)(2,1)S(1)}, u32[]{:S(2)}, u32[]{:S(2)}) collective-permute-start(bf16[256,1024]{1,0:T(8,128)(2,1)} %get-tuple-element.167), channel_id=1, source_target_pairs={{0,1},{1,0},{2,3},{3,2},{4,5},{5,4},{6,7},{7,6},{8,9},{9,8},{10,11... | collective-permute-start | bytes 1572872 | tf_op jit(solution)/shard_map/ppermute | solution.py:533
  373.6 34.0 %collective-permute-start.39 = (bf16[4,512,128]{2,1,0:T(8,128)(2,1)}, bf16[4,512,128]{2,1,0:T(8,128)(2,1)}, u32[]{:S(2)}, u32[]{:S(2)}) collective-permute-start(bf16[4,512,128]{2,1,0:T(8,128)(2,1)} %pad_maximum_fusion.8), channel_id=1, source_target_pairs={{0,4},{4,0},{8,12},{12,8},{16,20},{20,16},{24,28},{28,24},{1,5},{5... | collective-permute-start | bytes 1572872 | tf_op jit(solution)/shard_map/ppermute | solution.py:558
  381.4 10.8 %collective-permute-start.24 = (bf16[256,1024]{1,0:T(8,128)(2,1)S(1)}, bf16[256,1024]{1,0:T(8,128)(2,1)}, u32[]{:S(2)}, u32[]{:S(2)}) collective-permute-start(bf16[256,1024]{1,0:T(8,128)(2,1)S(1)} %copy-done.17), channel_id=1, source_target_pairs={{0,1},{1,0},{2,3},{3,2},{4,5},{5,4},{6,7},{7,6},{8,9},{9,8},{10,11... | collective-permute-start | bytes 1572872 | tf_op jit(solution)/shard_map/ppermute | solution.py:533
  389.7 15.2 %collective-permute-start.26 = (bf16[256,1024]{1,0:T(8,128)(2,1)}, bf16[256,1024]{1,0:T(8,128)(2,1)}, u32[]{:S(2)}, u32[]{:S(2)}) collective-permute-start(bf16[256,1024]{1,0:T(8,128)(2,1)} %add_convert_fusion.4), channel_id=1, source_target_pairs={{0,2},{1,3},{2,0},{3,1},{4,6},{5,7},{6,4},{7,5},{8,10},{9,11},{10,... | collective-permute-start | bytes 1572872 | tf_op jit(solution)/shard_map/ppermute | solution.py:533
  390.6 20.7 %collective-permute-start.45 = (bf16[4,512,128]{2,1,0:T(8,128)(2,1)}, bf16[4,512,128]{2,1,0:T(8,128)(2,1)}, u32[]{:S(2)}, u32[]{:S(2)}) collective-permute-start(bf16[4,512,128]{2,1,0:T(8,128)(2,1)} %pad_maximum_fusion.9), channel_id=1, source_target_pairs={{0,4},{4,0},{8,12},{12,8},{16,20},{20,16},{24,28},{28,24},{1,5},{5... | collective-permute-start | bytes 1572872 | tf_op jit(solution)/shard_map/ppermute | solution.py:558
  392.2 27.6 %collective-permute-start.29 = (bf16[256,1024]{1,0:T(8,128)(2,1)}, bf16[256,1024]{1,0:T(8,128)(2,1)S(1)}, u32[]{:S(2)}, u32[]{:S(2)}) collective-permute-start(bf16[256,1024]{1,0:T(8,128)(2,1)} %get-tuple-element.165), channel_id=1, source_target_pairs={{0,1},{1,0},{2,3},{3,2},{4,5},{5,4},{6,7},{7,6},{8,9},{9,8},{10,11... | collective-permute-start | bytes 1572872 | tf_op jit(solution)/shard_map/ppermute | solution.py:533
  392.2 27.6 %collective-permute-start.31 = (bf16[256,1024]{1,0:T(8,128)(2,1)}, bf16[256,1024]{1,0:T(8,128)(2,1)}, u32[]{:S(2)}, u32[]{:S(2)}) collective-permute-start(bf16[256,1024]{1,0:T(8,128)(2,1)} %add_convert_fusion.3), channel_id=1, source_target_pairs={{0,2},{1,3},{2,0},{3,1},{4,6},{5,7},{6,4},{7,5},{8,10},{9,11},{10,... | collective-permute-start | bytes 1572872 | tf_op jit(solution)/shard_map/ppermute | solution.py:533
  407.6 22.7 %collective-permute-start.27 = (bf16[1,128,1024]{2,1,0:T(8,128)(2,1)}, bf16[1,128,1024]{2,1,0:T(8,128)(2,1)S(1)}, u32[]{:S(2)}, u32[]{:S(2)}) collective-permute-start(bf16[1,128,1024]{2,1,0:T(8,128)(2,1)} %get-tuple-element.159), channel_id=1, source_target_pairs={{16,0},{24,1},{20,2},{28,3},{0,4},{8,5},{4,6},{12,7},{17,8},{25,9}... | collective-permute-start | bytes 786440 | tf_op jit(solution)/shard_map/ppermute | solution.py:519
  407.6 22.6 %collective-permute-start.28 = (bf16[1,128,1024]{2,1,0:T(8,128)(2,1)}, bf16[1,128,1024]{2,1,0:T(8,128)(2,1)S(1)}, u32[]{:S(2)}, u32[]{:S(2)}) collective-permute-start(bf16[1,128,1024]{2,1,0:T(8,128)(2,1)} %get-tuple-element.160), channel_id=1, source_target_pairs={{0,0},{8,1},{4,2},{12,3},{16,4},{24,5},{20,6},{28,7},{1,8},{9,9},{... | collective-permute-start | bytes 786440 | tf_op jit(solution)/shard_map/ppermute | solution.py:519
  424.0 24.9 %collective-permute-start.32 = (bf16[1,128,1024]{2,1,0:T(8,128)(2,1)}, bf16[1,128,1024]{2,1,0:T(8,128)(2,1)S(1)}, u32[]{:S(2)}, u32[]{:S(2)}) collective-permute-start(bf16[1,128,1024]{2,1,0:T(8,128)(2,1)} %get-tuple-element.169), channel_id=1, source_target_pairs={{16,0},{24,1},{20,2},{28,3},{0,4},{8,5},{4,6},{12,7},{17,8},{25,9}... | collective-permute-start | bytes 786440 | tf_op jit(solution)/shard_map/ppermute | solution.py:519
  428.7 20.2 %collective-permute-start.33 = (bf16[1,128,1024]{2,1,0:T(8,128)(2,1)}, bf16[1,128,1024]{2,1,0:T(8,128)(2,1)S(1)}, u32[]{:S(2)}, u32[]{:S(2)}) collective-permute-start(bf16[1,128,1024]{2,1,0:T(8,128)(2,1)} %get-tuple-element.170), channel_id=1, source_target_pairs={{0,0},{8,1},{4,2},{12,3},{16,4},{24,5},{20,6},{28,7},{1,8},{9,9},{... | collective-permute-start | bytes 786440 | tf_op jit(solution)/shard_map/ppermute | solution.py:519
  (39 other events, 292.6 us)
Sparse Core Ops, SparseCore 0:
  94.2 56.5 all-gather.5
  205.0 93.4 reduce-scatter.1
  311.0 72.7 all-gather.3

commit v3 on v2

v3 whole, which is shorter than its diff:
```python
import functools

import jax
import jax.numpy as jnp
from jax import lax
from jax.experimental import pallas as pl
from jax.experimental.pallas import tpu as pltpu
from jax.sharding import PartitionSpec as P

HEADS = 16
rope_base = 160000.0
norm_eps = 1e-05
masked_score = -1e30
bf16 = jnp.bfloat16
f32 = jnp.float32
NT = (((1,), (1,)), ((), ()))
NN = (((1,), (0,)), ((), ()))
TN = (((0,), (0,)), ((), ()))
TAG = 16


def mm(a, b, dims=NN):
    return lax.dot_general(a, b, dims, preferred_element_type=f32)


class Late:
    def __init__(self, value):
        self.value = self.shape_is = value


def copies(pairs, sems):
    return [pltpu.make_async_copy(a, b, sems.at[k]) for k, (a, b) in enumerate(pairs)]


def call(kernel, name, out_shape, grid, scratch, args, flops, limit=56):
    def spec(a):
        if isinstance(a, tuple):
            return a[1]
        if isinstance(a, Late):
            return pl.BlockSpec(memory_space=pl.ANY)
        if a.dtype == jnp.int32:
            return pl.BlockSpec(memory_space=pltpu.SMEM)
        return pl.BlockSpec(
            a.shape, lambda s, nd=len(a.shape): (0,) * nd, pipeline_mode=pl.Buffered(1)
        )

    specs = [spec(a) for a in args]
    args = [a[0] if isinstance(a, tuple) else getattr(a, "value", a) for a in args]
    outs = [spec(a) for a in out_shape]
    out_shape = [a[0] if isinstance(a, tuple) else getattr(a, "shape_is", a) for a in out_shape]
    moved = sum(a.size * a.dtype.itemsize for a in args)
    moved += sum(a.size * a.dtype.itemsize for a in out_shape)
    return pl.pallas_call(
        kernel,
        grid=(grid,),
        in_specs=specs,
        out_specs=outs,
        out_shape=out_shape,
        scratch_shapes=scratch,
        compiler_params=pltpu.CompilerParams(vmem_limit_bytes=limit << 20),
        cost_estimate=pl.CostEstimate(
            flops=int(flops), bytes_accessed=int(moved), transcendentals=0
        ),
        name=name,
    )(*args)


def shape_of(shape, dtype=bf16):
    return jax.ShapeDtypeStruct(shape, dtype)


def head_mask(shape, head, size):
    return lax.broadcasted_iota(jnp.int32, shape, 1) // size == head


def swap(values, size):
    width, half = values.shape[1], size // 2
    if width == size:
        return jnp.concatenate([values[:, half:], values[:, :half]], axis=1)
    lane = lax.broadcasted_iota(jnp.int32, values.shape, 1) % size
    return jnp.where(
        lane < half, pltpu.roll(values, width - half, 1), pltpu.roll(values, half, 1)
    )


def norm_stats(values):
    center = values - jnp.mean(values, axis=-1, keepdims=True)
    rate = lax.rsqrt(jnp.mean(center * center, axis=-1, keepdims=True) + norm_eps)
    return center * rate, rate


def norm_back(grad, unit, rate):
    return rate * (
        grad
        - jnp.mean(grad, axis=-1, keepdims=True)
        - unit * jnp.mean(grad * unit, axis=-1, keepdims=True)
    )


class Plan:
    def __init__(self, fsdp, ctx, batch, span, width, units, rows):
        self.fsdp, self.ctx, self.span, self.width = fsdp, ctx, span, width
        self.pieces = ctx // fsdp
        self.n = batch // self.pieces
        self.part = self.pieces * span
        self.own = self.n * self.part
        self.length = span * ctx
        self.heads = HEADS // fsdp
        self.size = width // HEADS
        self.cols = self.heads * self.size
        self.units, self.rows = units, rows
        self.padded = -(-units // 256) * 256
        self.small = rows // ctx
        self.groups = 2 if self.heads % 2 == 0 else 1
        self.lanes = self.cols // self.groups
        self.slab = self.lanes // ctx
        self.table = min(128, self.cols)
        bits = [1 << b for b in range(ctx.bit_length() - 1)]
        self.order = bits
        self.last_order = bits[1:] + bits[:1]

    def locations(self):
        return [
            (i, j, (i * self.pieces + j) * self.span)
            for i in range(self.n)
            for j in range(self.pieces)
        ]


def storage(x, order):
    at = 0
    for bit in order:
        at = at * 2 + x // bit % 2
    return at


def cut_kernel(w, gain, at_ref, mine, other, *, p, feed):
    half, here = p.rows // 2, at_ref[0]
    side = at_ref[1] % 2
    near = pl.ds(pl.multiple_of(side * half, half), half)
    far = pl.ds(pl.multiple_of((1 - side) * half, half), half)
    size = p.units if feed else p.cols
    if feed and p.padded != size:
        mine[:, :, size:] = jnp.zeros((p.fsdp, 2 * half, p.padded - size), bf16)
        other[:, :, size:] = jnp.zeros((2, 2 * half, p.padded - size), bf16)
    for t in range(p.fsdp):
        o = t ^ here
        for m in range(2 if feed else 3):
            at = (m * p.fsdp + t) * size
            if feed:
                there = slice(m * half, (m + 1) * half), slice(0, size)
            else:
                there = slice(None), slice(m * size, (m + 1) * size)
            value = w[near, at : at + size].astype(f32) * gain[near, :]
            mine[(o,) + there] = value.astype(bf16)

            @pl.when(o < 2)
            def _(at=at, there=there, o=o):
                value = w[far, at : at + size].astype(f32) * gain[far, :]
                other[(o,) + there] = value.astype(bf16)


def unit_kernel(*refs, p):
    pieces, unit = refs[:-1], refs[-1]
    unit[p.own :, :] = jnp.zeros((TAG, p.width), bf16)
    for i, j, at in p.locations():
        ref = pieces[j]
        value, _ = norm_stats(ref[i, : p.span].astype(f32))
        unit[at : at + p.span] = value.astype(bf16)
        unit[p.own :, at : at + p.span] = ref[i, p.span :, : p.span]


def project_kernel(*refs, p):
    fs, gs = p.fsdp, p.part
    xs, rest = refs[:fs], refs[fs:]
    near, other, rest = rest[:fs], rest[fs : 2 * fs], rest[2 * fs :]
    cos, sin, at_ref, q_ref, k_ref, v_ref, seg_ref, w, x, w_sems, x_sems = rest
    step = pl.program_id(0)
    scale = p.size**-0.5
    half, side = p.rows // 2, at_ref[1] % 2
    pairs = []
    for o in range(fs):
        base = (at_ref[0] ^ o) * 2
        for part, at in ((near[o], base + side), (other[o], base + 1 - side)):
            pairs.append((part, w.at[pl.ds(pl.multiple_of(at * half, half), half), :]))
    w_copies = copies(pairs, w_sems)
    x_copies = copies([(xs[o], x.at[o]) for o in range(fs)], x_sems)

    @pl.when(step == 0)
    def _():
        for copy in x_copies[:1] + w_copies + x_copies[1:]:
            copy.start()
        for copy in w_copies:
            copy.wait()

    for o in range(fs):

        @pl.when(step == o)
        def _(o=o):
            x_copies[o].wait()
            for i in range(p.n):
                tag = x[o, p.own : p.own + TAG, i * gs : (i + 1) * gs].astype(f32)
                seg_ref[i, :, o * gs : (o + 1) * gs] = tag[:8]

    mixed = mm(x[step, : p.own], w[...])
    rows = pl.ds(pl.multiple_of(step * gs, gs), gs)
    reps = p.cols // p.table
    cosine = jnp.concatenate([cos[rows, :]] * reps, axis=1)
    sine = jnp.concatenate([sin[rows, :]] * reps, axis=1)
    for i in range(p.n):
        own = mixed[i * gs : (i + 1) * gs]
        query, key = own[:, : p.cols], own[:, p.cols : 2 * p.cols]
        query = (query * cosine + swap(query, p.size) * sine) * scale
        q_ref[i, rows, :] = query.astype(bf16)
        k_ref[i, rows, :] = (key * cosine + swap(key, p.size) * sine).astype(bf16)
        v_ref[i, rows, :] = own[:, 2 * p.cols :].astype(bf16)


def attend_kernel(q_ref, k_ref, v_ref, seg_ref, wo, *rest, p):
    fs, gs = p.fsdp, p.part
    parts, (att_ref, norm_ref, made) = rest[:fs], rest[fs:]
    step = pl.program_id(0)
    i, o = step // fs, step % fs
    rows = pl.ds(pl.multiple_of(o * gs, gs), gs)
    q, k, v = q_ref[i, rows, :], k_ref[i], v_ref[i]
    allowed = seg_ref[i, :, rows].T[:, :1] == seg_ref[i, :1, :]
    attended = jnp.zeros(q.shape, f32)
    norms = jnp.zeros((gs, 128), f32)
    lane = lax.broadcasted_iota(jnp.int32, norms.shape, 1)
    for head in range(p.heads):
        here = head_mask(q.shape, head, p.size)
        scores = mm(jnp.where(here, q, jnp.zeros_like(q)), k, NT)
        scores = jnp.where(allowed, scores, masked_score)
        peak = jnp.max(scores, axis=1, keepdims=True)
        weights = jnp.exp(scores - peak)
        total = jnp.sum(weights, axis=1, keepdims=True)
        attended = jnp.where(here, mm(weights.astype(bf16), v) / total, attended)
        norms = jnp.where(lane == head, peak + jnp.log(total), norms)
    norm_ref[i, :, rows] = norms.T[:8]
    attended = attended.astype(bf16)
    att_ref[i, rows, :] = attended
    made[...] = mm(attended, wo[...]).astype(bf16)
    for oo in range(fs):

        @pl.when(o == oo)
        def _(oo=oo):
            parts[oo][pl.ds(pl.multiple_of(i * gs, gs), gs), :] = made[...]


def flip_kernel(*refs, p):
    xs, out = refs[:-1], refs[-1]
    gs = p.part
    for o in range(p.fsdp):

        @pl.when(pl.program_id(0) == o)
        def _(o=o):
            for i in range(p.n):
                out[i, :, o * gs : (o + 1) * gs] = xs[o][i * gs : (i + 1) * gs, :].T


def shares(span_ref, i, a, b, fs):
    one, two = (i * fs + a) * 2, (i * fs + b) * 2
    return jnp.logical_and(
        span_ref[one] <= span_ref[two + 1], span_ref[two] <= span_ref[one + 1]
    )


def backward_kernel(*refs, p, group):
    fs, gs, cols = p.fsdp, p.part, p.lanes
    gls, rest = refs[:fs], refs[fs:]
    xt, wo, rest = rest[0], rest[1], rest[2:]
    q_ref, k_ref, v_ref, att_ref, seg_ref, norm_ref, cos, sin, c_ref, span_ref = rest[:10]
    gm, sums, kt, dqt, dk, dv, gl, seg_col, sum_qkv, sum_out, flat, sems, flat_sem = rest[10:]
    step = pl.program_id(0)
    scale = p.size**-0.5
    reps = cols // p.table

    def turned(grad, rows):
        cosine = jnp.concatenate([cos[rows, :]] * reps, axis=1)
        sine = jnp.concatenate([sin[rows, :]] * reps, axis=1)
        return grad * cosine - swap(grad, p.size) * sine

    pairs = [
        (gls[o].at[i * gs : (i + 1) * gs], gl.at[i, o * gs : (o + 1) * gs])
        for i in range(p.n)
        for o in range(fs)
    ]
    low_copies = copies(pairs, sems)
    flat_copy = pltpu.make_async_copy(xt, flat, flat_sem.at[0])

    @pl.when(step == 0)
    def _():
        for copy in low_copies:
            copy.start()
        flat_copy.start()

    @pl.when(step < p.n * fs)
    def _():
        i, o = step // fs, step % fs
        rows = pl.ds(pl.multiple_of(o * gs, gs), gs)
        for k in range(p.n * fs):

            @pl.when(step == k)
            def _(k=k):
                low_copies[k].wait()

        q = q_ref[i, rows, :]

        @pl.when(o == 0)
        def _():
            kt[...] = k_ref[i].T
            dk[...] = jnp.zeros_like(dk)
            dv[...] = jnp.zeros_like(dv)
            seg_col[...] = seg_ref[i].T[:, :1]

        attended = att_ref[i, rows, :]
        g = mm(gl[i, rows, :], wo[...], NT).astype(bf16)
        count = p.heads // p.groups
        picks = lax.broadcasted_iota(jnp.int32, (8, cols), 0)
        picks = (lax.broadcasted_iota(jnp.int32, (8, cols), 1) // p.size == picks).astype(f32)
        deltas = lax.dot_general(
            picks,
            g.astype(f32) * attended.astype(f32),
            NT,
            precision=lax.Precision.HIGHEST,
            preferred_element_type=f32,
        )
        zero = jnp.zeros_like(q)
        masks = [head_mask(q.shape, h, p.size) for h in range(count)]
        own_q = [jnp.where(mask, q, zero) for mask in masks]
        own_g = [jnp.where(mask, g, zero) for mask in masks]
        mine = seg_ref[i, :1, rows]
        dqt[...] = jnp.zeros_like(dqt)
        for kk in range(fs):
            keys = slice(kk * gs, (kk + 1) * gs)

            @pl.when(shares(span_ref, i, o, kk, fs))
            def _(keys=keys):
                k, v = k_ref[i, keys, :], v_ref[i, keys, :]
                allowed = seg_col[keys, :] == mine
                for h in range(count):
                    first = group * count + h
                    scores = jnp.where(allowed, mm(k, own_q[h], NT), masked_score)
                    probs = jnp.exp(scores - norm_ref[i, first : first + 1, rows])
                    grad = mm(v, own_g[h], NT)
                    grad = (probs * (grad - deltas[h : h + 1, :])).astype(bf16)
                    dv[keys, :] += mm(probs.astype(bf16), own_g[h])
                    dk[keys, :] += mm(grad, own_q[h])
                    at = slice(h * p.size, (h + 1) * p.size)
                    dqt[at, :] += mm(kt[at, keys], grad)

        gm[i, rows, :cols] = (turned(dqt[...].T, rows) * scale).astype(bf16)

        @pl.when(o == fs - 1)
        def _():
            gm[i, :, cols : 2 * cols] = turned(dk[...], slice(None)).astype(bf16)
            gm[i, :, 2 * cols :] = dv[...].astype(bf16)

    @pl.when(step == p.n * fs)
    def _():
        flat_copy.wait()
        total = [mm(flat[i], gm[i]) for i in range(p.n)]
        sum_qkv[...] = sum(total[1:], total[0])
        total = [mm(att_ref[i].T, gl[i]) for i in range(p.n)]
        sum_out[...] = sum(total[1:], total[0])
        small, slab = p.small, p.slab
        for cc in range(p.ctx):
            away = storage(c_ref[0] ^ cc, p.order)
            for ff in range(fs):
                for m in range(3):
                    part = sum_qkv[
                        ff * p.rows + cc * small : ff * p.rows + (cc + 1) * small,
                        m * cols : (m + 1) * cols,
                    ]
                    at = (ff * 3 + m) * small
                    sums[away, at : at + small, :] = part.astype(bf16)
            for d in range(p.width // cols):
                part = sum_out[cc * slab : (cc + 1) * slab, d * cols : (d + 1) * cols]
                at = 3 * fs * small + d * slab
                sums[away, at : at + slab, :] = part.astype(bf16)


def spread_kernel(*refs, p):
    gms, w, parts, made = refs[: p.groups], refs[p.groups], refs[p.groups + 1 : -1], refs[-1]
    o, lanes = pl.program_id(0), p.lanes
    rows = pl.ds(pl.multiple_of(o * p.part, p.part), p.part)
    for i in range(p.n):
        grad = jnp.concatenate(
            [gm[i, rows, m * lanes : (m + 1) * lanes] for m in range(3) for gm in gms], axis=1
        )
        made[i * p.part : (i + 1) * p.part] = mm(grad, w[...], NT).astype(bf16)
    for oo in range(p.fsdp):

        @pl.when(o == oo)
        def _(oo=oo):
            parts[oo][...] = made[...]


def mlp_kernel(*refs, p):
    fs, units, pad = p.fsdp, p.units, p.padded
    xs, cs, rest = refs[:fs], refs[fs : 2 * fs], refs[2 * fs :]
    near, other, rest = rest[:fs], rest[fs : 2 * fs], rest[2 * fs :]
    w_out, at_ref, rest = rest[0], rest[1], rest[2:]
    outs, us, rest = rest[:fs], rest[fs : 2 * fs], rest[2 * fs :]
    act_ref, da_ref, dg_ref, wa, wg, wm, x, ct, made, made_u, w_sems, sems, out_sems = rest
    step = pl.program_id(0)
    half, side = p.rows // 2, at_ref[1] % 2
    pairs = []
    for o in range(fs):
        base = (at_ref[0] ^ o) * 2
        for part, at in ((near[o], base + side), (other[o], base + 1 - side)):
            at = pl.ds(pl.multiple_of(at * half, half), half)
            pairs.append((part.at[:half], wa.at[at, :]))
            pairs.append((part.at[half:], wg.at[at, :]))
    w_copies = copies(pairs, w_sems)
    pairs = []
    for o in range(fs):
        pairs += [(xs[o], x.at[o]), (cs[o], ct.at[o])]
    x_copies = copies(pairs, sems)
    pairs = []
    for o in range(fs):
        pairs += [(made.at[o], outs[o]), (made_u.at[o], us[o])]
    out_copies = copies(pairs, out_sems)

    @pl.when(step == 0)
    def _():
        for copy in x_copies[:1] + w_copies + x_copies[1:]:
            copy.start()
        if pad != units:
            wm[units:, :] = jnp.zeros((pad - units, p.width), bf16)
        wm[:units, :] = w_out[...]
        for copy in w_copies:
            copy.wait()

    for o in range(fs):

        @pl.when(step == o)
        def _(o=o):
            x_copies[2 * o].wait()
            x_copies[2 * o + 1].wait()

    act, gate = mm(x[step], wa[...]), mm(x[step], wg[...])
    phi = 0.5 * (1.0 + lax.erf(act * (2.0**-0.5)))
    gelu = act * phi
    active = (gelu * gate).astype(bf16)
    made[step] = mm(active, wm[...]).astype(bf16)
    grad = mm(ct[step], wm[...], NT)
    slope = phi + act * (jnp.exp(-0.5 * act * act) * 0.3989422804014327)
    da, dg = (grad * gate * slope).astype(bf16), (grad * gelu).astype(bf16)
    made_u[step] = (mm(da, wa[...], NT) + mm(dg, wg[...], NT)).astype(bf16)
    act_ref[...], da_ref[...], dg_ref[...] = active, da, dg
    for o in range(fs):

        @pl.when(step == o)
        def _(o=o):
            out_copies[2 * o].start()
            out_copies[2 * o + 1].start()

    @pl.when(step == fs - 1)
    def _():
        for copy in out_copies:
            copy.wait()


def mlp_sums_kernel(*refs, p):
    fs, units = p.fsdp, p.units
    xs, cs, rest = refs[:fs], refs[fs : 2 * fs], refs[2 * fs :]
    act_ref, da_ref, dg_ref, c_ref, one, two, sa, sg, sm, x, ct = rest
    step = pl.program_id(0)

    @pl.when(step == 0)
    def _():
        sa[...] = jnp.zeros_like(sa)
        sg[...] = jnp.zeros_like(sg)
        sm[...] = jnp.zeros_like(sm)

    for o in range(fs):

        @pl.when(step == o)
        def _(o=o):
            x[...] = xs[o][...]
            ct[...] = cs[o][...]

    rows = pl.ds(pl.multiple_of(step * p.own, p.own), p.own)
    sa[...] += mm(x[...], da_ref[rows, :], TN)
    sg[...] += mm(x[...], dg_ref[rows, :], TN)
    sm[...] += mm(ct[...], act_ref[rows, :], TN)

    @pl.when(step == fs - 1)
    def _():
        for cc in range(p.ctx):
            away = storage(c_ref[0] ^ cc, p.order)
            late = storage(c_ref[0] ^ cc, p.last_order)
            for ff in range(fs):
                at = slice(ff * p.rows + cc * p.small, ff * p.rows + (cc + 1) * p.small)
                one[away, ff, 0] = sa[at, :units].astype(bf16)
                one[away, ff, 1] = sm[at, :units].astype(bf16)
                two[late, ff] = sg[at, :units].astype(bf16)


def middle_kernel(*refs, p):
    g = p.pieces
    hidden, (a, b, c), (residual, unit) = refs[:g], refs[g : g + 3], refs[g + 3 :]
    for i, j, at in p.locations():
        rows = slice(at, at + p.span)
        total = a[rows].astype(f32) + b[rows].astype(f32) + c[rows].astype(f32)
        total = total + hidden[j][i, : p.span].astype(f32)
        residual[rows] = total
        unit[rows] = norm_stats(total)[0].astype(bf16)


def turn_kernel(a, b, c, residual, cot, grad, low, *, p):
    for _, _, at in p.locations():
        rows = slice(at, at + p.span)
        u = a[rows].astype(f32) + b[rows].astype(f32) + c[rows].astype(f32)
        unit, rate = norm_stats(residual[rows])
        total = cot[rows].astype(f32) + norm_back(u, unit, rate)
        grad[rows] = total
        low[rows] = total.astype(bf16)


def result_kernel(*refs, p):
    (a, b, residual), outs = refs[:3], refs[3:]
    for i, j, at in p.locations():
        rows = slice(at, at + p.span)
        total = a[rows].astype(f32) + b[rows].astype(f32)
        outs[j][i] = (total + residual[rows]).astype(bf16)


def last_kernel(*refs, p):
    g = p.pieces
    hidden, (a, b, c, grad), outs = refs[:g], refs[g : g + 4], refs[g + 4 :]
    for i, j, at in p.locations():
        rows = slice(at, at + p.span)
        u = a[rows].astype(f32) + b[rows].astype(f32) + c[rows].astype(f32)
        unit, rate = norm_stats(hidden[j][i, : p.span].astype(f32))
        outs[j][i] = (grad[rows] + norm_back(u, unit, rate)).astype(bf16)


def qkv_grad_kernel(*refs, p):
    stack, w, gain, c_ref, qkv, out, gain_grad = refs
    fs, small, slab, lanes = p.fsdp, p.small, p.slab, p.lanes
    for cc in range(p.ctx):
        away = storage(c_ref[0] ^ cc, p.last_order)
        rows = slice(cc * small, (cc + 1) * small)
        scale = gain[rows, :]
        total = jnp.zeros((small, lanes), f32)
        for g in range(p.groups):
            for ff in range(fs):
                for m in range(3):
                    at = (ff * 3 + m) * small
                    value = stack[away, g, at : at + small, :].astype(f32)
                    there = m * p.width + ff * p.cols + g * lanes
                    qkv[rows, there : there + lanes] = value * scale
                    total = total + value * w[rows, there : there + lanes].astype(f32)
            for d in range(p.width // lanes):
                at = 3 * fs * small + d * slab
                value = stack[away, g, at : at + slab, :].astype(f32)
                row = g * lanes + cc * slab
                out[row : row + slab, d * lanes : (d + 1) * lanes] = value
        gain_grad[rows, :] = jnp.sum(total, axis=1, keepdims=True)


def in_grad_kernel(table, low, high, w, gain, grad, gain_grad, *, top):
    def write(value):
        grad[...] = value * gain[...]
        gain_grad[...] = jnp.sum(value * w[...].astype(f32), axis=1, keepdims=True)

    step = pl.program_id(0)

    @pl.when(table[step] < top)
    def _():
        write(low[0].astype(f32))

    @pl.when(table[step] >= top)
    def _():
        write(high[0].astype(f32))


def out_grad_kernel(stack, c_ref, grad, *, p):
    for cc in range(p.ctx):
        away = storage(c_ref[0] ^ cc, p.order)
        for ff in range(p.fsdp):
            at = ff * p.rows + cc * p.small
            grad[:, at : at + p.small] = stack[away, ff].astype(f32).T


def on_device(
    hidden, segment_ids, cotangent, w_qkv, w_attn_out, w_in, w_mlp_out, gain_attn, gain_mlp
):
    fsdp, ctx = lax.axis_size("fsdp"), lax.axis_size("ctx")
    f, c = lax.axis_index("fsdp"), lax.axis_index("ctx")
    batch, span, width = hidden.shape
    p = Plan(fsdp, ctx, batch, span, width, w_mlp_out.shape[0], w_in.shape[0])
    n, own, cols, units, rows, small = p.n, p.own, p.cols, p.units, p.rows, p.small
    length, pieces = p.length, p.pieces
    both = ("ctx", "fsdp")
    slots = range(fsdp)
    tile = shape_of((own, width))
    bits = [fsdp >> 1 + b for b in range(fsdp.bit_length() - 1)]

    def mixed_bits(index):
        out = 0
        for bit in bits:
            out = out + index // (fsdp // 2 // bit) % 2 * bit
        return out

    def route(j):
        pairs = []
        for cc in range(ctx):
            for ff in range(fsdp):
                to_c = (cc + j) % pieces * fsdp + mixed_bits(ff)
                to_f = cc // pieces ^ ff % 2 * (fsdp // 2)
                pairs.append((cc * fsdp + ff, to_c * fsdp + to_f))
        return pairs

    def dealt(values):
        return [
            lax.dynamic_slice_in_dim(values, (c + j) % pieces * n, n, 0) for j in range(pieces)
        ]

    def deal(parts):
        return [lax.ppermute(part, both, route(j)) for j, part in enumerate(parts)]

    def undeal(parts):
        back = [
            lax.ppermute(part, both, [(b, a) for a, b in route(j)])
            for j, part in enumerate(parts)
        ]
        return back

    def assemble(back):
        if pieces == 1:
            return back[0]
        blocks = []
        for b in range(pieces):
            block = back[0]
            for j in range(1, pieces):
                block = jnp.where((c + j) % pieces == b, back[j], block)
            blocks.append(block)
        return jnp.concatenate(blocks, axis=0)

    def partner(values, bit):
        return lax.ppermute(values, "fsdp", [(i, i ^ bit) for i in range(fsdp)])

    def meet(*values):
        return lax.optimization_barrier(values)

    def first_hop(value):
        return [value, partner(value, bits[0])]

    def later_hops(held):
        held = {0: held[0], bits[0]: held[1]}
        for bit in bits[1:]:
            for o in list(held):
                held[o ^ bit] = partner(held[o], bit)
        return [held[o] for o in slots]

    def reduce(parts):
        held, side, last = dict(enumerate(parts)), None, None
        for bit in reversed(bits):
            for o in sorted(held, reverse=True):
                if not o & bit:
                    continue
                got, mine = partner(held.pop(o), bit), held[o ^ bit]
                if o == bits[0]:
                    last = got
                elif o == bits[1]:
                    side = got
                else:
                    held[o ^ bit] = (mine.astype(f32) + got.astype(f32)).astype(bf16)
        return held[0], side, last

    def away(values, bit):
        return lax.ppermute(values, "ctx", [(i, i ^ bit) for i in range(ctx)])

    def send(stack, bit):
        half = stack.shape[0] // 2
        return stack[:half], away(stack[half:], bit)

    def add(pair):
        return (pair[0].astype(f32) + pair[1].astype(f32)).astype(bf16)

    def grow(stack, bit):
        return stack, away(stack, bit)

    def join(pair):
        return jnp.concatenate(pair, axis=0)

    flip = c % fsdp // (fsdp // 2) * (fsdp // 2)
    blocks = [
        (f ^ o ^ flip) * pieces + (c // fsdp - j) % pieces for o in slots for j in range(pieces)
    ]
    positions = (jnp.stack(blocks)[:, None] * span + jnp.arange(span)[None, :]).reshape(length)
    turns = p.size // 2
    inverse = rope_base ** (-(jnp.arange(turns, dtype=f32) * 2.0 / p.size))
    angles = positions.astype(f32)[:, None] * inverse[None, :]
    cosine, sine = jnp.cos(angles), jnp.sin(angles)
    reps = p.table // p.size
    cosine = jnp.concatenate([cosine, cosine] * reps, axis=1)
    sine = jnp.concatenate([-sine, sine] * reps, axis=1)

    tags = jnp.pad(
        segment_ids.astype(bf16)[:, None, :], ((0, 0), (0, TAG - 1), (0, width - span))
    )
    hidden_cut, w_qkv, w_in = lax.optimization_barrier(
        (dealt(jnp.concatenate([hidden, tags], axis=1)), w_qkv, w_in)
    )
    hidden_parts = deal(hidden_cut)

    gain_a, gain_m = gain_attn.astype(f32)[:, None], gain_mlp.astype(f32)[:, None]
    here, place = jnp.reshape(c, (1,)), jnp.stack([f, c])
    half = rows // 2
    mine, other = call(
        functools.partial(cut_kernel, p=p, feed=False),
        "cut",
        [shape_of((fsdp, half, 3 * cols)), shape_of((2, half, 3 * cols))],
        1,
        [],
        [w_qkv, gain_a, place],
        1e6,
    )

    def spread_out(mine, other):
        near = [mine[0]] + [
            lax.ppermute(mine[o], "fsdp", [(i, i ^ o) for i in range(fsdp)]) for o in slots[1:]
        ]
        return near, [other[0], partner(other[1], 1)]

    near, other = spread_out(mine, other)
    hidden_parts, near, other, cosine, sine, cotangent, w_in = meet(
        hidden_parts, near, other, cosine, sine, cotangent, w_in
    )
    far = [away(part, 1) for part in near[2:]]
    cot_parts = deal(dealt(cotangent))
    unit1 = call(
        functools.partial(unit_kernel, p=p),
        "unit1",
        [shape_of((own + TAG, width))],
        1,
        [],
        hidden_parts,
        1e6,
    )[0]
    unit1, w_in_late = meet(unit1, w_in)
    mine_in, kept_in = call(
        functools.partial(cut_kernel, p=p, feed=True),
        "cut_in",
        [shape_of((fsdp, rows, p.padded)), shape_of((2, rows, p.padded))],
        1,
        [],
        [w_in_late, gain_m, place],
        1e6,
    )
    held, far, cot_parts, mine_in, kept_in = meet(
        first_hop(unit1), far, cot_parts, mine_in, kept_in
    )
    unit1_slots = later_hops(held)
    cot_own = jnp.stack(cot_parts, axis=1).reshape(own, width)
    unit1_slots, cot_own, mine_in, kept_in = meet(unit1_slots, cot_own, mine_in, kept_in)
    cot_held = first_hop(cot_own)
    near_in, other_in = spread_out(mine_in, kept_in)

    whole = shape_of((n, length, cols))
    q, k, v, segments, w_qkv_cols = call(
        functools.partial(project_kernel, p=p),
        "project",
        [whole] * 3 + [shape_of((n, 8, length), f32), shape_of((width, 3 * cols))],
        fsdp,
        [
            pltpu.VMEM((fsdp, own + TAG, width), bf16),
            pltpu.SemaphoreType.DMA((2 * fsdp,)),
            pltpu.SemaphoreType.DMA((fsdp,)),
        ],
        [Late(a) for a in unit1_slots + near + other + far] + [cosine, sine, place],
        4e9,
    )
    ranges = segments[:, 0].reshape(n, fsdp, p.part)
    spans = jnp.stack([jnp.min(ranges, axis=2), jnp.max(ranges, axis=2)], axis=2)
    spans = spans.astype(jnp.int32).reshape(2 * n * fsdp)
    made = call(
        functools.partial(attend_kernel, p=p),
        "attend",
        [tile] * fsdp + [whole, shape_of((n, 8, length), f32)],
        n * fsdp,
        [pltpu.VMEM((p.part, width), bf16)],
        [q, k, v, segments, w_attn_out],
        1.2e10,
    )
    made, cot_held, near_in, other_in = meet(made, cot_held, near_in, other_in)
    far_in = [away(part, 1) for part in near_in[2:]]
    cot_slots = later_hops(cot_held)
    attended_parts, attended, norms = made[:fsdp], made[fsdp], made[fsdp + 1]

    attended_parts = list(attended_parts)
    attended_parts[0], unit1_late = meet(attended_parts[0], unit1_slots)
    (flipped,) = call(
        functools.partial(flip_kernel, p=p),
        "flip",
        [shape_of((n, width, length))],
        fsdp,
        [],
        list(unit1_late),
        1e6,
    )
    addends = reduce(attended_parts)
    addends, flipped = meet(addends, flipped)
    residual, unit2 = call(
        functools.partial(middle_kernel, p=p),
        "middle",
        [shape_of((own, width), f32), tile],
        1,
        [],
        hidden_parts + list(addends),
        1e6,
    )
    unit2, far_in, cot_slots = meet(unit2, far_in, cot_slots)
    unit2_slots = later_hops(first_hop(unit2))

    wide = shape_of((fsdp * own, p.padded))
    made = call(
        functools.partial(mlp_kernel, p=p),
        "mlp",
        [Late(tile)] * (2 * fsdp)
        + [(wide, pl.BlockSpec((own, p.padded), lambda s: (s, 0)))] * 3,
        fsdp,
        [pltpu.VMEM((width, p.padded), bf16)] * 2
        + [pltpu.VMEM((p.padded, width), bf16)]
        + [pltpu.VMEM((fsdp, own, width), bf16)] * 4
        + [
            pltpu.SemaphoreType.DMA((4 * fsdp,)),
            pltpu.SemaphoreType.DMA((2 * fsdp,)),
            pltpu.SemaphoreType.DMA((2 * fsdp,)),
        ],
        [Late(a) for a in unit2_slots + cot_slots + near_in + other_in + far_in]
        + [w_mlp_out, place],
        1.2e10,
    )
    out_parts, u2_parts, (active, da, dg) = made[:fsdp], made[fsdp : 2 * fsdp], made[2 * fsdp :]

    u2 = reduce(u2_parts)
    mlp_sums, gate_sums = call(
        functools.partial(mlp_sums_kernel, p=p),
        "mlp_sums",
        [
            shape_of((ctx, fsdp, 2, small, units)),
            shape_of((ctx, fsdp, small, units)),
        ],
        fsdp,
        [pltpu.VMEM((width, p.padded), f32)] * 3 + [pltpu.VMEM((own, width), bf16)] * 2,
        unit2_slots + cot_slots + [active, da, dg, here],
        6e9,
    )
    u2, mlp_sums, gate_sums = lax.optimization_barrier((u2, mlp_sums, gate_sums))
    grad_residual, grad_low = call(
        functools.partial(turn_kernel, p=p),
        "turn",
        [shape_of((own, width), f32), tile],
        1,
        [],
        list(u2) + [residual, cot_own],
        1e6,
    )
    order = p.order
    gate_order = p.last_order
    piece = [shape_of((n, span, width))] * pieces
    grad_low, out_parts, mlp_sums, gate_sums = meet(
        grad_low, list(out_parts), mlp_sums, gate_sums
    )
    low_held = first_hop(grad_low)
    mlp_pair, gate_pair = send(mlp_sums, order[0]), send(gate_sums, gate_order[0])
    held = dict(enumerate(out_parts))
    for bit in reversed(bits[1:]):
        for o in sorted(held, reverse=True):
            if o & bit:
                held[o ^ bit] = add((held[o ^ bit], partner(held.pop(o), bit)))
    low_held, out_near, out_far, mlp_pair, gate_pair = meet(
        low_held, held[0], held[bits[0]], mlp_pair, gate_pair
    )
    mlp_sums, gate_sums = add(mlp_pair), add(gate_pair)
    low_slots = later_hops(low_held)
    low_slots, out_far, mlp_sums, gate_sums = meet(low_slots, out_far, mlp_sums, gate_sums)
    mlp_pair, gate_pair = send(mlp_sums, order[1]), send(gate_sums, gate_order[1])
    out_got = partner(out_far, bits[0])
    mixed, attention_sums = [], []
    for group in range(p.groups):
        some = pl.BlockSpec(
            (n, length, p.lanes),
            lambda s, group=group: (0, 0, group),
            pipeline_mode=pl.Buffered(1),
        )
        wo_rows = pl.BlockSpec(
            (p.lanes, width), lambda s, group=group: (group, 0), pipeline_mode=pl.Buffered(1)
        )
        grad_mixed, sums = call(
            functools.partial(backward_kernel, p=p, group=group),
            "attention_back",
            [
                shape_of((n, length, 3 * p.lanes)),
                shape_of((ctx, 4 * fsdp * small, p.lanes)),
            ],
            n * fsdp + 1,
            [
                pltpu.VMEM((p.lanes, length), bf16),
                pltpu.VMEM((p.lanes, p.part), f32),
                pltpu.VMEM((length, p.lanes), f32),
                pltpu.VMEM((length, p.lanes), f32),
                pltpu.VMEM((n, length, width), bf16),
                pltpu.VMEM((length, 1), f32),
                pltpu.VMEM((width, 3 * p.lanes), f32),
                pltpu.VMEM((p.lanes, width), f32),
                pltpu.VMEM((n, width, length), bf16),
                pltpu.SemaphoreType.DMA((n * fsdp,)),
                pltpu.SemaphoreType.DMA((1,)),
            ],
            [Late(a) for a in low_slots]
            + [Late(flipped), (w_attn_out, wo_rows), (q, some), (k, some), (v, some), (attended, some)]
            + [segments, norms, cosine, sine, here, spans],
            1.5e10,
        )
        mixed.append(grad_mixed)
        if group == 0:
            sums, low_slots, mlp_pair, gate_pair, out_got = meet(
                sums, low_slots, mlp_pair, gate_pair, out_got
            )
            pairs = [send(sums, order[0])]
            mlp_sums, gate_sums = add(mlp_pair), add(gate_pair)
            for bit, gate_bit in zip(order[2:-1], gate_order[2:-1]):
                mlp_sums, gate_sums = add(send(mlp_sums, bit)), add(send(gate_sums, gate_bit))
            mlp_pair, gate_pair = send(mlp_sums, order[-1]), send(gate_sums, gate_order[-1])
            result_parts = call(
                functools.partial(result_kernel, p=p),
                "result",
                piece,
                1,
                [],
                [out_near, out_got, residual],
                1e6,
            )
            low_slots, result_parts = meet(low_slots, result_parts)
            out_back = undeal(result_parts)
        else:
            sums, pairs, mlp_pair, gate_pair = meet(sums, pairs, mlp_pair, gate_pair)
            pairs = pairs + [send(sums, order[0])]

    def step_of(sums):
        return order[ctx.bit_length() - sums.shape[0].bit_length()]

    back_order = order[::-1]
    mlp_sums, gate_sums = add(mlp_pair)[0], add(gate_pair)[0]
    mlp_stack = grow(mlp_sums[None, :, 1], back_order[0])
    in_small = jnp.stack([mlp_sums[:, 0], gate_sums], axis=1)
    early, late = pairs[:-1], pairs[-1]
    if early:
        sums = add(early[0])
        early = [send(sums, step_of(sums))]
    u1_parts = call(
        functools.partial(spread_kernel, p=p),
        "spread",
        [tile] * fsdp,
        fsdp,
        [pltpu.VMEM((own, width), bf16)],
        mixed + [w_qkv_cols],
        2e9,
    )
    in_small = lax.all_to_all(in_small, "fsdp", 0, 0, tiled=True)
    in_small = in_small.transpose(2, 1, 0, 3).reshape(1, small, 2 * fsdp * units)
    u1_parts, early, late, mlp_stack, in_small = meet(
        list(u1_parts), early, late, mlp_stack, in_small
    )
    in_pair = grow(in_small, back_order[0])
    u1 = reduce(u1_parts)
    if early:
        sums = add(early[0])
        early = [send(sums, step_of(sums))]
    sums = add(late)
    late = send(sums, step_of(sums))
    mlp_stack = grow(join(mlp_stack), back_order[1])
    u1, early, late, mlp_stack, out_back = meet(u1, early, late, mlp_stack, out_back)
    back_parts = call(
        functools.partial(last_kernel, p=p),
        "last",
        piece,
        1,
        [],
        hidden_parts + list(u1) + [grad_residual],
        1e6,
    )
    sums = add(late)
    late = send(sums, step_of(sums))
    mlp_stack = grow(join(mlp_stack), back_order[2])
    back_parts, late, in_pair = meet(back_parts, late, in_pair)
    back = undeal(back_parts)
    in_pair = grow(join(in_pair), back_order[1])

    def finished(pair):
        sums = add(pair)
        while sums.shape[0] > 1:
            sums = add(send(sums, step_of(sums)))
        return sums

    sums = jnp.concatenate([finished(pair) for pair in early + [late]], axis=0)
    mine = sums[:, : 3 * fsdp * small].reshape(p.groups, fsdp, 3 * small, p.lanes)
    mine = lax.all_to_all(mine, "fsdp", 1, 1, tiled=True)
    mine = mine.reshape(p.groups, 3 * fsdp * small, p.lanes)
    stack = jnp.concatenate([mine, sums[:, 3 * fsdp * small :]], axis=1)[None]
    last_back = p.last_order[::-1]
    stack = grow(stack, last_back[0])
    for bit in back_order[3:]:
        mlp_stack = grow(join(mlp_stack), bit)
    stack, in_pair, mlp_stack = meet(stack, in_pair, mlp_stack)
    mlp_stack = join(mlp_stack)
    stack = grow(join(stack), last_back[1])
    for bit in back_order[2:]:
        in_pair = grow(join(in_pair), bit)
    stack, back, mlp_stack = meet(stack, back, mlp_stack)
    for bit in last_back[2:]:
        stack = grow(join(stack), bit)
    stack = join(stack)
    out, back = assemble(out_back), assemble(back).astype(f32)

    grad_qkv, grad_out, grad_gain_a = call(
        functools.partial(qkv_grad_kernel, p=p),
        "qkv_grad",
        [
            shape_of((rows, 3 * width), f32),
            shape_of((cols, width), f32),
            shape_of((rows, 1), f32),
        ],
        1,
        [],
        [stack, w_qkv, gain_a, here],
        1e6,
    )
    table = storage(c ^ jnp.arange(ctx, dtype=jnp.int32), order)
    low_part, high_part, block = in_pair[0], in_pair[1], small
    if small % 8:
        low_part = join(in_pair)
        parts = [
            lax.dynamic_slice_in_dim(low_part, storage(c ^ cc, order), 1, 0) for cc in range(ctx)
        ]
        low_part = jnp.concatenate(parts, axis=1)
        high_part, block, table = low_part, rows, jnp.zeros((1,), jnp.int32)
    top = low_part.shape[0]
    some = pl.BlockSpec((block, 2 * fsdp * units), lambda s, t: (s, 0))
    thin = pl.BlockSpec((block, 1), lambda s, t: (s, 0))
    one = (1, block, 2 * fsdp * units)
    grad_in, grad_gain_m = pl.pallas_call(
        functools.partial(in_grad_kernel, top=top),
        grid_spec=pltpu.PrefetchScalarGridSpec(
            num_scalar_prefetch=1,
            grid=(rows // block,),
            in_specs=[
                pl.BlockSpec(one, lambda s, t: (jnp.minimum(t[s], top - 1), 0, 0)),
                pl.BlockSpec(one, lambda s, t: (jnp.maximum(t[s] - top, 0), 0, 0)),
                some,
                thin,
            ],
            out_specs=[some, thin],
        ),
        out_shape=[shape_of(w_in.shape, f32), shape_of((rows, 1), f32)],
        compiler_params=pltpu.CompilerParams(vmem_limit_bytes=40 << 20),
        cost_estimate=pl.CostEstimate(
            flops=1000000, bytes_accessed=8 * w_in.size, transcendentals=0
        ),
        name="in_grad",
    )(table, low_part, high_part, w_in, gain_m)
    (grad_mlp_out,) = call(
        functools.partial(out_grad_kernel, p=p),
        "out_grad",
        [shape_of((units, width), f32)],
        1,
        [],
        [mlp_stack, here],
        1e6,
    )
    return (
        out,
        back,
        grad_qkv,
        grad_out,
        grad_in,
        grad_mlp_out,
        grad_gain_a.reshape(rows),
        grad_gain_m.reshape(rows),
    )


def solution(mesh):
    in_specs = (
        P("fsdp", "ctx", None),
        P("fsdp", "ctx"),
        P("fsdp", "ctx", None),
        P("fsdp", None),
        P("fsdp", None),
        P("fsdp", None),
        P("fsdp", None),
        P("fsdp"),
        P("fsdp"),
    )
    out_specs = (
        P("fsdp", "ctx", None),
        P("fsdp", "ctx", None),
        P("fsdp", None),
        P("fsdp", None),
        P("fsdp", None),
        P("fsdp", None),
        P("fsdp"),
        P("fsdp"),
    )
    return jax.shard_map(
        on_device, mesh=mesh, in_specs=in_specs, out_specs=out_specs, check_vma=False
    )
```

time: 472 us -> 450 us (0.953)
  waiting for transfers between devices: 195 us -> 160 us
  between operations: 14.8 us -> 2.16 us
  blocking collectives: 0 us -> 9.74 us
  Pallas kernels: 132 us -> 139 us
  local copies, waits for them, and re-layouts: 18.2 us -> 23.4 us
  starting transfers between devices: 76.8 us -> 81.7 us
    ppermute x24 -> x26, waiting for transfers between devices: 88.5 us -> 37.4 us  [partner(): return lax.ppermute(values, 'fsdp', [(i, i ^ bit) for i in range(fsdp)])]
    ppermute x18 -> x25, waiting for transfers between devices: 51.6 us -> 96.3 us  [away(): return lax.ppermute(values, 'ctx', [(i, i ^ bit) for i in range(ctx)])]
    all_to_all x3 -> x0, starting transfers between devices: 16.6 us -> none  [the longest x1 10 us: on_device(): cut = lax.all_to_all(cut, 'fsdp', 0, 0, tiled=True)]
    reduce_scatter x1 -> x0, waiting for transfers between devices: 14.4 us -> none  [on_device(): lax.psum_scatter(in_sums, 'ctx', scatter_dimension=0, tiled=False)]
    ppermute x18 -> x25, starting transfers between devices: 15.7 us -> 28.7 us  [away(): return lax.ppermute(values, 'ctx', [(i, i ^ bit) for i in range(ctx)])]
    ppermute x0 -> x6, waiting for transfers between devices: none -> 10.2 us  [spread_out(): lax.ppermute(mine[o], 'fsdp', [(i, i ^ o) for i in range(fsdp)])]
    all_to_all x0 -> x1, blocking collectives: none -> 9.74 us  [on_device(): mine = lax.all_to_all(mine, 'fsdp', 1, 1, tiled=True)]
    ppermute x4, waiting for transfers between devices: 9.33 us -> 0.01 us  [deal(): return [lax.ppermute(part, both, route(j)) for j, part in enumerate(parts)]]
  transfers between devices with their start and end apart: 57 -> 66, of which waited for: 24 -> 27; matrix products, arithmetic and copies ran while one was open for 8% -> 8% of each run, Pallas kernels for 23% -> 24%
where the time goes in v3:
time: 450 us; the launch traced here: 443 us
  waiting for transfers between devices  160 us (36%)
  Pallas kernels  139 us (31%)
  starting transfers between devices  81.7 us (18%)
  other arithmetic  27 us (6%)
  local copies, waits for them, and re-layouts  23.4 us (5%)
  blocking collectives  9.74 us (2%)
    pallas_call x17, Pallas kernels, call(): pl.pallas_call(kernel, grid=(grid,), in_specs=specs, out_specs=outs, out_...  134 us
    ppermute x25, waiting for transfers between devices, away(): return lax.ppermute(values, 'ctx', [(i, i ^ bit) for i in range(ctx)])  96.3 us
    ppermute x26, waiting for transfers between devices, partner(): return lax.ppermute(values, 'fsdp', [(i, i ^ bit) for i in range(fsdp)])  37.4 us
    ppermute x25, starting transfers between devices, away(): return lax.ppermute(values, 'ctx', [(i, i ^ bit) for i in range(ctx)])  28.7 us
    ppermute x26, starting transfers between devices, partner(): return lax.ppermute(values, 'fsdp', [(i, i ^ bit) for i in range(fsdp)])  16.1 us
    ppermute x4, waiting for transfers between devices, undeal(): lax.ppermute(part, both, [(b, a) for a, b in route(j)])  15.7 us
    ppermute x4, starting transfers between devices, deal(): return [lax.ppermute(part, both, route(j)) for j, part in enumerate(parts)]  15.5 us
    ppermute x4, starting transfers between devices, undeal(): lax.ppermute(part, both, [(b, a) for a, b in route(j)])  13.2 us
  transfers between devices with their start and end apart: 66, of which 27 were waited for; matrix products, arithmetic and copies ran while one was open for 8% of the time, Pallas kernels for 24%

profile of v3, /device:TPU:0, one launch (start us, length us, event | category | flops | bytes accessed | tf_op | source)
XLA Modules:
  0.0 442.6 jit_solution(17061764417468456700)
XLA Ops:
  3.2 8.5 %collective-permute-start.1 = (bf16[1,144,1024]{2,1,0:T(8,128)(2,1)S(1)}, bf16[1,144,1024]{2,1,0:T(8,128)(2,1)S(1)}, u32[]{:S(2)}, u32[]{:S(2)}) collective-permute-start(bf16[1,144,1024]{2,1,0:T(8,128)(2,1)S(1)} %get-tuple-element.210), channel_id=1, source_target_pairs={{0,16},{1,26},{2,20},{3,30},{4,0},{5,10},{6,4},{7,14},{8,17},{9,27... | collective-permute-start | bytes 884744 | tf_op jit(solution)/shard_map/ppermute | solution.py:623
  13.1 3.9 cut.1
  29.5 4.2 collective-permute-done.4.refs_7_
  40.1 5.5 %collective-permute-start.10 = (bf16[1,128,1024]{2,1,0:T(8,128)(2,1)S(1)}, bf16[1,128,1024]{2,1,0:T(8,128)(2,1)S(1)}, u32[]{:S(2)}, u32[]{:S(2)}) collective-permute-start(bf16[1,128,1024]{2,1,0:T(8,128)(2,1)S(1)} %get-tuple-element.446), channel_id=1, source_target_pairs={{0,16},{1,26},{2,20},{3,30},{4,0},{5,10},{6,4},{7,14},{8,17},{9,27... | collective-permute-start | bytes 786440 | tf_op jit(solution)/shard_map/ppermute | solution.py:623
  48.5 5.2 %cut_in.1 = (bf16[4,256,768]{2,1,0:T(8,128)(2,1)}, bf16[2,256,768]{2,1,0:T(8,128)(2,1)}) custom-call(bf16[256,5248]{1,0:T(8,128)(2,1)} %w.2, f32[256,1]{1,0:T(8,128)} %copy.44.gain, s32[2]{0:T(128)} %pad_add_fusion.at_ref.refs_14_.refs_17_), custom_call_target="tpu_custom_call" | custom-call | flops 1000000 | bytes 5047304 | tf_op jit(solution)/shard_map/cut_in/pallas_call | solution.py:53
  53.7 8.3 %collective-permute-done.7.refs_10_ = bf16[128,768]{1,0:T(8,128)(2,1)S(1)} collective-permute-done((bf16[128,768]{1,0:T(8,128)(2,1)S(1)}, bf16[128,768]{1,0:T(8,128)(2,1)S(1)}, u32[]{:S(2)}, u32[]{:S(2)}) %collective-permute-start.7) | collective-permute-done | bytes 196640 | tf_op jit(solution)/shard_map/ppermute | solution.py:675
  62.1 3.2 collective-permute-done.8.refs_11_
  68.1 2.4 slice_bitcast_fusion.2
  73.8 7.9 %project.1 = (bf16[1,1024,256]{2,1,0:T(8,128)(2,1)}, bf16[1,1024,256]{2,1,0:T(8,128)(2,1)}, bf16[1,1024,256]{2,1,0:T(8,128)(2,1)}, f32[1,8,1024]{2,1,0:T(8,128)}, bf16[1024,768]{1,0:T(8,128)(2,1)}) custom-call(bf16[272,1024]{1,0:T(8,128)(2,1)} %unit1.1.refs_0_, bf16[272,1024]{1,0:T(8,128)(2,1)} %copy-done.12, bf16[272,1024]{1,0:T(8,128)(2,1)} %copy-done.11, ...), custom_call_target="tpu_custom_call" | custom-call | flops 4000000000 | bytes 8028168 | tf_op jit(solution)/shard_map/project/pallas_call | solution.py:53
  81.7 12.7 %attend.1 = (bf16[256,1024]{1,0:T(8,128)(2,1)}, bf16[256,1024]{1,0:T(8,128)(2,1)}, bf16[256,1024]{1,0:T(8,128)(2,1)}, bf16[256,1024]{1,0:T(8,128)(2,1)}, bf16[1,...) custom-call(bf16[1,1024,256]{2,1,0:T(8,128)(2,1)} %get-tuple-element.243.q_ref.refs_6_, ...), custom_call_target="tpu_custom_call" | custom-call | flops 12000000000 | bytes 4784128 | tf_op jit(solution)/shard_map/attend/pallas_call | solution.py:53
  94.4 3.7 collective-permute-done.16.refs_11_
  104.7 3.8 flip.1.refs_4_
  108.6 7.5 %collective-permute-done.20.refs_4_ = bf16[256,1024]{1,0:T(8,128)(2,1)S(1)} collective-permute-done((bf16[256,1024]{1,0:T(8,128)(2,1)S(1)}, bf16[256,1024]{1,0:T(8,128)(2,1)S(1)}, u32[]{:S(2)}, u32[]{:S(2)}) %collective-permute-start.20) | collective-permute-done | bytes 524320 | tf_op jit(solution)/shard_map/ppermute | solution.py:644
  116.8 2.9 middle.1
  119.8 2.5 collective-permute-done.22.refs_15_
  124.0 11.7 %collective-permute-done.26.refs_2_ = bf16[256,1024]{1,0:T(8,128)(2,1)S(1)} collective-permute-done((bf16[256,1024]{1,0:T(8,128)(2,1)}, bf16[256,1024]{1,0:T(8,128)(2,1)S(1)}, u32[]{:S(2)}, u32[]{:S(2)}) %collective-permute-start.26) | collective-permute-done | bytes 524320 | tf_op jit(solution)/shard_map/ppermute | solution.py:644
  138.5 20.3 %mlp.1 = (bf16[256,1024]{1,0:T(8,128)(2,1)}, bf16[256,1024]{1,0:T(8,128)(2,1)}, bf16[256,1024]{1,0:T(8,128)(2,1)}, bf16[256,1024]{1,0:T(8,128)(2,1)}, bf16[256,1...) custom-call(bf16[256,1024]{1,0:T(8,128)(2,1)} %get-tuple-element.273, ...), custom_call_target="tpu_custom_call" | custom-call | flops 12000000000 | bytes 17596424 | tf_op jit(solution)/shard_map/mlp/pallas_call | solution.py:53
  163.9 13.3 %mlp_sums.1 = (bf16[8,4,2,32,656]{4,3,2,1,0:T(8,128)(2,1)}, bf16[8,4,32,656]{3,2,1,0:T(8,128)(2,1)}) custom-call(bf16[256,1024]{1,0:T(8,128)(2,1)} %get-tuple-element.273.refs_0_, bf16[256,1024]{1,0:T(8,128)(2,1)} %copy-done.37, bf16[256,1024]{1,0:T(8,128)(2,1)} %copy-done.36, bf16[256,1024]{1,0:T(8,128)(2,1)} %copy-done.38, bf16[256,1024]{1,0:T(8,128)(2,1)} %bitcast.59, ...), custom_call_target="tpu_custom_call" | custom-call | flops 6000000000 | bytes 12943364 | tf_op jit(solution)/shard_map/mlp_sums/pallas_call | solution.py:53
  178.1 3.9 turn.1
  187.9 2.5 collective-permute-start.35
  195.1 9.8 %collective-permute-done.31.refs_2_ = bf16[256,1024]{1,0:T(8,128)(2,1)S(1)} collective-permute-done((bf16[256,1024]{1,0:T(8,128)(2,1)}, bf16[256,1024]{1,0:T(8,128)(2,1)S(1)}, u32[]{:S(2)}, u32[]{:S(2)}) %collective-permute-start.31) | collective-permute-done | bytes 524320 | tf_op jit(solution)/shard_map/ppermute | solution.py:644
  205.0 3.3 collective-permute-done.35
  208.3 11.7 %collective-permute-done.34 = bf16[4,4,2,32,656]{4,3,1,2,0:T(8,128)(2,1)} collective-permute-done((bf16[4,4,2,32,656]{4,3,1,2,0:T(8,128)(2,1)}, bf16[4,4,2,32,656]{4,3,1,2,0:T(8,128)(2,1)}, u32[]{:S(2)}, u32[]{:S(2)}) %collective-permute-start.34) | collective-permute-done | bytes 1343520 | tf_op jit(solution)/shard_map/ppermute | solution.py:675
  224.4 2.5 collective-permute-start.38
  228.7 17.7 %attention_back.2 = (bf16[1,1024,384]{2,1,0:T(8,128)(2,1)}, bf16[8,512,128]{2,1,0:T(8,128)(2,1)}) custom-call(bf16[256,1024]{1,0:T(8,128)(2,1)} %get-tuple-element.338.refs_0_, bf16[256,1024]{1,0:T(8,128)(2,1)} %copy-done.34, bf16[256,1024]{1,0:T(8,128)(2,1)} %copy-done.31, bf16[256,1024]{1,0:T(8,128)(2,1)} %copy-done.35, ...), custom_call_target="tpu_custom_call" | custom-call | flops 15000000512 | bytes 9764900 | tf_op jit(solution)/shard_map/attention_back/pallas_call | solution.py:53
  246.4 5.9 %collective-permute-done.39 = bf16[2,4,32,656]{3,2,1,0:T(8,128)(2,1)S(1)} collective-permute-done((bf16[2,4,32,656]{3,2,1,0:T(8,128)(2,1)S(1)}, bf16[2,4,32,656]{3,2,1,0:T(8,128)(2,1)S(1)}, u32[]{:S(2)}, u32[]{:S(2)}) %collective-permute-start.39) | collective-permute-done | bytes 335904 | tf_op jit(solution)/shard_map/ppermute | solution.py:675
  253.1 2.4 result.1
  256.5 3.4 collective-permute-start.42
  261.6 18.0 %attention_back.3 = (bf16[1,1024,384]{2,1,0:T(8,128)(2,1)}, bf16[8,512,128]{2,1,0:T(8,128)(2,1)}) custom-call(bf16[256,1024]{1,0:T(8,128)(2,1)} %get-tuple-element.338.refs_0_, bf16[256,1024]{1,0:T(8,128)(2,1)} %copy-done.34, bf16[256,1024]{1,0:T(8,128)(2,1)} %copy-done.31, bf16[256,1024]{1,0:T(8,128)(2,1)} %copy-done.35, ...), custom_call_target="tpu_custom_call" | custom-call | flops 15000000512 | bytes 9764900 | tf_op jit(solution)/shard_map/attention_back/pallas_call | solution.py:53
  282.1 3.5 all-to-all-start
  287.1 5.7 %collective-permute-start.54 = (bf16[1,128,1024]{2,1,0:T(8,128)(2,1)}, bf16[1,128,1024]{2,1,0:T(8,128)(2,1)}, u32[]{:S(2)}, u32[]{:S(2)}) collective-permute-start(bf16[1,128,1024]{2,1,0:T(8,128)(2,1)} %get-tuple-element.372), channel_id=1, source_target_pairs={{16,0},{26,1},{20,2},{30,3},{0,4},{10,5},{4,6},{14,7},{17,8},{27,9... | collective-permute-start | bytes 786440 | tf_op jit(solution)/shard_map/ppermute | solution.py:627
  293.8 5.9 %spread.1 = (bf16[256,1024]{1,0:T(8,128)(2,1)}, bf16[256,1024]{1,0:T(8,128)(2,1)}, bf16[256,1024]{1,0:T(8,128)(2,1)}, bf16[256,1024]{1,0:T(8,128)(2,1)}) custom-call(bf16[1,1024,384]{2,1,0:T(8,128)(2,1)} %get-tuple-element.325.refs_0_, bf16[1,1024,384]{2,1,0:T(8,128)(2,1)} %get-tuple-element.342.refs_1_, bf16[1024,768]{1,0:T(8,128)(2,1)} %get-tuple-element.343.refs_2_), custom_call_target="tpu_custom_call" | custom-call | flops 2000000000 | bytes 5242880 | tf_op jit(solution)/shard_map/spread/pallas_call | solution.py:53
  300.4 12.6 %collective-permute-done.46 = bf16[1,4,32,656]{3,2,1,0:T(8,128)(2,1)} collective-permute-done((bf16[1,4,32,656]{3,2,1,0:T(8,128)(2,1)S(1)}, bf16[1,4,32,656]{3,2,1,0:T(8,128)(2,1)}, u32[]{:S(2)}, u32[]{:S(2)}) %collective-permute-start.46) | collective-permute-done | bytes 167968 | tf_op jit(solution)/shard_map/ppermute | solution.py:675
  316.1 2.5 collective-permute-start.49
  320.7 10.8 %collective-permute-done.50 = bf16[1,512,128]{2,1,0:T(8,128)(2,1)S(1)} collective-permute-done((bf16[1,512,128]{2,1,0:T(8,128)(2,1)S(1)}, bf16[1,512,128]{2,1,0:T(8,128)(2,1)S(1)}, u32[]{:S(2)}, u32[]{:S(2)}) %collective-permute-start.50) | collective-permute-done | bytes 131104 | tf_op jit(solution)/shard_map/ppermute | solution.py:675
  331.4 3.5 collective-permute-start.56
  336.8 3.4 last.1
  340.2 11.8 %collective-permute-done.56 = bf16[1,32,5248]{2,1,0:T(8,128)(2,1)S(1)} collective-permute-done((bf16[1,32,5248]{2,1,0:T(8,128)(2,1)S(1)}, bf16[1,32,5248]{2,1,0:T(8,128)(2,1)S(1)}, u32[]{:S(2)}, u32[]{:S(2)}) %collective-permute-start.56) | collective-permute-done | bytes 335904 | tf_op jit(solution)/shard_map/ppermute | solution.py:675
  354.2 9.7 %all_to_all.10 = bf16[2,4,96,128]{3,2,0,1:T(8,128)(2,1)S(1)} all-to-all(bf16[2,4,96,128]{3,2,0,1:T(8,128)(2,1)S(1)} %copy.50), channel_id=1, replica_groups=mesh['ctx'=8,'fsdp'=4] {'fsdp'}, dimensions={1} | all-to-all | bytes 393216 | tf_op jit(solution)/shard_map/all_to_all | solution.py:1004
  365.6 5.3 %collective-permute-start.62 = (bf16[1,128,1024]{2,1,0:T(8,128)(2,1)S(1)}, bf16[1,128,1024]{2,1,0:T(8,128)(2,1)S(1)}, u32[]{:S(2)}, u32[]{:S(2)}) collective-permute-start(bf16[1,128,1024]{2,1,0:T(8,128)(2,1)S(1)} %copy-done.45), channel_id=1, source_target_pairs={{16,0},{26,1},{20,2},{30,3},{0,4},{10,5},{4,6},{14,7},{17,8},{27,9... | collective-permute-start | bytes 786440 | tf_op jit(solution)/shard_map/ppermute | solution.py:627
  374.8 2.5 collective-permute-start.64
  378.7 15.7 %collective-permute-done.62 = bf16[1,128,1024]{2,1,0:T(8,128)(2,1)S(1)} collective-permute-done((bf16[1,128,1024]{2,1,0:T(8,128)(2,1)S(1)}, bf16[1,128,1024]{2,1,0:T(8,128)(2,1)S(1)}, u32[]{:S(2)}, u32[]{:S(2)}) %collective-permute-start.62) | collective-permute-done | bytes 262176 | tf_op jit(solution)/shard_map/ppermute | solution.py:627
  394.4 11.2 %collective-permute-done.60 = bf16[2,2,512,128]{3,2,1,0:T(8,128)(2,1)S(1)} collective-permute-done((bf16[2,2,512,128]{3,2,1,0:T(8,128)(2,1)S(1)}, bf16[2,2,512,128]{3,2,1,0:T(8,128)(2,1)S(1)}, u32[]{:S(2)}, u32[]{:S(2)}) %collective-permute-start.60) | collective-permute-done | bytes 524320 | tf_op jit(solution)/shard_map/ppermute | solution.py:675
  409.3 5.7 %out_grad.1 = f32[656,1024]{1,0:T(8,128)} custom-call(bf16[8,4,32,656]{3,2,1,0:T(8,128)(2,1)} %pad_maximum_fusion.1.stack, s32[1]{0:T(128)} %bitcast.3.refs_11_.refs_14_.refs_3_.c_ref), custom_call_target="tpu_custom_call" | custom-call | flops 1000000 | bytes 4030468 | tf_op jit(solution)/shard_map/out_grad/pallas_call | solution.py:53
  416.1 5.1 %in_grad.1 = (f32[256,5248]{1,0:T(8,128)}, f32[256,1]{1,0:T(8,128)S(1)}) custom-call(s32[8]{0:T(128)S(1)} %fusion.12.table, bf16[4,32,5248]{2,1,0:T(8,128)(2,1)S(1)} %constant_dynamic-update-slice_fusion.8.low, bf16[4,32,5248]{2,1,0:T(8,128)(2,1)S(1)} %collective-permute-done.64.high, bf16[256,5248]{1,0:T(8,128)(2,1)S(1)} %copy-done, f32[256,1]{1,0:T(8,128)S(1)} %copy-done.1), custom_call_target="tpu_custom_call" | custom-call | flops 1000000 | bytes 10747904 | tf_op jit(solution)/shard_map/in_grad/pallas_call | solution.py:1048
  421.8 11.1 %collective-permute-done.63 = bf16[4,2,512,128]{3,2,1,0:T(8,128)(2,1)} collective-permute-done((bf16[4,2,512,128]{3,2,1,0:T(8,128)(2,1)}, bf16[4,2,512,128]{3,2,1,0:T(8,128)(2,1)}, u32[]{:S(2)}, u32[]{:S(2)}) %collective-permute-start.63) | collective-permute-done | bytes 1048608 | tf_op jit(solution)/shard_map/ppermute | solution.py:675
  432.9 2.9 pad_maximum_fusion.refs_0_
  435.8 4.8 %qkv_grad.1 = (f32[256,3072]{1,0:T(8,128)}, f32[256,1024]{1,0:T(8,128)}, f32[256,1]{1,0:T(8,128)}) custom-call(bf16[8,2,512,128]{3,2,1,0:T(8,128)(2,1)} %pad_maximum_fusion.refs_0_, bf16[256,3072]{1,0:T(8,128)(2,1)} %refs_1_, f32[256,1]{1,0:T(8,128)} %copy.42.gain.refs_2_, s32[1]{0:T(128)} %bitcast.3.refs_11_.refs_14_.refs_3_.c_ref), custom_call_target="tpu_custom_call" | custom-call | flops 1000000 | bytes 7866372 | tf_op jit(solution)/shard_map/qkv_grad/pallas_call | solution.py:53
  (298 shorter events, 98.7 us)
Async XLA Ops:
  2.5 31.2 %collective-permute-start = (bf16[1,144,1024]{2,1,0:T(8,128)(2,1)S(1)}, bf16[1,144,1024]{2,1,0:T(8,128)(2,1)S(1)}, u32[]{:S(2)}, u32[]{:S(2)}) collective-permute-start(bf16[1,144,1024]{2,1,0:T(8,128)(2,1)S(1)} %get-tuple-element.209), channel_id=1, source_target_pairs={{0,0},{1,10},{2,4},{3,14},{4,16},{5,26},{6,20},{7,30},{8,1},{9,11}... | collective-permute-start | bytes 884744 | tf_op jit(solution)/shard_map/ppermute | solution.py:623
  3.2 30.6 %collective-permute-start.1 = (bf16[1,144,1024]{2,1,0:T(8,128)(2,1)S(1)}, bf16[1,144,1024]{2,1,0:T(8,128)(2,1)S(1)}, u32[]{:S(2)}, u32[]{:S(2)}) collective-permute-start(bf16[1,144,1024]{2,1,0:T(8,128)(2,1)S(1)} %get-tuple-element.210), channel_id=1, source_target_pairs={{0,16},{1,26},{2,20},{3,30},{4,0},{5,10},{6,4},{7,14},{8,17},{9,27... | collective-permute-start | bytes 884744 | tf_op jit(solution)/shard_map/ppermute | solution.py:623
  36.8 28.4 %collective-permute-start.6 = (bf16[272,1024]{1,0:T(8,128)(2,1)}, bf16[272,1024]{1,0:T(8,128)(2,1)S(1)}, u32[]{:S(2)}, u32[]{:S(2)}) collective-permute-start(bf16[272,1024]{1,0:T(8,128)(2,1)} %unit1.1.refs_0_), channel_id=1, source_target_pairs={{0,2},{1,3},{2,0},{3,1},{4,6},{5,7},{6,4},{7,5},{8,10},{9,11},{10,... | collective-permute-start | bytes 1671176 | tf_op jit(solution)/shard_map/ppermute | solution.py:644
  39.3 25.9 %collective-permute-start.9 = (bf16[1,128,1024]{2,1,0:T(8,128)(2,1)S(1)}, bf16[1,128,1024]{2,1,0:T(8,128)(2,1)S(1)}, u32[]{:S(2)}, u32[]{:S(2)}) collective-permute-start(bf16[1,128,1024]{2,1,0:T(8,128)(2,1)S(1)} %get-tuple-element.447), channel_id=1, source_target_pairs={{0,0},{1,10},{2,4},{3,14},{4,16},{5,26},{6,20},{7,30},{8,1},{9,11}... | collective-permute-start | bytes 786440 | tf_op jit(solution)/shard_map/ppermute | solution.py:623
  40.1 25.1 %collective-permute-start.10 = (bf16[1,128,1024]{2,1,0:T(8,128)(2,1)S(1)}, bf16[1,128,1024]{2,1,0:T(8,128)(2,1)S(1)}, u32[]{:S(2)}, u32[]{:S(2)}) collective-permute-start(bf16[1,128,1024]{2,1,0:T(8,128)(2,1)S(1)} %get-tuple-element.446), channel_id=1, source_target_pairs={{0,16},{1,26},{2,20},{3,30},{4,0},{5,10},{6,4},{7,14},{8,17},{9,27... | collective-permute-start | bytes 786440 | tf_op jit(solution)/shard_map/ppermute | solution.py:623
  45.6 16.5 %collective-permute-start.7 = (bf16[128,768]{1,0:T(8,128)(2,1)S(1)}, bf16[128,768]{1,0:T(8,128)(2,1)S(1)}, u32[]{:S(2)}, u32[]{:S(2)}) collective-permute-start(bf16[128,768]{1,0:T(8,128)(2,1)S(1)} %collective-permute-done.3.refs_6_), channel_id=1, source_target_pairs={{0,4},{4,0},{8,12},{12,8},{16,20},{20,16},{24,28},{28,24},{1,5},{5... | collective-permute-start | bytes 589832 | tf_op jit(solution)/shard_map/ppermute | solution.py:675
  45.7 19.5 %collective-permute-start.8 = (bf16[128,768]{1,0:T(8,128)(2,1)S(1)}, bf16[128,768]{1,0:T(8,128)(2,1)S(1)}, u32[]{:S(2)}, u32[]{:S(2)}) collective-permute-start(bf16[128,768]{1,0:T(8,128)(2,1)S(1)} %collective-permute-done.4.refs_7_), channel_id=1, source_target_pairs={{0,4},{4,0},{8,12},{12,8},{16,20},{20,16},{24,28},{28,24},{1,5},{5... | collective-permute-start | bytes 589832 | tf_op jit(solution)/shard_map/ppermute | solution.py:675
  68.1 30.0 %collective-permute-start.13 = (bf16[256,1024]{1,0:T(8,128)(2,1)S(1)}, bf16[256,1024]{1,0:T(8,128)(2,1)S(1)}, u32[]{:S(2)}, u32[]{:S(2)}) collective-permute-start(bf16[256,1024]{1,0:T(8,128)(2,1)S(1)} %bitcast.56), channel_id=1, source_target_pairs={{0,2},{1,3},{2,0},{3,1},{4,6},{5,7},{6,4},{7,5},{8,10},{9,11},{10,... | collective-permute-start | bytes 1572872 | tf_op jit(solution)/shard_map/ppermute | solution.py:644
  70.5 23.8 %collective-permute-start.14 = (bf16[256,768]{1,0:T(8,128)(2,1)S(1)}, bf16[256,768]{1,0:T(8,128)(2,1)S(1)}, u32[]{:S(2)}, u32[]{:S(2)}) collective-permute-start(bf16[256,768]{1,0:T(8,128)(2,1)S(1)} %get-tuple-element.420), channel_id=1, source_target_pairs={{0,1},{1,0},{2,3},{3,2},{4,5},{5,4},{6,7},{7,6},{8,9},{9,8},{10,11... | collective-permute-start | bytes 1179656 | tf_op jit(solution)/shard_map/ppermute | solution.py:726
  70.8 23.6 %collective-permute-start.15 = (bf16[256,768]{1,0:T(8,128)(2,1)S(1)}, bf16[256,768]{1,0:T(8,128)(2,1)S(1)}, u32[]{:S(2)}, u32[]{:S(2)}) collective-permute-start(bf16[256,768]{1,0:T(8,128)(2,1)S(1)} %get-tuple-element.419), channel_id=1, source_target_pairs={{0,2},{1,3},{2,0},{3,1},{4,6},{5,7},{6,4},{7,5},{8,10},{9,11},{10,... | collective-permute-start | bytes 1179656 | tf_op jit(solution)/shard_map/ppermute | solution.py:726
  72.5 25.6 %collective-permute-start.16 = (bf16[256,768]{1,0:T(8,128)(2,1)S(1)}, bf16[256,768]{1,0:T(8,128)(2,1)S(1)}, u32[]{:S(2)}, u32[]{:S(2)}) collective-permute-start(bf16[256,768]{1,0:T(8,128)(2,1)S(1)} %get-tuple-element.418), channel_id=1, source_target_pairs={{0,3},{1,2},{2,1},{3,0},{4,7},{5,6},{6,5},{7,4},{8,11},{9,10},{10,... | collective-permute-start | bytes 1179656 | tf_op jit(solution)/shard_map/ppermute | solution.py:726
  73.4 24.7 %collective-permute-start.17 = (bf16[256,768]{1,0:T(8,128)(2,1)S(1)}, bf16[256,768]{1,0:T(8,128)(2,1)S(1)}, u32[]{:S(2)}, u32[]{:S(2)}) collective-permute-start(bf16[256,768]{1,0:T(8,128)(2,1)S(1)} %get-tuple-element.430), channel_id=1, source_target_pairs={{0,1},{1,0},{2,3},{3,2},{4,5},{5,4},{6,7},{7,6},{8,9},{9,8},{10,11... | collective-permute-start | bytes 1179656 | tf_op jit(solution)/shard_map/ppermute | solution.py:644
  101.8 14.3 %collective-permute-start.20 = (bf16[256,1024]{1,0:T(8,128)(2,1)S(1)}, bf16[256,1024]{1,0:T(8,128)(2,1)S(1)}, u32[]{:S(2)}, u32[]{:S(2)}) collective-permute-start(bf16[256,1024]{1,0:T(8,128)(2,1)S(1)} %add_convert_fusion.9), channel_id=1, source_target_pairs={{0,2},{1,3},{2,0},{3,1},{4,6},{5,7},{6,4},{7,5},{8,10},{9,11},{10,... | collective-permute-start | bytes 1572872 | tf_op jit(solution)/shard_map/ppermute | solution.py:644
  102.2 20.1 %collective-permute-start.23 = (bf16[256,1024]{1,0:T(8,128)(2,1)S(1)}, bf16[256,1024]{1,0:T(8,128)(2,1)S(1)}, u32[]{:S(2)}, u32[]{:S(2)}) collective-permute-start(bf16[256,1024]{1,0:T(8,128)(2,1)S(1)} %bitcast.57), channel_id=1, source_target_pairs={{0,1},{1,0},{2,3},{3,2},{4,5},{5,4},{6,7},{7,6},{8,9},{9,8},{10,11... | collective-permute-start | bytes 1572872 | tf_op jit(solution)/shard_map/ppermute | solution.py:644
  102.3 20.0 %collective-permute-start.24 = (bf16[256,1024]{1,0:T(8,128)(2,1)S(1)}, bf16[256,1024]{1,0:T(8,128)(2,1)S(1)}, u32[]{:S(2)}, u32[]{:S(2)}) collective-permute-start(bf16[256,1024]{1,0:T(8,128)(2,1)S(1)} %collective-permute-done.13.refs_6_), channel_id=1, source_target_pairs={{0,1},{1,0},{2,3},{3,2},{4,5},{5,4},{6,7},{7,6},{8,9},{9,8},{10,11... | collective-permute-start | bytes 1572872 | tf_op jit(solution)/shard_map/ppermute | solution.py:644
  102.7 17.1 %collective-permute-start.21 = (bf16[256,768]{1,0:T(8,128)(2,1)S(1)}, bf16[256,768]{1,0:T(8,128)(2,1)S(1)}, u32[]{:S(2)}, u32[]{:S(2)}) collective-permute-start(bf16[256,768]{1,0:T(8,128)(2,1)S(1)} %collective-permute-done.15.refs_10_), channel_id=1, source_target_pairs={{0,4},{4,0},{8,12},{12,8},{16,20},{20,16},{24,28},{28,24},{1,5},{5... | collective-permute-start | bytes 1179656 | tf_op jit(solution)/shard_map/ppermute | solution.py:675
  102.7 19.5 %collective-permute-start.22 = (bf16[256,768]{1,0:T(8,128)(2,1)S(1)}, bf16[256,768]{1,0:T(8,128)(2,1)S(1)}, u32[]{:S(2)}, u32[]{:S(2)}) collective-permute-start(bf16[256,768]{1,0:T(8,128)(2,1)S(1)} %collective-permute-done.16.refs_11_), channel_id=1, source_target_pairs={{0,4},{4,0},{8,12},{12,8},{16,20},{20,16},{24,28},{28,24},{1,5},{5... | collective-permute-start | bytes 1179656 | tf_op jit(solution)/shard_map/ppermute | solution.py:675
  122.3 13.4 %collective-permute-start.26 = (bf16[256,1024]{1,0:T(8,128)(2,1)}, bf16[256,1024]{1,0:T(8,128)(2,1)S(1)}, u32[]{:S(2)}, u32[]{:S(2)}) collective-permute-start(bf16[256,1024]{1,0:T(8,128)(2,1)} %get-tuple-element.273.refs_0_), channel_id=1, source_target_pairs={{0,2},{1,3},{2,0},{3,1},{4,6},{5,7},{6,4},{7,5},{8,10},{9,11},{10,... | collective-permute-start | bytes 1572872 | tf_op jit(solution)/shard_map/ppermute | solution.py:644
  159.0 18.2 %collective-permute-start.28 = (bf16[256,1024]{1,0:T(8,128)(2,1)}, bf16[256,1024]{1,0:T(8,128)(2,1)S(1)}, u32[]{:S(2)}, u32[]{:S(2)}) collective-permute-start(bf16[256,1024]{1,0:T(8,128)(2,1)} %get-tuple-element.285), channel_id=1, source_target_pairs={{0,1},{1,0},{2,3},{3,2},{4,5},{5,4},{6,7},{7,6},{8,9},{9,8},{10,11... | collective-permute-start | bytes 1572872 | tf_op jit(solution)/shard_map/ppermute | solution.py:644
  162.2 15.0 %collective-permute-start.30 = (bf16[256,1024]{1,0:T(8,128)(2,1)S(1)}, bf16[256,1024]{1,0:T(8,128)(2,1)S(1)}, u32[]{:S(2)}, u32[]{:S(2)}) collective-permute-start(bf16[256,1024]{1,0:T(8,128)(2,1)S(1)} %add_convert_fusion.8), channel_id=1, source_target_pairs={{0,2},{1,3},{2,0},{3,1},{4,6},{5,7},{6,4},{7,5},{8,10},{9,11},{10,... | collective-permute-start | bytes 1572872 | tf_op jit(solution)/shard_map/ppermute | solution.py:644
  183.5 36.5 %collective-permute-start.34 = (bf16[4,4,2,32,656]{4,3,1,2,0:T(8,128)(2,1)}, bf16[4,4,2,32,656]{4,3,1,2,0:T(8,128)(2,1)}, u32[]{:S(2)}, u32[]{:S(2)}) collective-permute-start(bf16[4,4,2,32,656]{4,3,1,2,0:T(8,128)(2,1)} %get-tuple-element.412), channel_id=1, source_target_pairs={{0,4},{4,0},{8,12},{12,8},{16,20},{20,16},{24,28},{28,24},{1,5},{5... | collective-permute-start | bytes 4030472 | tf_op jit(solution)/shard_map/ppermute | solution.py:675
  187.9 20.4 %collective-permute-start.35 = (bf16[4,4,32,656]{3,2,1,0:T(8,128)(2,1)}, bf16[4,4,32,656]{3,2,1,0:T(8,128)(2,1)S(1)}, u32[]{:S(2)}, u32[]{:S(2)}) collective-permute-start(bf16[4,4,32,656]{3,2,1,0:T(8,128)(2,1)} %get-tuple-element.416), channel_id=1, source_target_pairs={{0,8},{4,12},{8,0},{12,4},{16,24},{20,28},{24,16},{28,20},{1,9},{5... | collective-permute-start | bytes 2015240 | tf_op jit(solution)/shard_map/ppermute | solution.py:675
  191.2 13.8 %collective-permute-start.31 = (bf16[256,1024]{1,0:T(8,128)(2,1)}, bf16[256,1024]{1,0:T(8,128)(2,1)S(1)}, u32[]{:S(2)}, u32[]{:S(2)}) collective-permute-start(bf16[256,1024]{1,0:T(8,128)(2,1)} %get-tuple-element.338.refs_0_), channel_id=1, source_target_pairs={{0,2},{1,3},{2,0},{3,1},{4,6},{5,7},{6,4},{7,5},{8,10},{9,11},{10,... | collective-permute-start | bytes 1572872 | tf_op jit(solution)/shard_map/ppermute | solution.py:644
  224.4 28.6 %collective-permute-start.38 = (bf16[2,4,2,32,656]{4,3,1,2,0:T(8,128)(2,1)S(1)}, bf16[2,4,2,32,656]{4,3,1,2,0:T(8,128)(2,1)S(1)}, u32[]{:S(2)}, u32[]{:S(2)}) collective-permute-start(bf16[2,4,2,32,656]{4,3,1,2,0:T(8,128)(2,1)S(1)} %get-tuple-element.414), channel_id=1, source_target_pairs={{0,8},{4,12},{8,0},{12,4},{16,24},{20,28},{24,16},{28,20},{1,9},{5... | collective-permute-start | bytes 2015240 | tf_op jit(solution)/shard_map/ppermute | solution.py:675
  226.9 25.3 %collective-permute-start.39 = (bf16[2,4,32,656]{3,2,1,0:T(8,128)(2,1)S(1)}, bf16[2,4,32,656]{3,2,1,0:T(8,128)(2,1)S(1)}, u32[]{:S(2)}, u32[]{:S(2)}) collective-permute-start(bf16[2,4,32,656]{3,2,1,0:T(8,128)(2,1)S(1)} %get-tuple-element.428), channel_id=1, source_target_pairs={{0,16},{4,20},{8,24},{12,28},{16,0},{20,4},{24,8},{28,12},{1,17},{... | collective-permute-start | bytes 1007624 | tf_op jit(solution)/shard_map/ppermute | solution.py:675
  227.1 25.2 %collective-permute-start.40 = (bf16[256,1024]{1,0:T(8,128)(2,1)S(1)}, bf16[256,1024]{1,0:T(8,128)(2,1)S(1)}, u32[]{:S(2)}, u32[]{:S(2)}) collective-permute-start(bf16[256,1024]{1,0:T(8,128)(2,1)S(1)} %add_convert_fusion.6), channel_id=1, source_target_pairs={{0,2},{1,3},{2,0},{3,1},{4,6},{5,7},{6,4},{7,5},{8,10},{9,11},{10,... | collective-permute-start | bytes 1572872 | tf_op jit(solution)/shard_map/ppermute | solution.py:644
  255.6 24.0 %collective-permute-start.41 = (bf16[4,512,128]{2,1,0:T(8,128)(2,1)S(1)}, bf16[4,512,128]{2,1,0:T(8,128)(2,1)S(1)}, u32[]{:S(2)}, u32[]{:S(2)}) collective-permute-start(bf16[4,512,128]{2,1,0:T(8,128)(2,1)S(1)} %get-tuple-element.424), channel_id=1, source_target_pairs={{0,4},{4,0},{8,12},{12,8},{16,20},{20,16},{24,28},{28,24},{1,5},{5... | collective-permute-start | bytes 1572872 | tf_op jit(solution)/shard_map/ppermute | solution.py:675
  256.5 23.1 %collective-permute-start.42 = (bf16[1,4,2,32,656]{4,3,1,2,0:T(8,128)(2,1)S(1)}, bf16[1,4,2,32,656]{4,3,1,2,0:T(8,128)(2,1)S(1)}, u32[]{:S(2)}, u32[]{:S(2)}) collective-permute-start(bf16[1,4,2,32,656]{4,3,1,2,0:T(8,128)(2,1)S(1)} %get-tuple-element.426), channel_id=1, source_target_pairs={{0,16},{4,20},{8,24},{12,28},{16,0},{20,4},{24,8},{28,12},{1,17},{... | collective-permute-start | bytes 1007624 | tf_op jit(solution)/shard_map/ppermute | solution.py:675
  260.1 19.5 %collective-permute-start.43 = (bf16[1,4,32,656]{3,2,1,0:T(8,128)(2,1)S(1)}, bf16[1,4,32,656]{3,2,1,0:T(8,128)(2,1)S(1)}, u32[]{:S(2)}, u32[]{:S(2)}) collective-permute-start(bf16[1,4,32,656]{3,2,1,0:T(8,128)(2,1)S(1)} %get-tuple-element.450), channel_id=1, source_target_pairs={{0,4},{4,0},{8,12},{12,8},{16,20},{20,16},{24,28},{28,24},{1,5},{5... | collective-permute-start | bytes 503816 | tf_op jit(solution)/shard_map/ppermute | solution.py:675
  280.5 32.4 %collective-permute-start.44 = (bf16[2,512,128]{2,1,0:T(8,128)(2,1)}, bf16[2,512,128]{2,1,0:T(8,128)(2,1)}, u32[]{:S(2)}, u32[]{:S(2)}) collective-permute-start(bf16[2,512,128]{2,1,0:T(8,128)(2,1)} %get-tuple-element.444), channel_id=1, source_target_pairs={{0,8},{4,12},{8,0},{12,4},{16,24},{20,28},{24,16},{28,20},{1,9},{5... | collective-permute-start | bytes 786440 | tf_op jit(solution)/shard_map/ppermute | solution.py:675
  281.0 31.9 %collective-permute-start.45 = (bf16[4,512,128]{2,1,0:T(8,128)(2,1)S(1)}, bf16[4,512,128]{2,1,0:T(8,128)(2,1)S(1)}, u32[]{:S(2)}, u32[]{:S(2)}) collective-permute-start(bf16[4,512,128]{2,1,0:T(8,128)(2,1)S(1)} %get-tuple-element.422), channel_id=1, source_target_pairs={{0,4},{4,0},{8,12},{12,8},{16,20},{20,16},{24,28},{28,24},{1,5},{5... | collective-permute-start | bytes 1572872 | tf_op jit(solution)/shard_map/ppermute | solution.py:675
  282.1 17.6 %all-to-all-start = ((bf16[4,2,32,656]{3,2,1,0:T(8,128)(2,1)}), bf16[4,2,32,656]{3,2,1,0:T(8,128)(2,1)S(1)}, u32[]{:S(2)}, u32[]{:S(2)}) async-start(bf16[4,2,32,656]{3,2,1,0:T(8,128)(2,1)} %copy.48), calls=%async_computation | async-start | bytes 786432 | tf_op jit(solution)/shard_map/all_to_all | solution.py:966
  285.5 34.0 %collective-permute-start.53 = (bf16[1,128,1024]{2,1,0:T(8,128)(2,1)}, bf16[1,128,1024]{2,1,0:T(8,128)(2,1)S(1)}, u32[]{:S(2)}, u32[]{:S(2)}) collective-permute-start(bf16[1,128,1024]{2,1,0:T(8,128)(2,1)} %get-tuple-element.371), channel_id=1, source_target_pairs={{0,0},{10,1},{4,2},{14,3},{16,4},{26,5},{20,6},{30,7},{1,8},{11,9}... | collective-permute-start | bytes 786440 | tf_op jit(solution)/shard_map/ppermute | solution.py:627
  287.1 33.4 %collective-permute-start.54 = (bf16[1,128,1024]{2,1,0:T(8,128)(2,1)}, bf16[1,128,1024]{2,1,0:T(8,128)(2,1)}, u32[]{:S(2)}, u32[]{:S(2)}) collective-permute-start(bf16[1,128,1024]{2,1,0:T(8,128)(2,1)} %get-tuple-element.372), channel_id=1, source_target_pairs={{16,0},{26,1},{20,2},{30,3},{0,4},{10,5},{4,6},{14,7},{17,8},{27,9... | collective-permute-start | bytes 786440 | tf_op jit(solution)/shard_map/ppermute | solution.py:627
  292.8 20.1 %collective-permute-start.46 = (bf16[1,4,32,656]{3,2,1,0:T(8,128)(2,1)S(1)}, bf16[1,4,32,656]{3,2,1,0:T(8,128)(2,1)}, u32[]{:S(2)}, u32[]{:S(2)}) collective-permute-start(bf16[1,4,32,656]{3,2,1,0:T(8,128)(2,1)S(1)} %get-tuple-element.369), channel_id=1, source_target_pairs={{0,16},{4,20},{8,24},{12,28},{16,0},{20,4},{24,8},{28,12},{1,17},{... | collective-permute-start | bytes 503816 | tf_op jit(solution)/shard_map/ppermute | solution.py:675
  312.9 22.0 %collective-permute-start.47 = (bf16[256,1024]{1,0:T(8,128)(2,1)}, bf16[256,1024]{1,0:T(8,128)(2,1)S(1)}, u32[]{:S(2)}, u32[]{:S(2)}) collective-permute-start(bf16[256,1024]{1,0:T(8,128)(2,1)} %get-tuple-element.362), channel_id=1, source_target_pairs={{0,1},{1,0},{2,3},{3,2},{4,5},{5,4},{6,7},{7,6},{8,9},{9,8},{10,11... | collective-permute-start | bytes 1572872 | tf_op jit(solution)/shard_map/ppermute | solution.py:644
  313.7 21.2 %collective-permute-start.51 = (bf16[2,512,128]{2,1,0:T(8,128)(2,1)S(1)}, bf16[2,512,128]{2,1,0:T(8,128)(2,1)S(1)}, u32[]{:S(2)}, u32[]{:S(2)}) collective-permute-start(bf16[2,512,128]{2,1,0:T(8,128)(2,1)S(1)} %get-tuple-element.442), channel_id=1, source_target_pairs={{0,8},{4,12},{8,0},{12,4},{16,24},{20,28},{24,16},{28,20},{1,9},{5... | collective-permute-start | bytes 786440 | tf_op jit(solution)/shard_map/ppermute | solution.py:675
  316.1 18.8 %collective-permute-start.49 = (bf16[256,1024]{1,0:T(8,128)(2,1)S(1)}, bf16[256,1024]{1,0:T(8,128)(2,1)S(1)}, u32[]{:S(2)}, u32[]{:S(2)}) collective-permute-start(bf16[256,1024]{1,0:T(8,128)(2,1)S(1)} %add_convert_fusion.4), channel_id=1, source_target_pairs={{0,2},{1,3},{2,0},{3,1},{4,6},{5,7},{6,4},{7,5},{8,10},{9,11},{10,... | collective-permute-start | bytes 1572872 | tf_op jit(solution)/shard_map/ppermute | solution.py:644
  319.5 15.4 %collective-permute-start.52 = (bf16[2,4,32,656]{3,2,1,0:T(8,128)(2,1)S(1)}, bf16[2,4,32,656]{3,2,1,0:T(8,128)(2,1)S(1)}, u32[]{:S(2)}, u32[]{:S(2)}) collective-permute-start(bf16[2,4,32,656]{3,2,1,0:T(8,128)(2,1)S(1)} %constant_dynamic-update-slice_fusion), channel_id=1, source_target_pairs={{0,8},{4,12},{8,0},{12,4},{16,24},{20,28},{24,16},{28,20},{1,9},{5... | collective-permute-start | bytes 1007624 | tf_op jit(solution)/shard_map/ppermute | solution.py:675
  331.4 20.6 %collective-permute-start.56 = (bf16[1,32,5248]{2,1,0:T(8,128)(2,1)S(1)}, bf16[1,32,5248]{2,1,0:T(8,128)(2,1)S(1)}, u32[]{:S(2)}, u32[]{:S(2)}) collective-permute-start(bf16[1,32,5248]{2,1,0:T(8,128)(2,1)S(1)} %reshape.139), channel_id=1, source_target_pairs={{0,16},{4,20},{8,24},{12,28},{16,0},{20,4},{24,8},{28,12},{1,17},{... | collective-permute-start | bytes 1007624 | tf_op jit(solution)/shard_map/ppermute | solution.py:675
  335.0 18.9 %collective-permute-start.55 = (bf16[1,512,128]{2,1,0:T(8,128)(2,1)S(1)}, bf16[1,512,128]{2,1,0:T(8,128)(2,1)S(1)}, u32[]{:S(2)}, u32[]{:S(2)}) collective-permute-start(bf16[1,512,128]{2,1,0:T(8,128)(2,1)S(1)} %get-tuple-element.454), channel_id=1, source_target_pairs={{0,16},{4,20},{8,24},{12,28},{16,0},{20,4},{24,8},{28,12},{1,17},{... | collective-permute-start | bytes 393224 | tf_op jit(solution)/shard_map/ppermute | solution.py:675
  335.2 37.1 %collective-permute-start.59 = (bf16[4,4,32,656]{3,2,1,0:T(8,128)(2,1)S(1)}, bf16[4,4,32,656]{3,2,1,0:T(8,128)(2,1)S(1)}, u32[]{:S(2)}, u32[]{:S(2)}) collective-permute-start(bf16[4,4,32,656]{3,2,1,0:T(8,128)(2,1)S(1)} %constant_dynamic-update-slice_fusion.4), channel_id=1, source_target_pairs={{0,4},{4,0},{8,12},{12,8},{16,20},{20,16},{24,28},{28,24},{1,5},{5... | collective-permute-start | bytes 2015240 | tf_op jit(solution)/shard_map/ppermute | solution.py:675
  354.1 18.2 %collective-permute-start.58 = (bf16[2,32,5248]{2,1,0:T(8,128)(2,1)S(1)}, bf16[2,32,5248]{2,1,0:T(8,128)(2,1)S(1)}, u32[]{:S(2)}, u32[]{:S(2)}) collective-permute-start(bf16[2,32,5248]{2,1,0:T(8,128)(2,1)S(1)} %constant_dynamic-update-slice_fusion.2), channel_id=1, source_target_pairs={{0,8},{4,12},{8,0},{12,4},{16,24},{20,28},{24,16},{28,20},{1,9},{5... | collective-permute-start | bytes 2015240 | tf_op jit(solution)/shard_map/ppermute | solution.py:675
  364.9 13.7 %collective-permute-start.61 = (bf16[1,128,1024]{2,1,0:T(8,128)(2,1)S(1)}, bf16[1,128,1024]{2,1,0:T(8,128)(2,1)S(1)}, u32[]{:S(2)}, u32[]{:S(2)}) collective-permute-start(bf16[1,128,1024]{2,1,0:T(8,128)(2,1)S(1)} %copy-done.46), channel_id=1, source_target_pairs={{0,0},{10,1},{4,2},{14,3},{16,4},{26,5},{20,6},{30,7},{1,8},{11,9}... | collective-permute-start | bytes 786440 | tf_op jit(solution)/shard_map/ppermute | solution.py:627
  365.6 28.7 %collective-permute-start.62 = (bf16[1,128,1024]{2,1,0:T(8,128)(2,1)S(1)}, bf16[1,128,1024]{2,1,0:T(8,128)(2,1)S(1)}, u32[]{:S(2)}, u32[]{:S(2)}) collective-permute-start(bf16[1,128,1024]{2,1,0:T(8,128)(2,1)S(1)} %copy-done.45), channel_id=1, source_target_pairs={{16,0},{26,1},{20,2},{30,3},{0,4},{10,5},{4,6},{14,7},{17,8},{27,9... | collective-permute-start | bytes 786440 | tf_op jit(solution)/shard_map/ppermute | solution.py:627
  372.3 33.3 %collective-permute-start.60 = (bf16[2,2,512,128]{3,2,1,0:T(8,128)(2,1)S(1)}, bf16[2,2,512,128]{3,2,1,0:T(8,128)(2,1)S(1)}, u32[]{:S(2)}, u32[]{:S(2)}) collective-permute-start(bf16[2,2,512,128]{3,2,1,0:T(8,128)(2,1)S(1)} %constant_dynamic-update-slice_fusion.6), channel_id=1, source_target_pairs={{0,16},{4,20},{8,24},{12,28},{16,0},{20,4},{24,8},{28,12},{1,17},{... | collective-permute-start | bytes 1572872 | tf_op jit(solution)/shard_map/ppermute | solution.py:675
  374.8 41.2 %collective-permute-start.64 = (bf16[4,32,5248]{2,1,0:T(8,128)(2,1)S(1)}, bf16[4,32,5248]{2,1,0:T(8,128)(2,1)S(1)}, u32[]{:S(2)}, u32[]{:S(2)}) collective-permute-start(bf16[4,32,5248]{2,1,0:T(8,128)(2,1)S(1)} %constant_dynamic-update-slice_fusion.8.low), channel_id=1, source_target_pairs={{0,4},{4,0},{8,12},{12,8},{16,20},{20,16},{24,28},{28,24},{1,5},{5... | collective-permute-start | bytes 4030472 | tf_op jit(solution)/shard_map/ppermute | solution.py:675
  407.4 25.5 %collective-permute-start.63 = (bf16[4,2,512,128]{3,2,1,0:T(8,128)(2,1)}, bf16[4,2,512,128]{3,2,1,0:T(8,128)(2,1)}, u32[]{:S(2)}, u32[]{:S(2)}) collective-permute-start(bf16[4,2,512,128]{3,2,1,0:T(8,128)(2,1)} %pad_maximum_fusion.2), channel_id=1, source_target_pairs={{0,8},{4,12},{8,0},{12,4},{16,24},{20,28},{24,16},{28,20},{1,9},{5... | collective-permute-start | bytes 3145736 | tf_op jit(solution)/shard_map/ppermute | solution.py:675
  (73 other events, 672.4 us)

commit v4 on v3

--- a/solution.py
+++ b/solution.py
@@ -465,7 +465,7 @@
 def mlp_sums_kernel(*refs, p):
     fs, units = p.fsdp, p.units
     xs, cs, rest = refs[:fs], refs[fs : 2 * fs], refs[2 * fs :]
-    act_ref, da_ref, dg_ref, c_ref, one, two, sa, sg, sm, x, ct = rest
+    act_ref, da_ref, dg_ref, c_ref, one, two, three, sa, sg, sm, x, ct = rest
     step = pl.program_id(0)
 
     @pl.when(step == 0)
@@ -493,9 +493,9 @@
             late = storage(c_ref[0] ^ cc, p.last_order)
             for ff in range(fs):
                 at = slice(ff * p.rows + cc * p.small, ff * p.rows + (cc + 1) * p.small)
-                one[away, ff, 0] = sa[at, :units].astype(bf16)
-                one[away, ff, 1] = sm[at, :units].astype(bf16)
+                one[away, ff] = sa[at, :units].astype(bf16)
                 two[late, ff] = sg[at, :units].astype(bf16)
+                three[away, ff] = sm[at, :units].astype(bf16)
 
 
 def middle_kernel(*refs, p):
@@ -537,9 +537,22 @@
         outs[j][i] = (grad[rows] + norm_back(u, unit, rate)).astype(bf16)
 
 
-def qkv_grad_kernel(*refs, p):
-    stack, w, gain, c_ref, qkv, out, gain_grad = refs
+def row_sums(values):
+    ones = jnp.ones((8, values.shape[1]), f32)
+    total = lax.dot_general(
+        ones, values, NT, precision=lax.Precision.HIGHEST, preferred_element_type=f32
+    )
+    return total[:1]
+
+
+def qkv_grad_kernel(low, high, w, gain, c_ref, qkv, out, gain_grad, stack, sems, *, p):
     fs, small, slab, lanes = p.fsdp, p.small, p.slab, p.lanes
+    top = low.shape[0]
+    loads = copies([(low, stack.at[:top]), (high, stack.at[top:])], sems)
+    for load in loads:
+        load.start()
+    for load in loads:
+        load.wait()
     for cc in range(p.ctx):
         away = storage(c_ref[0] ^ cc, p.last_order)
         rows = slice(cc * small, (cc + 1) * small)
@@ -558,23 +571,17 @@
                 value = stack[away, g, at : at + slab, :].astype(f32)
                 row = g * lanes + cc * slab
                 out[row : row + slab, d * lanes : (d + 1) * lanes] = value
-        gain_grad[rows, :] = jnp.sum(total, axis=1, keepdims=True)
-
-
-def in_grad_kernel(table, low, high, w, gain, grad, gain_grad, *, top):
-    def write(value):
-        grad[...] = value * gain[...]
-        gain_grad[...] = jnp.sum(value * w[...].astype(f32), axis=1, keepdims=True)
-
-    step = pl.program_id(0)
-
-    @pl.when(table[step] < top)
-    def _():
-        write(low[0].astype(f32))
-
-    @pl.when(table[step] >= top)
-    def _():
-        write(high[0].astype(f32))
+        gain_grad[:, rows] = row_sums(total)
+
+
+def in_grad_kernel(table, sums, w, gain, *rest):
+    grad, gain_grad = rest[-2:]
+    value = sums[0].astype(f32)
+    grad[...] = value * gain[...]
+    total = jnp.zeros((value.shape[0], 128), f32)
+    for at in range(0, value.shape[1], 128):
+        total = total + value[:, at : at + 128] * w[:, at : at + 128].astype(f32)
+    gain_grad[0] = row_sums(total)
 
 
 def out_grad_kernel(stack, c_ref, grad, *, p):
@@ -839,19 +846,16 @@
     out_parts, u2_parts, (active, da, dg) = made[:fsdp], made[fsdp : 2 * fsdp], made[2 * fsdp :]
 
     u2 = reduce(u2_parts)
-    mlp_sums, gate_sums = call(
+    act_sums, gate_sums, down_sums = call(
         functools.partial(mlp_sums_kernel, p=p),
         "mlp_sums",
-        [
-            shape_of((ctx, fsdp, 2, small, units)),
-            shape_of((ctx, fsdp, small, units)),
-        ],
+        [shape_of((ctx, fsdp, small, units))] * 3,
         fsdp,
         [pltpu.VMEM((width, p.padded), f32)] * 3 + [pltpu.VMEM((own, width), bf16)] * 2,
         unit2_slots + cot_slots + [active, da, dg, here],
         6e9,
     )
-    u2, mlp_sums, gate_sums = lax.optimization_barrier((u2, mlp_sums, gate_sums))
+    u2, act_sums, gate_sums, down_sums = meet(u2, act_sums, gate_sums, down_sums)
     grad_residual, grad_low = call(
         functools.partial(turn_kernel, p=p),
         "turn",
@@ -864,23 +868,26 @@
     order = p.order
     gate_order = p.last_order
     piece = [shape_of((n, span, width))] * pieces
-    grad_low, out_parts, mlp_sums, gate_sums = meet(
-        grad_low, list(out_parts), mlp_sums, gate_sums
+    grad_low, out_parts, act_sums, gate_sums = meet(
+        grad_low, list(out_parts), act_sums, gate_sums
     )
     low_held = first_hop(grad_low)
-    mlp_pair, gate_pair = send(mlp_sums, order[0]), send(gate_sums, gate_order[0])
+    act_pair, gate_pair = send(act_sums, order[0]), send(gate_sums, gate_order[0])
     held = dict(enumerate(out_parts))
     for bit in reversed(bits[1:]):
         for o in sorted(held, reverse=True):
             if o & bit:
                 held[o ^ bit] = add((held[o ^ bit], partner(held.pop(o), bit)))
-    low_held, out_near, out_far, mlp_pair, gate_pair = meet(
-        low_held, held[0], held[bits[0]], mlp_pair, gate_pair
-    )
-    mlp_sums, gate_sums = add(mlp_pair), add(gate_pair)
+    low_held, out_near, out_far, act_pair, gate_pair = meet(
+        low_held, held[0], held[bits[0]], act_pair, gate_pair
+    )
+    act_sums, gate_sums = add(act_pair), add(gate_pair)
     low_slots = later_hops(low_held)
-    low_slots, out_far, mlp_sums, gate_sums = meet(low_slots, out_far, mlp_sums, gate_sums)
-    mlp_pair, gate_pair = send(mlp_sums, order[1]), send(gate_sums, gate_order[1])
+    low_slots, out_far, act_sums, gate_sums, down_sums = meet(
+        low_slots, out_far, act_sums, gate_sums, down_sums
+    )
+    act_pair, gate_pair = send(act_sums, order[1]), send(gate_sums, gate_order[1])
+    down_pair = send(down_sums, order[0])
     out_got = partner(out_far, bits[0])
     mixed, attention_sums = [], []
     for group in range(p.groups):
@@ -920,14 +927,15 @@
         )
         mixed.append(grad_mixed)
         if group == 0:
-            sums, low_slots, mlp_pair, gate_pair, out_got = meet(
-                sums, low_slots, mlp_pair, gate_pair, out_got
+            sums, low_slots, act_pair, gate_pair, down_pair, out_got = meet(
+                sums, low_slots, act_pair, gate_pair, down_pair, out_got
             )
             pairs = [send(sums, order[0])]
-            mlp_sums, gate_sums = add(mlp_pair), add(gate_pair)
+            act_sums, gate_sums, down_sums = add(act_pair), add(gate_pair), add(down_pair)
             for bit, gate_bit in zip(order[2:-1], gate_order[2:-1]):
-                mlp_sums, gate_sums = add(send(mlp_sums, bit)), add(send(gate_sums, gate_bit))
-            mlp_pair, gate_pair = send(mlp_sums, order[-1]), send(gate_sums, gate_order[-1])
+                act_sums, gate_sums = add(send(act_sums, bit)), add(send(gate_sums, gate_bit))
+            act_pair, gate_pair = send(act_sums, order[-1]), send(gate_sums, gate_order[-1])
+            down_pair = send(down_sums, order[1])
             result_parts = call(
                 functools.partial(result_kernel, p=p),
                 "result",
@@ -940,16 +948,21 @@
             low_slots, result_parts = meet(low_slots, result_parts)
             out_back = undeal(result_parts)
         else:
-            sums, pairs, mlp_pair, gate_pair = meet(sums, pairs, mlp_pair, gate_pair)
+            sums, pairs, act_pair, gate_pair, down_pair, out_back = meet(
+                sums, pairs, act_pair, gate_pair, down_pair, out_back
+            )
             pairs = pairs + [send(sums, order[0])]
+
+    back_order = order[::-1]
 
     def step_of(sums):
         return order[ctx.bit_length() - sums.shape[0].bit_length()]
 
-    back_order = order[::-1]
-    mlp_sums, gate_sums = add(mlp_pair)[0], add(gate_pair)[0]
-    mlp_stack = grow(mlp_sums[None, :, 1], back_order[0])
-    in_small = jnp.stack([mlp_sums[:, 0], gate_sums], axis=1)
+    in_small = jnp.stack([add(act_pair)[0], add(gate_pair)[0]], axis=1)
+    down_sums = add(down_pair)
+    for bit in order[2:-1]:
+        down_sums = add(send(down_sums, bit))
+    down_pair = send(down_sums, order[-1])
     early, late = pairs[:-1], pairs[-1]
     if early:
         sums = add(early[0])
@@ -965,18 +978,14 @@
     )
     in_small = lax.all_to_all(in_small, "fsdp", 0, 0, tiled=True)
     in_small = in_small.transpose(2, 1, 0, 3).reshape(1, small, 2 * fsdp * units)
-    u1_parts, early, late, mlp_stack, in_small = meet(
-        list(u1_parts), early, late, mlp_stack, in_small
-    )
-    in_pair = grow(in_small, back_order[0])
+    u1_parts, early, late, in_small = meet(list(u1_parts), early, late, in_small)
     u1 = reduce(u1_parts)
     if early:
         sums = add(early[0])
         early = [send(sums, step_of(sums))]
     sums = add(late)
     late = send(sums, step_of(sums))
-    mlp_stack = grow(join(mlp_stack), back_order[1])
-    u1, early, late, mlp_stack, out_back = meet(u1, early, late, mlp_stack, out_back)
+    u1, early, late, down_pair = meet(u1, early, late, down_pair)
     back_parts = call(
         functools.partial(last_kernel, p=p),
         "last",
@@ -988,10 +997,8 @@
     )
     sums = add(late)
     late = send(sums, step_of(sums))
-    mlp_stack = grow(join(mlp_stack), back_order[2])
-    back_parts, late, in_pair = meet(back_parts, late, in_pair)
-    back = undeal(back_parts)
-    in_pair = grow(join(in_pair), back_order[1])
+    down = grow(add(down_pair), back_order[0])
+    late, down, in_small = meet(late, down, in_small)
 
     def finished(pair):
         sums = add(pair)
@@ -1000,23 +1007,27 @@
         return sums
 
     sums = jnp.concatenate([finished(pair) for pair in early + [late]], axis=0)
+    in_pair = grow(in_small, back_order[0])
+    back = undeal(back_parts)
+    down = grow(join(down), back_order[1])
     mine = sums[:, : 3 * fsdp * small].reshape(p.groups, fsdp, 3 * small, p.lanes)
     mine = lax.all_to_all(mine, "fsdp", 1, 1, tiled=True)
     mine = mine.reshape(p.groups, 3 * fsdp * small, p.lanes)
     stack = jnp.concatenate([mine, sums[:, 3 * fsdp * small :]], axis=1)[None]
     last_back = p.last_order[::-1]
     stack = grow(stack, last_back[0])
+    stack, in_pair, down, back = meet(stack, in_pair, down, back)
+    stack = grow(join(stack), last_back[1])
+    in_pair = grow(join(in_pair), back_order[1])
+    down = grow(join(down), back_order[2])
     for bit in back_order[3:]:
-        mlp_stack = grow(join(mlp_stack), bit)
-    stack, in_pair, mlp_stack = meet(stack, in_pair, mlp_stack)
-    mlp_stack = join(mlp_stack)
-    stack = grow(join(stack), last_back[1])
+        down = grow(join(down), bit)
+    stack, in_pair, down = meet(stack, in_pair, down)
+    mlp_stack = join(down)
     for bit in back_order[2:]:
         in_pair = grow(join(in_pair), bit)
-    stack, back, mlp_stack = meet(stack, back, mlp_stack)
     for bit in last_back[2:]:
         stack = grow(join(stack), bit)
-    stack = join(stack)
     out, back = assemble(out_back), assemble(back).astype(f32)
 
     grad_qkv, grad_out, grad_gain_a = call(
@@ -1025,46 +1036,61 @@
         [
             shape_of((rows, 3 * width), f32),
             shape_of((cols, width), f32),
-            shape_of((rows, 1), f32),
+            shape_of((1, rows), f32),
         ],
         1,
-        [],
-        [stack, w_qkv, gain_a, here],
+        [
+            pltpu.VMEM((ctx, p.groups, 4 * fsdp * small, p.lanes), bf16),
+            pltpu.SemaphoreType.DMA((2,)),
+        ],
+        [Late(stack[0]), Late(stack[1]), w_qkv, gain_a, here],
         1e6,
     )
-    table = storage(c ^ jnp.arange(ctx, dtype=jnp.int32), order)
-    low_part, high_part, block = in_pair[0], in_pair[1], small
+
+    wide_in = 2 * fsdp * units
+
+    def in_grads(table, sums, block, before):
+        some = pl.BlockSpec((block, wide_in), lambda s, t: (t[s], 0))
+        any_spec = pl.BlockSpec(memory_space=pl.ANY)
+        small_out = pl.BlockSpec((1, 1, block), lambda s, t: (t[s], 0, 0))
+        return pl.pallas_call(
+            in_grad_kernel,
+            grid_spec=pltpu.PrefetchScalarGridSpec(
+                num_scalar_prefetch=1,
+                grid=(sums.shape[0],),
+                in_specs=[
+                    pl.BlockSpec((1, block, wide_in), lambda s, t: (s, 0, 0)),
+                    some,
+                    pl.BlockSpec((block, 1), lambda s, t: (t[s], 0)),
+                ]
+                + [any_spec] * len(before),
+                out_specs=[some, small_out],
+            ),
+            out_shape=[
+                shape_of(w_in.shape, f32),
+                shape_of((rows // block, 1, block), f32),
+            ],
+            input_output_aliases={4 + k: k for k in range(len(before))},
+            compiler_params=pltpu.CompilerParams(vmem_limit_bytes=40 << 20),
+            cost_estimate=pl.CostEstimate(
+                flops=1000000, bytes_accessed=8 * w_in.size, transcendentals=0
+            ),
+            name="in_grad",
+        )(table, sums, w_in, gain_m, *before)
+
     if small % 8:
-        low_part = join(in_pair)
+        parts = join(in_pair)
         parts = [
-            lax.dynamic_slice_in_dim(low_part, storage(c ^ cc, order), 1, 0) for cc in range(ctx)
+            lax.dynamic_slice_in_dim(parts, storage(c ^ cc, order), 1, 0) for cc in range(ctx)
         ]
-        low_part = jnp.concatenate(parts, axis=1)
-        high_part, block, table = low_part, rows, jnp.zeros((1,), jnp.int32)
-    top = low_part.shape[0]
-    some = pl.BlockSpec((block, 2 * fsdp * units), lambda s, t: (s, 0))
-    thin = pl.BlockSpec((block, 1), lambda s, t: (s, 0))
-    one = (1, block, 2 * fsdp * units)
-    grad_in, grad_gain_m = pl.pallas_call(
-        functools.partial(in_grad_kernel, top=top),
-        grid_spec=pltpu.PrefetchScalarGridSpec(
-            num_scalar_prefetch=1,
-            grid=(rows // block,),
-            in_specs=[
-                pl.BlockSpec(one, lambda s, t: (jnp.minimum(t[s], top - 1), 0, 0)),
-                pl.BlockSpec(one, lambda s, t: (jnp.maximum(t[s] - top, 0), 0, 0)),
-                some,
-                thin,
-            ],
-            out_specs=[some, thin],
-        ),
-        out_shape=[shape_of(w_in.shape, f32), shape_of((rows, 1), f32)],
-        compiler_params=pltpu.CompilerParams(vmem_limit_bytes=40 << 20),
-        cost_estimate=pl.CostEstimate(
-            flops=1000000, bytes_accessed=8 * w_in.size, transcendentals=0
-        ),
-        name="in_grad",
-    )(table, low_part, high_part, w_in, gain_m)
+        parts = jnp.concatenate(parts, axis=1)
+        grad_in, grad_gain_m = in_grads(jnp.zeros((1,), jnp.int32), parts, rows, [])
+    else:
+        place_of = {storage(x, order): x for x in range(ctx)}
+        table = jnp.stack([c ^ place_of[at] for at in range(ctx)])
+        top = ctx // 2
+        before = in_grads(table[:top], in_pair[0], small, [])
+        grad_in, grad_gain_m = in_grads(table[top:], in_pair[1], small, list(before))
     (grad_mlp_out,) = call(
         functools.partial(out_grad_kernel, p=p),
         "out_grad",

time: 450 us -> 430 us (0.956)
  waiting for transfers between devices: 160 us -> 138 us
  starting transfers between devices: 81.7 us -> 100 us
  blocking collectives: 9.74 us -> 0 us
  other arithmetic: 27 us -> 21.4 us
    ppermute x4, waiting for transfers between devices: 15.7 us -> 0.01 us  [undeal(): lax.ppermute(part, both, [(b, a) for a, b in route(j)])]
    ppermute x25 -> x28, waiting for transfers between devices: 96.3 us -> 81 us  [away(): return lax.ppermute(values, 'ctx', [(i, i ^ bit) for i in range(ctx)])]
    all_to_all x0 -> x1, starting transfers between devices: none -> 12.9 us  [on_device(): mine = lax.all_to_all(mine, 'fsdp', 1, 1, tiled=True)]
    all_to_all x1 -> x0, blocking collectives: 9.74 us -> none  [on_device(): mine = lax.all_to_all(mine, 'fsdp', 1, 1, tiled=True)]
    ppermute x25 -> x28, starting transfers between devices: 28.7 us -> 37.3 us  [away(): return lax.ppermute(values, 'ctx', [(i, i ^ bit) for i in range(ctx)])]
    all_to_all x1, waiting for transfers between devices: 0.01 us -> 7.31 us  [on_device(): in_small = lax.all_to_all(in_small, 'fsdp', 0, 0, tiled=True)]
    unnamed x115 -> x134, local copies, waits for them, and re-layouts: 6.58 us -> 9.3 us
  transfers between devices with their start and end apart: 66 -> 70, of which waited for: 27 -> 29; matrix products, arithmetic and copies ran while one was open for 8% -> 8% of each run, Pallas kernels for 24% -> 25%
where the time goes in v4:
time: 430 us; the launch traced here: 423 us
  waiting for transfers between devices  138 us (32%)
  Pallas kernels  135 us (31%)
  starting transfers between devices  100 us (23%)
  local copies, waits for them, and re-layouts  26.3 us (6%)
  other arithmetic  21.4 us (5%)
    pallas_call x17, Pallas kernels, call(): pl.pallas_call(kernel, grid=(grid,), in_specs=specs, out_specs=outs, out_...  130 us
    ppermute x28, waiting for transfers between devices, away(): return lax.ppermute(values, 'ctx', [(i, i ^ bit) for i in range(ctx)])  81 us
    ppermute x28, starting transfers between devices, away(): return lax.ppermute(values, 'ctx', [(i, i ^ bit) for i in range(ctx)])  37.3 us
    ppermute x26, waiting for transfers between devices, partner(): return lax.ppermute(values, 'fsdp', [(i, i ^ bit) for i in range(fsdp)])  36.9 us
    ppermute x4, starting transfers between devices, deal(): return [lax.ppermute(part, both, route(j)) for j, part in enumerate(parts)]  15.5 us
    ppermute x26, starting transfers between devices, partner(): return lax.ppermute(values, 'fsdp', [(i, i ^ bit) for i in range(fsdp)])  13.7 us
    all_to_all x1, starting transfers between devices, on_device(): mine = lax.all_to_all(mine, 'fsdp', 1, 1, tiled=True)  12.9 us
    ppermute x4, starting transfers between devices, undeal(): lax.ppermute(part, both, [(b, a) for a, b in route(j)])  12.4 us
  transfers between devices with their start and end apart: 70, of which 29 were waited for; matrix products, arithmetic and copies ran while one was open for 8% of the time, Pallas kernels for 25%

profile of v4, /device:TPU:0, one launch (start us, length us, event | category | flops | bytes accessed | tf_op | source)
XLA Modules:
  0.0 423.0 jit_solution(9844894301440928726)
XLA Ops:
  3.2 8.5 %collective-permute-start.1 = (bf16[1,144,1024]{2,1,0:T(8,128)(2,1)S(1)}, bf16[1,144,1024]{2,1,0:T(8,128)(2,1)S(1)}, u32[]{:S(2)}, u32[]{:S(2)}) collective-permute-start(bf16[1,144,1024]{2,1,0:T(8,128)(2,1)S(1)} %get-tuple-element.219), channel_id=1, source_target_pairs={{0,16},{1,26},{2,20},{3,30},{4,0},{5,10},{6,4},{7,14},{8,17},{9,27... | collective-permute-start | bytes 884744 | tf_op jit(solution)/shard_map/ppermute | solution.py:630
  13.1 3.9 cut.1
  27.2 2.3 collective-permute-done.3.refs_6_
  29.5 4.2 collective-permute-done.4.refs_7_
  36.8 2.4 collective-permute-start.6
  40.1 5.5 %collective-permute-start.10 = (bf16[1,128,1024]{2,1,0:T(8,128)(2,1)S(1)}, bf16[1,128,1024]{2,1,0:T(8,128)(2,1)S(1)}, u32[]{:S(2)}, u32[]{:S(2)}) collective-permute-start(bf16[1,128,1024]{2,1,0:T(8,128)(2,1)S(1)} %get-tuple-element.466), channel_id=1, source_target_pairs={{0,16},{1,26},{2,20},{3,30},{4,0},{5,10},{6,4},{7,14},{8,17},{9,27... | collective-permute-start | bytes 786440 | tf_op jit(solution)/shard_map/ppermute | solution.py:630
  48.5 5.2 %cut_in.1 = (bf16[4,256,768]{2,1,0:T(8,128)(2,1)}, bf16[2,256,768]{2,1,0:T(8,128)(2,1)}) custom-call(bf16[256,5248]{1,0:T(8,128)(2,1)} %w.4, f32[256,1]{1,0:T(8,128)} %copy.43.gain, s32[2]{0:T(128)} %pad_add_fusion.at_ref.refs_14_.refs_17_), custom_call_target="tpu_custom_call" | custom-call | flops 1000000 | bytes 5047304 | tf_op jit(solution)/shard_map/cut_in/pallas_call | solution.py:53
  53.7 8.3 %collective-permute-done.7.refs_10_ = bf16[128,768]{1,0:T(8,128)(2,1)S(1)} collective-permute-done((bf16[128,768]{1,0:T(8,128)(2,1)S(1)}, bf16[128,768]{1,0:T(8,128)(2,1)S(1)}, u32[]{:S(2)}, u32[]{:S(2)}) %collective-permute-start.7) | collective-permute-done | bytes 196640 | tf_op jit(solution)/shard_map/ppermute | solution.py:682
  62.1 3.2 collective-permute-done.8.refs_11_
  68.1 2.4 slice_bitcast_fusion.2
  73.8 7.9 %project.1 = (bf16[1,1024,256]{2,1,0:T(8,128)(2,1)}, bf16[1,1024,256]{2,1,0:T(8,128)(2,1)}, bf16[1,1024,256]{2,1,0:T(8,128)(2,1)}, f32[1,8,1024]{2,1,0:T(8,128)}, bf16[1024,768]{1,0:T(8,128)(2,1)}) custom-call(bf16[272,1024]{1,0:T(8,128)(2,1)} %unit1.1.refs_0_, bf16[272,1024]{1,0:T(8,128)(2,1)} %copy-done.16, bf16[272,1024]{1,0:T(8,128)(2,1)} %copy-done.15, ...), custom_call_target="tpu_custom_call" | custom-call | flops 4000000000 | bytes 8028168 | tf_op jit(solution)/shard_map/project/pallas_call | solution.py:53
  81.7 12.6 %attend.1 = (bf16[256,1024]{1,0:T(8,128)(2,1)}, bf16[256,1024]{1,0:T(8,128)(2,1)}, bf16[256,1024]{1,0:T(8,128)(2,1)}, bf16[256,1024]{1,0:T(8,128)(2,1)}, bf16[1,...) custom-call(bf16[1,1024,256]{2,1,0:T(8,128)(2,1)} %get-tuple-element.252.q_ref.refs_6_, ...), custom_call_target="tpu_custom_call" | custom-call | flops 12000000000 | bytes 4784128 | tf_op jit(solution)/shard_map/attend/pallas_call | solution.py:53
  94.4 3.7 collective-permute-done.16.refs_11_
  104.8 3.8 flip.1.refs_4_
  108.6 7.5 %collective-permute-done.20.refs_4_ = bf16[256,1024]{1,0:T(8,128)(2,1)S(1)} collective-permute-done((bf16[256,1024]{1,0:T(8,128)(2,1)S(1)}, bf16[256,1024]{1,0:T(8,128)(2,1)S(1)}, u32[]{:S(2)}, u32[]{:S(2)}) %collective-permute-start.20) | collective-permute-done | bytes 524320 | tf_op jit(solution)/shard_map/ppermute | solution.py:651
  116.9 3.0 middle.1
  119.8 2.4 collective-permute-done.22.refs_15_
  124.0 11.7 %collective-permute-done.26.refs_2_ = bf16[256,1024]{1,0:T(8,128)(2,1)S(1)} collective-permute-done((bf16[256,1024]{1,0:T(8,128)(2,1)}, bf16[256,1024]{1,0:T(8,128)(2,1)S(1)}, u32[]{:S(2)}, u32[]{:S(2)}) %collective-permute-start.26) | collective-permute-done | bytes 524320 | tf_op jit(solution)/shard_map/ppermute | solution.py:651
  138.4 20.3 %mlp.1 = (bf16[256,1024]{1,0:T(8,128)(2,1)}, bf16[256,1024]{1,0:T(8,128)(2,1)}, bf16[256,1024]{1,0:T(8,128)(2,1)}, bf16[256,1024]{1,0:T(8,128)(2,1)}, bf16[256,1...) custom-call(bf16[256,1024]{1,0:T(8,128)(2,1)} %get-tuple-element.282, ...), custom_call_target="tpu_custom_call" | custom-call | flops 12000000000 | bytes 17596424 | tf_op jit(solution)/shard_map/mlp/pallas_call | solution.py:53
  163.9 13.3 %mlp_sums.1 = (bf16[8,4,32,656]{3,2,1,0:T(8,128)(2,1)}, bf16[8,4,32,656]{3,2,1,0:T(8,128)(2,1)}, bf16[8,4,32,656]{3,2,1,0:T(8,128)(2,1)}) custom-call(bf16[256,1024]{1,0:T(8,128)(2,1)} %get-tuple-element.282.refs_0_, bf16[256,1024]{1,0:T(8,128)(2,1)} %copy-done.46, bf16[256,1024]{1,0:T(8,128)(2,1)} %copy-done.45, bf16[256,1024]{1,0:T(8,128)(2,1)} %copy-done.47, ...), custom_call_target="tpu_custom_call" | custom-call | flops 6000000000 | bytes 12943364 | tf_op jit(solution)/shard_map/mlp_sums/pallas_call | solution.py:53
  178.2 3.9 turn.1
  185.2 2.5 collective-permute-start.35
  192.5 9.6 %collective-permute-done.31.refs_2_ = bf16[256,1024]{1,0:T(8,128)(2,1)S(1)} collective-permute-done((bf16[256,1024]{1,0:T(8,128)(2,1)}, bf16[256,1024]{1,0:T(8,128)(2,1)S(1)}, u32[]{:S(2)}, u32[]{:S(2)}) %collective-permute-start.31) | collective-permute-done | bytes 524320 | tf_op jit(solution)/shard_map/ppermute | solution.py:651
  214.1 15.1 %attention_back.2 = (bf16[1,1024,384]{2,1,0:T(8,128)(2,1)}, bf16[8,512,128]{2,1,0:T(8,128)(2,1)}) custom-call(bf16[256,1024]{1,0:T(8,128)(2,1)} %get-tuple-element.349.refs_0_, bf16[256,1024]{1,0:T(8,128)(2,1)} %copy-done.42, bf16[256,1024]{1,0:T(8,128)(2,1)} %copy-done.41, bf16[256,1024]{1,0:T(8,128)(2,1)} %collective-permute-done.37.refs_3_, ...), custom_call_target="tpu_custom_call" | custom-call | flops 15000000512 | bytes 9764900 | tf_op jit(solution)/shard_map/attention_back/pallas_call | solution.py:53
  231.8 2.4 result.1
  239.1 6.1 %collective-permute-start.47 = (bf16[1,128,1024]{2,1,0:T(8,128)(2,1)S(1)}, bf16[1,128,1024]{2,1,0:T(8,128)(2,1)S(1)}, u32[]{:S(2)}, u32[]{:S(2)}) collective-permute-start(bf16[1,128,1024]{2,1,0:T(8,128)(2,1)S(1)} %copy-done.54), channel_id=1, source_target_pairs={{16,0},{26,1},{20,2},{30,3},{0,4},{10,5},{4,6},{14,7},{17,8},{27,9... | collective-permute-start | bytes 786440 | tf_op jit(solution)/shard_map/ppermute | solution.py:634
  245.2 15.5 %attention_back.3 = (bf16[1,1024,384]{2,1,0:T(8,128)(2,1)}, bf16[8,512,128]{2,1,0:T(8,128)(2,1)}) custom-call(bf16[256,1024]{1,0:T(8,128)(2,1)} %get-tuple-element.349.refs_0_, bf16[256,1024]{1,0:T(8,128)(2,1)} %copy-done.42, bf16[256,1024]{1,0:T(8,128)(2,1)} %copy-done.41, bf16[256,1024]{1,0:T(8,128)(2,1)} %collective-permute-done.37.refs_3_, ...), custom_call_target="tpu_custom_call" | custom-call | flops 15000000512 | bytes 9764900 | tf_op jit(solution)/shard_map/attention_back/pallas_call | solution.py:53
  260.9 5.9 %spread.1 = (bf16[256,1024]{1,0:T(8,128)(2,1)}, bf16[256,1024]{1,0:T(8,128)(2,1)}, bf16[256,1024]{1,0:T(8,128)(2,1)}, bf16[256,1024]{1,0:T(8,128)(2,1)}) custom-call(bf16[1,1024,384]{2,1,0:T(8,128)(2,1)} %get-tuple-element.365.refs_0_, bf16[1,1024,384]{2,1,0:T(8,128)(2,1)} %get-tuple-element.366.refs_1_, bf16[1024,768]{1,0:T(8,128)(2,1)} %get-tuple-element.367.refs_2_), custom_call_target="tpu_custom_call" | custom-call | flops 2000000000 | bytes 5242880 | tf_op jit(solution)/shard_map/spread/pallas_call | solution.py:53
  267.8 3.2 collective-permute-start.48
  274.1 3.5 all-to-all-start
  277.6 7.3 %all-to-all-done = bf16[4,2,32,656]{3,2,1,0:T(8,128)(2,1)S(1)} async-done(((bf16[4,2,32,656]{3,2,1,0:T(8,128)(2,1)}), bf16[4,2,32,656]{3,2,1,0:T(8,128)(2,1)S(1)}, u32[]{:S(2)}, u32[]{:S(2)}) %all-to-all-start) | async-done | bytes 335904 | tf_op jit(solution)/shard_map/all_to_all | solution.py:979
  291.5 6.9 %collective-permute-done.55 = bf16[1,4,32,656]{3,2,1,0:T(8,128)(2,1)S(1)} collective-permute-done((bf16[1,4,32,656]{3,2,1,0:T(8,128)(2,1)S(1)}, bf16[1,4,32,656]{3,2,1,0:T(8,128)(2,1)S(1)}, u32[]{:S(2)}, u32[]{:S(2)}) %collective-permute-start.55) | collective-permute-done | bytes 167968 | tf_op jit(solution)/shard_map/ppermute | solution.py:682
  298.3 5.5 %collective-permute-done.53 = bf16[1,512,128]{2,1,0:T(8,128)(2,1)S(1)} collective-permute-done((bf16[1,512,128]{2,1,0:T(8,128)(2,1)S(1)}, bf16[1,512,128]{2,1,0:T(8,128)(2,1)S(1)}, u32[]{:S(2)}, u32[]{:S(2)}) %collective-permute-start.53) | collective-permute-done | bytes 131104 | tf_op jit(solution)/shard_map/ppermute | solution.py:682
  304.5 2.6 collective-permute-start.57
  307.1 3.4 last.1
  312.1 4.0 collective-permute-start.62
  316.6 4.2 collective-permute-done.57
  321.6 12.9 %all-to-all-start.1 = ((bf16[2,4,96,128]{3,2,0,1:T(8,128)(2,1)}), bf16[2,4,96,128]{3,2,0,1:T(8,128)(2,1)S(1)}, u32[]{:S(2)}, u32[]{:S(2)}) async-start(bf16[2,4,96,128]{3,2,0,1:T(8,128)(2,1)} %copy.47), calls=%async_computation.1 | async-start | bytes 393216 | tf_op jit(solution)/shard_map/all_to_all | solution.py:1014
  334.6 2.9 collective-permute-start.60
  337.5 2.3 all-to-all-done.1
  341.9 10.9 %collective-permute-done.59 = bf16[1,32,5248]{2,1,0:T(8,128)(2,1)S(1)} collective-permute-done((bf16[1,32,5248]{2,1,0:T(8,128)(2,1)S(1)}, bf16[1,32,5248]{2,1,0:T(8,128)(2,1)S(1)}, u32[]{:S(2)}, u32[]{:S(2)}) %collective-permute-start.59) | collective-permute-done | bytes 335904 | tf_op jit(solution)/shard_map/ppermute | solution.py:682
  358.0 22.1 %collective-permute-done.63 = bf16[2,2,512,128]{3,2,1,0:T(8,128)(2,1)S(1)} collective-permute-done((bf16[2,2,512,128]{3,2,1,0:T(8,128)(2,1)S(1)}, bf16[2,2,512,128]{3,2,1,0:T(8,128)(2,1)S(1)}, u32[]{:S(2)}, u32[]{:S(2)}) %collective-permute-start.63) | collective-permute-done | bytes 524320 | tf_op jit(solution)/shard_map/ppermute | solution.py:682
  393.0 2.9 in_grad.2
  395.9 2.4 pad_maximum_fusion.stack
  398.3 5.5 %out_grad.1 = f32[656,1024]{1,0:T(8,128)} custom-call(bf16[8,4,32,656]{3,2,1,0:T(8,128)(2,1)} %pad_maximum_fusion.stack, s32[1]{0:T(128)} %bitcast.3.refs_11_.refs_14_.c_ref), custom_call_target="tpu_custom_call" | custom-call | flops 1000000 | bytes 4030468 | tf_op jit(solution)/shard_map/out_grad/pallas_call | solution.py:53
  403.8 8.4 %collective-permute-done.66.high = bf16[4,2,512,128]{3,2,1,0:T(8,128)(2,1)} collective-permute-done((bf16[4,2,512,128]{3,2,1,0:T(8,128)(2,1)}, bf16[4,2,512,128]{3,2,1,0:T(8,128)(2,1)}, u32[]{:S(2)}, u32[]{:S(2)}) %collective-permute-start.66) | collective-permute-done | bytes 1048608 | tf_op jit(solution)/shard_map/ppermute | solution.py:682
  412.2 5.7 %qkv_grad.1 = (f32[256,3072]{1,0:T(8,128)}, f32[256,1024]{1,0:T(8,128)}, f32[1,256]{1,0:T(1,128)}) custom-call(bf16[4,2,512,128]{3,2,1,0:T(8,128)(2,1)} %constant_dynamic-update-slice_fusion.8.low, bf16[4,2,512,128]{3,2,1,0:T(8,128)(2,1)} %collective-permute-done.66.high, bf16[256,3072]{1,0:T(8,128)(2,1)} %w.2, f32[256,1]{1,0:T(8,128)} %copy.41.gain, ...), custom_call_target="tpu_custom_call" | custom-call | flops 1000000 | bytes 7866372 | tf_op jit(solution)/shard_map/qkv_grad/pallas_call | solution.py:53
  417.8 2.9 in_grad.3
  (331 shorter events, 108.2 us)
Async XLA Ops:
  2.5 31.2 %collective-permute-start = (bf16[1,144,1024]{2,1,0:T(8,128)(2,1)S(1)}, bf16[1,144,1024]{2,1,0:T(8,128)(2,1)S(1)}, u32[]{:S(2)}, u32[]{:S(2)}) collective-permute-start(bf16[1,144,1024]{2,1,0:T(8,128)(2,1)S(1)} %get-tuple-element.218), channel_id=1, source_target_pairs={{0,0},{1,10},{2,4},{3,14},{4,16},{5,26},{6,20},{7,30},{8,1},{9,11}... | collective-permute-start | bytes 884744 | tf_op jit(solution)/shard_map/ppermute | solution.py:630
  3.2 30.6 %collective-permute-start.1 = (bf16[1,144,1024]{2,1,0:T(8,128)(2,1)S(1)}, bf16[1,144,1024]{2,1,0:T(8,128)(2,1)S(1)}, u32[]{:S(2)}, u32[]{:S(2)}) collective-permute-start(bf16[1,144,1024]{2,1,0:T(8,128)(2,1)S(1)} %get-tuple-element.219), channel_id=1, source_target_pairs={{0,16},{1,26},{2,20},{3,30},{4,0},{5,10},{6,4},{7,14},{8,17},{9,27... | collective-permute-start | bytes 884744 | tf_op jit(solution)/shard_map/ppermute | solution.py:630
  36.8 28.4 %collective-permute-start.6 = (bf16[272,1024]{1,0:T(8,128)(2,1)}, bf16[272,1024]{1,0:T(8,128)(2,1)S(1)}, u32[]{:S(2)}, u32[]{:S(2)}) collective-permute-start(bf16[272,1024]{1,0:T(8,128)(2,1)} %unit1.1.refs_0_), channel_id=1, source_target_pairs={{0,2},{1,3},{2,0},{3,1},{4,6},{5,7},{6,4},{7,5},{8,10},{9,11},{10,... | collective-permute-start | bytes 1671176 | tf_op jit(solution)/shard_map/ppermute | solution.py:651
  39.3 25.9 %collective-permute-start.9 = (bf16[1,128,1024]{2,1,0:T(8,128)(2,1)S(1)}, bf16[1,128,1024]{2,1,0:T(8,128)(2,1)S(1)}, u32[]{:S(2)}, u32[]{:S(2)}) collective-permute-start(bf16[1,128,1024]{2,1,0:T(8,128)(2,1)S(1)} %get-tuple-element.467), channel_id=1, source_target_pairs={{0,0},{1,10},{2,4},{3,14},{4,16},{5,26},{6,20},{7,30},{8,1},{9,11}... | collective-permute-start | bytes 786440 | tf_op jit(solution)/shard_map/ppermute | solution.py:630
  40.1 25.1 %collective-permute-start.10 = (bf16[1,128,1024]{2,1,0:T(8,128)(2,1)S(1)}, bf16[1,128,1024]{2,1,0:T(8,128)(2,1)S(1)}, u32[]{:S(2)}, u32[]{:S(2)}) collective-permute-start(bf16[1,128,1024]{2,1,0:T(8,128)(2,1)S(1)} %get-tuple-element.466), channel_id=1, source_target_pairs={{0,16},{1,26},{2,20},{3,30},{4,0},{5,10},{6,4},{7,14},{8,17},{9,27... | collective-permute-start | bytes 786440 | tf_op jit(solution)/shard_map/ppermute | solution.py:630
  45.6 16.5 %collective-permute-start.7 = (bf16[128,768]{1,0:T(8,128)(2,1)S(1)}, bf16[128,768]{1,0:T(8,128)(2,1)S(1)}, u32[]{:S(2)}, u32[]{:S(2)}) collective-permute-start(bf16[128,768]{1,0:T(8,128)(2,1)S(1)} %collective-permute-done.3.refs_6_), channel_id=1, source_target_pairs={{0,4},{4,0},{8,12},{12,8},{16,20},{20,16},{24,28},{28,24},{1,5},{5... | collective-permute-start | bytes 589832 | tf_op jit(solution)/shard_map/ppermute | solution.py:682
  45.7 19.5 %collective-permute-start.8 = (bf16[128,768]{1,0:T(8,128)(2,1)S(1)}, bf16[128,768]{1,0:T(8,128)(2,1)S(1)}, u32[]{:S(2)}, u32[]{:S(2)}) collective-permute-start(bf16[128,768]{1,0:T(8,128)(2,1)S(1)} %collective-permute-done.4.refs_7_), channel_id=1, source_target_pairs={{0,4},{4,0},{8,12},{12,8},{16,20},{20,16},{24,28},{28,24},{1,5},{5... | collective-permute-start | bytes 589832 | tf_op jit(solution)/shard_map/ppermute | solution.py:682
  68.1 30.0 %collective-permute-start.13 = (bf16[256,1024]{1,0:T(8,128)(2,1)S(1)}, bf16[256,1024]{1,0:T(8,128)(2,1)S(1)}, u32[]{:S(2)}, u32[]{:S(2)}) collective-permute-start(bf16[256,1024]{1,0:T(8,128)(2,1)S(1)} %bitcast.62), channel_id=1, source_target_pairs={{0,2},{1,3},{2,0},{3,1},{4,6},{5,7},{6,4},{7,5},{8,10},{9,11},{10,... | collective-permute-start | bytes 1572872 | tf_op jit(solution)/shard_map/ppermute | solution.py:651
  70.5 23.8 %collective-permute-start.14 = (bf16[256,768]{1,0:T(8,128)(2,1)S(1)}, bf16[256,768]{1,0:T(8,128)(2,1)S(1)}, u32[]{:S(2)}, u32[]{:S(2)}) collective-permute-start(bf16[256,768]{1,0:T(8,128)(2,1)S(1)} %get-tuple-element.438), channel_id=1, source_target_pairs={{0,1},{1,0},{2,3},{3,2},{4,5},{5,4},{6,7},{7,6},{8,9},{9,8},{10,11... | collective-permute-start | bytes 1179656 | tf_op jit(solution)/shard_map/ppermute | solution.py:733
  70.8 23.6 %collective-permute-start.15 = (bf16[256,768]{1,0:T(8,128)(2,1)S(1)}, bf16[256,768]{1,0:T(8,128)(2,1)S(1)}, u32[]{:S(2)}, u32[]{:S(2)}) collective-permute-start(bf16[256,768]{1,0:T(8,128)(2,1)S(1)} %get-tuple-element.437), channel_id=1, source_target_pairs={{0,2},{1,3},{2,0},{3,1},{4,6},{5,7},{6,4},{7,5},{8,10},{9,11},{10,... | collective-permute-start | bytes 1179656 | tf_op jit(solution)/shard_map/ppermute | solution.py:733
  72.5 25.6 %collective-permute-start.16 = (bf16[256,768]{1,0:T(8,128)(2,1)S(1)}, bf16[256,768]{1,0:T(8,128)(2,1)S(1)}, u32[]{:S(2)}, u32[]{:S(2)}) collective-permute-start(bf16[256,768]{1,0:T(8,128)(2,1)S(1)} %get-tuple-element.436), channel_id=1, source_target_pairs={{0,3},{1,2},{2,1},{3,0},{4,7},{5,6},{6,5},{7,4},{8,11},{9,10},{10,... | collective-permute-start | bytes 1179656 | tf_op jit(solution)/shard_map/ppermute | solution.py:733
  73.4 24.7 %collective-permute-start.17 = (bf16[256,768]{1,0:T(8,128)(2,1)S(1)}, bf16[256,768]{1,0:T(8,128)(2,1)S(1)}, u32[]{:S(2)}, u32[]{:S(2)}) collective-permute-start(bf16[256,768]{1,0:T(8,128)(2,1)S(1)} %get-tuple-element.450), channel_id=1, source_target_pairs={{0,1},{1,0},{2,3},{3,2},{4,5},{5,4},{6,7},{7,6},{8,9},{9,8},{10,11... | collective-permute-start | bytes 1179656 | tf_op jit(solution)/shard_map/ppermute | solution.py:651
  101.8 14.3 %collective-permute-start.20 = (bf16[256,1024]{1,0:T(8,128)(2,1)S(1)}, bf16[256,1024]{1,0:T(8,128)(2,1)S(1)}, u32[]{:S(2)}, u32[]{:S(2)}) collective-permute-start(bf16[256,1024]{1,0:T(8,128)(2,1)S(1)} %add_convert_fusion.9), channel_id=1, source_target_pairs={{0,2},{1,3},{2,0},{3,1},{4,6},{5,7},{6,4},{7,5},{8,10},{9,11},{10,... | collective-permute-start | bytes 1572872 | tf_op jit(solution)/shard_map/ppermute | solution.py:651
  102.2 20.1 %collective-permute-start.23 = (bf16[256,1024]{1,0:T(8,128)(2,1)S(1)}, bf16[256,1024]{1,0:T(8,128)(2,1)S(1)}, u32[]{:S(2)}, u32[]{:S(2)}) collective-permute-start(bf16[256,1024]{1,0:T(8,128)(2,1)S(1)} %bitcast.63), channel_id=1, source_target_pairs={{0,1},{1,0},{2,3},{3,2},{4,5},{5,4},{6,7},{7,6},{8,9},{9,8},{10,11... | collective-permute-start | bytes 1572872 | tf_op jit(solution)/shard_map/ppermute | solution.py:651
  102.3 20.0 %collective-permute-start.24 = (bf16[256,1024]{1,0:T(8,128)(2,1)S(1)}, bf16[256,1024]{1,0:T(8,128)(2,1)S(1)}, u32[]{:S(2)}, u32[]{:S(2)}) collective-permute-start(bf16[256,1024]{1,0:T(8,128)(2,1)S(1)} %collective-permute-done.13.refs_6_), channel_id=1, source_target_pairs={{0,1},{1,0},{2,3},{3,2},{4,5},{5,4},{6,7},{7,6},{8,9},{9,8},{10,11... | collective-permute-start | bytes 1572872 | tf_op jit(solution)/shard_map/ppermute | solution.py:651
  102.7 17.1 %collective-permute-start.21 = (bf16[256,768]{1,0:T(8,128)(2,1)S(1)}, bf16[256,768]{1,0:T(8,128)(2,1)S(1)}, u32[]{:S(2)}, u32[]{:S(2)}) collective-permute-start(bf16[256,768]{1,0:T(8,128)(2,1)S(1)} %collective-permute-done.15.refs_10_), channel_id=1, source_target_pairs={{0,4},{4,0},{8,12},{12,8},{16,20},{20,16},{24,28},{28,24},{1,5},{5... | collective-permute-start | bytes 1179656 | tf_op jit(solution)/shard_map/ppermute | solution.py:682
  102.7 19.5 %collective-permute-start.22 = (bf16[256,768]{1,0:T(8,128)(2,1)S(1)}, bf16[256,768]{1,0:T(8,128)(2,1)S(1)}, u32[]{:S(2)}, u32[]{:S(2)}) collective-permute-start(bf16[256,768]{1,0:T(8,128)(2,1)S(1)} %collective-permute-done.16.refs_11_), channel_id=1, source_target_pairs={{0,4},{4,0},{8,12},{12,8},{16,20},{20,16},{24,28},{28,24},{1,5},{5... | collective-permute-start | bytes 1179656 | tf_op jit(solution)/shard_map/ppermute | solution.py:682
  159.7 17.4 %collective-permute-start.28 = (bf16[256,1024]{1,0:T(8,128)(2,1)}, bf16[256,1024]{1,0:T(8,128)(2,1)S(1)}, u32[]{:S(2)}, u32[]{:S(2)}) collective-permute-start(bf16[256,1024]{1,0:T(8,128)(2,1)} %get-tuple-element.294), channel_id=1, source_target_pairs={{0,1},{1,0},{2,3},{3,2},{4,5},{5,4},{6,7},{7,6},{8,9},{9,8},{10,11... | collective-permute-start | bytes 1572872 | tf_op jit(solution)/shard_map/ppermute | solution.py:651
  162.2 15.0 %collective-permute-start.30 = (bf16[256,1024]{1,0:T(8,128)(2,1)S(1)}, bf16[256,1024]{1,0:T(8,128)(2,1)S(1)}, u32[]{:S(2)}, u32[]{:S(2)}) collective-permute-start(bf16[256,1024]{1,0:T(8,128)(2,1)S(1)} %add_convert_fusion.8), channel_id=1, source_target_pairs={{0,2},{1,3},{2,0},{3,1},{4,6},{5,7},{6,4},{7,5},{8,10},{9,11},{10,... | collective-permute-start | bytes 1572872 | tf_op jit(solution)/shard_map/ppermute | solution.py:651
  183.6 19.7 %collective-permute-start.34 = (bf16[4,4,32,656]{3,2,1,0:T(8,128)(2,1)}, bf16[4,4,32,656]{3,2,1,0:T(8,128)(2,1)S(1)}, u32[]{:S(2)}, u32[]{:S(2)}) collective-permute-start(bf16[4,4,32,656]{3,2,1,0:T(8,128)(2,1)} %get-tuple-element.434), channel_id=1, source_target_pairs={{0,4},{4,0},{8,12},{12,8},{16,20},{20,16},{24,28},{28,24},{1,5},{5... | collective-permute-start | bytes 2015240 | tf_op jit(solution)/shard_map/ppermute | solution.py:682
  185.2 20.1 %collective-permute-start.35 = (bf16[4,4,32,656]{3,2,1,0:T(8,128)(2,1)}, bf16[4,4,32,656]{3,2,1,0:T(8,128)(2,1)S(1)}, u32[]{:S(2)}, u32[]{:S(2)}) collective-permute-start(bf16[4,4,32,656]{3,2,1,0:T(8,128)(2,1)} %get-tuple-element.432), channel_id=1, source_target_pairs={{0,8},{4,12},{8,0},{12,4},{16,24},{20,28},{24,16},{28,20},{1,9},{5... | collective-permute-start | bytes 2015240 | tf_op jit(solution)/shard_map/ppermute | solution.py:682
  188.6 13.5 %collective-permute-start.31 = (bf16[256,1024]{1,0:T(8,128)(2,1)}, bf16[256,1024]{1,0:T(8,128)(2,1)S(1)}, u32[]{:S(2)}, u32[]{:S(2)}) collective-permute-start(bf16[256,1024]{1,0:T(8,128)(2,1)} %get-tuple-element.349.refs_0_), channel_id=1, source_target_pairs={{0,2},{1,3},{2,0},{3,1},{4,6},{5,7},{6,4},{7,5},{8,10},{9,11},{10,... | collective-permute-start | bytes 1572872 | tf_op jit(solution)/shard_map/ppermute | solution.py:651
  208.8 20.4 %collective-permute-start.38 = (bf16[2,4,32,656]{3,2,1,0:T(8,128)(2,1)S(1)}, bf16[2,4,32,656]{3,2,1,0:T(8,128)(2,1)S(1)}, u32[]{:S(2)}, u32[]{:S(2)}) collective-permute-start(bf16[2,4,32,656]{3,2,1,0:T(8,128)(2,1)S(1)} %get-tuple-element.448), channel_id=1, source_target_pairs={{0,8},{4,12},{8,0},{12,4},{16,24},{20,28},{24,16},{28,20},{1,9},{5... | collective-permute-start | bytes 1007624 | tf_op jit(solution)/shard_map/ppermute | solution.py:682
  210.7 20.3 %collective-permute-start.39 = (bf16[2,4,32,656]{3,2,1,0:T(8,128)(2,1)S(1)}, bf16[2,4,32,656]{3,2,1,0:T(8,128)(2,1)S(1)}, u32[]{:S(2)}, u32[]{:S(2)}) collective-permute-start(bf16[2,4,32,656]{3,2,1,0:T(8,128)(2,1)S(1)} %get-tuple-element.446), channel_id=1, source_target_pairs={{0,16},{4,20},{8,24},{12,28},{16,0},{20,4},{24,8},{28,12},{1,17},{... | collective-permute-start | bytes 1007624 | tf_op jit(solution)/shard_map/ppermute | solution.py:682
  211.0 20.1 %collective-permute-start.40 = (bf16[4,4,32,656]{3,2,1,0:T(8,128)(2,1)S(1)}, bf16[4,4,32,656]{3,2,1,0:T(8,128)(2,1)S(1)}, u32[]{:S(2)}, u32[]{:S(2)}) collective-permute-start(bf16[4,4,32,656]{3,2,1,0:T(8,128)(2,1)S(1)} %get-tuple-element.430), channel_id=1, source_target_pairs={{0,4},{4,0},{8,12},{12,8},{16,20},{20,16},{24,28},{28,24},{1,5},{5... | collective-permute-start | bytes 2015240 | tf_op jit(solution)/shard_map/ppermute | solution.py:682
  212.6 18.5 %collective-permute-start.41 = (bf16[256,1024]{1,0:T(8,128)(2,1)S(1)}, bf16[256,1024]{1,0:T(8,128)(2,1)S(1)}, u32[]{:S(2)}, u32[]{:S(2)}) collective-permute-start(bf16[256,1024]{1,0:T(8,128)(2,1)S(1)} %add_convert_fusion.6), channel_id=1, source_target_pairs={{0,2},{1,3},{2,0},{3,1},{4,6},{5,7},{6,4},{7,5},{8,10},{9,11},{10,... | collective-permute-start | bytes 1572872 | tf_op jit(solution)/shard_map/ppermute | solution.py:651
  234.3 32.5 %collective-permute-start.42 = (bf16[4,512,128]{2,1,0:T(8,128)(2,1)S(1)}, bf16[4,512,128]{2,1,0:T(8,128)(2,1)S(1)}, u32[]{:S(2)}, u32[]{:S(2)}) collective-permute-start(bf16[4,512,128]{2,1,0:T(8,128)(2,1)S(1)} %get-tuple-element.442), channel_id=1, source_target_pairs={{0,4},{4,0},{8,12},{12,8},{16,20},{20,16},{24,28},{28,24},{1,5},{5... | collective-permute-start | bytes 1572872 | tf_op jit(solution)/shard_map/ppermute | solution.py:682
  236.0 24.8 %collective-permute-start.43 = (bf16[1,4,32,656]{3,2,1,0:T(8,128)(2,1)S(1)}, bf16[1,4,32,656]{3,2,1,0:T(8,128)(2,1)S(1)}, u32[]{:S(2)}, u32[]{:S(2)}) collective-permute-start(bf16[1,4,32,656]{3,2,1,0:T(8,128)(2,1)S(1)} %get-tuple-element.472), channel_id=1, source_target_pairs={{0,16},{4,20},{8,24},{12,28},{16,0},{20,4},{24,8},{28,12},{1,17},{... | collective-permute-start | bytes 503816 | tf_op jit(solution)/shard_map/ppermute | solution.py:682
  237.5 29.4 %collective-permute-start.45 = (bf16[2,4,32,656]{3,2,1,0:T(8,128)(2,1)S(1)}, bf16[2,4,32,656]{3,2,1,0:T(8,128)(2,1)S(1)}, u32[]{:S(2)}, u32[]{:S(2)}) collective-permute-start(bf16[2,4,32,656]{3,2,1,0:T(8,128)(2,1)S(1)} %get-tuple-element.444), channel_id=1, source_target_pairs={{0,8},{4,12},{8,0},{12,4},{16,24},{20,28},{24,16},{28,20},{1,9},{5... | collective-permute-start | bytes 1007624 | tf_op jit(solution)/shard_map/ppermute | solution.py:682
  238.4 28.4 %collective-permute-start.46 = (bf16[1,128,1024]{2,1,0:T(8,128)(2,1)S(1)}, bf16[1,128,1024]{2,1,0:T(8,128)(2,1)S(1)}, u32[]{:S(2)}, u32[]{:S(2)}) collective-permute-start(bf16[1,128,1024]{2,1,0:T(8,128)(2,1)S(1)} %copy-done.55), channel_id=1, source_target_pairs={{0,0},{10,1},{4,2},{14,3},{16,4},{26,5},{20,6},{30,7},{1,8},{11,9}... | collective-permute-start | bytes 786440 | tf_op jit(solution)/shard_map/ppermute | solution.py:634
  239.1 27.8 %collective-permute-start.47 = (bf16[1,128,1024]{2,1,0:T(8,128)(2,1)S(1)}, bf16[1,128,1024]{2,1,0:T(8,128)(2,1)S(1)}, u32[]{:S(2)}, u32[]{:S(2)}) collective-permute-start(bf16[1,128,1024]{2,1,0:T(8,128)(2,1)S(1)} %copy-done.54), channel_id=1, source_target_pairs={{16,0},{26,1},{20,2},{30,3},{0,4},{10,5},{4,6},{14,7},{17,8},{27,9... | collective-permute-start | bytes 786440 | tf_op jit(solution)/shard_map/ppermute | solution.py:634
  267.8 17.8 %collective-permute-start.48 = (bf16[2,512,128]{2,1,0:T(8,128)(2,1)}, bf16[2,512,128]{2,1,0:T(8,128)(2,1)}, u32[]{:S(2)}, u32[]{:S(2)}) collective-permute-start(bf16[2,512,128]{2,1,0:T(8,128)(2,1)} %get-tuple-element.462), channel_id=1, source_target_pairs={{0,8},{4,12},{8,0},{12,4},{16,24},{20,28},{24,16},{28,20},{1,9},{5... | collective-permute-start | bytes 786440 | tf_op jit(solution)/shard_map/ppermute | solution.py:682
  271.1 14.6 %collective-permute-start.49 = (bf16[4,512,128]{2,1,0:T(8,128)(2,1)S(1)}, bf16[4,512,128]{2,1,0:T(8,128)(2,1)S(1)}, u32[]{:S(2)}, u32[]{:S(2)}) collective-permute-start(bf16[4,512,128]{2,1,0:T(8,128)(2,1)S(1)} %get-tuple-element.440), channel_id=1, source_target_pairs={{0,4},{4,0},{8,12},{12,8},{16,20},{20,16},{24,28},{28,24},{1,5},{5... | collective-permute-start | bytes 1572872 | tf_op jit(solution)/shard_map/ppermute | solution.py:682
  287.5 16.4 %collective-permute-start.50 = (bf16[256,1024]{1,0:T(8,128)(2,1)}, bf16[256,1024]{1,0:T(8,128)(2,1)S(1)}, u32[]{:S(2)}, u32[]{:S(2)}) collective-permute-start(bf16[256,1024]{1,0:T(8,128)(2,1)} %get-tuple-element.380), channel_id=1, source_target_pairs={{0,1},{1,0},{2,3},{3,2},{4,5},{5,4},{6,7},{7,6},{8,9},{9,8},{10,11... | collective-permute-start | bytes 1572872 | tf_op jit(solution)/shard_map/ppermute | solution.py:651
  287.9 16.0 %collective-permute-start.54 = (bf16[2,512,128]{2,1,0:T(8,128)(2,1)S(1)}, bf16[2,512,128]{2,1,0:T(8,128)(2,1)S(1)}, u32[]{:S(2)}, u32[]{:S(2)}) collective-permute-start(bf16[2,512,128]{2,1,0:T(8,128)(2,1)S(1)} %get-tuple-element.460), channel_id=1, source_target_pairs={{0,8},{4,12},{8,0},{12,4},{16,24},{20,28},{24,16},{28,20},{1,9},{5... | collective-permute-start | bytes 786440 | tf_op jit(solution)/shard_map/ppermute | solution.py:682
  288.9 15.0 %collective-permute-start.52 = (bf16[256,1024]{1,0:T(8,128)(2,1)S(1)}, bf16[256,1024]{1,0:T(8,128)(2,1)S(1)}, u32[]{:S(2)}, u32[]{:S(2)}) collective-permute-start(bf16[256,1024]{1,0:T(8,128)(2,1)S(1)} %add_convert_fusion.4), channel_id=1, source_target_pairs={{0,2},{1,3},{2,0},{3,1},{4,6},{5,7},{6,4},{7,5},{8,10},{9,11},{10,... | collective-permute-start | bytes 1572872 | tf_op jit(solution)/shard_map/ppermute | solution.py:651
  304.5 16.3 %collective-permute-start.57 = (bf16[1,4,32,656]{3,2,1,0:T(8,128)(2,1)S(1)}, bf16[1,4,32,656]{3,2,1,0:T(8,128)(2,1)S(1)}, u32[]{:S(2)}, u32[]{:S(2)}) collective-permute-start(bf16[1,4,32,656]{3,2,1,0:T(8,128)(2,1)S(1)} %add_convert_fusion.15), channel_id=1, source_target_pairs={{0,16},{4,20},{8,24},{12,28},{16,0},{20,4},{24,8},{28,12},{1,17},{... | collective-permute-start | bytes 503816 | tf_op jit(solution)/shard_map/ppermute | solution.py:682
  310.5 31.3 %collective-permute-start.61 = (bf16[1,128,1024]{2,1,0:T(8,128)(2,1)}, bf16[1,128,1024]{2,1,0:T(8,128)(2,1)S(1)}, u32[]{:S(2)}, u32[]{:S(2)}) collective-permute-start(bf16[1,128,1024]{2,1,0:T(8,128)(2,1)} %get-tuple-element.405), channel_id=1, source_target_pairs={{0,0},{10,1},{4,2},{14,3},{16,4},{26,5},{20,6},{30,7},{1,8},{11,9}... | collective-permute-start | bytes 786440 | tf_op jit(solution)/shard_map/ppermute | solution.py:634
  312.1 29.7 %collective-permute-start.62 = (bf16[1,128,1024]{2,1,0:T(8,128)(2,1)}, bf16[1,128,1024]{2,1,0:T(8,128)(2,1)S(1)}, u32[]{:S(2)}, u32[]{:S(2)}) collective-permute-start(bf16[1,128,1024]{2,1,0:T(8,128)(2,1)} %get-tuple-element.406), channel_id=1, source_target_pairs={{16,0},{26,1},{20,2},{30,3},{0,4},{10,5},{4,6},{14,7},{17,8},{27,9... | collective-permute-start | bytes 786440 | tf_op jit(solution)/shard_map/ppermute | solution.py:634
  321.6 18.2 %all-to-all-start.1 = ((bf16[2,4,96,128]{3,2,0,1:T(8,128)(2,1)}), bf16[2,4,96,128]{3,2,0,1:T(8,128)(2,1)S(1)}, u32[]{:S(2)}, u32[]{:S(2)}) async-start(bf16[2,4,96,128]{3,2,0,1:T(8,128)(2,1)} %copy.47), calls=%async_computation.1 | async-start | bytes 393216 | tf_op jit(solution)/shard_map/all_to_all | solution.py:1014
  334.5 18.2 %collective-permute-start.59 = (bf16[1,32,5248]{2,1,0:T(8,128)(2,1)S(1)}, bf16[1,32,5248]{2,1,0:T(8,128)(2,1)S(1)}, u32[]{:S(2)}, u32[]{:S(2)}) collective-permute-start(bf16[1,32,5248]{2,1,0:T(8,128)(2,1)S(1)} %reshape.139), channel_id=1, source_target_pairs={{0,16},{4,20},{8,24},{12,28},{16,0},{20,4},{24,8},{28,12},{1,17},{... | collective-permute-start | bytes 1007624 | tf_op jit(solution)/shard_map/ppermute | solution.py:682
  334.6 19.6 %collective-permute-start.60 = (bf16[2,4,32,656]{3,2,1,0:T(8,128)(2,1)S(1)}, bf16[2,4,32,656]{3,2,1,0:T(8,128)(2,1)S(1)}, u32[]{:S(2)}, u32[]{:S(2)}) collective-permute-start(bf16[2,4,32,656]{3,2,1,0:T(8,128)(2,1)S(1)} %constant_dynamic-update-slice_fusion), channel_id=1, source_target_pairs={{0,8},{4,12},{8,0},{12,4},{16,24},{20,28},{24,16},{28,20},{1,9},{5... | collective-permute-start | bytes 1007624 | tf_op jit(solution)/shard_map/ppermute | solution.py:682
  339.8 14.4 %collective-permute-start.58 = (bf16[1,2,512,128]{3,2,1,0:T(8,128)(2,1)S(1)}, bf16[1,2,512,128]{3,2,1,0:T(8,128)(2,1)S(1)}, u32[]{:S(2)}, u32[]{:S(2)}) collective-permute-start(bf16[1,2,512,128]{3,2,1,0:T(8,128)(2,1)S(1)} %fusion.6), channel_id=1, source_target_pairs={{0,4},{4,0},{8,12},{12,8},{16,20},{20,16},{24,28},{28,24},{1,5},{5... | collective-permute-start | bytes 786440 | tf_op jit(solution)/shard_map/ppermute | solution.py:682
  354.3 28.1 %collective-permute-start.64 = (bf16[2,32,5248]{2,1,0:T(8,128)(2,1)S(1)}, bf16[2,32,5248]{2,1,0:T(8,128)(2,1)S(1)}, u32[]{:S(2)}, u32[]{:S(2)}) collective-permute-start(bf16[2,32,5248]{2,1,0:T(8,128)(2,1)S(1)} %constant_dynamic-update-slice_fusion.4), channel_id=1, source_target_pairs={{0,8},{4,12},{8,0},{12,4},{16,24},{20,28},{24,16},{28,20},{1,9},{5... | collective-permute-start | bytes 2015240 | tf_op jit(solution)/shard_map/ppermute | solution.py:682
  354.5 28.8 %collective-permute-start.65 = (bf16[4,4,32,656]{3,2,1,0:T(8,128)(2,1)S(1)}, bf16[4,4,32,656]{3,2,1,0:T(8,128)(2,1)}, u32[]{:S(2)}, u32[]{:S(2)}) collective-permute-start(bf16[4,4,32,656]{3,2,1,0:T(8,128)(2,1)S(1)} %constant_dynamic-update-slice_fusion.6), channel_id=1, source_target_pairs={{0,4},{4,0},{8,12},{12,8},{16,20},{20,16},{24,28},{28,24},{1,5},{5... | collective-permute-start | bytes 2015240 | tf_op jit(solution)/shard_map/ppermute | solution.py:682
  355.9 24.3 %collective-permute-start.63 = (bf16[2,2,512,128]{3,2,1,0:T(8,128)(2,1)S(1)}, bf16[2,2,512,128]{3,2,1,0:T(8,128)(2,1)S(1)}, u32[]{:S(2)}, u32[]{:S(2)}) collective-permute-start(bf16[2,2,512,128]{3,2,1,0:T(8,128)(2,1)S(1)} %constant_dynamic-update-slice_fusion.2), channel_id=1, source_target_pairs={{0,16},{4,20},{8,24},{12,28},{16,0},{20,4},{24,8},{28,12},{1,17},{... | collective-permute-start | bytes 1572872 | tf_op jit(solution)/shard_map/ppermute | solution.py:682
  384.4 33.4 %collective-permute-start.67 = (bf16[4,32,5248]{2,1,0:T(8,128)(2,1)S(1)}, bf16[4,32,5248]{2,1,0:T(8,128)(2,1)S(1)}, u32[]{:S(2)}, u32[]{:S(2)}) collective-permute-start(bf16[4,32,5248]{2,1,0:T(8,128)(2,1)S(1)} %constant_dynamic-update-slice_fusion.10.sums), channel_id=1, source_target_pairs={{0,4},{4,0},{8,12},{12,8},{16,20},{20,16},{24,28},{28,24},{1,5},{5... | collective-permute-start | bytes 4030472 | tf_op jit(solution)/shard_map/ppermute | solution.py:682
  388.2 23.9 %collective-permute-start.66 = (bf16[4,2,512,128]{3,2,1,0:T(8,128)(2,1)}, bf16[4,2,512,128]{3,2,1,0:T(8,128)(2,1)}, u32[]{:S(2)}, u32[]{:S(2)}) collective-permute-start(bf16[4,2,512,128]{3,2,1,0:T(8,128)(2,1)} %constant_dynamic-update-slice_fusion.8.low), channel_id=1, source_target_pairs={{0,8},{4,12},{8,0},{12,4},{16,24},{20,28},{24,16},{28,20},{1,9},{5... | collective-permute-start | bytes 3145736 | tf_op jit(solution)/shard_map/ppermute | solution.py:682
  (86 other events, 716.6 us)

commit v5 on v4

--- a/solution.py
+++ b/solution.py
@@ -946,10 +946,9 @@
                 1e6,
             )
             low_slots, result_parts = meet(low_slots, result_parts)
-            out_back = undeal(result_parts)
         else:
-            sums, pairs, act_pair, gate_pair, down_pair, out_back = meet(
-                sums, pairs, act_pair, gate_pair, down_pair, out_back
+            sums, pairs, act_pair, gate_pair, down_pair = meet(
+                sums, pairs, act_pair, gate_pair, down_pair
             )
             pairs = pairs + [send(sums, order[0])]
 
@@ -998,7 +997,8 @@
     sums = add(late)
     late = send(sums, step_of(sums))
     down = grow(add(down_pair), back_order[0])
-    late, down, in_small = meet(late, down, in_small)
+    late, down, in_small, result_parts = meet(late, down, in_small, result_parts)
+    out_back = undeal(result_parts)
 
     def finished(pair):
         sums = add(pair)

time: 430 us -> 424 us (0.986)
  waiting for transfers between devices: 138 us -> 132 us
  Pallas kernels: 135 us -> 140 us
  starting transfers between devices: 100 us -> 95.1 us
    ppermute x28, waiting for transfers between devices: 81 us -> 74.1 us  [away(): return lax.ppermute(values, 'ctx', [(i, i ^ bit) for i in range(ctx)])]
    pallas_call x17, Pallas kernels: 130 us -> 135 us  [call(): pl.pallas_call(kernel, grid=(grid,), in_specs=specs, out_specs=outs, out_...]
    ppermute x28, starting transfers between devices: 37.3 us -> 32.7 us  [away(): return lax.ppermute(values, 'ctx', [(i, i ^ bit) for i in range(ctx)])]
    unnamed x134 -> x124, local copies, waits for them, and re-layouts: 9.3 us -> 9.54 us
  transfers between devices with their start and end apart: 70 -> 70, of which waited for: 29 -> 28; matrix products, arithmetic and copies ran while one was open for 8% -> 9% of each run, Pallas kernels for 25% -> 26%
where the time goes in v5:
time: 424 us; the launch traced here: 417 us
  Pallas kernels  140 us (33%)
  waiting for transfers between devices  132 us (31%)
  starting transfers between devices  95.1 us (22%)
  local copies, waits for them, and re-layouts  26.4 us (6%)
  other arithmetic  21.4 us (5%)
    pallas_call x17, Pallas kernels, call(): pl.pallas_call(kernel, grid=(grid,), in_specs=specs, out_specs=outs, out_...  135 us
    ppermute x28, waiting for transfers between devices, away(): return lax.ppermute(values, 'ctx', [(i, i ^ bit) for i in range(ctx)])  74.1 us
    ppermute x26, waiting for transfers between devices, partner(): return lax.ppermute(values, 'fsdp', [(i, i ^ bit) for i in range(fsdp)])  37 us
    ppermute x28, starting transfers between devices, away(): return lax.ppermute(values, 'ctx', [(i, i ^ bit) for i in range(ctx)])  32.7 us
    ppermute x4, starting transfers between devices, deal(): return [lax.ppermute(part, both, route(j)) for j, part in enumerate(parts)]  15.5 us
    ppermute x26, starting transfers between devices, partner(): return lax.ppermute(values, 'fsdp', [(i, i ^ bit) for i in range(fsdp)])  13.7 us
    all_to_all x1, starting transfers between devices, on_device(): mine = lax.all_to_all(mine, 'fsdp', 1, 1, tiled=True)  12.8 us
    ppermute x4, starting transfers between devices, undeal(): lax.ppermute(part, both, [(b, a) for a, b in route(j)])  12.3 us
  transfers between devices with their start and end apart: 70, of which 28 were waited for; matrix products, arithmetic and copies ran while one was open for 9% of the time, Pallas kernels for 26%

profile of v5, /device:TPU:0, one launch (start us, length us, event | category | flops | bytes accessed | tf_op | source)
XLA Modules:
  0.0 417.2 jit_solution(6072674231782562939)
XLA Ops:
  3.2 8.5 %collective-permute-start.1 = (bf16[1,144,1024]{2,1,0:T(8,128)(2,1)S(1)}, bf16[1,144,1024]{2,1,0:T(8,128)(2,1)S(1)}, u32[]{:S(2)}, u32[]{:S(2)}) collective-permute-start(bf16[1,144,1024]{2,1,0:T(8,128)(2,1)S(1)} %get-tuple-element.219), channel_id=1, source_target_pairs={{0,16},{1,26},{2,20},{3,30},{4,0},{5,10},{6,4},{7,14},{8,17},{9,27... | collective-permute-start | bytes 884744 | tf_op jit(solution)/shard_map/ppermute | solution.py:630
  13.1 3.9 cut.1
  27.2 2.3 collective-permute-done.3.refs_6_
  29.5 4.2 %collective-permute-done.4.refs_7_ = bf16[128,768]{1,0:T(8,128)(2,1)S(1)} collective-permute-done((bf16[128,768]{1,0:T(8,128)(2,1)S(1)}, bf16[128,768]{1,0:T(8,128)(2,1)S(1)}, u32[]{:S(2)}, u32[]{:S(2)}) %collective-permute-start.4) | collective-permute-done | bytes 196640 | tf_op jit(solution)/shard_map/ppermute | solution.py:733
  36.8 2.4 collective-permute-start.6
  40.1 5.5 %collective-permute-start.10 = (bf16[1,128,1024]{2,1,0:T(8,128)(2,1)S(1)}, bf16[1,128,1024]{2,1,0:T(8,128)(2,1)S(1)}, u32[]{:S(2)}, u32[]{:S(2)}) collective-permute-start(bf16[1,128,1024]{2,1,0:T(8,128)(2,1)S(1)} %get-tuple-element.466), channel_id=1, source_target_pairs={{0,16},{1,26},{2,20},{3,30},{4,0},{5,10},{6,4},{7,14},{8,17},{9,27... | collective-permute-start | bytes 786440 | tf_op jit(solution)/shard_map/ppermute | solution.py:630
  48.5 5.2 %cut_in.1 = (bf16[4,256,768]{2,1,0:T(8,128)(2,1)}, bf16[2,256,768]{2,1,0:T(8,128)(2,1)}) custom-call(bf16[256,5248]{1,0:T(8,128)(2,1)} %w.4, f32[256,1]{1,0:T(8,128)} %copy.43.gain, s32[2]{0:T(128)} %pad_add_fusion.at_ref.refs_14_.refs_17_), custom_call_target="tpu_custom_call" | custom-call | flops 1000000 | bytes 5047304 | tf_op jit(solution)/shard_map/cut_in/pallas_call | solution.py:53
  53.7 8.3 %collective-permute-done.7.refs_10_ = bf16[128,768]{1,0:T(8,128)(2,1)S(1)} collective-permute-done((bf16[128,768]{1,0:T(8,128)(2,1)S(1)}, bf16[128,768]{1,0:T(8,128)(2,1)S(1)}, u32[]{:S(2)}, u32[]{:S(2)}) %collective-permute-start.7) | collective-permute-done | bytes 196640 | tf_op jit(solution)/shard_map/ppermute | solution.py:682
  62.0 3.2 collective-permute-done.8.refs_11_
  68.0 2.4 slice_bitcast_fusion.2
  73.7 7.9 %project.1 = (bf16[1,1024,256]{2,1,0:T(8,128)(2,1)}, bf16[1,1024,256]{2,1,0:T(8,128)(2,1)}, bf16[1,1024,256]{2,1,0:T(8,128)(2,1)}, f32[1,8,1024]{2,1,0:T(8,128)}, bf16[1024,768]{1,0:T(8,128)(2,1)}) custom-call(bf16[272,1024]{1,0:T(8,128)(2,1)} %unit1.1.refs_0_, bf16[272,1024]{1,0:T(8,128)(2,1)} %copy-done.16, bf16[272,1024]{1,0:T(8,128)(2,1)} %copy-done.15, ...), custom_call_target="tpu_custom_call" | custom-call | flops 4000000000 | bytes 8028168 | tf_op jit(solution)/shard_map/project/pallas_call | solution.py:53
  81.7 12.7 %attend.1 = (bf16[256,1024]{1,0:T(8,128)(2,1)}, bf16[256,1024]{1,0:T(8,128)(2,1)}, bf16[256,1024]{1,0:T(8,128)(2,1)}, bf16[256,1024]{1,0:T(8,128)(2,1)}, bf16[1,...) custom-call(bf16[1,1024,256]{2,1,0:T(8,128)(2,1)} %get-tuple-element.252.q_ref.refs_6_, ...), custom_call_target="tpu_custom_call" | custom-call | flops 12000000000 | bytes 4784128 | tf_op jit(solution)/shard_map/attend/pallas_call | solution.py:53
  94.4 3.7 collective-permute-done.16.refs_11_
  104.7 3.8 flip.1.refs_4_
  108.5 7.5 %collective-permute-done.20.refs_4_ = bf16[256,1024]{1,0:T(8,128)(2,1)S(1)} collective-permute-done((bf16[256,1024]{1,0:T(8,128)(2,1)S(1)}, bf16[256,1024]{1,0:T(8,128)(2,1)S(1)}, u32[]{:S(2)}, u32[]{:S(2)}) %collective-permute-start.20) | collective-permute-done | bytes 524320 | tf_op jit(solution)/shard_map/ppermute | solution.py:651
  116.8 3.0 middle.1
  119.8 2.5 collective-permute-done.22.refs_15_
  124.0 11.7 %collective-permute-done.26.refs_2_ = bf16[256,1024]{1,0:T(8,128)(2,1)S(1)} collective-permute-done((bf16[256,1024]{1,0:T(8,128)(2,1)}, bf16[256,1024]{1,0:T(8,128)(2,1)S(1)}, u32[]{:S(2)}, u32[]{:S(2)}) %collective-permute-start.26) | collective-permute-done | bytes 524320 | tf_op jit(solution)/shard_map/ppermute | solution.py:651
  138.4 20.3 %mlp.1 = (bf16[256,1024]{1,0:T(8,128)(2,1)}, bf16[256,1024]{1,0:T(8,128)(2,1)}, bf16[256,1024]{1,0:T(8,128)(2,1)}, bf16[256,1024]{1,0:T(8,128)(2,1)}, bf16[256,1...) custom-call(bf16[256,1024]{1,0:T(8,128)(2,1)} %get-tuple-element.282, ...), custom_call_target="tpu_custom_call" | custom-call | flops 12000000000 | bytes 17596424 | tf_op jit(solution)/shard_map/mlp/pallas_call | solution.py:53
  163.8 13.3 %mlp_sums.1 = (bf16[8,4,32,656]{3,2,1,0:T(8,128)(2,1)}, bf16[8,4,32,656]{3,2,1,0:T(8,128)(2,1)}, bf16[8,4,32,656]{3,2,1,0:T(8,128)(2,1)}) custom-call(bf16[256,1024]{1,0:T(8,128)(2,1)} %get-tuple-element.282.refs_0_, bf16[256,1024]{1,0:T(8,128)(2,1)} %copy-done.43, bf16[256,1024]{1,0:T(8,128)(2,1)} %copy-done.42, bf16[256,1024]{1,0:T(8,128)(2,1)} %copy-done.44, ...), custom_call_target="tpu_custom_call" | custom-call | flops 6000000000 | bytes 12943364 | tf_op jit(solution)/shard_map/mlp_sums/pallas_call | solution.py:53
  178.2 3.9 turn.1
  185.2 2.5 collective-permute-start.35
  192.5 9.6 %collective-permute-done.31.refs_2_ = bf16[256,1024]{1,0:T(8,128)(2,1)S(1)} collective-permute-done((bf16[256,1024]{1,0:T(8,128)(2,1)}, bf16[256,1024]{1,0:T(8,128)(2,1)S(1)}, u32[]{:S(2)}, u32[]{:S(2)}) %collective-permute-start.31) | collective-permute-done | bytes 524320 | tf_op jit(solution)/shard_map/ppermute | solution.py:651
  214.0 17.7 %attention_back.2 = (bf16[1,1024,384]{2,1,0:T(8,128)(2,1)}, bf16[8,512,128]{2,1,0:T(8,128)(2,1)}) custom-call(bf16[256,1024]{1,0:T(8,128)(2,1)} %get-tuple-element.350.refs_0_, bf16[256,1024]{1,0:T(8,128)(2,1)} %copy-done.38, bf16[256,1024]{1,0:T(8,128)(2,1)} %copy-done.37, bf16[256,1024]{1,0:T(8,128)(2,1)} %copy-done.39, ...), custom_call_target="tpu_custom_call" | custom-call | flops 15000000512 | bytes 9764900 | tf_op jit(solution)/shard_map/attention_back/pallas_call | solution.py:53
  232.5 2.4 result.1
  239.9 17.7 %attention_back.3 = (bf16[1,1024,384]{2,1,0:T(8,128)(2,1)}, bf16[8,512,128]{2,1,0:T(8,128)(2,1)}) custom-call(bf16[256,1024]{1,0:T(8,128)(2,1)} %get-tuple-element.350.refs_0_, bf16[256,1024]{1,0:T(8,128)(2,1)} %copy-done.38, bf16[256,1024]{1,0:T(8,128)(2,1)} %copy-done.37, bf16[256,1024]{1,0:T(8,128)(2,1)} %copy-done.39, ...), custom_call_target="tpu_custom_call" | custom-call | flops 15000000512 | bytes 9764900 | tf_op jit(solution)/shard_map/attention_back/pallas_call | solution.py:53
  257.6 6.1 %spread.1 = (bf16[256,1024]{1,0:T(8,128)(2,1)}, bf16[256,1024]{1,0:T(8,128)(2,1)}, bf16[256,1024]{1,0:T(8,128)(2,1)}, bf16[256,1024]{1,0:T(8,128)(2,1)}) custom-call(bf16[1,1024,384]{2,1,0:T(8,128)(2,1)} %get-tuple-element.336.refs_0_, bf16[1,1024,384]{2,1,0:T(8,128)(2,1)} %get-tuple-element.354.refs_1_, bf16[1024,768]{1,0:T(8,128)(2,1)} %get-tuple-element.355.refs_2_), custom_call_target="tpu_custom_call" | custom-call | flops 2000000000 | bytes 5242880 | tf_op jit(solution)/shard_map/spread/pallas_call | solution.py:53
  267.5 3.5 all-to-all-start
  271.1 7.3 %all-to-all-done = bf16[4,2,32,656]{3,2,1,0:T(8,128)(2,1)S(1)} async-done(((bf16[4,2,32,656]{3,2,1,0:T(8,128)(2,1)}), bf16[4,2,32,656]{3,2,1,0:T(8,128)(2,1)S(1)}, u32[]{:S(2)}, u32[]{:S(2)}) %all-to-all-start) | async-done | bytes 335904 | tf_op jit(solution)/shard_map/all_to_all | solution.py:978
  284.8 6.9 %collective-permute-done.53 = bf16[1,4,32,656]{3,2,1,0:T(8,128)(2,1)S(1)} collective-permute-done((bf16[1,4,32,656]{3,2,1,0:T(8,128)(2,1)S(1)}, bf16[1,4,32,656]{3,2,1,0:T(8,128)(2,1)S(1)}, u32[]{:S(2)}, u32[]{:S(2)}) %collective-permute-start.53) | collective-permute-done | bytes 167968 | tf_op jit(solution)/shard_map/ppermute | solution.py:682
  291.7 5.5 %collective-permute-done.51 = bf16[1,512,128]{2,1,0:T(8,128)(2,1)S(1)} collective-permute-done((bf16[1,512,128]{2,1,0:T(8,128)(2,1)S(1)}, bf16[1,512,128]{2,1,0:T(8,128)(2,1)S(1)}, u32[]{:S(2)}, u32[]{:S(2)}) %collective-permute-start.51) | collective-permute-done | bytes 131104 | tf_op jit(solution)/shard_map/ppermute | solution.py:682
  297.5 2.9 collective-permute-start.55
  300.4 3.4 last.1
  305.4 4.0 collective-permute-start.62
  309.5 4.1 collective-permute-done.55
  314.4 12.8 %all-to-all-start.1 = ((bf16[2,4,96,128]{3,2,0,1:T(8,128)(2,1)}), bf16[2,4,96,128]{3,2,0,1:T(8,128)(2,1)S(1)}, u32[]{:S(2)}, u32[]{:S(2)}) async-start(bf16[2,4,96,128]{3,2,0,1:T(8,128)(2,1)} %copy.47), calls=%async_computation.1 | async-start | bytes 393216 | tf_op jit(solution)/shard_map/all_to_all | solution.py:1014
  329.4 3.1 all-to-all-done.1
  333.5 11.1 %collective-permute-done.59 = bf16[1,32,5248]{2,1,0:T(8,128)(2,1)S(1)} collective-permute-done((bf16[1,32,5248]{2,1,0:T(8,128)(2,1)S(1)}, bf16[1,32,5248]{2,1,0:T(8,128)(2,1)S(1)}, u32[]{:S(2)}, u32[]{:S(2)}) %collective-permute-start.59) | collective-permute-done | bytes 335904 | tf_op jit(solution)/shard_map/ppermute | solution.py:682
  347.5 2.7 collective-permute-start.63
  350.2 3.0 collective-permute-start.56
  353.3 3.6 collective-permute-start.57
  356.9 16.2 %collective-permute-done.63 = bf16[2,2,512,128]{3,2,1,0:T(8,128)(2,1)S(1)} collective-permute-done((bf16[2,2,512,128]{3,2,1,0:T(8,128)(2,1)S(1)}, bf16[2,2,512,128]{3,2,1,0:T(8,128)(2,1)S(1)}, u32[]{:S(2)}, u32[]{:S(2)}) %collective-permute-start.63) | collective-permute-done | bytes 524320 | tf_op jit(solution)/shard_map/ppermute | solution.py:682
  385.3 2.9 in_grad.2
  388.2 2.4 pad_maximum_fusion.stack
  390.6 5.5 %out_grad.1 = f32[656,1024]{1,0:T(8,128)} custom-call(bf16[8,4,32,656]{3,2,1,0:T(8,128)(2,1)} %pad_maximum_fusion.stack, s32[1]{0:T(128)} %bitcast.3.refs_11_.refs_14_.c_ref), custom_call_target="tpu_custom_call" | custom-call | flops 1000000 | bytes 4030468 | tf_op jit(solution)/shard_map/out_grad/pallas_call | solution.py:53
  396.2 10.3 %collective-permute-done.66.high = bf16[4,2,512,128]{3,2,1,0:T(8,128)(2,1)} collective-permute-done((bf16[4,2,512,128]{3,2,1,0:T(8,128)(2,1)}, bf16[4,2,512,128]{3,2,1,0:T(8,128)(2,1)}, u32[]{:S(2)}, u32[]{:S(2)}) %collective-permute-start.66) | collective-permute-done | bytes 1048608 | tf_op jit(solution)/shard_map/ppermute | solution.py:682
  406.4 5.7 %qkv_grad.1 = (f32[256,3072]{1,0:T(8,128)}, f32[256,1024]{1,0:T(8,128)}, f32[1,256]{1,0:T(1,128)}) custom-call(bf16[4,2,512,128]{3,2,1,0:T(8,128)(2,1)} %constant_dynamic-update-slice_fusion.8.low, bf16[4,2,512,128]{3,2,1,0:T(8,128)(2,1)} %collective-permute-done.66.high, bf16[256,3072]{1,0:T(8,128)(2,1)} %w.2, f32[256,1]{1,0:T(8,128)} %copy.41.gain, ...), custom_call_target="tpu_custom_call" | custom-call | flops 1000000 | bytes 7866372 | tf_op jit(solution)/shard_map/qkv_grad/pallas_call | solution.py:53
  412.1 2.9 in_grad.3
  (321 shorter events, 103.2 us)
Async XLA Ops:
  2.5 31.2 %collective-permute-start = (bf16[1,144,1024]{2,1,0:T(8,128)(2,1)S(1)}, bf16[1,144,1024]{2,1,0:T(8,128)(2,1)S(1)}, u32[]{:S(2)}, u32[]{:S(2)}) collective-permute-start(bf16[1,144,1024]{2,1,0:T(8,128)(2,1)S(1)} %get-tuple-element.218), channel_id=1, source_target_pairs={{0,0},{1,10},{2,4},{3,14},{4,16},{5,26},{6,20},{7,30},{8,1},{9,11}... | collective-permute-start | bytes 884744 | tf_op jit(solution)/shard_map/ppermute | solution.py:630
  3.2 30.6 %collective-permute-start.1 = (bf16[1,144,1024]{2,1,0:T(8,128)(2,1)S(1)}, bf16[1,144,1024]{2,1,0:T(8,128)(2,1)S(1)}, u32[]{:S(2)}, u32[]{:S(2)}) collective-permute-start(bf16[1,144,1024]{2,1,0:T(8,128)(2,1)S(1)} %get-tuple-element.219), channel_id=1, source_target_pairs={{0,16},{1,26},{2,20},{3,30},{4,0},{5,10},{6,4},{7,14},{8,17},{9,27... | collective-permute-start | bytes 884744 | tf_op jit(solution)/shard_map/ppermute | solution.py:630
  36.8 28.4 %collective-permute-start.6 = (bf16[272,1024]{1,0:T(8,128)(2,1)}, bf16[272,1024]{1,0:T(8,128)(2,1)S(1)}, u32[]{:S(2)}, u32[]{:S(2)}) collective-permute-start(bf16[272,1024]{1,0:T(8,128)(2,1)} %unit1.1.refs_0_), channel_id=1, source_target_pairs={{0,2},{1,3},{2,0},{3,1},{4,6},{5,7},{6,4},{7,5},{8,10},{9,11},{10,... | collective-permute-start | bytes 1671176 | tf_op jit(solution)/shard_map/ppermute | solution.py:651
  39.2 25.9 %collective-permute-start.9 = (bf16[1,128,1024]{2,1,0:T(8,128)(2,1)S(1)}, bf16[1,128,1024]{2,1,0:T(8,128)(2,1)S(1)}, u32[]{:S(2)}, u32[]{:S(2)}) collective-permute-start(bf16[1,128,1024]{2,1,0:T(8,128)(2,1)S(1)} %get-tuple-element.467), channel_id=1, source_target_pairs={{0,0},{1,10},{2,4},{3,14},{4,16},{5,26},{6,20},{7,30},{8,1},{9,11}... | collective-permute-start | bytes 786440 | tf_op jit(solution)/shard_map/ppermute | solution.py:630
  40.1 25.1 %collective-permute-start.10 = (bf16[1,128,1024]{2,1,0:T(8,128)(2,1)S(1)}, bf16[1,128,1024]{2,1,0:T(8,128)(2,1)S(1)}, u32[]{:S(2)}, u32[]{:S(2)}) collective-permute-start(bf16[1,128,1024]{2,1,0:T(8,128)(2,1)S(1)} %get-tuple-element.466), channel_id=1, source_target_pairs={{0,16},{1,26},{2,20},{3,30},{4,0},{5,10},{6,4},{7,14},{8,17},{9,27... | collective-permute-start | bytes 786440 | tf_op jit(solution)/shard_map/ppermute | solution.py:630
  45.6 16.5 %collective-permute-start.7 = (bf16[128,768]{1,0:T(8,128)(2,1)S(1)}, bf16[128,768]{1,0:T(8,128)(2,1)S(1)}, u32[]{:S(2)}, u32[]{:S(2)}) collective-permute-start(bf16[128,768]{1,0:T(8,128)(2,1)S(1)} %collective-permute-done.3.refs_6_), channel_id=1, source_target_pairs={{0,4},{4,0},{8,12},{12,8},{16,20},{20,16},{24,28},{28,24},{1,5},{5... | collective-permute-start | bytes 589832 | tf_op jit(solution)/shard_map/ppermute | solution.py:682
  45.7 19.5 %collective-permute-start.8 = (bf16[128,768]{1,0:T(8,128)(2,1)S(1)}, bf16[128,768]{1,0:T(8,128)(2,1)S(1)}, u32[]{:S(2)}, u32[]{:S(2)}) collective-permute-start(bf16[128,768]{1,0:T(8,128)(2,1)S(1)} %collective-permute-done.4.refs_7_), channel_id=1, source_target_pairs={{0,4},{4,0},{8,12},{12,8},{16,20},{20,16},{24,28},{28,24},{1,5},{5... | collective-permute-start | bytes 589832 | tf_op jit(solution)/shard_map/ppermute | solution.py:682
  68.0 30.0 %collective-permute-start.13 = (bf16[256,1024]{1,0:T(8,128)(2,1)S(1)}, bf16[256,1024]{1,0:T(8,128)(2,1)S(1)}, u32[]{:S(2)}, u32[]{:S(2)}) collective-permute-start(bf16[256,1024]{1,0:T(8,128)(2,1)S(1)} %bitcast.62), channel_id=1, source_target_pairs={{0,2},{1,3},{2,0},{3,1},{4,6},{5,7},{6,4},{7,5},{8,10},{9,11},{10,... | collective-permute-start | bytes 1572872 | tf_op jit(solution)/shard_map/ppermute | solution.py:651
  70.5 23.8 %collective-permute-start.14 = (bf16[256,768]{1,0:T(8,128)(2,1)S(1)}, bf16[256,768]{1,0:T(8,128)(2,1)S(1)}, u32[]{:S(2)}, u32[]{:S(2)}) collective-permute-start(bf16[256,768]{1,0:T(8,128)(2,1)S(1)} %get-tuple-element.438), channel_id=1, source_target_pairs={{0,1},{1,0},{2,3},{3,2},{4,5},{5,4},{6,7},{7,6},{8,9},{9,8},{10,11... | collective-permute-start | bytes 1179656 | tf_op jit(solution)/shard_map/ppermute | solution.py:733
  70.7 23.6 %collective-permute-start.15 = (bf16[256,768]{1,0:T(8,128)(2,1)S(1)}, bf16[256,768]{1,0:T(8,128)(2,1)S(1)}, u32[]{:S(2)}, u32[]{:S(2)}) collective-permute-start(bf16[256,768]{1,0:T(8,128)(2,1)S(1)} %get-tuple-element.437), channel_id=1, source_target_pairs={{0,2},{1,3},{2,0},{3,1},{4,6},{5,7},{6,4},{7,5},{8,10},{9,11},{10,... | collective-permute-start | bytes 1179656 | tf_op jit(solution)/shard_map/ppermute | solution.py:733
  72.5 25.6 %collective-permute-start.16 = (bf16[256,768]{1,0:T(8,128)(2,1)S(1)}, bf16[256,768]{1,0:T(8,128)(2,1)S(1)}, u32[]{:S(2)}, u32[]{:S(2)}) collective-permute-start(bf16[256,768]{1,0:T(8,128)(2,1)S(1)} %get-tuple-element.436), channel_id=1, source_target_pairs={{0,3},{1,2},{2,1},{3,0},{4,7},{5,6},{6,5},{7,4},{8,11},{9,10},{10,... | collective-permute-start | bytes 1179656 | tf_op jit(solution)/shard_map/ppermute | solution.py:733
  73.3 24.7 %collective-permute-start.17 = (bf16[256,768]{1,0:T(8,128)(2,1)S(1)}, bf16[256,768]{1,0:T(8,128)(2,1)S(1)}, u32[]{:S(2)}, u32[]{:S(2)}) collective-permute-start(bf16[256,768]{1,0:T(8,128)(2,1)S(1)} %get-tuple-element.450), channel_id=1, source_target_pairs={{0,1},{1,0},{2,3},{3,2},{4,5},{5,4},{6,7},{7,6},{8,9},{9,8},{10,11... | collective-permute-start | bytes 1179656 | tf_op jit(solution)/shard_map/ppermute | solution.py:651
  101.8 14.3 %collective-permute-start.20 = (bf16[256,1024]{1,0:T(8,128)(2,1)S(1)}, bf16[256,1024]{1,0:T(8,128)(2,1)S(1)}, u32[]{:S(2)}, u32[]{:S(2)}) collective-permute-start(bf16[256,1024]{1,0:T(8,128)(2,1)S(1)} %add_convert_fusion.9), channel_id=1, source_target_pairs={{0,2},{1,3},{2,0},{3,1},{4,6},{5,7},{6,4},{7,5},{8,10},{9,11},{10,... | collective-permute-start | bytes 1572872 | tf_op jit(solution)/shard_map/ppermute | solution.py:651
  102.2 20.1 %collective-permute-start.23 = (bf16[256,1024]{1,0:T(8,128)(2,1)S(1)}, bf16[256,1024]{1,0:T(8,128)(2,1)S(1)}, u32[]{:S(2)}, u32[]{:S(2)}) collective-permute-start(bf16[256,1024]{1,0:T(8,128)(2,1)S(1)} %bitcast.63), channel_id=1, source_target_pairs={{0,1},{1,0},{2,3},{3,2},{4,5},{5,4},{6,7},{7,6},{8,9},{9,8},{10,11... | collective-permute-start | bytes 1572872 | tf_op jit(solution)/shard_map/ppermute | solution.py:651
  102.3 20.0 %collective-permute-start.24 = (bf16[256,1024]{1,0:T(8,128)(2,1)S(1)}, bf16[256,1024]{1,0:T(8,128)(2,1)S(1)}, u32[]{:S(2)}, u32[]{:S(2)}) collective-permute-start(bf16[256,1024]{1,0:T(8,128)(2,1)S(1)} %collective-permute-done.13.refs_6_), channel_id=1, source_target_pairs={{0,1},{1,0},{2,3},{3,2},{4,5},{5,4},{6,7},{7,6},{8,9},{9,8},{10,11... | collective-permute-start | bytes 1572872 | tf_op jit(solution)/shard_map/ppermute | solution.py:651
  102.7 17.1 %collective-permute-start.21 = (bf16[256,768]{1,0:T(8,128)(2,1)S(1)}, bf16[256,768]{1,0:T(8,128)(2,1)S(1)}, u32[]{:S(2)}, u32[]{:S(2)}) collective-permute-start(bf16[256,768]{1,0:T(8,128)(2,1)S(1)} %collective-permute-done.15.refs_10_), channel_id=1, source_target_pairs={{0,4},{4,0},{8,12},{12,8},{16,20},{20,16},{24,28},{28,24},{1,5},{5... | collective-permute-start | bytes 1179656 | tf_op jit(solution)/shard_map/ppermute | solution.py:682
  102.7 19.5 %collective-permute-start.22 = (bf16[256,768]{1,0:T(8,128)(2,1)S(1)}, bf16[256,768]{1,0:T(8,128)(2,1)S(1)}, u32[]{:S(2)}, u32[]{:S(2)}) collective-permute-start(bf16[256,768]{1,0:T(8,128)(2,1)S(1)} %collective-permute-done.16.refs_11_), channel_id=1, source_target_pairs={{0,4},{4,0},{8,12},{12,8},{16,20},{20,16},{24,28},{28,24},{1,5},{5... | collective-permute-start | bytes 1179656 | tf_op jit(solution)/shard_map/ppermute | solution.py:682
  159.7 17.5 %collective-permute-start.28 = (bf16[256,1024]{1,0:T(8,128)(2,1)}, bf16[256,1024]{1,0:T(8,128)(2,1)S(1)}, u32[]{:S(2)}, u32[]{:S(2)}) collective-permute-start(bf16[256,1024]{1,0:T(8,128)(2,1)} %get-tuple-element.294), channel_id=1, source_target_pairs={{0,1},{1,0},{2,3},{3,2},{4,5},{5,4},{6,7},{7,6},{8,9},{9,8},{10,11... | collective-permute-start | bytes 1572872 | tf_op jit(solution)/shard_map/ppermute | solution.py:651
  162.1 15.0 %collective-permute-start.30 = (bf16[256,1024]{1,0:T(8,128)(2,1)S(1)}, bf16[256,1024]{1,0:T(8,128)(2,1)S(1)}, u32[]{:S(2)}, u32[]{:S(2)}) collective-permute-start(bf16[256,1024]{1,0:T(8,128)(2,1)S(1)} %add_convert_fusion.8), channel_id=1, source_target_pairs={{0,2},{1,3},{2,0},{3,1},{4,6},{5,7},{6,4},{7,5},{8,10},{9,11},{10,... | collective-permute-start | bytes 1572872 | tf_op jit(solution)/shard_map/ppermute | solution.py:651
  183.6 19.7 %collective-permute-start.34 = (bf16[4,4,32,656]{3,2,1,0:T(8,128)(2,1)}, bf16[4,4,32,656]{3,2,1,0:T(8,128)(2,1)S(1)}, u32[]{:S(2)}, u32[]{:S(2)}) collective-permute-start(bf16[4,4,32,656]{3,2,1,0:T(8,128)(2,1)} %get-tuple-element.434), channel_id=1, source_target_pairs={{0,4},{4,0},{8,12},{12,8},{16,20},{20,16},{24,28},{28,24},{1,5},{5... | collective-permute-start | bytes 2015240 | tf_op jit(solution)/shard_map/ppermute | solution.py:682
  185.2 20.1 %collective-permute-start.35 = (bf16[4,4,32,656]{3,2,1,0:T(8,128)(2,1)}, bf16[4,4,32,656]{3,2,1,0:T(8,128)(2,1)S(1)}, u32[]{:S(2)}, u32[]{:S(2)}) collective-permute-start(bf16[4,4,32,656]{3,2,1,0:T(8,128)(2,1)} %get-tuple-element.432), channel_id=1, source_target_pairs={{0,8},{4,12},{8,0},{12,4},{16,24},{20,28},{24,16},{28,20},{1,9},{5... | collective-permute-start | bytes 2015240 | tf_op jit(solution)/shard_map/ppermute | solution.py:682
  208.8 22.9 %collective-permute-start.38 = (bf16[2,4,32,656]{3,2,1,0:T(8,128)(2,1)S(1)}, bf16[2,4,32,656]{3,2,1,0:T(8,128)(2,1)S(1)}, u32[]{:S(2)}, u32[]{:S(2)}) collective-permute-start(bf16[2,4,32,656]{3,2,1,0:T(8,128)(2,1)S(1)} %get-tuple-element.448), channel_id=1, source_target_pairs={{0,8},{4,12},{8,0},{12,4},{16,24},{20,28},{24,16},{28,20},{1,9},{5... | collective-permute-start | bytes 1007624 | tf_op jit(solution)/shard_map/ppermute | solution.py:682
  210.6 21.1 %collective-permute-start.39 = (bf16[2,4,32,656]{3,2,1,0:T(8,128)(2,1)S(1)}, bf16[2,4,32,656]{3,2,1,0:T(8,128)(2,1)S(1)}, u32[]{:S(2)}, u32[]{:S(2)}) collective-permute-start(bf16[2,4,32,656]{3,2,1,0:T(8,128)(2,1)S(1)} %get-tuple-element.446), channel_id=1, source_target_pairs={{0,16},{4,20},{8,24},{12,28},{16,0},{20,4},{24,8},{28,12},{1,17},{... | collective-permute-start | bytes 1007624 | tf_op jit(solution)/shard_map/ppermute | solution.py:682
  210.9 20.9 %collective-permute-start.40 = (bf16[4,4,32,656]{3,2,1,0:T(8,128)(2,1)S(1)}, bf16[4,4,32,656]{3,2,1,0:T(8,128)(2,1)S(1)}, u32[]{:S(2)}, u32[]{:S(2)}) collective-permute-start(bf16[4,4,32,656]{3,2,1,0:T(8,128)(2,1)S(1)} %get-tuple-element.430), channel_id=1, source_target_pairs={{0,4},{4,0},{8,12},{12,8},{16,20},{20,16},{24,28},{28,24},{1,5},{5... | collective-permute-start | bytes 2015240 | tf_op jit(solution)/shard_map/ppermute | solution.py:682
  212.4 19.3 %collective-permute-start.41 = (bf16[256,1024]{1,0:T(8,128)(2,1)S(1)}, bf16[256,1024]{1,0:T(8,128)(2,1)S(1)}, u32[]{:S(2)}, u32[]{:S(2)}) collective-permute-start(bf16[256,1024]{1,0:T(8,128)(2,1)S(1)} %add_convert_fusion.6), channel_id=1, source_target_pairs={{0,2},{1,3},{2,0},{3,1},{4,6},{5,7},{6,4},{7,5},{8,10},{9,11},{10,... | collective-permute-start | bytes 1572872 | tf_op jit(solution)/shard_map/ppermute | solution.py:651
  235.0 28.7 %collective-permute-start.42 = (bf16[4,512,128]{2,1,0:T(8,128)(2,1)S(1)}, bf16[4,512,128]{2,1,0:T(8,128)(2,1)S(1)}, u32[]{:S(2)}, u32[]{:S(2)}) collective-permute-start(bf16[4,512,128]{2,1,0:T(8,128)(2,1)S(1)} %get-tuple-element.442), channel_id=1, source_target_pairs={{0,4},{4,0},{8,12},{12,8},{16,20},{20,16},{24,28},{28,24},{1,5},{5... | collective-permute-start | bytes 1572872 | tf_op jit(solution)/shard_map/ppermute | solution.py:682
  235.9 27.9 %collective-permute-start.43 = (bf16[1,4,32,656]{3,2,1,0:T(8,128)(2,1)S(1)}, bf16[1,4,32,656]{3,2,1,0:T(8,128)(2,1)S(1)}, u32[]{:S(2)}, u32[]{:S(2)}) collective-permute-start(bf16[1,4,32,656]{3,2,1,0:T(8,128)(2,1)S(1)} %get-tuple-element.472), channel_id=1, source_target_pairs={{0,16},{4,20},{8,24},{12,28},{16,0},{20,4},{24,8},{28,12},{1,17},{... | collective-permute-start | bytes 503816 | tf_op jit(solution)/shard_map/ppermute | solution.py:682
  237.2 26.6 %collective-permute-start.44 = (bf16[1,4,32,656]{3,2,1,0:T(8,128)(2,1)S(1)}, bf16[1,4,32,656]{3,2,1,0:T(8,128)(2,1)S(1)}, u32[]{:S(2)}, u32[]{:S(2)}) collective-permute-start(bf16[1,4,32,656]{3,2,1,0:T(8,128)(2,1)S(1)} %get-tuple-element.470), channel_id=1, source_target_pairs={{0,4},{4,0},{8,12},{12,8},{16,20},{20,16},{24,28},{28,24},{1,5},{5... | collective-permute-start | bytes 503816 | tf_op jit(solution)/shard_map/ppermute | solution.py:682
  239.5 24.2 %collective-permute-start.45 = (bf16[2,4,32,656]{3,2,1,0:T(8,128)(2,1)S(1)}, bf16[2,4,32,656]{3,2,1,0:T(8,128)(2,1)S(1)}, u32[]{:S(2)}, u32[]{:S(2)}) collective-permute-start(bf16[2,4,32,656]{3,2,1,0:T(8,128)(2,1)S(1)} %get-tuple-element.444), channel_id=1, source_target_pairs={{0,8},{4,12},{8,0},{12,4},{16,24},{20,28},{24,16},{28,20},{1,9},{5... | collective-permute-start | bytes 1007624 | tf_op jit(solution)/shard_map/ppermute | solution.py:682
  264.6 14.4 %collective-permute-start.46 = (bf16[2,512,128]{2,1,0:T(8,128)(2,1)}, bf16[2,512,128]{2,1,0:T(8,128)(2,1)}, u32[]{:S(2)}, u32[]{:S(2)}) collective-permute-start(bf16[2,512,128]{2,1,0:T(8,128)(2,1)} %get-tuple-element.464), channel_id=1, source_target_pairs={{0,8},{4,12},{8,0},{12,4},{16,24},{20,28},{24,16},{28,20},{1,9},{5... | collective-permute-start | bytes 786440 | tf_op jit(solution)/shard_map/ppermute | solution.py:682
  265.1 13.9 %collective-permute-start.47 = (bf16[4,512,128]{2,1,0:T(8,128)(2,1)S(1)}, bf16[4,512,128]{2,1,0:T(8,128)(2,1)S(1)}, u32[]{:S(2)}, u32[]{:S(2)}) collective-permute-start(bf16[4,512,128]{2,1,0:T(8,128)(2,1)S(1)} %get-tuple-element.440), channel_id=1, source_target_pairs={{0,4},{4,0},{8,12},{12,8},{16,20},{20,16},{24,28},{28,24},{1,5},{5... | collective-permute-start | bytes 1572872 | tf_op jit(solution)/shard_map/ppermute | solution.py:682
  280.5 16.7 %collective-permute-start.48 = (bf16[256,1024]{1,0:T(8,128)(2,1)}, bf16[256,1024]{1,0:T(8,128)(2,1)S(1)}, u32[]{:S(2)}, u32[]{:S(2)}) collective-permute-start(bf16[256,1024]{1,0:T(8,128)(2,1)} %get-tuple-element.376), channel_id=1, source_target_pairs={{0,1},{1,0},{2,3},{3,2},{4,5},{5,4},{6,7},{7,6},{8,9},{9,8},{10,11... | collective-permute-start | bytes 1572872 | tf_op jit(solution)/shard_map/ppermute | solution.py:651
  280.9 16.3 %collective-permute-start.52 = (bf16[2,512,128]{2,1,0:T(8,128)(2,1)S(1)}, bf16[2,512,128]{2,1,0:T(8,128)(2,1)S(1)}, u32[]{:S(2)}, u32[]{:S(2)}) collective-permute-start(bf16[2,512,128]{2,1,0:T(8,128)(2,1)S(1)} %get-tuple-element.462), channel_id=1, source_target_pairs={{0,8},{4,12},{8,0},{12,4},{16,24},{20,28},{24,16},{28,20},{1,9},{5... | collective-permute-start | bytes 786440 | tf_op jit(solution)/shard_map/ppermute | solution.py:682
  281.5 15.7 %collective-permute-start.50 = (bf16[256,1024]{1,0:T(8,128)(2,1)S(1)}, bf16[256,1024]{1,0:T(8,128)(2,1)S(1)}, u32[]{:S(2)}, u32[]{:S(2)}) collective-permute-start(bf16[256,1024]{1,0:T(8,128)(2,1)S(1)} %add_convert_fusion.4), channel_id=1, source_target_pairs={{0,2},{1,3},{2,0},{3,1},{4,6},{5,7},{6,4},{7,5},{8,10},{9,11},{10,... | collective-permute-start | bytes 1572872 | tf_op jit(solution)/shard_map/ppermute | solution.py:651
  283.0 14.2 %collective-permute-start.51 = (bf16[1,512,128]{2,1,0:T(8,128)(2,1)S(1)}, bf16[1,512,128]{2,1,0:T(8,128)(2,1)S(1)}, u32[]{:S(2)}, u32[]{:S(2)}) collective-permute-start(bf16[1,512,128]{2,1,0:T(8,128)(2,1)S(1)} %get-tuple-element.478), channel_id=1, source_target_pairs={{0,16},{4,20},{8,24},{12,28},{16,0},{20,4},{24,8},{28,12},{1,17},{... | collective-permute-start | bytes 393224 | tf_op jit(solution)/shard_map/ppermute | solution.py:682
  297.5 16.1 %collective-permute-start.55 = (bf16[1,4,32,656]{3,2,1,0:T(8,128)(2,1)S(1)}, bf16[1,4,32,656]{3,2,1,0:T(8,128)(2,1)S(1)}, u32[]{:S(2)}, u32[]{:S(2)}) collective-permute-start(bf16[1,4,32,656]{3,2,1,0:T(8,128)(2,1)S(1)} %add_convert_fusion.15), channel_id=1, source_target_pairs={{0,16},{4,20},{8,24},{12,28},{16,0},{20,4},{24,8},{28,12},{1,17},{... | collective-permute-start | bytes 503816 | tf_op jit(solution)/shard_map/ppermute | solution.py:682
  303.8 29.7 %collective-permute-start.61 = (bf16[1,128,1024]{2,1,0:T(8,128)(2,1)}, bf16[1,128,1024]{2,1,0:T(8,128)(2,1)S(1)}, u32[]{:S(2)}, u32[]{:S(2)}) collective-permute-start(bf16[1,128,1024]{2,1,0:T(8,128)(2,1)} %get-tuple-element.405), channel_id=1, source_target_pairs={{0,0},{10,1},{4,2},{14,3},{16,4},{26,5},{20,6},{30,7},{1,8},{11,9}... | collective-permute-start | bytes 786440 | tf_op jit(solution)/shard_map/ppermute | solution.py:634
  305.4 28.1 %collective-permute-start.62 = (bf16[1,128,1024]{2,1,0:T(8,128)(2,1)}, bf16[1,128,1024]{2,1,0:T(8,128)(2,1)S(1)}, u32[]{:S(2)}, u32[]{:S(2)}) collective-permute-start(bf16[1,128,1024]{2,1,0:T(8,128)(2,1)} %get-tuple-element.406), channel_id=1, source_target_pairs={{16,0},{26,1},{20,2},{30,3},{0,4},{10,5},{4,6},{14,7},{17,8},{27,9... | collective-permute-start | bytes 786440 | tf_op jit(solution)/shard_map/ppermute | solution.py:634
  314.4 18.1 %all-to-all-start.1 = ((bf16[2,4,96,128]{3,2,0,1:T(8,128)(2,1)}), bf16[2,4,96,128]{3,2,0,1:T(8,128)(2,1)S(1)}, u32[]{:S(2)}, u32[]{:S(2)}) async-start(bf16[2,4,96,128]{3,2,0,1:T(8,128)(2,1)} %copy.47), calls=%async_computation.1 | async-start | bytes 393216 | tf_op jit(solution)/shard_map/all_to_all | solution.py:1014
  327.2 17.4 %collective-permute-start.59 = (bf16[1,32,5248]{2,1,0:T(8,128)(2,1)S(1)}, bf16[1,32,5248]{2,1,0:T(8,128)(2,1)S(1)}, u32[]{:S(2)}, u32[]{:S(2)}) collective-permute-start(bf16[1,32,5248]{2,1,0:T(8,128)(2,1)S(1)} %reshape.139), channel_id=1, source_target_pairs={{0,16},{4,20},{8,24},{12,28},{16,0},{20,4},{24,8},{28,12},{1,17},{... | collective-permute-start | bytes 1007624 | tf_op jit(solution)/shard_map/ppermute | solution.py:682
  327.2 18.9 %collective-permute-start.60 = (bf16[2,4,32,656]{3,2,1,0:T(8,128)(2,1)S(1)}, bf16[2,4,32,656]{3,2,1,0:T(8,128)(2,1)S(1)}, u32[]{:S(2)}, u32[]{:S(2)}) collective-permute-start(bf16[2,4,32,656]{3,2,1,0:T(8,128)(2,1)S(1)} %constant_dynamic-update-slice_fusion), channel_id=1, source_target_pairs={{0,8},{4,12},{8,0},{12,4},{16,24},{20,28},{24,16},{28,20},{1,9},{5... | collective-permute-start | bytes 1007624 | tf_op jit(solution)/shard_map/ppermute | solution.py:682
  346.2 28.2 %collective-permute-start.64 = (bf16[2,32,5248]{2,1,0:T(8,128)(2,1)S(1)}, bf16[2,32,5248]{2,1,0:T(8,128)(2,1)S(1)}, u32[]{:S(2)}, u32[]{:S(2)}) collective-permute-start(bf16[2,32,5248]{2,1,0:T(8,128)(2,1)S(1)} %constant_dynamic-update-slice_fusion.4), channel_id=1, source_target_pairs={{0,8},{4,12},{8,0},{12,4},{16,24},{20,28},{24,16},{28,20},{1,9},{5... | collective-permute-start | bytes 2015240 | tf_op jit(solution)/shard_map/ppermute | solution.py:682
  346.4 28.8 %collective-permute-start.65 = (bf16[4,4,32,656]{3,2,1,0:T(8,128)(2,1)S(1)}, bf16[4,4,32,656]{3,2,1,0:T(8,128)(2,1)}, u32[]{:S(2)}, u32[]{:S(2)}) collective-permute-start(bf16[4,4,32,656]{3,2,1,0:T(8,128)(2,1)S(1)} %constant_dynamic-update-slice_fusion.6), channel_id=1, source_target_pairs={{0,4},{4,0},{8,12},{12,8},{16,20},{20,16},{24,28},{28,24},{1,5},{5... | collective-permute-start | bytes 2015240 | tf_op jit(solution)/shard_map/ppermute | solution.py:682
  347.5 25.6 %collective-permute-start.63 = (bf16[2,2,512,128]{3,2,1,0:T(8,128)(2,1)S(1)}, bf16[2,2,512,128]{3,2,1,0:T(8,128)(2,1)S(1)}, u32[]{:S(2)}, u32[]{:S(2)}) collective-permute-start(bf16[2,2,512,128]{3,2,1,0:T(8,128)(2,1)S(1)} %constant_dynamic-update-slice_fusion.2), channel_id=1, source_target_pairs={{0,16},{4,20},{8,24},{12,28},{16,0},{20,4},{24,8},{28,12},{1,17},{... | collective-permute-start | bytes 1572872 | tf_op jit(solution)/shard_map/ppermute | solution.py:682
  350.2 31.8 %collective-permute-start.56 = (bf16[1,128,1024]{2,1,0:T(8,128)(2,1)}, bf16[1,128,1024]{2,1,0:T(8,128)(2,1)}, u32[]{:S(2)}, u32[]{:S(2)}) collective-permute-start(bf16[1,128,1024]{2,1,0:T(8,128)(2,1)} %get-tuple-element.392), channel_id=1, source_target_pairs={{16,0},{26,1},{20,2},{30,3},{0,4},{10,5},{4,6},{14,7},{17,8},{27,9... | collective-permute-start | bytes 786440 | tf_op jit(solution)/shard_map/ppermute | solution.py:634
  353.3 28.8 %collective-permute-start.57 = (bf16[1,128,1024]{2,1,0:T(8,128)(2,1)}, bf16[1,128,1024]{2,1,0:T(8,128)(2,1)}, u32[]{:S(2)}, u32[]{:S(2)}) collective-permute-start(bf16[1,128,1024]{2,1,0:T(8,128)(2,1)} %get-tuple-element.393), channel_id=1, source_target_pairs={{0,0},{10,1},{4,2},{14,3},{16,4},{26,5},{20,6},{30,7},{1,8},{11,9}... | collective-permute-start | bytes 786440 | tf_op jit(solution)/shard_map/ppermute | solution.py:634
  376.4 35.7 %collective-permute-start.67 = (bf16[4,32,5248]{2,1,0:T(8,128)(2,1)S(1)}, bf16[4,32,5248]{2,1,0:T(8,128)(2,1)S(1)}, u32[]{:S(2)}, u32[]{:S(2)}) collective-permute-start(bf16[4,32,5248]{2,1,0:T(8,128)(2,1)S(1)} %constant_dynamic-update-slice_fusion.10.sums), channel_id=1, source_target_pairs={{0,4},{4,0},{8,12},{12,8},{16,20},{20,16},{24,28},{28,24},{1,5},{5... | collective-permute-start | bytes 4030472 | tf_op jit(solution)/shard_map/ppermute | solution.py:682
  380.0 26.4 %collective-permute-start.66 = (bf16[4,2,512,128]{3,2,1,0:T(8,128)(2,1)}, bf16[4,2,512,128]{3,2,1,0:T(8,128)(2,1)}, u32[]{:S(2)}, u32[]{:S(2)}) collective-permute-start(bf16[4,2,512,128]{3,2,1,0:T(8,128)(2,1)} %constant_dynamic-update-slice_fusion.8.low), channel_id=1, source_target_pairs={{0,8},{4,12},{8,0},{12,4},{16,24},{20,28},{24,16},{28,20},{1,9},{5... | collective-permute-start | bytes 3145736 | tf_op jit(solution)/shard_map/ppermute | solution.py:682
  (81 other events, 690.9 us)

commit v6 on v5

--- a/solution.py
+++ b/solution.py
@@ -936,16 +936,6 @@
                 act_sums, gate_sums = add(send(act_sums, bit)), add(send(gate_sums, gate_bit))
             act_pair, gate_pair = send(act_sums, order[-1]), send(gate_sums, gate_order[-1])
             down_pair = send(down_sums, order[1])
-            result_parts = call(
-                functools.partial(result_kernel, p=p),
-                "result",
-                piece,
-                1,
-                [],
-                [out_near, out_got, residual],
-                1e6,
-            )
-            low_slots, result_parts = meet(low_slots, result_parts)
         else:
             sums, pairs, act_pair, gate_pair, down_pair = meet(
                 sums, pairs, act_pair, gate_pair, down_pair
@@ -984,7 +974,16 @@
         early = [send(sums, step_of(sums))]
     sums = add(late)
     late = send(sums, step_of(sums))
-    u1, early, late, down_pair = meet(u1, early, late, down_pair)
+    u1, early, late, down_pair, out_got = meet(u1, early, late, down_pair, out_got)
+    result_parts = call(
+        functools.partial(result_kernel, p=p),
+        "result",
+        piece,
+        1,
+        [],
+        [out_near, out_got, residual],
+        1e6,
+    )
     back_parts = call(
         functools.partial(last_kernel, p=p),
         "last",

time: 424 us -> 425 us (level)
  Pallas kernels: 140 us -> 135 us
    pallas_call x17, Pallas kernels: 135 us -> 130 us  [call(): pl.pallas_call(kernel, grid=(grid,), in_specs=specs, out_specs=outs, out_...]
    unnamed x124 -> x126, local copies, waits for them, and re-layouts: 9.54 us -> 9.12 us
  transfers between devices with their start and end apart: 70 -> 70, of which waited for: 28 -> 29; matrix products, arithmetic and copies ran while one was open for 9% -> 9% of each run, Pallas kernels for 26% -> 25%
where the time goes in v6:
time: 425 us; the launch traced here: 417 us
  Pallas kernels  135 us (32%)
  waiting for transfers between devices  132 us (31%)
  starting transfers between devices  98.1 us (23%)
  local copies, waits for them, and re-layouts  27.4 us (6%)
  other arithmetic  21.4 us (5%)
    pallas_call x17, Pallas kernels, call(): pl.pallas_call(kernel, grid=(grid,), in_specs=specs, out_specs=outs, out_...  130 us
    ppermute x28, waiting for transfers between devices, away(): return lax.ppermute(values, 'ctx', [(i, i ^ bit) for i in range(ctx)])  75.9 us
    ppermute x26, waiting for transfers between devices, partner(): return lax.ppermute(values, 'fsdp', [(i, i ^ bit) for i in range(fsdp)])  37 us
    ppermute x28, starting transfers between devices, away(): return lax.ppermute(values, 'ctx', [(i, i ^ bit) for i in range(ctx)])  34.6 us
    ppermute x4, starting transfers between devices, deal(): return [lax.ppermute(part, both, route(j)) for j, part in enumerate(parts)]  15.5 us
    ppermute x26, starting transfers between devices, partner(): return lax.ppermute(values, 'fsdp', [(i, i ^ bit) for i in range(fsdp)])  14 us
    ppermute x4, starting transfers between devices, undeal(): lax.ppermute(part, both, [(b, a) for a, b in route(j)])  13 us
    all_to_all x1, starting transfers between devices, on_device(): mine = lax.all_to_all(mine, 'fsdp', 1, 1, tiled=True)  12.8 us
  transfers between devices with their start and end apart: 70, of which 29 were waited for; matrix products, arithmetic and copies ran while one was open for 9% of the time, Pallas kernels for 25%

profile of v6, /device:TPU:0, one launch (start us, length us, event | category | flops | bytes accessed | tf_op | source)
XLA Modules:
  0.0 416.9 jit_solution(2468904345751229938)
XLA Ops:
  3.2 8.5 %collective-permute-start.1 = (bf16[1,144,1024]{2,1,0:T(8,128)(2,1)S(1)}, bf16[1,144,1024]{2,1,0:T(8,128)(2,1)S(1)}, u32[]{:S(2)}, u32[]{:S(2)}) collective-permute-start(bf16[1,144,1024]{2,1,0:T(8,128)(2,1)S(1)} %get-tuple-element.214), channel_id=1, source_target_pairs={{0,16},{1,26},{2,20},{3,30},{4,0},{5,10},{6,4},{7,14},{8,17},{9,27... | collective-permute-start | bytes 884744 | tf_op jit(solution)/shard_map/ppermute | solution.py:630
  13.1 3.9 cut.1
  27.2 2.3 collective-permute-done.3.refs_6_
  29.5 4.2 %collective-permute-done.4.refs_7_ = bf16[128,768]{1,0:T(8,128)(2,1)S(1)} collective-permute-done((bf16[128,768]{1,0:T(8,128)(2,1)S(1)}, bf16[128,768]{1,0:T(8,128)(2,1)S(1)}, u32[]{:S(2)}, u32[]{:S(2)}) %collective-permute-start.4) | collective-permute-done | bytes 196640 | tf_op jit(solution)/shard_map/ppermute | solution.py:733
  36.8 2.4 collective-permute-start.6
  40.1 5.5 %collective-permute-start.10 = (bf16[1,128,1024]{2,1,0:T(8,128)(2,1)S(1)}, bf16[1,128,1024]{2,1,0:T(8,128)(2,1)S(1)}, u32[]{:S(2)}, u32[]{:S(2)}) collective-permute-start(bf16[1,128,1024]{2,1,0:T(8,128)(2,1)S(1)} %get-tuple-element.456), channel_id=1, source_target_pairs={{0,16},{1,26},{2,20},{3,30},{4,0},{5,10},{6,4},{7,14},{8,17},{9,27... | collective-permute-start | bytes 786440 | tf_op jit(solution)/shard_map/ppermute | solution.py:630
  48.5 5.2 %cut_in.1 = (bf16[4,256,768]{2,1,0:T(8,128)(2,1)}, bf16[2,256,768]{2,1,0:T(8,128)(2,1)}) custom-call(bf16[256,5248]{1,0:T(8,128)(2,1)} %w.4, f32[256,1]{1,0:T(8,128)} %copy.43.gain, s32[2]{0:T(128)} %pad_add_fusion.at_ref.refs_14_.refs_17_), custom_call_target="tpu_custom_call" | custom-call | flops 1000000 | bytes 5047304 | tf_op jit(solution)/shard_map/cut_in/pallas_call | solution.py:53
  53.7 8.4 %collective-permute-done.7.refs_10_ = bf16[128,768]{1,0:T(8,128)(2,1)S(1)} collective-permute-done((bf16[128,768]{1,0:T(8,128)(2,1)S(1)}, bf16[128,768]{1,0:T(8,128)(2,1)S(1)}, u32[]{:S(2)}, u32[]{:S(2)}) %collective-permute-start.7) | collective-permute-done | bytes 196640 | tf_op jit(solution)/shard_map/ppermute | solution.py:682
  62.0 3.2 collective-permute-done.8.refs_11_
  68.1 2.4 slice_bitcast_fusion.2
  73.8 7.9 %project.1 = (bf16[1,1024,256]{2,1,0:T(8,128)(2,1)}, bf16[1,1024,256]{2,1,0:T(8,128)(2,1)}, bf16[1,1024,256]{2,1,0:T(8,128)(2,1)}, f32[1,8,1024]{2,1,0:T(8,128)}, bf16[1024,768]{1,0:T(8,128)(2,1)}) custom-call(bf16[272,1024]{1,0:T(8,128)(2,1)} %unit1.1.refs_0_, bf16[272,1024]{1,0:T(8,128)(2,1)} %copy-done.15, bf16[272,1024]{1,0:T(8,128)(2,1)} %copy-done.14, ...), custom_call_target="tpu_custom_call" | custom-call | flops 4000000000 | bytes 8028168 | tf_op jit(solution)/shard_map/project/pallas_call | solution.py:53
  81.7 12.7 %attend.1 = (bf16[256,1024]{1,0:T(8,128)(2,1)}, bf16[256,1024]{1,0:T(8,128)(2,1)}, bf16[256,1024]{1,0:T(8,128)(2,1)}, bf16[256,1024]{1,0:T(8,128)(2,1)}, bf16[1,...) custom-call(bf16[1,1024,256]{2,1,0:T(8,128)(2,1)} %get-tuple-element.247.q_ref.refs_6_, ...), custom_call_target="tpu_custom_call" | custom-call | flops 12000000000 | bytes 4784128 | tf_op jit(solution)/shard_map/attend/pallas_call | solution.py:53
  94.4 3.7 collective-permute-done.16.refs_11_
  104.7 3.8 flip.1.refs_4_
  108.5 7.5 %collective-permute-done.20.refs_4_ = bf16[256,1024]{1,0:T(8,128)(2,1)S(1)} collective-permute-done((bf16[256,1024]{1,0:T(8,128)(2,1)S(1)}, bf16[256,1024]{1,0:T(8,128)(2,1)S(1)}, u32[]{:S(2)}, u32[]{:S(2)}) %collective-permute-start.20) | collective-permute-done | bytes 524320 | tf_op jit(solution)/shard_map/ppermute | solution.py:651
  116.8 3.0 middle.1
  119.8 2.4 collective-permute-done.22.refs_15_
  124.0 11.7 %collective-permute-done.26.refs_2_ = bf16[256,1024]{1,0:T(8,128)(2,1)S(1)} collective-permute-done((bf16[256,1024]{1,0:T(8,128)(2,1)}, bf16[256,1024]{1,0:T(8,128)(2,1)S(1)}, u32[]{:S(2)}, u32[]{:S(2)}) %collective-permute-start.26) | collective-permute-done | bytes 524320 | tf_op jit(solution)/shard_map/ppermute | solution.py:651
  138.4 20.3 %mlp.1 = (bf16[256,1024]{1,0:T(8,128)(2,1)}, bf16[256,1024]{1,0:T(8,128)(2,1)}, bf16[256,1024]{1,0:T(8,128)(2,1)}, bf16[256,1024]{1,0:T(8,128)(2,1)}, bf16[256,1...) custom-call(bf16[256,1024]{1,0:T(8,128)(2,1)} %get-tuple-element.277, ...), custom_call_target="tpu_custom_call" | custom-call | flops 12000000000 | bytes 17596424 | tf_op jit(solution)/shard_map/mlp/pallas_call | solution.py:53
  163.8 13.3 %mlp_sums.1 = (bf16[8,4,32,656]{3,2,1,0:T(8,128)(2,1)}, bf16[8,4,32,656]{3,2,1,0:T(8,128)(2,1)}, bf16[8,4,32,656]{3,2,1,0:T(8,128)(2,1)}) custom-call(bf16[256,1024]{1,0:T(8,128)(2,1)} %get-tuple-element.277.refs_0_, bf16[256,1024]{1,0:T(8,128)(2,1)} %copy-done.44, bf16[256,1024]{1,0:T(8,128)(2,1)} %copy-done.43, bf16[256,1024]{1,0:T(8,128)(2,1)} %copy-done.45, ...), custom_call_target="tpu_custom_call" | custom-call | flops 6000000000 | bytes 12943364 | tf_op jit(solution)/shard_map/mlp_sums/pallas_call | solution.py:53
  178.2 3.9 turn.1
  185.2 2.5 collective-permute-start.35
  192.5 9.6 %collective-permute-done.31.refs_2_ = bf16[256,1024]{1,0:T(8,128)(2,1)S(1)} collective-permute-done((bf16[256,1024]{1,0:T(8,128)(2,1)}, bf16[256,1024]{1,0:T(8,128)(2,1)S(1)}, u32[]{:S(2)}, u32[]{:S(2)}) %collective-permute-start.31) | collective-permute-done | bytes 524320 | tf_op jit(solution)/shard_map/ppermute | solution.py:651
  214.0 15.1 %attention_back.2 = (bf16[1,1024,384]{2,1,0:T(8,128)(2,1)}, bf16[8,512,128]{2,1,0:T(8,128)(2,1)}) custom-call(bf16[256,1024]{1,0:T(8,128)(2,1)} %get-tuple-element.337.refs_0_, bf16[256,1024]{1,0:T(8,128)(2,1)} %copy-done.39, bf16[256,1024]{1,0:T(8,128)(2,1)} %copy-done.38, bf16[256,1024]{1,0:T(8,128)(2,1)} %copy-done.40, ...), custom_call_target="tpu_custom_call" | custom-call | flops 15000000512 | bytes 9764900 | tf_op jit(solution)/shard_map/attention_back/pallas_call | solution.py:53
  238.1 15.2 %attention_back.3 = (bf16[1,1024,384]{2,1,0:T(8,128)(2,1)}, bf16[8,512,128]{2,1,0:T(8,128)(2,1)}) custom-call(bf16[256,1024]{1,0:T(8,128)(2,1)} %get-tuple-element.337.refs_0_, bf16[256,1024]{1,0:T(8,128)(2,1)} %copy-done.39, bf16[256,1024]{1,0:T(8,128)(2,1)} %copy-done.38, bf16[256,1024]{1,0:T(8,128)(2,1)} %copy-done.40, ...), custom_call_target="tpu_custom_call" | custom-call | flops 15000000512 | bytes 9764900 | tf_op jit(solution)/shard_map/attention_back/pallas_call | solution.py:53
  253.2 6.1 %spread.1 = (bf16[256,1024]{1,0:T(8,128)(2,1)}, bf16[256,1024]{1,0:T(8,128)(2,1)}, bf16[256,1024]{1,0:T(8,128)(2,1)}, bf16[256,1024]{1,0:T(8,128)(2,1)}) custom-call(bf16[1,1024,384]{2,1,0:T(8,128)(2,1)} %get-tuple-element.331.refs_0_, bf16[1,1024,384]{2,1,0:T(8,128)(2,1)} %get-tuple-element.341.refs_1_, bf16[1024,768]{1,0:T(8,128)(2,1)} %get-tuple-element.342.refs_2_), custom_call_target="tpu_custom_call" | custom-call | flops 2000000000 | bytes 5242880 | tf_op jit(solution)/shard_map/spread/pallas_call | solution.py:53
  262.1 4.1 collective-permute-start.47
  267.1 3.5 all-to-all-start
  270.6 7.3 %all-to-all-done = bf16[4,2,32,656]{3,2,1,0:T(8,128)(2,1)S(1)} async-done(((bf16[4,2,32,656]{3,2,1,0:T(8,128)(2,1)}), bf16[4,2,32,656]{3,2,1,0:T(8,128)(2,1)S(1)}, u32[]{:S(2)}, u32[]{:S(2)}) %all-to-all-start) | async-done | bytes 335904 | tf_op jit(solution)/shard_map/all_to_all | solution.py:968
  284.2 6.9 %collective-permute-done.53 = bf16[1,4,32,656]{3,2,1,0:T(8,128)(2,1)S(1)} collective-permute-done((bf16[1,4,32,656]{3,2,1,0:T(8,128)(2,1)S(1)}, bf16[1,4,32,656]{3,2,1,0:T(8,128)(2,1)S(1)}, u32[]{:S(2)}, u32[]{:S(2)}) %collective-permute-start.53) | collective-permute-done | bytes 167968 | tf_op jit(solution)/shard_map/ppermute | solution.py:682
  291.1 5.5 %collective-permute-done.51 = bf16[1,512,128]{2,1,0:T(8,128)(2,1)S(1)} collective-permute-done((bf16[1,512,128]{2,1,0:T(8,128)(2,1)S(1)}, bf16[1,512,128]{2,1,0:T(8,128)(2,1)S(1)}, u32[]{:S(2)}, u32[]{:S(2)}) %collective-permute-start.51) | collective-permute-done | bytes 131104 | tf_op jit(solution)/shard_map/ppermute | solution.py:682
  296.9 3.0 collective-permute-start.55
  299.9 3.4 last.1
  304.8 4.0 collective-permute-start.62
  308.9 2.4 result.1
  313.8 12.8 %all-to-all-start.1 = ((bf16[2,4,96,128]{3,2,0,1:T(8,128)(2,1)}), bf16[2,4,96,128]{3,2,0,1:T(8,128)(2,1)S(1)}, u32[]{:S(2)}, u32[]{:S(2)}) async-start(bf16[2,4,96,128]{3,2,0,1:T(8,128)(2,1)} %copy.47), calls=%async_computation.1 | async-start | bytes 393216 | tf_op jit(solution)/shard_map/all_to_all | solution.py:1013
  326.7 3.2 collective-permute-start.60
  332.8 12.3 %collective-permute-done.59 = bf16[1,32,5248]{2,1,0:T(8,128)(2,1)S(1)} collective-permute-done((bf16[1,32,5248]{2,1,0:T(8,128)(2,1)S(1)}, bf16[1,32,5248]{2,1,0:T(8,128)(2,1)S(1)}, u32[]{:S(2)}, u32[]{:S(2)}) %collective-permute-start.59) | collective-permute-done | bytes 335904 | tf_op jit(solution)/shard_map/ppermute | solution.py:682
  347.0 2.3 collective-permute-start.63
  349.3 3.7 collective-permute-start.56
  353.0 3.6 collective-permute-start.57
  356.6 16.9 %collective-permute-done.63 = bf16[2,2,512,128]{3,2,1,0:T(8,128)(2,1)S(1)} collective-permute-done((bf16[2,2,512,128]{3,2,1,0:T(8,128)(2,1)S(1)}, bf16[2,2,512,128]{3,2,1,0:T(8,128)(2,1)S(1)}, u32[]{:S(2)}, u32[]{:S(2)}) %collective-permute-start.63) | collective-permute-done | bytes 524320 | tf_op jit(solution)/shard_map/ppermute | solution.py:682
  385.1 2.9 in_grad.2
  388.0 2.4 pad_maximum_fusion.stack
  390.4 5.5 %out_grad.1 = f32[656,1024]{1,0:T(8,128)} custom-call(bf16[8,4,32,656]{3,2,1,0:T(8,128)(2,1)} %pad_maximum_fusion.stack, s32[1]{0:T(128)} %bitcast.3.refs_11_.refs_14_.c_ref), custom_call_target="tpu_custom_call" | custom-call | flops 1000000 | bytes 4030468 | tf_op jit(solution)/shard_map/out_grad/pallas_call | solution.py:53
  395.9 10.1 %collective-permute-done.66.high = bf16[4,2,512,128]{3,2,1,0:T(8,128)(2,1)} collective-permute-done((bf16[4,2,512,128]{3,2,1,0:T(8,128)(2,1)}, bf16[4,2,512,128]{3,2,1,0:T(8,128)(2,1)}, u32[]{:S(2)}, u32[]{:S(2)}) %collective-permute-start.66) | collective-permute-done | bytes 1048608 | tf_op jit(solution)/shard_map/ppermute | solution.py:682
  406.0 5.7 %qkv_grad.1 = (f32[256,3072]{1,0:T(8,128)}, f32[256,1024]{1,0:T(8,128)}, f32[1,256]{1,0:T(1,128)}) custom-call(bf16[4,2,512,128]{3,2,1,0:T(8,128)(2,1)} %constant_dynamic-update-slice_fusion.8.low, bf16[4,2,512,128]{3,2,1,0:T(8,128)(2,1)} %collective-permute-done.66.high, bf16[256,3072]{1,0:T(8,128)(2,1)} %w.2, f32[256,1]{1,0:T(8,128)} %copy.41.gain, ...), custom_call_target="tpu_custom_call" | custom-call | flops 1000000 | bytes 7866372 | tf_op jit(solution)/shard_map/qkv_grad/pallas_call | solution.py:53
  411.7 2.9 in_grad.3
  (323 shorter events, 105.7 us)
Async XLA Ops:
  2.5 31.2 %collective-permute-start = (bf16[1,144,1024]{2,1,0:T(8,128)(2,1)S(1)}, bf16[1,144,1024]{2,1,0:T(8,128)(2,1)S(1)}, u32[]{:S(2)}, u32[]{:S(2)}) collective-permute-start(bf16[1,144,1024]{2,1,0:T(8,128)(2,1)S(1)} %get-tuple-element.213), channel_id=1, source_target_pairs={{0,0},{1,10},{2,4},{3,14},{4,16},{5,26},{6,20},{7,30},{8,1},{9,11}... | collective-permute-start | bytes 884744 | tf_op jit(solution)/shard_map/ppermute | solution.py:630
  3.2 30.6 %collective-permute-start.1 = (bf16[1,144,1024]{2,1,0:T(8,128)(2,1)S(1)}, bf16[1,144,1024]{2,1,0:T(8,128)(2,1)S(1)}, u32[]{:S(2)}, u32[]{:S(2)}) collective-permute-start(bf16[1,144,1024]{2,1,0:T(8,128)(2,1)S(1)} %get-tuple-element.214), channel_id=1, source_target_pairs={{0,16},{1,26},{2,20},{3,30},{4,0},{5,10},{6,4},{7,14},{8,17},{9,27... | collective-permute-start | bytes 884744 | tf_op jit(solution)/shard_map/ppermute | solution.py:630
  36.8 28.4 %collective-permute-start.6 = (bf16[272,1024]{1,0:T(8,128)(2,1)}, bf16[272,1024]{1,0:T(8,128)(2,1)S(1)}, u32[]{:S(2)}, u32[]{:S(2)}) collective-permute-start(bf16[272,1024]{1,0:T(8,128)(2,1)} %unit1.1.refs_0_), channel_id=1, source_target_pairs={{0,2},{1,3},{2,0},{3,1},{4,6},{5,7},{6,4},{7,5},{8,10},{9,11},{10,... | collective-permute-start | bytes 1671176 | tf_op jit(solution)/shard_map/ppermute | solution.py:651
  39.3 25.9 %collective-permute-start.9 = (bf16[1,128,1024]{2,1,0:T(8,128)(2,1)S(1)}, bf16[1,128,1024]{2,1,0:T(8,128)(2,1)S(1)}, u32[]{:S(2)}, u32[]{:S(2)}) collective-permute-start(bf16[1,128,1024]{2,1,0:T(8,128)(2,1)S(1)} %get-tuple-element.457), channel_id=1, source_target_pairs={{0,0},{1,10},{2,4},{3,14},{4,16},{5,26},{6,20},{7,30},{8,1},{9,11}... | collective-permute-start | bytes 786440 | tf_op jit(solution)/shard_map/ppermute | solution.py:630
  40.1 25.1 %collective-permute-start.10 = (bf16[1,128,1024]{2,1,0:T(8,128)(2,1)S(1)}, bf16[1,128,1024]{2,1,0:T(8,128)(2,1)S(1)}, u32[]{:S(2)}, u32[]{:S(2)}) collective-permute-start(bf16[1,128,1024]{2,1,0:T(8,128)(2,1)S(1)} %get-tuple-element.456), channel_id=1, source_target_pairs={{0,16},{1,26},{2,20},{3,30},{4,0},{5,10},{6,4},{7,14},{8,17},{9,27... | collective-permute-start | bytes 786440 | tf_op jit(solution)/shard_map/ppermute | solution.py:630
  45.6 16.5 %collective-permute-start.7 = (bf16[128,768]{1,0:T(8,128)(2,1)S(1)}, bf16[128,768]{1,0:T(8,128)(2,1)S(1)}, u32[]{:S(2)}, u32[]{:S(2)}) collective-permute-start(bf16[128,768]{1,0:T(8,128)(2,1)S(1)} %collective-permute-done.3.refs_6_), channel_id=1, source_target_pairs={{0,4},{4,0},{8,12},{12,8},{16,20},{20,16},{24,28},{28,24},{1,5},{5... | collective-permute-start | bytes 589832 | tf_op jit(solution)/shard_map/ppermute | solution.py:682
  45.7 19.5 %collective-permute-start.8 = (bf16[128,768]{1,0:T(8,128)(2,1)S(1)}, bf16[128,768]{1,0:T(8,128)(2,1)S(1)}, u32[]{:S(2)}, u32[]{:S(2)}) collective-permute-start(bf16[128,768]{1,0:T(8,128)(2,1)S(1)} %collective-permute-done.4.refs_7_), channel_id=1, source_target_pairs={{0,4},{4,0},{8,12},{12,8},{16,20},{20,16},{24,28},{28,24},{1,5},{5... | collective-permute-start | bytes 589832 | tf_op jit(solution)/shard_map/ppermute | solution.py:682
  68.1 30.0 %collective-permute-start.13 = (bf16[256,1024]{1,0:T(8,128)(2,1)S(1)}, bf16[256,1024]{1,0:T(8,128)(2,1)S(1)}, u32[]{:S(2)}, u32[]{:S(2)}) collective-permute-start(bf16[256,1024]{1,0:T(8,128)(2,1)S(1)} %bitcast.62), channel_id=1, source_target_pairs={{0,2},{1,3},{2,0},{3,1},{4,6},{5,7},{6,4},{7,5},{8,10},{9,11},{10,... | collective-permute-start | bytes 1572872 | tf_op jit(solution)/shard_map/ppermute | solution.py:651
  70.5 23.8 %collective-permute-start.14 = (bf16[256,768]{1,0:T(8,128)(2,1)S(1)}, bf16[256,768]{1,0:T(8,128)(2,1)S(1)}, u32[]{:S(2)}, u32[]{:S(2)}) collective-permute-start(bf16[256,768]{1,0:T(8,128)(2,1)S(1)} %get-tuple-element.428), channel_id=1, source_target_pairs={{0,1},{1,0},{2,3},{3,2},{4,5},{5,4},{6,7},{7,6},{8,9},{9,8},{10,11... | collective-permute-start | bytes 1179656 | tf_op jit(solution)/shard_map/ppermute | solution.py:733
  70.7 23.6 %collective-permute-start.15 = (bf16[256,768]{1,0:T(8,128)(2,1)S(1)}, bf16[256,768]{1,0:T(8,128)(2,1)S(1)}, u32[]{:S(2)}, u32[]{:S(2)}) collective-permute-start(bf16[256,768]{1,0:T(8,128)(2,1)S(1)} %get-tuple-element.427), channel_id=1, source_target_pairs={{0,2},{1,3},{2,0},{3,1},{4,6},{5,7},{6,4},{7,5},{8,10},{9,11},{10,... | collective-permute-start | bytes 1179656 | tf_op jit(solution)/shard_map/ppermute | solution.py:733
  72.5 25.6 %collective-permute-start.16 = (bf16[256,768]{1,0:T(8,128)(2,1)S(1)}, bf16[256,768]{1,0:T(8,128)(2,1)S(1)}, u32[]{:S(2)}, u32[]{:S(2)}) collective-permute-start(bf16[256,768]{1,0:T(8,128)(2,1)S(1)} %get-tuple-element.426), channel_id=1, source_target_pairs={{0,3},{1,2},{2,1},{3,0},{4,7},{5,6},{6,5},{7,4},{8,11},{9,10},{10,... | collective-permute-start | bytes 1179656 | tf_op jit(solution)/shard_map/ppermute | solution.py:733
  73.4 24.7 %collective-permute-start.17 = (bf16[256,768]{1,0:T(8,128)(2,1)S(1)}, bf16[256,768]{1,0:T(8,128)(2,1)S(1)}, u32[]{:S(2)}, u32[]{:S(2)}) collective-permute-start(bf16[256,768]{1,0:T(8,128)(2,1)S(1)} %get-tuple-element.440), channel_id=1, source_target_pairs={{0,1},{1,0},{2,3},{3,2},{4,5},{5,4},{6,7},{7,6},{8,9},{9,8},{10,11... | collective-permute-start | bytes 1179656 | tf_op jit(solution)/shard_map/ppermute | solution.py:651
  102.2 20.1 %collective-permute-start.23 = (bf16[256,1024]{1,0:T(8,128)(2,1)S(1)}, bf16[256,1024]{1,0:T(8,128)(2,1)S(1)}, u32[]{:S(2)}, u32[]{:S(2)}) collective-permute-start(bf16[256,1024]{1,0:T(8,128)(2,1)S(1)} %bitcast.63), channel_id=1, source_target_pairs={{0,1},{1,0},{2,3},{3,2},{4,5},{5,4},{6,7},{7,6},{8,9},{9,8},{10,11... | collective-permute-start | bytes 1572872 | tf_op jit(solution)/shard_map/ppermute | solution.py:651
  102.3 20.0 %collective-permute-start.24 = (bf16[256,1024]{1,0:T(8,128)(2,1)S(1)}, bf16[256,1024]{1,0:T(8,128)(2,1)S(1)}, u32[]{:S(2)}, u32[]{:S(2)}) collective-permute-start(bf16[256,1024]{1,0:T(8,128)(2,1)S(1)} %collective-permute-done.13.refs_6_), channel_id=1, source_target_pairs={{0,1},{1,0},{2,3},{3,2},{4,5},{5,4},{6,7},{7,6},{8,9},{9,8},{10,11... | collective-permute-start | bytes 1572872 | tf_op jit(solution)/shard_map/ppermute | solution.py:651
  102.7 17.1 %collective-permute-start.21 = (bf16[256,768]{1,0:T(8,128)(2,1)S(1)}, bf16[256,768]{1,0:T(8,128)(2,1)S(1)}, u32[]{:S(2)}, u32[]{:S(2)}) collective-permute-start(bf16[256,768]{1,0:T(8,128)(2,1)S(1)} %collective-permute-done.15.refs_10_), channel_id=1, source_target_pairs={{0,4},{4,0},{8,12},{12,8},{16,20},{20,16},{24,28},{28,24},{1,5},{5... | collective-permute-start | bytes 1179656 | tf_op jit(solution)/shard_map/ppermute | solution.py:682
  102.7 19.5 %collective-permute-start.22 = (bf16[256,768]{1,0:T(8,128)(2,1)S(1)}, bf16[256,768]{1,0:T(8,128)(2,1)S(1)}, u32[]{:S(2)}, u32[]{:S(2)}) collective-permute-start(bf16[256,768]{1,0:T(8,128)(2,1)S(1)} %collective-permute-done.16.refs_11_), channel_id=1, source_target_pairs={{0,4},{4,0},{8,12},{12,8},{16,20},{20,16},{24,28},{28,24},{1,5},{5... | collective-permute-start | bytes 1179656 | tf_op jit(solution)/shard_map/ppermute | solution.py:682
  159.7 17.5 %collective-permute-start.28 = (bf16[256,1024]{1,0:T(8,128)(2,1)}, bf16[256,1024]{1,0:T(8,128)(2,1)S(1)}, u32[]{:S(2)}, u32[]{:S(2)}) collective-permute-start(bf16[256,1024]{1,0:T(8,128)(2,1)} %get-tuple-element.289), channel_id=1, source_target_pairs={{0,1},{1,0},{2,3},{3,2},{4,5},{5,4},{6,7},{7,6},{8,9},{9,8},{10,11... | collective-permute-start | bytes 1572872 | tf_op jit(solution)/shard_map/ppermute | solution.py:651
  162.2 15.0 %collective-permute-start.30 = (bf16[256,1024]{1,0:T(8,128)(2,1)S(1)}, bf16[256,1024]{1,0:T(8,128)(2,1)S(1)}, u32[]{:S(2)}, u32[]{:S(2)}) collective-permute-start(bf16[256,1024]{1,0:T(8,128)(2,1)S(1)} %add_convert_fusion.8), channel_id=1, source_target_pairs={{0,2},{1,3},{2,0},{3,1},{4,6},{5,7},{6,4},{7,5},{8,10},{9,11},{10,... | collective-permute-start | bytes 1572872 | tf_op jit(solution)/shard_map/ppermute | solution.py:651
  183.6 19.7 %collective-permute-start.34 = (bf16[4,4,32,656]{3,2,1,0:T(8,128)(2,1)}, bf16[4,4,32,656]{3,2,1,0:T(8,128)(2,1)S(1)}, u32[]{:S(2)}, u32[]{:S(2)}) collective-permute-start(bf16[4,4,32,656]{3,2,1,0:T(8,128)(2,1)} %get-tuple-element.424), channel_id=1, source_target_pairs={{0,4},{4,0},{8,12},{12,8},{16,20},{20,16},{24,28},{28,24},{1,5},{5... | collective-permute-start | bytes 2015240 | tf_op jit(solution)/shard_map/ppermute | solution.py:682
  185.2 20.1 %collective-permute-start.35 = (bf16[4,4,32,656]{3,2,1,0:T(8,128)(2,1)}, bf16[4,4,32,656]{3,2,1,0:T(8,128)(2,1)S(1)}, u32[]{:S(2)}, u32[]{:S(2)}) collective-permute-start(bf16[4,4,32,656]{3,2,1,0:T(8,128)(2,1)} %get-tuple-element.422), channel_id=1, source_target_pairs={{0,8},{4,12},{8,0},{12,4},{16,24},{20,28},{24,16},{28,20},{1,9},{5... | collective-permute-start | bytes 2015240 | tf_op jit(solution)/shard_map/ppermute | solution.py:682
  208.8 20.3 %collective-permute-start.38 = (bf16[2,4,32,656]{3,2,1,0:T(8,128)(2,1)S(1)}, bf16[2,4,32,656]{3,2,1,0:T(8,128)(2,1)S(1)}, u32[]{:S(2)}, u32[]{:S(2)}) collective-permute-start(bf16[2,4,32,656]{3,2,1,0:T(8,128)(2,1)S(1)} %get-tuple-element.438), channel_id=1, source_target_pairs={{0,8},{4,12},{8,0},{12,4},{16,24},{20,28},{24,16},{28,20},{1,9},{5... | collective-permute-start | bytes 1007624 | tf_op jit(solution)/shard_map/ppermute | solution.py:682
  210.6 20.3 %collective-permute-start.39 = (bf16[2,4,32,656]{3,2,1,0:T(8,128)(2,1)S(1)}, bf16[2,4,32,656]{3,2,1,0:T(8,128)(2,1)S(1)}, u32[]{:S(2)}, u32[]{:S(2)}) collective-permute-start(bf16[2,4,32,656]{3,2,1,0:T(8,128)(2,1)S(1)} %get-tuple-element.436), channel_id=1, source_target_pairs={{0,16},{4,20},{8,24},{12,28},{16,0},{20,4},{24,8},{28,12},{1,17},{... | collective-permute-start | bytes 1007624 | tf_op jit(solution)/shard_map/ppermute | solution.py:682
  210.9 20.1 %collective-permute-start.40 = (bf16[4,4,32,656]{3,2,1,0:T(8,128)(2,1)S(1)}, bf16[4,4,32,656]{3,2,1,0:T(8,128)(2,1)S(1)}, u32[]{:S(2)}, u32[]{:S(2)}) collective-permute-start(bf16[4,4,32,656]{3,2,1,0:T(8,128)(2,1)S(1)} %get-tuple-element.420), channel_id=1, source_target_pairs={{0,4},{4,0},{8,12},{12,8},{16,20},{20,16},{24,28},{28,24},{1,5},{5... | collective-permute-start | bytes 2015240 | tf_op jit(solution)/shard_map/ppermute | solution.py:682
  212.4 18.5 %collective-permute-start.41 = (bf16[256,1024]{1,0:T(8,128)(2,1)S(1)}, bf16[256,1024]{1,0:T(8,128)(2,1)S(1)}, u32[]{:S(2)}, u32[]{:S(2)}) collective-permute-start(bf16[256,1024]{1,0:T(8,128)(2,1)S(1)} %add_convert_fusion.6), channel_id=1, source_target_pairs={{0,2},{1,3},{2,0},{3,1},{4,6},{5,7},{6,4},{7,5},{8,10},{9,11},{10,... | collective-permute-start | bytes 1572872 | tf_op jit(solution)/shard_map/ppermute | solution.py:651
  232.4 27.0 %collective-permute-start.42 = (bf16[4,512,128]{2,1,0:T(8,128)(2,1)S(1)}, bf16[4,512,128]{2,1,0:T(8,128)(2,1)S(1)}, u32[]{:S(2)}, u32[]{:S(2)}) collective-permute-start(bf16[4,512,128]{2,1,0:T(8,128)(2,1)S(1)} %get-tuple-element.432), channel_id=1, source_target_pairs={{0,4},{4,0},{8,12},{12,8},{16,20},{20,16},{24,28},{28,24},{1,5},{5... | collective-permute-start | bytes 1572872 | tf_op jit(solution)/shard_map/ppermute | solution.py:682
  234.1 25.3 %collective-permute-start.43 = (bf16[1,4,32,656]{3,2,1,0:T(8,128)(2,1)S(1)}, bf16[1,4,32,656]{3,2,1,0:T(8,128)(2,1)S(1)}, u32[]{:S(2)}, u32[]{:S(2)}) collective-permute-start(bf16[1,4,32,656]{3,2,1,0:T(8,128)(2,1)S(1)} %get-tuple-element.462), channel_id=1, source_target_pairs={{0,16},{4,20},{8,24},{12,28},{16,0},{20,4},{24,8},{28,12},{1,17},{... | collective-permute-start | bytes 503816 | tf_op jit(solution)/shard_map/ppermute | solution.py:682
  236.0 23.4 %collective-permute-start.44 = (bf16[1,4,32,656]{3,2,1,0:T(8,128)(2,1)S(1)}, bf16[1,4,32,656]{3,2,1,0:T(8,128)(2,1)S(1)}, u32[]{:S(2)}, u32[]{:S(2)}) collective-permute-start(bf16[1,4,32,656]{3,2,1,0:T(8,128)(2,1)S(1)} %get-tuple-element.460), channel_id=1, source_target_pairs={{0,4},{4,0},{8,12},{12,8},{16,20},{20,16},{24,28},{28,24},{1,5},{5... | collective-permute-start | bytes 503816 | tf_op jit(solution)/shard_map/ppermute | solution.py:682
  236.9 22.4 %collective-permute-start.45 = (bf16[2,4,32,656]{3,2,1,0:T(8,128)(2,1)S(1)}, bf16[2,4,32,656]{3,2,1,0:T(8,128)(2,1)S(1)}, u32[]{:S(2)}, u32[]{:S(2)}) collective-permute-start(bf16[2,4,32,656]{3,2,1,0:T(8,128)(2,1)S(1)} %get-tuple-element.434), channel_id=1, source_target_pairs={{0,8},{4,12},{8,0},{12,4},{16,24},{20,28},{24,16},{28,20},{1,9},{5... | collective-permute-start | bytes 1007624 | tf_op jit(solution)/shard_map/ppermute | solution.py:682
  261.0 17.6 %collective-permute-start.46 = (bf16[2,512,128]{2,1,0:T(8,128)(2,1)}, bf16[2,512,128]{2,1,0:T(8,128)(2,1)}, u32[]{:S(2)}, u32[]{:S(2)}) collective-permute-start(bf16[2,512,128]{2,1,0:T(8,128)(2,1)} %get-tuple-element.454), channel_id=1, source_target_pairs={{0,8},{4,12},{8,0},{12,4},{16,24},{20,28},{24,16},{28,20},{1,9},{5... | collective-permute-start | bytes 786440 | tf_op jit(solution)/shard_map/ppermute | solution.py:682
  262.1 16.6 %collective-permute-start.47 = (bf16[4,512,128]{2,1,0:T(8,128)(2,1)S(1)}, bf16[4,512,128]{2,1,0:T(8,128)(2,1)S(1)}, u32[]{:S(2)}, u32[]{:S(2)}) collective-permute-start(bf16[4,512,128]{2,1,0:T(8,128)(2,1)S(1)} %get-tuple-element.430), channel_id=1, source_target_pairs={{0,4},{4,0},{8,12},{12,8},{16,20},{20,16},{24,28},{28,24},{1,5},{5... | collective-permute-start | bytes 1572872 | tf_op jit(solution)/shard_map/ppermute | solution.py:682
  278.8 17.8 %collective-permute-start.48 = (bf16[256,1024]{1,0:T(8,128)(2,1)}, bf16[256,1024]{1,0:T(8,128)(2,1)S(1)}, u32[]{:S(2)}, u32[]{:S(2)}) collective-permute-start(bf16[256,1024]{1,0:T(8,128)(2,1)} %get-tuple-element.363), channel_id=1, source_target_pairs={{0,1},{1,0},{2,3},{3,2},{4,5},{5,4},{6,7},{7,6},{8,9},{9,8},{10,11... | collective-permute-start | bytes 1572872 | tf_op jit(solution)/shard_map/ppermute | solution.py:651
  279.6 17.0 %collective-permute-start.52 = (bf16[2,512,128]{2,1,0:T(8,128)(2,1)S(1)}, bf16[2,512,128]{2,1,0:T(8,128)(2,1)S(1)}, u32[]{:S(2)}, u32[]{:S(2)}) collective-permute-start(bf16[2,512,128]{2,1,0:T(8,128)(2,1)S(1)} %get-tuple-element.452), channel_id=1, source_target_pairs={{0,8},{4,12},{8,0},{12,4},{16,24},{20,28},{24,16},{28,20},{1,9},{5... | collective-permute-start | bytes 786440 | tf_op jit(solution)/shard_map/ppermute | solution.py:682
  281.1 15.5 %collective-permute-start.50 = (bf16[256,1024]{1,0:T(8,128)(2,1)S(1)}, bf16[256,1024]{1,0:T(8,128)(2,1)S(1)}, u32[]{:S(2)}, u32[]{:S(2)}) collective-permute-start(bf16[256,1024]{1,0:T(8,128)(2,1)S(1)} %add_convert_fusion.4), channel_id=1, source_target_pairs={{0,2},{1,3},{2,0},{3,1},{4,6},{5,7},{6,4},{7,5},{8,10},{9,11},{10,... | collective-permute-start | bytes 1572872 | tf_op jit(solution)/shard_map/ppermute | solution.py:651
  296.7 14.6 %collective-permute-start.54 = (bf16[1,512,128]{2,1,0:T(8,128)(2,1)S(1)}, bf16[1,512,128]{2,1,0:T(8,128)(2,1)S(1)}, u32[]{:S(2)}, u32[]{:S(2)}) collective-permute-start(bf16[1,512,128]{2,1,0:T(8,128)(2,1)S(1)} %get-tuple-element.466), channel_id=1, source_target_pairs={{0,16},{4,20},{8,24},{12,28},{16,0},{20,4},{24,8},{28,12},{1,17},{... | collective-permute-start | bytes 393224 | tf_op jit(solution)/shard_map/ppermute | solution.py:682
  296.9 16.2 %collective-permute-start.55 = (bf16[1,4,32,656]{3,2,1,0:T(8,128)(2,1)S(1)}, bf16[1,4,32,656]{3,2,1,0:T(8,128)(2,1)S(1)}, u32[]{:S(2)}, u32[]{:S(2)}) collective-permute-start(bf16[1,4,32,656]{3,2,1,0:T(8,128)(2,1)S(1)} %add_convert_fusion.15), channel_id=1, source_target_pairs={{0,16},{4,20},{8,24},{12,28},{16,0},{20,4},{24,8},{28,12},{1,17},{... | collective-permute-start | bytes 503816 | tf_op jit(solution)/shard_map/ppermute | solution.py:682
  303.2 29.6 %collective-permute-start.61 = (bf16[1,128,1024]{2,1,0:T(8,128)(2,1)}, bf16[1,128,1024]{2,1,0:T(8,128)(2,1)S(1)}, u32[]{:S(2)}, u32[]{:S(2)}) collective-permute-start(bf16[1,128,1024]{2,1,0:T(8,128)(2,1)} %get-tuple-element.395), channel_id=1, source_target_pairs={{0,0},{10,1},{4,2},{14,3},{16,4},{26,5},{20,6},{30,7},{1,8},{11,9}... | collective-permute-start | bytes 786440 | tf_op jit(solution)/shard_map/ppermute | solution.py:634
  304.8 28.0 %collective-permute-start.62 = (bf16[1,128,1024]{2,1,0:T(8,128)(2,1)}, bf16[1,128,1024]{2,1,0:T(8,128)(2,1)S(1)}, u32[]{:S(2)}, u32[]{:S(2)}) collective-permute-start(bf16[1,128,1024]{2,1,0:T(8,128)(2,1)} %get-tuple-element.396), channel_id=1, source_target_pairs={{16,0},{26,1},{20,2},{30,3},{0,4},{10,5},{4,6},{14,7},{17,8},{27,9... | collective-permute-start | bytes 786440 | tf_op jit(solution)/shard_map/ppermute | solution.py:634
  313.8 18.2 %all-to-all-start.1 = ((bf16[2,4,96,128]{3,2,0,1:T(8,128)(2,1)}), bf16[2,4,96,128]{3,2,0,1:T(8,128)(2,1)S(1)}, u32[]{:S(2)}, u32[]{:S(2)}) async-start(bf16[2,4,96,128]{3,2,0,1:T(8,128)(2,1)} %copy.47), calls=%async_computation.1 | async-start | bytes 393216 | tf_op jit(solution)/shard_map/all_to_all | solution.py:1013
  326.7 18.5 %collective-permute-start.59 = (bf16[1,32,5248]{2,1,0:T(8,128)(2,1)S(1)}, bf16[1,32,5248]{2,1,0:T(8,128)(2,1)S(1)}, u32[]{:S(2)}, u32[]{:S(2)}) collective-permute-start(bf16[1,32,5248]{2,1,0:T(8,128)(2,1)S(1)} %reshape.139), channel_id=1, source_target_pairs={{0,16},{4,20},{8,24},{12,28},{16,0},{20,4},{24,8},{28,12},{1,17},{... | collective-permute-start | bytes 1007624 | tf_op jit(solution)/shard_map/ppermute | solution.py:682
  326.7 19.9 %collective-permute-start.60 = (bf16[2,4,32,656]{3,2,1,0:T(8,128)(2,1)S(1)}, bf16[2,4,32,656]{3,2,1,0:T(8,128)(2,1)S(1)}, u32[]{:S(2)}, u32[]{:S(2)}) collective-permute-start(bf16[2,4,32,656]{3,2,1,0:T(8,128)(2,1)S(1)} %constant_dynamic-update-slice_fusion), channel_id=1, source_target_pairs={{0,8},{4,12},{8,0},{12,4},{16,24},{20,28},{24,16},{28,20},{1,9},{5... | collective-permute-start | bytes 1007624 | tf_op jit(solution)/shard_map/ppermute | solution.py:682
  332.0 14.6 %collective-permute-start.58 = (bf16[1,2,512,128]{3,2,1,0:T(8,128)(2,1)S(1)}, bf16[1,2,512,128]{3,2,1,0:T(8,128)(2,1)S(1)}, u32[]{:S(2)}, u32[]{:S(2)}) collective-permute-start(bf16[1,2,512,128]{3,2,1,0:T(8,128)(2,1)S(1)} %fusion.6), channel_id=1, source_target_pairs={{0,4},{4,0},{8,12},{12,8},{16,20},{20,16},{24,28},{28,24},{1,5},{5... | collective-permute-start | bytes 786440 | tf_op jit(solution)/shard_map/ppermute | solution.py:682
  346.7 28.8 %collective-permute-start.64 = (bf16[2,32,5248]{2,1,0:T(8,128)(2,1)S(1)}, bf16[2,32,5248]{2,1,0:T(8,128)(2,1)S(1)}, u32[]{:S(2)}, u32[]{:S(2)}) collective-permute-start(bf16[2,32,5248]{2,1,0:T(8,128)(2,1)S(1)} %constant_dynamic-update-slice_fusion.4), channel_id=1, source_target_pairs={{0,8},{4,12},{8,0},{12,4},{16,24},{20,28},{24,16},{28,20},{1,9},{5... | collective-permute-start | bytes 2015240 | tf_op jit(solution)/shard_map/ppermute | solution.py:682
  346.8 29.5 %collective-permute-start.65 = (bf16[4,4,32,656]{3,2,1,0:T(8,128)(2,1)S(1)}, bf16[4,4,32,656]{3,2,1,0:T(8,128)(2,1)}, u32[]{:S(2)}, u32[]{:S(2)}) collective-permute-start(bf16[4,4,32,656]{3,2,1,0:T(8,128)(2,1)S(1)} %constant_dynamic-update-slice_fusion.6), channel_id=1, source_target_pairs={{0,4},{4,0},{8,12},{12,8},{16,20},{20,16},{24,28},{28,24},{1,5},{5... | collective-permute-start | bytes 2015240 | tf_op jit(solution)/shard_map/ppermute | solution.py:682
  347.0 26.5 %collective-permute-start.63 = (bf16[2,2,512,128]{3,2,1,0:T(8,128)(2,1)S(1)}, bf16[2,2,512,128]{3,2,1,0:T(8,128)(2,1)S(1)}, u32[]{:S(2)}, u32[]{:S(2)}) collective-permute-start(bf16[2,2,512,128]{3,2,1,0:T(8,128)(2,1)S(1)} %constant_dynamic-update-slice_fusion.2), channel_id=1, source_target_pairs={{0,16},{4,20},{8,24},{12,28},{16,0},{20,4},{24,8},{28,12},{1,17},{... | collective-permute-start | bytes 1572872 | tf_op jit(solution)/shard_map/ppermute | solution.py:682
  349.3 32.5 %collective-permute-start.56 = (bf16[1,128,1024]{2,1,0:T(8,128)(2,1)}, bf16[1,128,1024]{2,1,0:T(8,128)(2,1)}, u32[]{:S(2)}, u32[]{:S(2)}) collective-permute-start(bf16[1,128,1024]{2,1,0:T(8,128)(2,1)} %get-tuple-element.382), channel_id=1, source_target_pairs={{16,0},{26,1},{20,2},{30,3},{0,4},{10,5},{4,6},{14,7},{17,8},{27,9... | collective-permute-start | bytes 786440 | tf_op jit(solution)/shard_map/ppermute | solution.py:634
  353.0 28.8 %collective-permute-start.57 = (bf16[1,128,1024]{2,1,0:T(8,128)(2,1)}, bf16[1,128,1024]{2,1,0:T(8,128)(2,1)}, u32[]{:S(2)}, u32[]{:S(2)}) collective-permute-start(bf16[1,128,1024]{2,1,0:T(8,128)(2,1)} %get-tuple-element.383), channel_id=1, source_target_pairs={{0,0},{10,1},{4,2},{14,3},{16,4},{26,5},{20,6},{30,7},{1,8},{11,9}... | collective-permute-start | bytes 786440 | tf_op jit(solution)/shard_map/ppermute | solution.py:634
  377.5 34.2 %collective-permute-start.67 = (bf16[4,32,5248]{2,1,0:T(8,128)(2,1)S(1)}, bf16[4,32,5248]{2,1,0:T(8,128)(2,1)S(1)}, u32[]{:S(2)}, u32[]{:S(2)}) collective-permute-start(bf16[4,32,5248]{2,1,0:T(8,128)(2,1)S(1)} %constant_dynamic-update-slice_fusion.10.sums), channel_id=1, source_target_pairs={{0,4},{4,0},{8,12},{12,8},{16,20},{20,16},{24,28},{28,24},{1,5},{5... | collective-permute-start | bytes 4030472 | tf_op jit(solution)/shard_map/ppermute | solution.py:682
  381.6 24.4 %collective-permute-start.66 = (bf16[4,2,512,128]{3,2,1,0:T(8,128)(2,1)}, bf16[4,2,512,128]{3,2,1,0:T(8,128)(2,1)}, u32[]{:S(2)}, u32[]{:S(2)}) collective-permute-start(bf16[4,2,512,128]{3,2,1,0:T(8,128)(2,1)} %constant_dynamic-update-slice_fusion.8.low), channel_id=1, source_target_pairs={{0,8},{4,12},{8,0},{12,4},{16,24},{20,28},{24,16},{28,20},{1,9},{5... | collective-permute-start | bytes 3145736 | tf_op jit(solution)/shard_map/ppermute | solution.py:682
  (82 other events, 703.2 us)
